TPU v7x, 32 devices: a whole 2x2x4 slice. The times are simulated.
32 devices in a mesh: section: 2 (over core), tensor: 4 (over z), dp: 4 (over y, x).
Axes of the slice: x: 2, y: 2, z: 4, core: 2. Of those that a mesh axis runs over, the one named last changes fastest.
Arguments:
- inputs: bfloat16 [2, 2560, 2048], P(None, 'dp'), may hold values from -6 to 6
- cotangent: bfloat16 [2, 2560, 2048], P(None, 'dp'), may hold values from -6 to 6
- seg_ids: int32 [2, 2560], replicated, may hold values from 0 to 12, as said below
- positions: int32 [2, 2560], replicated, may hold values from 0 to 1343, as said below
- parents: int32 [2, 13], replicated, may hold values from 0 to 12, as said below
- gain_attn: float32 [2, 2048], P('section', 'dp'), may hold values from 0.5 to 1.5
- w_query: float32 [2, 2048, 2048], P('section', 'dp', 'tensor'), may hold values from -0.125 to 0.125
- key_weight: float32 [2, 2048, 256], P('section', 'dp', 'tensor'), may hold values from -0.125 to 0.125
- value_weight: float32 [2, 2048, 256], P('section', 'dp', 'tensor'), may hold values from -0.125 to 0.125
- w_out: float32 [2, 2048, 2048], P('section', 'tensor', 'dp'), may hold values from -1 to 1
- gain_mlp: float32 [2, 2048], P('section', 'dp'), may hold values from 0.5 to 1.5
- w_gate: float32 [2, 2048, 5632], P('section', 'dp', 'tensor'), may hold values from -0.125 to 0.125
- w_up: float32 [2, 2048, 5632], P('section', 'dp', 'tensor'), may hold values from -0.125 to 0.125
- w_down: float32 [2, 5632, 2048], P('section', 'tensor', 'dp'), may hold values from -0.078125 to 0.078125
Outputs:
- layer_output: bfloat16 [2, 2, 2560, 2048], P('section', None, 'dp')
- input_grad: float32 [2, 2, 2560, 2048], P('section', None, 'dp')
- grad_gain_attn: float32 [2, 2048], P('section', 'dp')
- grad_w_query: float32 [2, 2048, 2048], P('section', 'dp', 'tensor')
- grad_w_key: float32 [2, 2048, 256], P('section', 'dp', 'tensor')
- grad_w_value: float32 [2, 2048, 256], P('section', 'dp', 'tensor')
- grad_w_out: float32 [2, 2048, 2048], P('section', 'tensor', 'dp')
- grad_gain_mlp: float32 [2, 2048], P('section', 'dp')
- grad_w_gate: float32 [2, 2048, 5632], P('section', 'dp', 'tensor')
- grad_w_up: float32 [2, 2048, 5632], P('section', 'dp', 'tensor')
- grad_w_down: float32 [2, 5632, 2048], P('section', 'tensor', 'dp')
Inputs may be any that keep to these rules, and one draw needn't show every extreme that they name: `seg_ids`: each tree is a trunk of 1024 tokens followed by 4 groups of 384 tokens, each group a branch and then its two leaves with varying lengths; segment numbers label the tree's segments in a drawn order. `positions`: positions count along the trunk from 0 and go on along the branch and then the leaf. `parents`: the trunk's entry is its own number, a branch's is the trunk's, a leaf's is its branch's.
All inputs are finite; a program needn't handle non-finite values.
Results may differ from a plain program's by a relative error of at most 0.03.
Values may be sent and summed in bfloat16 or wider, within the bound.
A program may use at most 512 MiB of HBM per device.

v0:
```python
import jax
import jax.numpy as jnp
from jax import lax
from jax.sharding import PartitionSpec as P

HEAD_DIMENSION = 64


EPSILON = 1e-05
THETA = 10000.0
MASKED = -1e30


def passed_along(x, axis, by):
    devices = lax.axis_size(axis)
    pairs = [(i, i + by) for i in range(devices) if 0 <= i + by < devices]
    return lax.ppermute(x, axis, pairs)


def rope_tables(position_rows, head_size):
    half_dim = head_size // 2
    frequency = THETA ** (-(jnp.arange(half_dim, dtype=jnp.float32) * 2.0 / head_size))
    angles = position_rows.astype(jnp.float32)[:, None] * frequency[None, :]
    return (jnp.cos(angles)[:, None, :], jnp.sin(angles)[:, None, :])


def apply_rotary(rotated_in, cosine_table, sine_values):
    half_dim = rotated_in.shape[-1] // 2
    first_half = rotated_in[..., :half_dim]
    second_half = rotated_in[..., half_dim:]
    return jnp.concatenate(
        [
            first_half * cosine_table - second_half * sine_values,
            second_half * cosine_table + first_half * sine_values,
        ],
        -1,
    )


def rotate_back(grad_in, cosine_table, sine_values):
    half_dim = grad_in.shape[-1] // 2
    first_half = grad_in[..., :half_dim]
    second_half = grad_in[..., half_dim:]
    return jnp.concatenate(
        [
            first_half * cosine_table + second_half * sine_values,
            second_half * cosine_table - first_half * sine_values,
        ],
        -1,
    )


def inverse_rms(hidden):
    return lax.rsqrt(jnp.mean(hidden * hidden, -1, keepdims=True) + EPSILON)


def norm_back(grad_normed, hidden, scale_rows, gain_full):
    unit_rows = hidden * scale_rows
    grad_unit = grad_normed * gain_full
    grad_hidden = scale_rows * (
        grad_unit - unit_rows * jnp.mean(grad_unit * unit_rows, -1, keepdims=True)
    )
    return (grad_hidden, jnp.sum(grad_normed * unit_rows, 0))


def path_mask(segment_all, position_all, parent_row, row_start, row_count):
    seg_count = parent_row.shape[0]
    labels = jnp.arange(seg_count, dtype=jnp.int32)
    parent_hot = (parent_row[:, None] == labels[None, :]).astype(jnp.float32)
    ancestry = jnp.eye(seg_count, dtype=jnp.float32) + parent_hot + jnp.dot(parent_hot, parent_hot)
    ancestry = (ancestry > 0.5).astype(jnp.float32)
    segment_rows = lax.dynamic_slice_in_dim(segment_all, row_start, row_count, 0)
    position_rows = lax.dynamic_slice_in_dim(position_all, row_start, row_count, 0)
    query_hot = (segment_rows[:, None] == labels[None, :]).astype(jnp.float32)
    key_hot = (segment_all[:, None] == labels[None, :]).astype(jnp.float32)
    reachable = jnp.dot(jnp.dot(query_hot, ancestry), key_hot.T)
    return ((reachable > 0.5) & (position_all[None, :] <= position_rows[:, None]), position_rows)


def split_packed(packed_all, key_heads, head_size):
    span = key_heads * head_size
    key_all = packed_all[:, :span].reshape(-1, key_heads, head_size)
    value_all = packed_all[:, span:].reshape(-1, key_heads, head_size)
    return (key_all, value_all)


def score_block(query_groups, key_all, path_allow, score_scale):
    scores = (
        jnp.einsum("tkgd,skd->kgts", query_groups, key_all, preferred_element_type=jnp.float32)
        * score_scale
    )
    return jnp.where(path_allow[None, None], scores, MASKED)


def project_queries(first_normed, w_query, cosine_table, sine_values, key_heads, head_size):
    row_count = first_normed.shape[0]
    projected = jnp.dot(first_normed, w_query, preferred_element_type=jnp.float32)
    query_heads = projected.shape[1] // head_size
    turned = apply_rotary(
        projected.reshape(row_count, query_heads, head_size), cosine_table, sine_values
    ).astype(jnp.bfloat16)
    return turned.reshape(row_count, key_heads, query_heads // key_heads, head_size)


def layer_forward(layer_in, weights, path_allow, cosine_table, sine_values, head_size):
    gain_one, w_query, key_weight, value_weight, w_out, gain_two, w_gate, w_up, w_down = weights
    row_count = layer_in.shape[0]
    key_heads = key_weight.shape[1] // head_size
    hidden = layer_in.astype(jnp.float32)
    scale_one = inverse_rms(hidden)
    first_normed = (hidden * scale_one * gain_one.astype(jnp.float32)).astype(jnp.bfloat16)
    query_groups = project_queries(
        first_normed, w_query, cosine_table, sine_values, key_heads, head_size
    )
    key_matrix = apply_rotary(
        jnp.dot(first_normed, key_weight, preferred_element_type=jnp.float32).reshape(
            row_count, key_heads, head_size
        ),
        cosine_table,
        sine_values,
    )
    key_matrix = key_matrix.astype(jnp.bfloat16).reshape(row_count, key_heads * head_size)
    value_matrix = jnp.dot(first_normed, value_weight, preferred_element_type=jnp.float32).astype(
        jnp.bfloat16
    )
    packed_all = lax.all_gather(
        jnp.concatenate([key_matrix, value_matrix], 1), "dp", axis=0, tiled=True
    )
    key_all, value_all = split_packed(packed_all, key_heads, head_size)
    scores = score_block(query_groups, key_all, path_allow, head_size ** (-0.5))
    row_max = jnp.max(scores, -1, keepdims=True)
    exponent = jnp.exp(scores - row_max)
    row_sum = jnp.sum(exponent, -1, keepdims=True)
    attn_probs = (exponent / row_sum).astype(jnp.bfloat16)
    log_sum = row_max + jnp.log(row_sum)
    context = jnp.einsum(
        "kgts,skd->tkgd", attn_probs, value_all, preferred_element_type=jnp.float32
    )
    context = context.reshape(row_count, -1).astype(jnp.bfloat16)
    attn_part = jnp.dot(context, w_out, preferred_element_type=jnp.float32)
    gain_two_full = gain_two.astype(jnp.float32)
    middle = hidden + lax.psum(attn_part.astype(jnp.bfloat16), "tensor").astype(jnp.float32)
    scale_two = inverse_rms(middle)
    normed_two = (middle * scale_two * gain_two_full).astype(jnp.bfloat16)
    gate_proj = jnp.dot(normed_two, w_gate, preferred_element_type=jnp.float32)
    up_proj = jnp.dot(normed_two, w_up, preferred_element_type=jnp.float32)
    inner_act = (gate_proj * jax.nn.sigmoid(gate_proj) * up_proj).astype(jnp.bfloat16)
    mlp_part = jnp.dot(inner_act, w_down, preferred_element_type=jnp.float32)
    result = (
        middle + lax.psum(mlp_part.astype(jnp.bfloat16), "tensor").astype(jnp.float32)
    ).astype(jnp.bfloat16)
    kept = (middle,)
    return (result, kept, log_sum, packed_all)


def layer_backward(
    layer_in,
    grad_out,
    weights,
    path_allow,
    cosine_table,
    sine_values,
    head_size,
    kept,
    log_sum,
    packed_all,
):
    gain_one, w_query, key_weight, value_weight, w_out, gain_two, w_gate, w_up, w_down = weights
    row_count = layer_in.shape[0]
    key_heads = key_weight.shape[1] // head_size
    score_scale = head_size ** (-0.5)
    hidden = layer_in.astype(jnp.float32)
    scale_one = inverse_rms(hidden)
    gain_one_full = gain_one.astype(jnp.float32)
    first_normed = (hidden * scale_one * gain_one_full).astype(jnp.bfloat16)
    query_groups = project_queries(
        first_normed, w_query, cosine_table, sine_values, key_heads, head_size
    )
    key_all, value_all = split_packed(packed_all, key_heads, head_size)
    scores = score_block(query_groups, key_all, path_allow, score_scale)
    probs_full = jnp.exp(scores - log_sum)
    attn_probs = probs_full.astype(jnp.bfloat16)
    context = jnp.einsum(
        "kgts,skd->tkgd", attn_probs, value_all, preferred_element_type=jnp.float32
    )
    context = context.reshape(row_count, -1).astype(jnp.bfloat16)
    gain_two_full = gain_two.astype(jnp.float32)
    middle = kept[0]
    scale_two = inverse_rms(middle)
    normed_two = (middle * scale_two * gain_two_full).astype(jnp.bfloat16)
    gate_proj = jnp.dot(normed_two, w_gate, preferred_element_type=jnp.float32)
    up_proj = jnp.dot(normed_two, w_up, preferred_element_type=jnp.float32)
    sigmoid_gate = jax.nn.sigmoid(gate_proj)
    silu_gate = gate_proj * sigmoid_gate
    inner_act = (silu_gate * up_proj).astype(jnp.bfloat16)
    grad_branch = grad_out.astype(jnp.bfloat16)
    grad_w_down = jnp.einsum(
        "ti,tj->ij", inner_act, grad_branch, preferred_element_type=jnp.float32
    )
    grad_inner = jnp.einsum("tj,ij->ti", grad_branch, w_down, preferred_element_type=jnp.float32)
    grad_gate = (
        grad_inner * up_proj * sigmoid_gate * (1.0 + gate_proj * (1.0 - sigmoid_gate))
    ).astype(jnp.bfloat16)
    grad_up = (grad_inner * silu_gate).astype(jnp.bfloat16)
    grad_w_gate = jnp.einsum("ti,tj->ij", normed_two, grad_gate, preferred_element_type=jnp.float32)
    grad_w_up = jnp.einsum("ti,tj->ij", normed_two, grad_up, preferred_element_type=jnp.float32)
    normed_two_part = jnp.einsum("tj,ij->ti", grad_gate, w_gate, preferred_element_type=jnp.float32)
    normed_two_part = normed_two_part + jnp.einsum(
        "tj,ij->ti", grad_up, w_up, preferred_element_type=jnp.float32
    )
    grad_normed_two = lax.psum(normed_two_part.astype(jnp.bfloat16), "tensor").astype(jnp.float32)
    grad_middle_norm, grad_gain_two = norm_back(grad_normed_two, middle, scale_two, gain_two_full)
    grad_middle = grad_out + grad_middle_norm
    grad_attn = grad_middle.astype(jnp.bfloat16)
    grad_w_out = jnp.einsum("ti,tj->ij", context, grad_attn, preferred_element_type=jnp.float32)
    grad_context = jnp.einsum("tj,ij->ti", grad_attn, w_out, preferred_element_type=jnp.float32)
    grad_context = grad_context.astype(jnp.bfloat16).reshape(query_groups.shape)
    grad_probs = jnp.einsum(
        "tkgd,skd->kgts", grad_context, value_all, preferred_element_type=jnp.float32
    )
    grad_value_all = jnp.einsum(
        "kgts,tkgd->skd", attn_probs, grad_context, preferred_element_type=jnp.float32
    )
    inner_sum = jnp.sum(probs_full * grad_probs, -1, keepdims=True)
    grad_scores = (probs_full * (grad_probs - inner_sum)).astype(jnp.bfloat16)
    grad_queries = (
        jnp.einsum("kgts,skd->tkgd", grad_scores, key_all, preferred_element_type=jnp.float32)
        * score_scale
    )
    grad_key_all = (
        jnp.einsum("kgts,tkgd->skd", grad_scores, query_groups, preferred_element_type=jnp.float32)
        * score_scale
    )
    grad_key_rows, grad_value_rows = (
        lax.psum_scatter(
            grad_key_all.astype(jnp.bfloat16), "dp", scatter_dimension=0, tiled=True
        ).astype(jnp.float32),
        lax.psum_scatter(
            grad_value_all.astype(jnp.bfloat16), "dp", scatter_dimension=0, tiled=True
        ).astype(jnp.float32),
    )
    grad_query = rotate_back(
        grad_queries.reshape(row_count, -1, head_size), cosine_table, sine_values
    )
    grad_query = grad_query.reshape(row_count, -1).astype(jnp.bfloat16)
    grad_key = (
        rotate_back(grad_key_rows, cosine_table, sine_values)
        .reshape(row_count, -1)
        .astype(jnp.bfloat16)
    )
    grad_value = grad_value_rows.reshape(row_count, -1).astype(jnp.bfloat16)
    grad_w_query = jnp.einsum(
        "ti,tj->ij", first_normed, grad_query, preferred_element_type=jnp.float32
    )
    grad_w_key = jnp.einsum("ti,tj->ij", first_normed, grad_key, preferred_element_type=jnp.float32)
    grad_w_value = jnp.einsum(
        "ti,tj->ij", first_normed, grad_value, preferred_element_type=jnp.float32
    )
    normed_one_part = jnp.einsum(
        "tj,ij->ti", grad_query, w_query, preferred_element_type=jnp.float32
    )
    normed_one_part = normed_one_part + jnp.einsum(
        "tj,ij->ti", grad_key, key_weight, preferred_element_type=jnp.float32
    )
    normed_one_part = normed_one_part + jnp.einsum(
        "tj,ij->ti", grad_value, value_weight, preferred_element_type=jnp.float32
    )
    grad_normed_one = lax.psum(normed_one_part.astype(jnp.bfloat16), "tensor").astype(jnp.float32)
    grad_hidden_norm, grad_gain_one = norm_back(grad_normed_one, hidden, scale_one, gain_one_full)
    grad_input = grad_middle + grad_hidden_norm
    return (
        grad_input,
        (
            grad_gain_one,
            grad_w_query,
            grad_w_key,
            grad_w_value,
            grad_w_out,
            grad_gain_two,
            grad_w_gate,
            grad_w_up,
            grad_w_down,
        ),
    )


def pick_slot(buffer, slot_index):
    return lax.dynamic_index_in_dim(buffer, slot_index, 0, keepdims=False)


def place_slot(buffer, new_value, slot_index, is_valid):
    old_value = pick_slot(buffer, slot_index)
    return lax.dynamic_update_index_in_dim(
        buffer, jnp.where(is_valid, new_value, old_value), slot_index, 0
    )


def shards(
    inputs,
    cotangent,
    seg_ids,
    positions,
    parents,
    gain_attn,
    w_query,
    key_weight,
    value_weight,
    w_out,
    gain_mlp,
    w_gate,
    w_up,
    w_down,
):
    section_index = lax.axis_index("section")
    data_index = lax.axis_index("dp")
    micro_count = inputs.shape[0]
    row_count = inputs.shape[1]
    model_width = inputs.shape[2]
    tree_len = seg_ids.shape[1]
    row_start = data_index * row_count
    key_heads = key_weight.shape[2] // HEAD_DIMENSION
    query_heads = w_query.shape[2] // HEAD_DIMENSION
    packed_width = 2 * key_weight.shape[2]
    is_first = section_index == 0
    weights = (
        lax.all_gather(gain_attn[0].astype(jnp.bfloat16), "dp", axis=0, tiled=True),
        lax.all_gather(w_query[0].astype(jnp.bfloat16), "dp", axis=0, tiled=True),
        lax.all_gather(key_weight[0].astype(jnp.bfloat16), "dp", axis=0, tiled=True),
        lax.all_gather(value_weight[0].astype(jnp.bfloat16), "dp", axis=0, tiled=True),
        lax.all_gather(w_out[0].astype(jnp.bfloat16), "dp", axis=1, tiled=True),
        lax.all_gather(gain_mlp[0].astype(jnp.bfloat16), "dp", axis=0, tiled=True),
        lax.all_gather(w_gate[0].astype(jnp.bfloat16), "dp", axis=0, tiled=True),
        lax.all_gather(w_up[0].astype(jnp.bfloat16), "dp", axis=0, tiled=True),
        lax.all_gather(w_down[0].astype(jnp.bfloat16), "dp", axis=1, tiled=True),
    )

    def tables(micro_index):
        segment_all = pick_slot(seg_ids, micro_index)
        position_all = pick_slot(positions, micro_index)
        parent_row = pick_slot(parents, micro_index)
        path_allow, position_rows = path_mask(
            segment_all, position_all, parent_row, row_start, row_count
        )
        cosine_table, sine_values = rope_tables(position_rows, HEAD_DIMENSION)
        return (path_allow, cosine_table, sine_values)

    accumulated = tuple((jnp.zeros(member.shape, jnp.float32) for member in weights))
    kept_start = (jnp.zeros((micro_count, row_count, model_width), jnp.float32),)
    loop_start = (
        jnp.zeros((row_count, model_width), jnp.bfloat16),
        jnp.zeros((row_count, model_width), jnp.bfloat16),
        kept_start,
        jnp.zeros((micro_count, key_heads, query_heads // key_heads, row_count, 1), jnp.float32),
        jnp.zeros((micro_count, tree_len, packed_width), jnp.bfloat16),
        jnp.zeros((micro_count, row_count, model_width), jnp.bfloat16),
        jnp.zeros((micro_count, row_count, model_width), jnp.float32),
        accumulated,
    )

    def advance(tick_index, loop_state):
        (
            arrived_acts,
            arrived_grads,
            kept_buffer,
            logsum_buffer,
            packed_buffer,
            output_buffer,
            grad_buffer,
            totals,
        ) = loop_state
        forward_micro = jnp.where(is_first, tick_index, tick_index - 1)
        forward_valid = (forward_micro >= 0) & (forward_micro < micro_count)
        forward_slot = jnp.clip(forward_micro, 0, micro_count - 1)
        forward_in = jnp.where(is_first, pick_slot(inputs, forward_slot), arrived_acts)
        path_allow, cosine_table, sine_values = tables(forward_slot)
        sent_rows, kept, log_sum, packed_all = layer_forward(
            forward_in, weights, path_allow, cosine_table, sine_values, HEAD_DIMENSION
        )
        output_buffer = place_slot(output_buffer, sent_rows, forward_slot, forward_valid)
        kept_buffer = tuple(
            (
                place_slot(buffer, member, forward_slot, forward_valid)
                for buffer, member in zip(kept_buffer, kept)
            )
        )
        logsum_buffer = place_slot(logsum_buffer, log_sum, forward_slot, forward_valid)
        packed_buffer = place_slot(packed_buffer, packed_all, forward_slot, forward_valid)
        backward_micro = jnp.where(is_first, tick_index - 2, tick_index - 1)
        backward_valid = (backward_micro >= 0) & (backward_micro < micro_count)
        backward_slot = jnp.clip(backward_micro, 0, micro_count - 1)
        backward_in = jnp.where(is_first, pick_slot(inputs, backward_slot), forward_in)
        backward_grad = jnp.where(
            is_first, arrived_grads, pick_slot(cotangent, backward_slot)
        ).astype(jnp.float32)
        back_allow, back_cosine, back_sine = tables(backward_slot)
        kept_back = tuple((pick_slot(buffer, backward_slot) for buffer in kept_buffer))
        grad_input, grad_terms = layer_backward(
            backward_in,
            backward_grad,
            weights,
            back_allow,
            back_cosine,
            back_sine,
            HEAD_DIMENSION,
            kept_back,
            pick_slot(logsum_buffer, backward_slot),
            pick_slot(packed_buffer, backward_slot),
        )
        grad_buffer = place_slot(grad_buffer, grad_input, backward_slot, backward_valid)
        keep_factor = backward_valid.astype(jnp.float32)
        totals = tuple(
            (
                total_term + keep_factor * grad_term
                for total_term, grad_term in zip(totals, grad_terms)
            )
        )
        arrived_acts = passed_along(sent_rows, "section", 1)
        arrived_grads = passed_along(grad_input.astype(jnp.bfloat16), "section", -1)
        return (
            arrived_acts,
            arrived_grads,
            kept_buffer,
            logsum_buffer,
            packed_buffer,
            output_buffer,
            grad_buffer,
            totals,
        )

    finished = lax.fori_loop(0, micro_count + 2, advance, loop_start)
    totals = finished[7]
    shares = (
        lax.psum_scatter(
            totals[0].astype(jnp.bfloat16), "dp", scatter_dimension=0, tiled=True
        ).astype(jnp.float32),
        lax.psum_scatter(
            totals[1].astype(jnp.bfloat16), "dp", scatter_dimension=0, tiled=True
        ).astype(jnp.float32),
        lax.psum_scatter(
            totals[2].astype(jnp.bfloat16), "dp", scatter_dimension=0, tiled=True
        ).astype(jnp.float32),
        lax.psum_scatter(
            totals[3].astype(jnp.bfloat16), "dp", scatter_dimension=0, tiled=True
        ).astype(jnp.float32),
        lax.psum_scatter(
            totals[4].astype(jnp.bfloat16), "dp", scatter_dimension=1, tiled=True
        ).astype(jnp.float32),
        lax.psum_scatter(
            totals[5].astype(jnp.bfloat16), "dp", scatter_dimension=0, tiled=True
        ).astype(jnp.float32),
        lax.psum_scatter(
            totals[6].astype(jnp.bfloat16), "dp", scatter_dimension=0, tiled=True
        ).astype(jnp.float32),
        lax.psum_scatter(
            totals[7].astype(jnp.bfloat16), "dp", scatter_dimension=0, tiled=True
        ).astype(jnp.float32),
        lax.psum_scatter(
            totals[8].astype(jnp.bfloat16), "dp", scatter_dimension=1, tiled=True
        ).astype(jnp.float32),
    )
    return (
        finished[5][None],
        finished[6][None],
        shares[0][None],
        shares[1][None],
        shares[2][None],
        shares[3][None],
        shares[4][None],
        shares[5][None],
        shares[6][None],
        shares[7][None],
        shares[8][None],
    )


def solution(mesh):
    in_specs = (
        P(None, "dp", None),
        P(None, "dp", None),
        P(),
        P(),
        P(),
        P("section", "dp"),
        P("section", "dp", "tensor"),
        P("section", "dp", "tensor"),
        P("section", "dp", "tensor"),
        P("section", "tensor", "dp"),
        P("section", "dp"),
        P("section", "dp", "tensor"),
        P("section", "dp", "tensor"),
        P("section", "tensor", "dp"),
    )
    out_specs = (
        P("section", None, "dp", None),
        P("section", None, "dp", None),
        P("section", "dp"),
        P("section", "dp", "tensor"),
        P("section", "dp", "tensor"),
        P("section", "dp", "tensor"),
        P("section", "tensor", "dp"),
        P("section", "dp"),
        P("section", "dp", "tensor"),
        P("section", "dp", "tensor"),
        P("section", "tensor", "dp"),
    )
    return jax.shard_map(shards, mesh=mesh, in_specs=in_specs, out_specs=out_specs, check_vma=False)
```

profile of v0, /device:TPU:1, one launch (start us, length us, event | category | flops | bytes accessed | tf_op | source)
XLA Modules:
  0.0 3804.0 jit_solution(16127515303362760340)
XLA Ops:
  50.9 37.5 all-gather.17.cloned.1.call-done
  88.4 68.3 %all-gather.19.cloned.1.call-done = bf16[1,2048,1408]{2,1,0:T(8,128)(2,1)} async-done(((bf16[1,512,1408]{2,1,0:T(8,128)(2,1)}), bf16[1,2048,1408]{2,1,0:T(8,128)(2,1)}) %all-gather.19.cloned.1.call-update) | async-done | bytes 5767184 | tf_op jit(solution)/shard_map/all_gather | solution.py:332
  156.6 68.1 %all-gather.21.cloned.1.call-done = bf16[1,2048,1408]{2,1,0:T(8,128)(2,1)} async-done(((bf16[1,512,1408]{2,1,0:T(8,128)(2,1)}), bf16[1,2048,1408]{2,1,0:T(8,128)(2,1)}) %all-gather.21.cloned.1.call-update) | async-done | bytes 5767184 | tf_op jit(solution)/shard_map/all_gather | solution.py:333
  224.7 67.9 %all-gather.23.cloned.1.call-done = bf16[1,1408,2048]{2,1,0:T(8,128)(2,1)} async-done(((bf16[1,1408,512]{2,1,0:T(8,128)(2,1)}), bf16[1,1408,2048]{2,1,0:T(8,128)(2,1)}) %all-gather.23.cloned.1.call-update) | async-done | bytes 5767184 | tf_op jit(solution)/shard_map/all_gather | solution.py:334
  311.8 3142.9 %while.47 = (s32[]{:T(128)}, bf16[640,2048]{1,0:T(8,128)(2,1)}, bf16[640,2048]{1,0:T(8,128)(2,1)}, f32[2,640,2048]{2,1,0:T(8,128)}, f32[2,1,8,640,1]{3,2,4,1,0:T...) while((s32[]{:T(128)}, bf16[640,2048]{1,0:T(8,128)(2,1)}, ...), condition=%wide.region_18.19_spmd.clone, body=%wide.region_0.18_spmd.clone.sunk | while | flops 65157103616 | bytes 1747576704 | solution.py:430
  482.0 42.8 %all-reduce.10.cloned.1.call-done = bf16[640,2048]{1,0:T(8,128)(2,1)} async-done(((bf16[640,2048]{1,0:T(8,128)(2,1)}), bf16[640,2048]{1,0:T(8,128)(2,1)}) %all-reduce.10.cloned.1.call-update) | async-done | bytes 2621456 | tf_op jit(solution)/shard_map/while/body/eval_jaxpr/psum | solution.py:142
  602.7 74.5 %all-reduce.12.cloned.1.call-done = bf16[640,2048]{1,0:T(8,128)(2,1)} async-done(((bf16[640,2048]{1,0:T(8,128)(2,1)}), bf16[640,2048]{1,0:T(8,128)(2,1)}) %all-reduce.12.cloned.1.call-update) | async-done | bytes 2621456 | tf_op jit(solution)/shard_map/while/body/eval_jaxpr/psum | solution.py:211
  689.7 35.3 fusion.313
  745.1 41.7 %fusion.314 = bf16[8,640,2560]{1,2,0:T(8,128)(2,1)} fusion(f32[2560,640,8]{1,0,2:T(8,128)} %get-tuple-element.1409, f32[2560,640,8]{1,0,2:T(8,128)} %fusion.304, f32[8,640]{1,0:T(8,128)S(1)} %get-tuple-element.1410, f32[8,640]{1,0:T(8,128)S(1)} %dynamic-slice_bitcast_fusion.5, pred[640,2560]{0,1:T(8,128)(4,1)S(1)} %copy-done.6), kind=kLoop, calls=%fused_computation.15.clone.1 | loop fusion | flops 78643200 | bytes 132751360 | tf_op jit(solution)/shard_map/reshape.606
  842.1 23.4 reduce-scatter.34.cloned.1.call-done
  916.9 144.6 %all-reduce.14.cloned.1.call-done = (bf16[640,2048]{1,0:T(8,128)(2,1)}, bf16[640,2048]{1,0:T(8,128)(2,1)}) async-done(((bf16[640,2048]{1,0:T(8,128)(2,1)}, bf16[640,2048]{1,0:T(8,128)(2,1)}), (bf16[640,2048]{1,0:T(8,128)(2,1)}, bf16[640,2048]{1,0:T(8,128)(2,1)})) %all-reduce.14.cloned.1.call-update) | async-done | bytes 5242896 | tf_op jit(solution)/shard_map/while/body/eval_jaxpr/psum | solution.py:150
  1266.6 41.6 %all-reduce.10.cloned.1.call-done = bf16[640,2048]{1,0:T(8,128)(2,1)} async-done(((bf16[640,2048]{1,0:T(8,128)(2,1)}), bf16[640,2048]{1,0:T(8,128)(2,1)}) %all-reduce.10.cloned.1.call-update) | async-done | bytes 2621456 | tf_op jit(solution)/shard_map/while/body/eval_jaxpr/psum | solution.py:142
  1386.1 74.4 %all-reduce.12.cloned.1.call-done = bf16[640,2048]{1,0:T(8,128)(2,1)} async-done(((bf16[640,2048]{1,0:T(8,128)(2,1)}), bf16[640,2048]{1,0:T(8,128)(2,1)}) %all-reduce.12.cloned.1.call-update) | async-done | bytes 2621456 | tf_op jit(solution)/shard_map/while/body/eval_jaxpr/psum | solution.py:211
  1473.0 35.3 fusion.313
  1528.4 41.7 %fusion.314 = bf16[8,640,2560]{1,2,0:T(8,128)(2,1)} fusion(f32[2560,640,8]{1,0,2:T(8,128)} %get-tuple-element.1409, f32[2560,640,8]{1,0,2:T(8,128)} %fusion.304, f32[8,640]{1,0:T(8,128)S(1)} %get-tuple-element.1410, f32[8,640]{1,0:T(8,128)S(1)} %dynamic-slice_bitcast_fusion.5, pred[640,2560]{0,1:T(8,128)(4,1)S(1)} %copy-done.6), kind=kLoop, calls=%fused_computation.15.clone.1 | loop fusion | flops 78643200 | bytes 132751360 | tf_op jit(solution)/shard_map/reshape.606
  1707.2 137.4 %all-reduce.14.cloned.1.call-done = (bf16[640,2048]{1,0:T(8,128)(2,1)}, bf16[640,2048]{1,0:T(8,128)(2,1)}) async-done(((bf16[640,2048]{1,0:T(8,128)(2,1)}, bf16[640,2048]{1,0:T(8,128)(2,1)}), (bf16[640,2048]{1,0:T(8,128)(2,1)}, bf16[640,2048]{1,0:T(8,128)(2,1)})) %all-reduce.14.cloned.1.call-update) | async-done | bytes 5242896 | tf_op jit(solution)/shard_map/while/body/eval_jaxpr/psum | solution.py:150
  2051.0 41.6 %all-reduce.10.cloned.1.call-done = bf16[640,2048]{1,0:T(8,128)(2,1)} async-done(((bf16[640,2048]{1,0:T(8,128)(2,1)}), bf16[640,2048]{1,0:T(8,128)(2,1)}) %all-reduce.10.cloned.1.call-update) | async-done | bytes 2621456 | tf_op jit(solution)/shard_map/while/body/eval_jaxpr/psum | solution.py:142
  2170.4 74.5 %all-reduce.12.cloned.1.call-done = bf16[640,2048]{1,0:T(8,128)(2,1)} async-done(((bf16[640,2048]{1,0:T(8,128)(2,1)}), bf16[640,2048]{1,0:T(8,128)(2,1)}) %all-reduce.12.cloned.1.call-update) | async-done | bytes 2621456 | tf_op jit(solution)/shard_map/while/body/eval_jaxpr/psum | solution.py:211
  2257.5 35.3 fusion.313
  2312.8 41.7 %fusion.314 = bf16[8,640,2560]{1,2,0:T(8,128)(2,1)} fusion(f32[2560,640,8]{1,0,2:T(8,128)} %get-tuple-element.1409, f32[2560,640,8]{1,0,2:T(8,128)} %fusion.304, f32[8,640]{1,0:T(8,128)S(1)} %get-tuple-element.1410, f32[8,640]{1,0:T(8,128)S(1)} %dynamic-slice_bitcast_fusion.5, pred[640,2560]{0,1:T(8,128)(4,1)S(1)} %copy-done.6), kind=kLoop, calls=%fused_computation.15.clone.1 | loop fusion | flops 78643200 | bytes 132751360 | tf_op jit(solution)/shard_map/reshape.606
  2409.8 23.4 reduce-scatter.34.cloned.1.call-done
  2491.8 137.4 %all-reduce.14.cloned.1.call-done = (bf16[640,2048]{1,0:T(8,128)(2,1)}, bf16[640,2048]{1,0:T(8,128)(2,1)}) async-done(((bf16[640,2048]{1,0:T(8,128)(2,1)}, bf16[640,2048]{1,0:T(8,128)(2,1)}), (bf16[640,2048]{1,0:T(8,128)(2,1)}, bf16[640,2048]{1,0:T(8,128)(2,1)})) %all-reduce.14.cloned.1.call-update) | async-done | bytes 5242896 | tf_op jit(solution)/shard_map/while/body/eval_jaxpr/psum | solution.py:150
  2835.5 41.6 %all-reduce.10.cloned.1.call-done = bf16[640,2048]{1,0:T(8,128)(2,1)} async-done(((bf16[640,2048]{1,0:T(8,128)(2,1)}), bf16[640,2048]{1,0:T(8,128)(2,1)}) %all-reduce.10.cloned.1.call-update) | async-done | bytes 2621456 | tf_op jit(solution)/shard_map/while/body/eval_jaxpr/psum | solution.py:142
  2954.8 74.5 %all-reduce.12.cloned.1.call-done = bf16[640,2048]{1,0:T(8,128)(2,1)} async-done(((bf16[640,2048]{1,0:T(8,128)(2,1)}), bf16[640,2048]{1,0:T(8,128)(2,1)}) %all-reduce.12.cloned.1.call-update) | async-done | bytes 2621456 | tf_op jit(solution)/shard_map/while/body/eval_jaxpr/psum | solution.py:211
  3041.9 35.3 fusion.313
  3097.3 41.7 %fusion.314 = bf16[8,640,2560]{1,2,0:T(8,128)(2,1)} fusion(f32[2560,640,8]{1,0,2:T(8,128)} %get-tuple-element.1409, f32[2560,640,8]{1,0,2:T(8,128)} %fusion.304, f32[8,640]{1,0:T(8,128)S(1)} %get-tuple-element.1410, f32[8,640]{1,0:T(8,128)S(1)} %dynamic-slice_bitcast_fusion.5, pred[640,2560]{0,1:T(8,128)(4,1)S(1)} %copy-done.6), kind=kLoop, calls=%fused_computation.15.clone.1 | loop fusion | flops 78643200 | bytes 132751360 | tf_op jit(solution)/shard_map/reshape.606
  3276.1 137.4 %all-reduce.14.cloned.1.call-done = (bf16[640,2048]{1,0:T(8,128)(2,1)}, bf16[640,2048]{1,0:T(8,128)(2,1)}) async-done(((bf16[640,2048]{1,0:T(8,128)(2,1)}, bf16[640,2048]{1,0:T(8,128)(2,1)}), (bf16[640,2048]{1,0:T(8,128)(2,1)}, bf16[640,2048]{1,0:T(8,128)(2,1)})) %all-reduce.14.cloned.1.call-update) | async-done | bytes 5242896 | tf_op jit(solution)/shard_map/while/body/eval_jaxpr/psum | solution.py:150
  3510.8 37.7 reduce-scatter.24.cloned.1.call-done
  3550.7 36.9 reduce-scatter.18.cloned.1.call-done
  3589.8 66.5 %reduce-scatter.30.cloned.1.call-done = bf16[1408,512]{1,0:T(8,128)(2,1)} async-done(((bf16[1408,2048]{1,0:T(8,128)(2,1)}), bf16[1408,512]{1,0:T(8,128)(2,1)}) %reduce-scatter.30.cloned.1.call-update) | async-done | bytes 1441808 | tf_op jit(solution)/shard_map/reduce_scatter | solution.py:457
  3659.6 65.5 %reduce-scatter.28.cloned.1.call-done = bf16[512,1408]{1,0:T(8,128)(2,1)} async-done(((bf16[2048,1408]{1,0:T(8,128)(2,1)}), bf16[512,1408]{1,0:T(8,128)(2,1)}) %reduce-scatter.28.cloned.1.call-update) | async-done | bytes 1441808 | tf_op jit(solution)/shard_map/reduce_scatter | solution.py:454
  3728.3 65.7 %reduce-scatter.26.cloned.1.call-done = bf16[512,1408]{1,0:T(8,128)(2,1)} async-done(((bf16[2048,1408]{1,0:T(8,128)(2,1)}), bf16[512,1408]{1,0:T(8,128)(2,1)}) %reduce-scatter.26.cloned.1.call-update) | async-done | bytes 1441808 | tf_op jit(solution)/shard_map/reduce_scatter | solution.py:451
  (1255 shorter events, 1887.7 us)
Async XLA Ops:
  7.2 43.7 %all-gather.15.cloned.1.call-start = ((), (), s32[]{:S(2)}) async-start(), calls=%async_computation.16 | async-start | bytes 2621440 | tf_op jit(solution)/shard_map/all_gather | solution.py:327
  9.5 78.9 %all-gather.17.cloned.1.call-start = ((), (), s32[]{:S(2)}) async-start(), calls=%async_computation.17 | async-start | bytes 2621440 | tf_op jit(solution)/shard_map/all_gather | solution.py:330
  11.7 145.0 %all-gather.19.cloned.1.call-start = ((), (), s32[]{:S(2)}) async-start(), calls=%async_computation.18 | async-start | bytes 7208960 | tf_op jit(solution)/shard_map/all_gather | solution.py:332
  13.0 211.7 %all-gather.21.cloned.1.call-start = ((), (), s32[]{:S(2)}) async-start(), calls=%async_computation.19 | async-start | bytes 7208960 | tf_op jit(solution)/shard_map/all_gather | solution.py:333
  16.3 276.4 %all-gather.23.cloned.1.call-start = ((), (), s32[]{:S(2)}) async-start(), calls=%async_computation.20 | async-start | bytes 7208960 | tf_op jit(solution)/shard_map/all_gather | solution.py:334
  311.8 213.0 %all-reduce.10.cloned.1.call-start = ((), (), s32[]{:S(2)}) async-start(), calls=%async_computation.21 | async-start | bytes 5242880 | tf_op jit(solution)/shard_map/while/body/eval_jaxpr/psum | solution.py:142
  420.0 257.2 %all-reduce.12.cloned.1.call-start = ((), (), s32[]{:S(2)}) async-start(), calls=%async_computation.22 | async-start | bytes 5242880 | tf_op jit(solution)/shard_map/while/body/eval_jaxpr/psum | solution.py:211
  573.9 262.5 %reduce-scatter.32.cloned.1.call-start = ((), (), s32[]{:S(2)}) async-start(), calls=%async_computation.23 | async-start | bytes 819200 | tf_op jit(solution)/shard_map/while
  811.7 53.8 %reduce-scatter.34.cloned.1.call-start = ((), (), s32[]{:S(2)}) async-start(), calls=%async_computation.24 | async-start | bytes 819200 | tf_op jit(solution)/shard_map/while/body/eval_jaxpr/convert_element_type | solution.py:251
  819.1 242.4 %all-reduce.14.cloned.1.call-start = ((), (), s32[]{:S(2)}) async-start(), calls=%async_computation.25 | async-start | bytes 10485760 | tf_op jit(solution)/shard_map/while/body/eval_jaxpr/psum | solution.py:150
  1097.8 210.4 %all-reduce.10.cloned.1.call-start = ((), (), s32[]{:S(2)}) async-start(), calls=%async_computation.21 | async-start | bytes 5242880 | tf_op jit(solution)/shard_map/while/body/eval_jaxpr/psum | solution.py:142
  1204.6 255.9 %all-reduce.12.cloned.1.call-start = ((), (), s32[]{:S(2)}) async-start(), calls=%async_computation.22 | async-start | bytes 5242880 | tf_op jit(solution)/shard_map/while/body/eval_jaxpr/psum | solution.py:211
  1357.3 262.4 %reduce-scatter.32.cloned.1.call-start = ((), (), s32[]{:S(2)}) async-start(), calls=%async_computation.23 | async-start | bytes 819200 | tf_op jit(solution)/shard_map/while
  1595.0 53.6 %reduce-scatter.34.cloned.1.call-start = ((), (), s32[]{:S(2)}) async-start(), calls=%async_computation.24 | async-start | bytes 819200 | tf_op jit(solution)/shard_map/while/body/eval_jaxpr/convert_element_type | solution.py:251
  1602.4 242.3 %all-reduce.14.cloned.1.call-start = ((), (), s32[]{:S(2)}) async-start(), calls=%async_computation.25 | async-start | bytes 10485760 | tf_op jit(solution)/shard_map/while/body/eval_jaxpr/psum | solution.py:150
  1882.3 210.4 %all-reduce.10.cloned.1.call-start = ((), (), s32[]{:S(2)}) async-start(), calls=%async_computation.21 | async-start | bytes 5242880 | tf_op jit(solution)/shard_map/while/body/eval_jaxpr/psum | solution.py:142
  1989.0 255.9 %all-reduce.12.cloned.1.call-start = ((), (), s32[]{:S(2)}) async-start(), calls=%async_computation.22 | async-start | bytes 5242880 | tf_op jit(solution)/shard_map/while/body/eval_jaxpr/psum | solution.py:211
  2141.6 262.5 %reduce-scatter.32.cloned.1.call-start = ((), (), s32[]{:S(2)}) async-start(), calls=%async_computation.23 | async-start | bytes 819200 | tf_op jit(solution)/shard_map/while
  2379.4 53.8 %reduce-scatter.34.cloned.1.call-start = ((), (), s32[]{:S(2)}) async-start(), calls=%async_computation.24 | async-start | bytes 819200 | tf_op jit(solution)/shard_map/while/body/eval_jaxpr/convert_element_type | solution.py:251
  2386.8 242.4 %all-reduce.14.cloned.1.call-start = ((), (), s32[]{:S(2)}) async-start(), calls=%async_computation.25 | async-start | bytes 10485760 | tf_op jit(solution)/shard_map/while/body/eval_jaxpr/psum | solution.py:150
  2666.8 210.3 %all-reduce.10.cloned.1.call-start = ((), (), s32[]{:S(2)}) async-start(), calls=%async_computation.21 | async-start | bytes 5242880 | tf_op jit(solution)/shard_map/while/body/eval_jaxpr/psum | solution.py:142
  2773.4 255.9 %all-reduce.12.cloned.1.call-start = ((), (), s32[]{:S(2)}) async-start(), calls=%async_computation.22 | async-start | bytes 5242880 | tf_op jit(solution)/shard_map/while/body/eval_jaxpr/psum | solution.py:211
  2926.1 262.5 %reduce-scatter.32.cloned.1.call-start = ((), (), s32[]{:S(2)}) async-start(), calls=%async_computation.23 | async-start | bytes 819200 | tf_op jit(solution)/shard_map/while
  3163.9 53.6 %reduce-scatter.34.cloned.1.call-start = ((), (), s32[]{:S(2)}) async-start(), calls=%async_computation.24 | async-start | bytes 819200 | tf_op jit(solution)/shard_map/while/body/eval_jaxpr/convert_element_type | solution.py:251
  3171.3 242.3 %all-reduce.14.cloned.1.call-start = ((), (), s32[]{:S(2)}) async-start(), calls=%async_computation.25 | async-start | bytes 10485760 | tf_op jit(solution)/shard_map/while/body/eval_jaxpr/psum | solution.py:150
  3454.6 44.7 %reduce-scatter.22.cloned.1.call-start = ((), (), s32[]{:S(2)}) async-start(), calls=%async_computation.11 | async-start | bytes 327680 | tf_op jit(solution)/shard_map/reduce_scatter | solution.py:442
  3456.5 52.9 %reduce-scatter.20.cloned.1.call-start = ((), (), s32[]{:S(2)}) async-start(), calls=%async_computation.10 | async-start | bytes 327680 | tf_op jit(solution)/shard_map/reduce_scatter | solution.py:439
  3458.3 90.2 %reduce-scatter.24.cloned.1.call-start = ((), (), s32[]{:S(2)}) async-start(), calls=%async_computation.12 | async-start | bytes 2621440 | tf_op jit(solution)/shard_map/reduce_scatter | solution.py:445
  3462.2 125.4 %reduce-scatter.18.cloned.1.call-start = ((), (), s32[]{:S(2)}) async-start(), calls=%async_computation.9 | async-start | bytes 2621440 | tf_op jit(solution)/shard_map/reduce_scatter | solution.py:436
  3466.1 190.2 %reduce-scatter.30.cloned.1.call-start = ((), (), s32[]{:S(2)}) async-start(), calls=%async_computation.15 | async-start | bytes 7208960 | tf_op jit(solution)/shard_map/reduce_scatter | solution.py:457
  3473.9 251.2 %reduce-scatter.28.cloned.1.call-start = ((), (), s32[]{:S(2)}) async-start(), calls=%async_computation.14 | async-start | bytes 7208960 | tf_op jit(solution)/shard_map/reduce_scatter | solution.py:454
  3481.3 312.7 %reduce-scatter.26.cloned.1.call-start = ((), (), s32[]{:S(2)}) async-start(), calls=%async_computation.13 | async-start | bytes 7208960 | tf_op jit(solution)/shard_map/reduce_scatter | solution.py:451
  (377 other events, 5911.1 us)
Sparse Core Ops, SparseCore 0:
  10.4 40.3 all-gather.14
  53.3 35.0 all-gather.16
  90.8 65.7 all-gather.18
  158.9 65.7 all-gather.20
  227.0 65.6 all-gather.22
  420.1 104.6 all-reduce.9
  574.0 103.1 all-reduce.11
  811.8 24.4 reduce-scatter.31
  840.0 25.3 reduce-scatter.33
  872.1 189.3 all-reduce.13
  1204.7 103.4 all-reduce.9
  1357.4 103.0 all-reduce.11
  1595.1 24.4 reduce-scatter.31
  1623.2 25.3 reduce-scatter.33
  1655.3 189.3 all-reduce.13
  1989.1 103.4 all-reduce.9
  2141.7 103.1 all-reduce.11
  2379.5 24.4 reduce-scatter.31
  2407.7 25.3 reduce-scatter.33
  2439.8 189.3 all-reduce.13
  2773.6 103.5 all-reduce.9
  2926.2 103.1 all-reduce.11
  3164.0 24.4 reduce-scatter.31
  3192.1 25.3 reduce-scatter.33
  3224.2 189.3 all-reduce.13
  3458.5 23.1 reduce-scatter.21
  3485.1 24.1 reduce-scatter.19
  3512.8 35.6 reduce-scatter.23
  3552.4 35.2 reduce-scatter.17
  3590.4 65.8 reduce-scatter.29
  3659.3 65.8 reduce-scatter.27
  3728.1 65.8 reduce-scatter.25
where the time goes:
time: 3810 us; the launch traced here: 3800 us
  waiting for transfers between devices  1710 us (45%)
  matrix products  1230 us (32%)
  other arithmetic  519 us (14%)
  local copies, waits for them, and re-layouts  215 us (6%)
  blocking collectives  80.7 us (2%)
    psum x4, waiting for transfers between devices, layer_forward(): lax.psum(mlp_part.astype(jnp.bfloat16), 'tensor').astype(jnp.float32)  557 us
    psum x4, waiting for transfers between devices, layer_backward(): lax.psum(normed_two_part.astype(jnp.bfloat16), 'tensor').astype(jnp.float32)  298 us
    another operation x16, other arithmetic  174 us
    dot_general x8, matrix products, score_block(): jnp.einsum('tkgd,skd->kgts', query_groups, key_all, preferred_element_typ...  173 us
    psum x4, waiting for transfers between devices, layer_forward(): lax.psum(attn_part.astype(jnp.bfloat16), 'tensor').astype(jnp.float32)  168 us
    dot_general x4, matrix products, layer_backward(): jnp.einsum('tkgd,skd->kgts', grad_context, value_all, preferred_element_t...  141 us
    convert_element_type x4, waiting for transfers between devices, layer_backward(): grad_value = grad_value_rows.reshape(row_count, -1).astype(jnp.bfloat16)  93.2 us
    dot_general x4, matrix products, layer_backward(): jnp.einsum('kgts,skd->tkgd', attn_probs, value_all, preferred_element_typ...  87.4 us
  transfers between devices with their start and end apart: 40, of which 31 were waited for; matrix products, arithmetic and copies ran while one was open for 19% of the time, Pallas kernels for 0%

commit v1 on v0

v1 whole, which is shorter than its diff:
```python
import functools

import jax
import jax.numpy as jnp
from jax import lax
from jax.experimental import pallas as pl
from jax.experimental.pallas import tpu as pltpu
from jax.sharding import PartitionSpec as P

HEAD = 64
HALF = HEAD // 2
TRUNK = 1024
GROUP = 384
EPSILON = 1e-05
THETA = 10000.0
MASKED = -1e30
BF = jnp.bfloat16
F32 = jnp.float32
MESH = pl.DeviceIdType.MESH


def dot_f32(a, b, ca, cb):
    return lax.dot_general(a, b, (((ca,), (cb,)), ((), ())), preferred_element_type=F32)


def sum_kernel(pieces, p_ref, o_ref, a_buf, s_buf, b_buf, sa, ra, sb, rb, sc, rc):
    t = lax.axis_index("tensor")
    sec = lax.axis_index("section")
    dat = lax.axis_index("dp")
    inner = (t == 1) | (t == 2)
    pair = (sec, t + 1 - 2 * lax.rem(t, 2), dat)
    mid = (sec, 3 - t, dat)
    rows = p_ref.shape[0] // pieces

    def part(ref, i):
        return ref.at[pl.ds(i * rows, rows)]

    def to_inner(i):
        return pltpu.make_async_remote_copy(
            part(p_ref, i), part(a_buf, i), sa.at[i], ra.at[i], device_id=pair, device_id_type=MESH
        )

    def across(i):
        return pltpu.make_async_remote_copy(
            part(s_buf, i), part(b_buf, i), sb.at[i], rb.at[i], device_id=mid, device_id_type=MESH
        )

    def to_outer(i):
        return pltpu.make_async_remote_copy(
            part(o_ref, i), part(o_ref, i), sc.at[i], rc.at[i], device_id=pair, device_id_type=MESH
        )

    barrier = pltpu.get_barrier_semaphore()
    pl.semaphore_signal(barrier, inc=1, device_id=pair, device_id_type=MESH)

    @pl.when(inner)
    def _():
        pl.semaphore_signal(barrier, inc=1, device_id=mid, device_id_type=MESH)
        pl.semaphore_wait(barrier, 2)

    @pl.when(jnp.logical_not(inner))
    def _():
        pl.semaphore_wait(barrier, 1)
        for i in range(pieces):
            to_inner(i).start()
        for i in range(pieces):
            to_inner(i).wait_send()
        for i in range(pieces):
            to_outer(i).wait_recv()

    @pl.when(inner)
    def _():
        def first(i):
            to_inner(i).wait_recv()
            at = pl.ds(i * rows, rows)
            s_buf[at] = (p_ref[at].astype(F32) + a_buf[at].astype(F32)).astype(BF)
            across(i).start()

        def second(i):
            across(i).wait_recv()
            at = pl.ds(i * rows, rows)
            o_ref[at] = (s_buf[at].astype(F32) + b_buf[at].astype(F32)).astype(BF)
            to_outer(i).start()

        for i in range(pieces):
            first(i)
            if i >= 1:
                second(i - 1)
        second(pieces - 1)
        for i in range(pieces):
            across(i).wait_send()
            to_outer(i).wait_send()


def sum_over_tensor(part):
    if lax.axis_size("tensor") != 4:
        return lax.psum(part, "tensor")
    rows, width = part.shape
    pieces = next(n for n in (10, 5, 4, 2, 1) if rows % (16 * n) == 0)
    buf = pltpu.VMEM((rows, width), BF)
    sem = pltpu.SemaphoreType.DMA((pieces,))
    return pl.pallas_call(
        functools.partial(sum_kernel, pieces),
        out_shape=jax.ShapeDtypeStruct((rows, width), BF),
        in_specs=[pl.BlockSpec(memory_space=pltpu.VMEM)],
        out_specs=pl.BlockSpec(memory_space=pltpu.VMEM),
        scratch_shapes=[buf, buf, buf, sem, sem, sem, sem, sem, sem],
        compiler_params=pltpu.CompilerParams(
            collective_id=1, has_side_effects=True, vmem_limit_bytes=24 << 20
        ),
        name="sum_tensor",
    )(part)


def group_start(first_row):
    past = lax.max(first_row - TRUNK, 0)
    return pl.multiple_of(TRUNK + GROUP * lax.div(past, GROUP), 128)


def windows(tree_len, rows, tile, first_row):
    if tile % 128 == 0 and GROUP % tile == 0 and TRUNK % tile == 0 and rows % tile == 0:
        return (pl.ds(0, TRUNK), pl.ds(group_start(first_row), GROUP))
    return (pl.ds(0, tree_len),)


def beside(ref, head, count):
    parts = [ref[HEAD * (head + k) : HEAD * (head + k + 1), :] for k in range(count)]
    return parts[0] if count == 1 else jnp.concatenate(parts, axis=1)


def row_beside(ref, head, count):
    parts = [ref[head + k : head + k + 1, :] for k in range(count)]
    return parts[0] if count == 1 else jnp.concatenate(parts, axis=1)


def attend_kernel(rows, step, start_ref, q_ref, kv_ref, kvt_ref, bias_ref, o_ref, lse_ref):
    tile = q_ref.shape[1]
    heads = q_ref.shape[0] // HEAD
    first_row = start_ref[0] + pl.program_id(0) * tile
    wins = windows(kv_ref.shape[0], rows, tile, first_row)
    for head in range(0, heads, step):
        q = beside(q_ref, head, step)
        scores = []
        for win in wins:
            bias = bias_ref[win, :].astype(F32)
            bias = bias if step == 1 else jnp.concatenate([bias] * step, axis=1)
            scores.append(dot_f32(kv_ref[win, :HEAD], q, 1, 0) + bias)
        top = functools.reduce(jnp.maximum, [jnp.max(s, 0, keepdims=True) for s in scores])
        expo = [jnp.exp(s - top) for s in scores]
        total = sum(jnp.sum(e, 0, keepdims=True) for e in expo)
        out = sum(dot_f32(kvt_ref[HEAD:, win], e.astype(BF), 1, 0) for win, e in zip(wins, expo))
        out = (out / total).astype(BF)
        lse = top + jnp.log(total)
        for k in range(step):
            o_ref[HEAD * (head + k) : HEAD * (head + k + 1), :] = out[:, k * tile : (k + 1) * tile]
            lse_ref[head + k : head + k + 1, :] = lse[:, k * tile : (k + 1) * tile]


def attend_back_kernel(
    rows, step, start_ref, q_ref, do_ref, o_ref, lse_ref, kv_ref, kvt_ref, bias_ref, cos_ref, sin_ref,
    dq_ref, dkv_ref, dk_acc, dv_acc,
):
    tile = q_ref.shape[1]
    heads = q_ref.shape[0] // HEAD
    first_row = start_ref[0] + pl.program_id(0) * tile
    wins = windows(kv_ref.shape[0], rows, tile, first_row)

    @pl.when(pl.program_id(0) == 0)
    def _():
        dk_acc[...] = jnp.zeros_like(dk_acc)
        dv_acc[...] = jnp.zeros_like(dv_acc)

    for head in range(0, heads, step):
        q = beside(q_ref, head, step)
        do = beside(do_ref, head, step)
        out = beside(o_ref, head, step)
        lse = row_beside(lse_ref, head, step)
        delta = jnp.sum(do.astype(F32) * out.astype(F32), 0, keepdims=True)
        dq = jnp.zeros((HEAD, step * tile), F32)
        for win in wins:
            bias = bias_ref[win, :].astype(F32)
            bias = bias if step == 1 else jnp.concatenate([bias] * step, axis=1)
            p = jnp.exp(dot_f32(kv_ref[win, :HEAD], q, 1, 0) + bias - lse)
            dp = dot_f32(kv_ref[win, HEAD:], do, 1, 0)
            ds = (p * (dp - delta)).astype(BF)
            dk_acc[win, :] += dot_f32(ds, q, 1, 1)
            dv_acc[win, :] += dot_f32(p.astype(BF), do, 1, 1)
            dq = dq + dot_f32(kvt_ref[:HEAD, win], ds, 1, 0)
        dq = dq * HEAD**-0.5
        cos, sin = cos_ref[...], sin_ref[...]
        for k in range(step):
            first = dq[:HALF, k * tile : (k + 1) * tile]
            second = dq[HALF:, k * tile : (k + 1) * tile]
            base = HEAD * (head + k)
            dq_ref[base : base + HALF, :] = (first * cos + second * sin).astype(BF)
            dq_ref[base + HALF : base + HEAD, :] = (second * cos - first * sin).astype(BF)

    @pl.when(pl.program_id(0) == pl.num_programs(0) - 1)
    def _():
        dkv_ref[...] = jnp.concatenate([dk_acc[...], dv_acc[...]], axis=1).astype(BF)


def row_tile(rows):
    return 128 if rows % 128 == 0 else rows


def attend(start, q_t, kv, kv_t, bias_t):
    width, rows = q_t.shape
    heads, tree_len, tile = width // HEAD, kv.shape[0], row_tile(rows)
    step = 2 if tile % 128 == 0 and heads % 2 == 0 else 1
    column = lambda i, s: (0, i)
    whole = lambda i, s: (0, 0)
    return pl.pallas_call(
        functools.partial(attend_kernel, rows, step),
        out_shape=(
            jax.ShapeDtypeStruct((width, rows), BF),
            jax.ShapeDtypeStruct((heads, rows), F32),
        ),
        grid_spec=pltpu.PrefetchScalarGridSpec(
            num_scalar_prefetch=1,
            grid=(rows // tile,),
            in_specs=[
                pl.BlockSpec((width, tile), column),
                pl.BlockSpec((tree_len, 2 * HEAD), whole),
                pl.BlockSpec((2 * HEAD, tree_len), whole),
                pl.BlockSpec((tree_len, tile), column),
            ],
            out_specs=(pl.BlockSpec((width, tile), column), pl.BlockSpec((heads, tile), column)),
        ),
        compiler_params=pltpu.CompilerParams(vmem_limit_bytes=40 << 20),
        cost_estimate=pl.CostEstimate(
            flops=16 * heads * rows * tree_len * HEAD,
            transcendentals=heads * rows * tree_len,
            bytes_accessed=2 * rows * tree_len,
        ),
        name="attend",
    )(start, q_t, kv, kv_t, bias_t)


def attend_back(start, q_t, do_t, o_t, lse, kv, kv_t, bias_t, cos_t, sin_t):
    width, rows = q_t.shape
    heads, tree_len, tile = width // HEAD, kv.shape[0], row_tile(rows)
    step = 2 if tile % 128 == 0 and heads % 2 == 0 else 1
    column = lambda i, s: (0, i)
    whole = lambda i, s: (0, 0)
    return pl.pallas_call(
        functools.partial(attend_back_kernel, rows, step),
        out_shape=(
            jax.ShapeDtypeStruct((width, rows), BF),
            jax.ShapeDtypeStruct((tree_len, 2 * HEAD), BF),
        ),
        grid_spec=pltpu.PrefetchScalarGridSpec(
            num_scalar_prefetch=1,
            grid=(rows // tile,),
            in_specs=[
                pl.BlockSpec((width, tile), column),
                pl.BlockSpec((width, tile), column),
                pl.BlockSpec((width, tile), column),
                pl.BlockSpec((heads, tile), column),
                pl.BlockSpec((tree_len, 2 * HEAD), whole),
                pl.BlockSpec((2 * HEAD, tree_len), whole),
                pl.BlockSpec((tree_len, tile), column),
                pl.BlockSpec((HALF, tile), column),
                pl.BlockSpec((HALF, tile), column),
            ],
            out_specs=(
                pl.BlockSpec((width, tile), column),
                pl.BlockSpec((tree_len, 2 * HEAD), whole),
            ),
            scratch_shapes=[pltpu.VMEM((tree_len, HEAD), F32), pltpu.VMEM((tree_len, HEAD), F32)],
        ),
        compiler_params=pltpu.CompilerParams(vmem_limit_bytes=48 << 20),
        cost_estimate=pl.CostEstimate(
            flops=40 * heads * rows * tree_len * HEAD,
            transcendentals=heads * rows * tree_len,
            bytes_accessed=2 * rows * tree_len,
        ),
        name="attend_back",
    )(start, q_t, do_t, o_t, lse, kv, kv_t, bias_t, cos_t, sin_t)


def inverse_rms(hidden):
    return lax.rsqrt(jnp.mean(hidden * hidden, -1, keepdims=True) + EPSILON)


def norm_back(grad_normed, hidden, scale_rows, gain):
    unit = hidden * scale_rows
    grad_unit = grad_normed * gain
    grad_hidden = scale_rows * (grad_unit - unit * jnp.mean(grad_unit * unit, -1, keepdims=True))
    return grad_hidden, jnp.sum(grad_normed * unit, 0)


def rope_t(x, cos_t, sin_t):
    heads = x.shape[0] // HEAD
    halves = x.reshape(heads, 2, HALF, x.shape[1])
    first, second = halves[:, 0], halves[:, 1]
    turned = jnp.stack(
        [first * cos_t - second * sin_t, second * cos_t + first * sin_t], axis=1
    )
    return turned.reshape(x.shape).astype(BF)


def layer_forward(hidden, weights, tables):
    gain_one, gain_two, w_in, w_out, w_gu, w_down = weights
    start, bias_t, cos_t, sin_t = tables
    width = w_out.shape[0]
    span = (w_in.shape[1] - width) // 2
    scale_one = inverse_rms(hidden)
    normed_one = (hidden * scale_one * gain_one).astype(BF)
    qkv_t = dot_f32(w_in, normed_one, 0, 1)
    q_t = rope_t(qkv_t[:width], cos_t, sin_t) * jnp.asarray(HEAD**-0.5, BF)
    k_t = rope_t(qkv_t[width : width + span], cos_t, sin_t)
    kv_rows = jnp.concatenate([k_t, qkv_t[width + span :].astype(BF)], 0).T
    kv = lax.all_gather(kv_rows, "dp", axis=0, tiled=True)
    kv_t = kv.T
    o_t, lse = attend(start, q_t, kv, kv_t, bias_t)
    attn_part = dot_f32(o_t, w_out, 0, 0).astype(BF)
    middle = hidden + sum_over_tensor(attn_part).astype(F32)
    scale_two = inverse_rms(middle)
    normed_two = (middle * scale_two * gain_two).astype(BF)
    gate_up = jnp.dot(normed_two, w_gu, preferred_element_type=F32)
    units = w_down.shape[0]
    gate, up = gate_up[:, :units], gate_up[:, units:]
    inner = (gate * jax.nn.sigmoid(gate) * up).astype(BF)
    mlp_part = jnp.dot(inner, w_down, preferred_element_type=F32).astype(BF)
    result = (middle + sum_over_tensor(mlp_part).astype(F32)).astype(BF)
    kept = (hidden, scale_one, normed_one, q_t, kv, kv_t, o_t, lse, middle, scale_two, normed_two, gate_up, inner)
    return result, kept


def layer_backward(grad_out, weights, tables, rope_rows, kept):
    gain_one, gain_two, w_in, w_out, w_gu, w_down = weights
    start, bias_t, cos_t, sin_t = tables
    cos_rows, sin_rows = rope_rows
    hidden, scale_one, normed_one, q_t, kv, kv_t, o_t, lse, middle, scale_two, normed_two, gate_up, inner = kept
    units = w_down.shape[0]
    gate, up = gate_up[:, :units], gate_up[:, units:]
    branch = grad_out.astype(BF)
    d_w_down = dot_f32(inner, branch, 0, 0).astype(BF)
    d_inner = dot_f32(branch, w_down, 1, 1)
    sig = jax.nn.sigmoid(gate)
    d_gate = (d_inner * up * sig * (1.0 + gate * (1.0 - sig))).astype(BF)
    d_up = (d_inner * gate * sig).astype(BF)
    d_gu = jnp.concatenate([d_gate, d_up], 1)
    d_w_gu = dot_f32(normed_two, d_gu, 0, 0).astype(BF)
    d_two = sum_over_tensor(dot_f32(d_gu, w_gu, 1, 1).astype(BF)).astype(F32)
    grad_norm, d_gain_two = norm_back(d_two, middle, scale_two, gain_two)
    grad_middle = grad_out + grad_norm
    grad_attn = grad_middle.astype(BF)
    d_w_out = dot_f32(o_t, grad_attn, 1, 0).astype(BF)
    do_t = dot_f32(w_out, grad_attn, 1, 1).astype(BF)
    dq_t, dkv_part = attend_back(start, q_t, do_t, o_t, lse, kv, kv_t, bias_t, cos_t, sin_t)
    dkv = lax.psum_scatter(dkv_part, "dp", scatter_dimension=0, tiled=True).astype(F32)
    first, second = dkv[:, :HALF], dkv[:, HALF:HEAD]
    dkv = jnp.concatenate(
        [first * cos_rows + second * sin_rows, second * cos_rows - first * sin_rows, dkv[:, HEAD:]], 1
    ).astype(BF)
    d_in = jnp.concatenate([dq_t.T, dkv], 1)
    d_w_in = dot_f32(normed_one, d_in, 0, 0).astype(BF)
    d_one = sum_over_tensor(dot_f32(d_in, w_in, 1, 1).astype(BF)).astype(F32)
    grad_norm, d_gain_one = norm_back(d_one, hidden, scale_one, gain_one)
    grad_input = grad_middle + grad_norm
    return grad_input, (d_w_in, d_w_out, d_w_gu, d_w_down), (d_gain_one, d_gain_two)


def shards(
    inputs, cotangent, seg_ids, positions, parents, gain_attn, w_query, key_weight, value_weight,
    w_out, gain_mlp, w_gate, w_up, w_down,
):
    sec = lax.axis_index("section")
    data = lax.axis_index("dp")
    sections = lax.axis_size("section")
    devices = lax.axis_size("dp")
    assert sections == 2 and inputs.shape[0] == 2
    first_core = sec == 0
    rows, model = inputs.shape[1], inputs.shape[2]
    swap = [(0, 1), (1, 0)]
    both = ("dp", "section")

    hidden = lax.dynamic_index_in_dim(inputs, sec, 0, keepdims=False).astype(F32)
    cot = lax.dynamic_index_in_dim(cotangent, sec, 0, keepdims=False).astype(F32)
    segments = lax.dynamic_index_in_dim(seg_ids, sec, 0, keepdims=False)
    places = lax.dynamic_index_in_dim(positions, sec, 0, keepdims=False)
    parent = lax.dynamic_index_in_dim(parents, sec, 0, keepdims=False)

    shard_list = (
        (jnp.concatenate([w_query[0], key_weight[0], value_weight[0]], 1).astype(BF), 0),
        (w_out[0].astype(BF), 1),
        (jnp.concatenate([w_gate[0], w_up[0]], 1).astype(BF), 0),
        (w_down[0].astype(BF), 1),
    )
    gains_all = lax.all_gather(
        jnp.concatenate([gain_attn, gain_mlp], 0).astype(BF), ("section", "dp"), axis=0, tiled=False
    )
    gains_all = gains_all.reshape(sections, devices, 2, -1).astype(F32)
    gain = [[gains_all[l, :, k].reshape(-1) for k in range(2)] for l in range(2)]
    halves = []
    for shard, axis in shard_list:
        half = shard.shape[axis] // 2
        low = lax.slice_in_dim(shard, 0, half, axis=axis)
        high = lax.slice_in_dim(shard, half, 2 * half, axis=axis)
        got = lax.ppermute(jnp.where(first_core, high, low), "section", swap)
        halves.append((jnp.where(first_core, low, got), jnp.where(first_core, got, high), axis))
    weights = []
    for l in range(2):
        whole = [lax.all_gather(h[l], both, axis=h[2], tiled=True) for h in halves]
        weights.append((gain[l][0], gain[l][1], *whole))

    seg_count = parent.shape[0]
    labels = jnp.arange(seg_count, dtype=jnp.int32)
    parent_hot = (parent[:, None] == labels[None, :]).astype(F32)
    ancestry = jnp.eye(seg_count, dtype=F32) + parent_hot + jnp.dot(parent_hot, parent_hot)
    ancestry = (ancestry > 0.5).astype(F32)
    row_start = data * rows
    seg_rows = lax.dynamic_slice_in_dim(segments, row_start, rows, 0)
    pos_rows = lax.dynamic_slice_in_dim(places, row_start, rows, 0)
    key_hot = (segments[:, None] == labels[None, :]).astype(F32)
    query_hot = (labels[:, None] == seg_rows[None, :]).astype(F32)
    reach = jnp.dot(key_hot, jnp.dot(ancestry.T, query_hot))
    allowed = (reach > 0.5) & (places[:, None] <= pos_rows[None, :])
    bias_t = jnp.where(allowed, 0.0, MASKED).astype(BF)
    frequency = THETA ** (-(jnp.arange(HALF, dtype=F32) * 2.0 / HEAD))
    angles = frequency[:, None] * pos_rows.astype(F32)[None, :]
    cos_t, sin_t = jnp.cos(angles), jnp.sin(angles)
    tables = (row_start.astype(jnp.int32).reshape(1), bias_t, cos_t, sin_t)
    rope_rows = (cos_t.T, sin_t.T)

    out_zero, kept_zero = layer_forward(hidden, weights[0], tables)
    out_one, kept_one = layer_forward(out_zero.astype(F32), weights[1], tables)
    grad_one, d_one, d_gain_one = layer_backward(cot, weights[1], tables, rope_rows, kept_one)
    grad_zero, d_zero, d_gain_zero = layer_backward(
        grad_one.astype(BF).astype(F32), weights[0], tables, rope_rows, kept_zero
    )

    out_got = lax.ppermute(jnp.where(first_core, out_one, out_zero), "section", swap)
    layer_output = jnp.stack(
        [jnp.where(first_core, out_zero, out_got), jnp.where(first_core, out_got, out_one)]
    )
    one_got = lax.ppermute(grad_one.astype(BF), "section", [(0, 1)]).astype(F32)
    zero_got = lax.ppermute(grad_zero.astype(BF), "section", [(1, 0)]).astype(F32)
    input_grad = jnp.stack(
        [jnp.where(first_core, grad_zero, one_got), jnp.where(first_core, zero_got, grad_one)]
    )

    def own_shard(zero, one, axis):
        zero = lax.psum_scatter(zero, both, scatter_dimension=axis, tiled=True)
        one = lax.psum_scatter(one, both, scatter_dimension=axis, tiled=True)
        got = lax.ppermute(jnp.where(first_core, one, zero), "section", swap)
        low = jnp.where(first_core, zero, got)
        high = jnp.where(first_core, got, one)
        return jnp.concatenate([low, high], axis).astype(F32)

    g_in, g_out, g_gu, g_down = [
        own_shard(zero, one, axis) for zero, one, axis in zip(d_zero, d_one, (0, 1, 0, 1))
    ]
    g_gain = lax.psum(jnp.stack([*d_gain_zero, *d_gain_one]).reshape(2, 2, model), both)
    g_gain = lax.dynamic_index_in_dim(g_gain, sec, 0, keepdims=False)
    g_gain = lax.dynamic_slice_in_dim(g_gain, data * (model // devices), model // devices, 1)
    width, span = w_query.shape[2], key_weight.shape[2]
    units = w_gate.shape[2]
    return (
        layer_output[None],
        input_grad[None],
        g_gain[0][None],
        g_in[None, :, :width],
        g_in[None, :, width : width + span],
        g_in[None, :, width + span :],
        g_out[None],
        g_gain[1][None],
        g_gu[None, :, :units],
        g_gu[None, :, units:],
        g_down[None],
    )


def solution(mesh):
    in_specs = (
        P(None, "dp", None),
        P(None, "dp", None),
        P(),
        P(),
        P(),
        P("section", "dp"),
        P("section", "dp", "tensor"),
        P("section", "dp", "tensor"),
        P("section", "dp", "tensor"),
        P("section", "tensor", "dp"),
        P("section", "dp"),
        P("section", "dp", "tensor"),
        P("section", "dp", "tensor"),
        P("section", "tensor", "dp"),
    )
    out_specs = (
        P("section", None, "dp", None),
        P("section", None, "dp", None),
        P("section", "dp"),
        P("section", "dp", "tensor"),
        P("section", "dp", "tensor"),
        P("section", "dp", "tensor"),
        P("section", "tensor", "dp"),
        P("section", "dp"),
        P("section", "dp", "tensor"),
        P("section", "dp", "tensor"),
        P("section", "tensor", "dp"),
    )
    return jax.shard_map(shards, mesh=mesh, in_specs=in_specs, out_specs=out_specs, check_vma=False)
```

time: 3810 us -> 1310 us (0.34)
  waiting for transfers between devices: 1710 us -> 263 us
  matrix products: 1230 us -> 186 us
  Pallas kernels: 0 us -> 635 us
  other arithmetic: 519 us -> 92.4 us
  local copies, waits for them, and re-layouts: 215 us -> 32.1 us
    dot_general x140 -> x26, matrix products: 1230 us -> 186 us  [the longest x20 141 us: dot_f32(): lax.dot_general(a, b, (((ca,), (cb,)), ((), ())), preferred_element_type=...]
    psum x12 -> x0, waiting for transfers between devices: 1020 us -> none  [the longest x4 557 us: layer_forward(): lax.psum(mlp_part.astype(jnp.bfloat16), 'tensor').astype(jnp.float32)]
    pallas_call x0 -> x12, Pallas kernels: none -> 635 us  [the longest x8 557 us: sum_over_tensor(): pl.pallas_call(functools.partial(sum_kernel, pieces), out_shape=jax.Shape...]
    all_gather x5 -> x8, waiting for transfers between devices: 243 us -> 0.3 us  [shards(): whole = [lax.all_gather(h[l], both, axis=h[2], tiled=True) for h in halves]]
    another operation x16 -> x12, other arithmetic: 174 us -> 22.2 us  [the longest x2 10.8 us: shards(): jnp.stack([jnp.where(first_core, grad_zero, one_got), jnp.where(first_cor...]
    reduce_sum x12 -> x4, other arithmetic: 105 us -> 9.01 us  [norm_back(): return (grad_hidden, jnp.sum(grad_normed * unit, 0))]
    convert_element_type x4 -> x0, waiting for transfers between devices: 93.2 us -> none  [layer_backward(): grad_value = grad_value_rows.reshape(row_count, -1).astype(jnp.bfloat16)]
    dynamic_slice x28 -> x2, local copies, waits for them, and re-layouts: 76.9 us -> 0.16 us  [the longest x1 0.1 us: shards(): seg_rows = lax.dynamic_slice_in_dim(segments, row_start, rows, 0)]
  transfers between devices with their start and end apart: 40 -> 29, of which waited for: 31 -> 10; matrix products, arithmetic and copies ran while one was open for 19% -> 16% of each run, Pallas kernels for 0% -> 30%
where the time goes in v1:
time: 1310 us
  Pallas kernels  635 us (48%)
  waiting for transfers between devices  263 us (20%)
  matrix products  186 us (14%)
  other arithmetic  92.4 us (7%)
  blocking collectives  66.7 us (5%)
  local copies, waits for them, and re-layouts  32.1 us (2%)
  between operations  16.2 us (1%)
  starting transfers between devices  15.5 us (1%)
    pallas_call x8, Pallas kernels, sum_over_tensor(): pl.pallas_call(functools.partial(sum_kernel, pieces), out_shape=jax.Shape...  557 us
    dot_general x20, matrix products, dot_f32(): lax.dot_general(a, b, (((ca,), (cb,)), ((), ())), preferred_element_type=...  141 us
    reduce_scatter x4, waiting for transfers between devices, own_shard(): zero = lax.psum_scatter(zero, both, scatter_dimension=axis, tiled=True)  118 us
    reduce_scatter x4, waiting for transfers between devices, own_shard(): one = lax.psum_scatter(one, both, scatter_dimension=axis, tiled=True)  87.5 us
    reduce_scatter x2, waiting for transfers between devices, layer_backward(): lax.psum_scatter(dkv_part, 'dp', scatter_dimension=0, tiled=True)  47.1 us
    pallas_call x2, Pallas kernels, attend_back(): pl.pallas_call(functools.partial(attend_back_kernel, rows, step), out_sha...  46.9 us
    pallas_call x2, Pallas kernels, attend(): pl.pallas_call(functools.partial(attend_kernel, rows, step), out_shape=(j...  31 us
    dot_general x2, matrix products, layer_forward(): gate_up = jnp.dot(normed_two, w_gu, preferred_element_type=F32)  26.5 us
  transfers between devices with their start and end apart: 29, of which 10 were waited for; matrix products, arithmetic and copies ran while one was open for 16% of the time, Pallas kernels for 30%

profile of v1, /device:TPU:1, one launch (start us, length us, event | category | flops | bytes accessed | tf_op | source)
XLA Modules:
  0.0 1306.3 jit_solution(6926717174070518367)
XLA Ops:
  31.7 21.8 %all_gather.35 = bf16[8,2,512]{2,1,0:T(2,128)(2,1)S(1)} all-gather(bf16[1,2,512]{2,1,0:T(2,128)(2,1)S(1)} %pad_maximum_fusion.17), channel_id=1, replica_groups=mesh['section'=2,'tensor'=4,'dp'=4] {'section','dp'}, dimensions={0}, use_global_device_ids=true | all-gather | bytes 18432 | tf_op jit(solution)/shard_map/all_gather | solution.py:392
  65.4 14.1 %all_gather.36 = bf16[2560,128]{0,1:T(8,128)(2,1)S(1)} all-gather(bf16[640,128]{0,1:T(8,128)(2,1)S(1)} %maximum_bitcast_fusion.2), channel_id=1, replica_groups=mesh['section'=2,'tensor'=4,'dp'=4] {'dp'}, dimensions={0}, use_global_device_ids=true | all-gather | bytes 819200 | tf_op jit(solution)/shard_map/all_gather | solution.py:314
  82.1 15.5 %attend.2 = (bf16[512,640]{1,0:T(8,128)(2,1)S(1)}, f32[8,640]{1,0:T(8,128)S(1)}) custom-call(s32[1]{0:T(128)} %bitcast.1.start_ref, bf16[512,640]{1,0:T(8,128)(2,1)S(1)} %bitcast.144, bf16[2560,128]{1,0:T(8,128)(2,1)S(1)} %copy.69.kv_ref, bf16[128,2560]{1,0:T(8,128)(2,1)S(1)} %bitcast.140, bf16[2560,640]{1,0:T(8,128)(2,1)S(1)} %copy-done.19), custom_call_target="tpu_custom_call" | custom-call | flops 13421772800 | bytes 3276800 | tf_op jit(solution)/shard_map/attend/pallas_call | solution.py:213
  102.5 71.7 %sum_tensor.8 = bf16[640,2048]{1,0:T(8,128)(2,1)S(1)} custom-call(bf16[640,2048]{1,0:T(8,128)(2,1)S(1)} %convolution_convert_fusion.13.p_ref), custom_call_target="tpu_custom_call" | custom-call | tf_op jit(solution)/shard_map/sum_tensor/pallas_call | solution.py:102
  178.4 12.4 fusion.103
  203.7 72.7 %sum_tensor.9 = bf16[640,2048]{1,0:T(8,128)(2,1)S(1)} custom-call(bf16[640,2048]{1,0:T(8,128)(2,1)S(1)} %convolution_convert_fusion.12.p_ref), custom_call_target="tpu_custom_call" | custom-call | tf_op jit(solution)/shard_map/sum_tensor/pallas_call | solution.py:102
  286.9 10.0 all_gather.41
  299.4 15.5 %attend.3 = (bf16[512,640]{1,0:T(8,128)(2,1)S(1)}, f32[8,640]{1,0:T(8,128)S(1)}) custom-call(s32[1]{0:T(128)} %bitcast.1.start_ref, bf16[512,640]{1,0:T(8,128)(2,1)S(1)} %bitcast.146, bf16[2560,128]{1,0:T(8,128)(2,1)S(1)} %copy.70.kv_ref, bf16[128,2560]{1,0:T(8,128)(2,1)S(1)} %bitcast.142, bf16[2560,640]{1,0:T(8,128)(2,1)S(1)} %copy-done.20), custom_call_target="tpu_custom_call" | custom-call | flops 13421772800 | bytes 3276800 | tf_op jit(solution)/shard_map/attend/pallas_call | solution.py:213
  319.8 65.2 %sum_tensor.10 = bf16[640,2048]{1,0:T(8,128)(2,1)S(1)} custom-call(bf16[640,2048]{1,0:T(8,128)(2,1)S(1)} %convolution_convert_fusion.11.p_ref), custom_call_target="tpu_custom_call" | custom-call | tf_op jit(solution)/shard_map/sum_tensor/pallas_call | solution.py:102
  386.1 14.1 %fusion.102 = f32[640,2816]{1,0:T(8,128)} fusion(bf16[2048,2816]{1,0:T(8,128)(2,1)} %all-gather.21.cloned.1.call-done, bf16[640,2048]{1,0:T(8,128)(2,1)S(1)} %sum_tensor.10, bf16[640,2048]{1,0:T(8,128)(2,1)} %get-tuple-element.80, f32[2048]{0:T(1024)S(1)} %bitcast.186, f32[640]{0:T(1024)S(1)} %add_rsqrt_fusion), kind=kOutput, calls=%fused_computation.241 | convolution fusion | flops 7389839360 | bytes 23996928 | tf_op jit(solution)/shard_map/dot_general | solution.py:321
  400.2 12.3 multiply_convert_fusion.5
  414.3 10.6 convolution_convert_fusion.9.p_ref
  424.9 62.0 %sum_tensor.12 = bf16[640,2048]{1,0:T(8,128)(2,1)S(1)} custom-call(bf16[640,2048]{1,0:T(8,128)(2,1)S(1)} %convolution_convert_fusion.9.p_ref), custom_call_target="tpu_custom_call" | custom-call | tf_op jit(solution)/shard_map/sum_tensor/pallas_call | solution.py:102
  495.5 23.4 %attend_back.2 = (bf16[512,640]{1,0:T(8,128)(2,1)S(1)}, bf16[2560,128]{1,0:T(8,128)(2,1)}) custom-call(s32[1]{0:T(128)} %bitcast.1.start_ref, bf16[512,640]{1,0:T(8,128)(2,1)S(1)} %bitcast.147, bf16[512,640]{1,0:T(8,128)(2,1)S(1)} %convolution_convert_fusion.17.do_ref, bf16[512,640]{1,0:T(8,128)(2,1)S(1)} %copy-done.24, ...), custom_call_target="tpu_custom_call" | custom-call | flops 33554432000 | bytes 3276800 | tf_op jit(solution)/shard_map/attend_back/pallas_call | solution.py:246
  519.4 37.3 %reduce-scatter.11.cloned.1.call-done = bf16[640,128]{1,0:T(8,128)(2,1)} async-done(((bf16[2560,128]{1,0:T(8,128)(2,1)}), bf16[640,128]{1,0:T(8,128)(2,1)}) %reduce-scatter.11.cloned.1.call-update) | async-done | bytes 163856 | tf_op jit(solution)/shard_map/reduce_scatter | solution.py:353
  564.8 70.8 %sum_tensor.13 = bf16[640,2048]{1,0:T(8,128)(2,1)S(1)} custom-call(bf16[640,2048]{1,0:T(8,128)(2,1)S(1)} %convolution_convert_fusion.8.p_ref), custom_call_target="tpu_custom_call" | custom-call | tf_op jit(solution)/shard_map/sum_tensor/pallas_call | solution.py:102
  639.8 9.6 multiply_convert_fusion.3
  649.4 11.7 convolution_convert_fusion.7.p_ref
  661.1 69.7 %sum_tensor.14 = bf16[640,2048]{1,0:T(8,128)(2,1)S(1)} custom-call(bf16[640,2048]{1,0:T(8,128)(2,1)S(1)} %convolution_convert_fusion.7.p_ref), custom_call_target="tpu_custom_call" | custom-call | tf_op jit(solution)/shard_map/sum_tensor/pallas_call | solution.py:102
  739.9 23.4 %attend_back.3 = (bf16[512,640]{1,0:T(8,128)(2,1)S(1)}, bf16[2560,128]{1,0:T(8,128)(2,1)}) custom-call(s32[1]{0:T(128)} %bitcast.1.start_ref, bf16[512,640]{1,0:T(8,128)(2,1)S(1)} %bitcast.145, bf16[512,640]{1,0:T(8,128)(2,1)S(1)} %convolution_convert_fusion.16.do_ref, bf16[512,640]{1,0:T(8,128)(2,1)S(1)} %copy-done.22, ...), custom_call_target="tpu_custom_call" | custom-call | flops 33554432000 | bytes 3276800 | tf_op jit(solution)/shard_map/attend_back/pallas_call | solution.py:246
  781.3 9.8 reduce-scatter.13.cloned.1.call-done
  801.2 8.7 convolution_convert_fusion.2
  811.7 8.1 convolution_convert_fusion.3
  821.5 15.0 %convolution_convert_fusion = bf16[2048,2816]{1,0:T(8,128)(2,1)} fusion(bf16[640,1408]{1,0:T(8,128)(2,1)} %copy-done.72, bf16[640,1408]{1,0:T(8,128)(2,1)} %copy-done.71, bf16[640,2048]{1,0:T(8,128)(2,1)S(1)} %copy-done.3, bf16[640,2048]{1,0:T(8,128)(2,1)} %get-tuple-element.80, f32[2048]{0:T(1024)S(1)} %bitcast.189, f32[640]{0:T(1024)S(1)} %copy-done.59), kind=kOutput, calls=%fused_computation | convolution fusion | flops 7402815488 | bytes 20392448 | tf_op jit(solution)/shard_map/dot_general | solution.py:23
  836.6 15.2 %convolution_convert_fusion.1 = bf16[2048,2816]{1,0:T(8,128)(2,1)} fusion(bf16[640,1408]{1,0:T(8,128)(2,1)} %get-tuple-element.84, bf16[640,1408]{1,0:T(8,128)(2,1)} %get-tuple-element.83, bf16[640,2048]{1,0:T(8,128)(2,1)} %copy-done.4, f32[2048]{0:T(1024)S(1)} %bitcast.185, f32[640]{0:T(1024)S(1)} %copy-done.57, bf16[2,640,2048]{2,1,0:T(8,128)(2,1)} %param.14, ...), kind=kOutput, calls=%fused_computation.1 | convolution fusion | flops 7402815488 | bytes 20392452 | tf_op jit(solution)/shard_map/dot_general | solution.py:23
  853.4 7.4 convolution_convert_fusion.10.p_ref
  860.8 72.9 %sum_tensor.11 = bf16[640,2048]{1,0:T(8,128)(2,1)S(1)} custom-call(bf16[640,2048]{1,0:T(8,128)(2,1)S(1)} %convolution_convert_fusion.10.p_ref), custom_call_target="tpu_custom_call" | custom-call | tf_op jit(solution)/shard_map/sum_tensor/pallas_call | solution.py:102
  941.2 71.9 %sum_tensor.15 = bf16[640,2048]{1,0:T(8,128)(2,1)S(1)} custom-call(bf16[640,2048]{1,0:T(8,128)(2,1)S(1)} %convolution_convert_fusion.6.p_ref), custom_call_target="tpu_custom_call" | custom-call | tf_op jit(solution)/shard_map/sum_tensor/pallas_call | solution.py:102
  1036.2 20.7 %psum.7 = f32[2,2,2048]{2,1,0:T(2,128)S(1)} all-reduce(f32[2,2,2048]{2,1,0:T(2,128)S(1)} %reshape.456), channel_id=1, replica_groups=mesh['section'=2,'tensor'=4,'dp'=4] {'dp','section'}, use_global_device_ids=true, to_apply=%region_14.15 | all-reduce | flops 8192 | bytes 65536 | tf_op jit(solution)/shard_map/psum | solution.py:456
  1075.1 27.9 %reduce-scatter.27.cloned.1.call-done = bf16[1408,256]{1,0:T(8,128)(2,1)} async-done(((bf16[1408,2048]{1,0:T(8,128)(2,1)}), bf16[1408,256]{1,0:T(8,128)(2,1)}) %reduce-scatter.27.cloned.1.call-update) | async-done | bytes 720912 | tf_op jit(solution)/shard_map/reduce_scatter | solution.py:446
  1105.8 87.4 %reduce-scatter.25.cloned.1.call-done = bf16[256,2816]{1,0:T(8,128)(2,1)} async-done(((bf16[2048,2816]{1,0:T(8,128)(2,1)}), bf16[256,2816]{1,0:T(8,128)(2,1)}) %reduce-scatter.25.cloned.1.call-update) | async-done | bytes 1441808 | tf_op jit(solution)/shard_map/reduce_scatter | solution.py:447
  1193.2 90.2 %reduce-scatter.23.cloned.1.call-done = bf16[256,2816]{1,0:T(8,128)(2,1)} async-done(((bf16[2048,2816]{1,0:T(8,128)(2,1)}), bf16[256,2816]{1,0:T(8,128)(2,1)}) %reduce-scatter.23.cloned.1.call-update) | async-done | bytes 1441808 | tf_op jit(solution)/shard_map/reduce_scatter | solution.py:446
  (367 shorter events, 210.9 us)
Async XLA Ops:
  7.2 52.7 %all-gather.9.cloned.1.call-start = ((), (), s32[]{:S(2)}) async-start(), calls=%async_computation.10 | async-start | bytes 2949120 | tf_op jit(solution)/shard_map/all_gather | solution.py:406
  10.8 1.7 collective-permute-start
  13.4 85.1 %all-gather.11.cloned.1.call-start = ((), (), s32[]{:S(2)}) async-start(), calls=%async_computation.11 | async-start | bytes 2359296 | tf_op jit(solution)/shard_map/all_gather | solution.py:406
  14.8 1.6 collective-permute-start.1
  17.3 161.1 %all-gather.13.cloned.1.call-start = ((), (), s32[]{:S(2)}) async-start(), calls=%async_computation.12 | async-start | bytes 12976128 | tf_op jit(solution)/shard_map/all_gather | solution.py:406
  20.1 3.3 collective-permute-start.2
  25.5 170.8 %all-gather.15.cloned.1.call-start = ((), (), s32[]{:S(2)}) async-start(), calls=%async_computation.13 | async-start | bytes 6488064 | tf_op jit(solution)/shard_map/all_gather | solution.py:406
  25.9 2.3 collective-permute-start.3
  29.4 252.0 %all-gather.17.cloned.1.call-start = ((), (), s32[]{:S(2)}) async-start(), calls=%async_computation.14 | async-start | bytes 2949120 | tf_op jit(solution)/shard_map/all_gather | solution.py:406
  30.0 285.8 %all-gather.19.cloned.1.call-start = ((), (), s32[]{:S(2)}) async-start(), calls=%async_computation.15 | async-start | bytes 2359296 | tf_op jit(solution)/shard_map/all_gather | solution.py:406
  30.6 355.5 %all-gather.21.cloned.1.call-start = ((), (), s32[]{:S(2)}) async-start(), calls=%async_computation.16 | async-start | bytes 12976128 | tf_op jit(solution)/shard_map/all_gather | solution.py:406
  31.3 368.9 %all-gather.23.cloned.1.call-start = ((), (), s32[]{:S(2)}) async-start(), calls=%async_computation.17 | async-start | bytes 6488064 | tf_op jit(solution)/shard_map/all_gather | solution.py:406
  56.2 122.1 %copy-start.46 = (f32[1,4,1,512]{3,2,1,0:T(1,128)}, f32[1,4,1,512]{3,2,1,0:T(1,128)S(1)}, u32[]{:S(2)}) copy-start(f32[1,4,1,512]{3,2,1,0:T(1,128)S(1)} %get-tuple-element.126) | copy-start | bytes 24580
  56.2 433.3 %copy-start.48 = (f32[1,4,1,512]{3,2,1,0:T(1,128)}, f32[1,4,1,512]{3,2,1,0:T(1,128)S(1)}, u32[]{:S(2)}) copy-start(f32[1,4,1,512]{3,2,1,0:T(1,128)S(1)} %get-tuple-element.124) | copy-start | bytes 24580
  59.8 496.9 %reduce-scatter.11.cloned.1.call-start = ((), (), s32[]{:S(2)}) async-start(), calls=%async_computation.18 | async-start | bytes 819200 | tf_op jit(solution)/shard_map/reduce_scatter | solution.py:353
  385.1 104.4 %copy-start.2 = (bf16[640,2048]{1,0:T(8,128)(2,1)}, bf16[640,2048]{1,0:T(8,128)(2,1)S(1)}, u32[]{:S(2)}) copy-start(bf16[640,2048]{1,0:T(8,128)(2,1)S(1)} %sum_tensor.10) | copy-start | bytes 7864324
  519.0 272.2 %reduce-scatter.13.cloned.1.call-start = ((), (), s32[]{:S(2)}) async-start(), calls=%async_computation.19 | async-start | bytes 819200 | tf_op jit(solution)/shard_map/reduce_scatter | solution.py:353
  763.4 271.4 %reduce-scatter.21.cloned.1.call-start = ((), (), s32[]{:S(2)}) async-start(), calls=%async_computation.23 | async-start | bytes 2359296 | tf_op jit(solution)/shard_map/reduce_scatter | solution.py:447
  769.1 265.7 %reduce-scatter.19.cloned.1.call-start = ((), (), s32[]{:S(2)}) async-start(), calls=%async_computation.22 | async-start | bytes 2359296 | tf_op jit(solution)/shard_map/reduce_scatter | solution.py:446
  775.1 284.6 %reduce-scatter.17.cloned.1.call-start = ((), (), s32[]{:S(2)}) async-start(), calls=%async_computation.21 | async-start | bytes 2949120 | tf_op jit(solution)/shard_map/reduce_scatter | solution.py:447
  781.3 278.5 %reduce-scatter.15.cloned.1.call-start = ((), (), s32[]{:S(2)}) async-start(), calls=%async_computation.20 | async-start | bytes 2949120 | tf_op jit(solution)/shard_map/reduce_scatter | solution.py:446
  801.2 274.0 %reduce-scatter.29.cloned.1.call-start = ((), (), s32[]{:S(2)}) async-start(), calls=%async_computation.27 | async-start | bytes 6488064 | tf_op jit(solution)/shard_map/reduce_scatter | solution.py:447
  810.0 293.0 %reduce-scatter.27.cloned.1.call-start = ((), (), s32[]{:S(2)}) async-start(), calls=%async_computation.26 | async-start | bytes 6488064 | tf_op jit(solution)/shard_map/reduce_scatter | solution.py:446
  819.8 373.4 %reduce-scatter.25.cloned.1.call-start = ((), (), s32[]{:S(2)}) async-start(), calls=%async_computation.25 | async-start | bytes 12976128 | tf_op jit(solution)/shard_map/reduce_scatter | solution.py:447
  836.6 446.8 %reduce-scatter.23.cloned.1.call-start = ((), (), s32[]{:S(2)}) async-start(), calls=%async_computation.24 | async-start | bytes 12976128 | tf_op jit(solution)/shard_map/reduce_scatter | solution.py:446
  851.9 163.0 %collective-permute-start.5 = (bf16[640,2048]{1,0:T(8,128)(2,1)}, bf16[640,2048]{1,0:T(8,128)(2,1)S(1)}, u32[]{:S(2)}, u32[]{:S(2)}) collective-permute-start(bf16[640,2048]{1,0:T(8,128)(2,1)} %copy-done.31), channel_id=1, source_target_pairs={{0,16},{1,17},{2,18},{3,19},{4,20},{5,21},{6,22},{7,23},{8,24},{9,... | collective-permute-start | bytes 7864328 | tf_op jit(solution)/shard_map/ppermute | solution.py:439
  937.0 87.8 %collective-permute-start.4 = (bf16[640,2048]{1,0:T(8,128)(2,1)}, bf16[640,2048]{1,0:T(8,128)(2,1)}, u32[]{:S(2)}, u32[]{:S(2)}) collective-permute-start(bf16[640,2048]{1,0:T(8,128)(2,1)} %broadcast_select_fusion), channel_id=1, source_target_pairs={{0,16},{16,0},{1,17},{17,1},{2,18},{18,2},{3,19},{19,3},{4,20},{20... | collective-permute-start | bytes 7864328 | tf_op jit(solution)/shard_map/ppermute | solution.py:435
  1019.9 44.3 %collective-permute-start.6 = (bf16[640,2048]{1,0:T(8,128)(2,1)}, bf16[640,2048]{1,0:T(8,128)(2,1)}, u32[]{:S(2)}, u32[]{:S(2)}) collective-permute-start(bf16[640,2048]{1,0:T(8,128)(2,1)} %get-tuple-element.82), channel_id=1, source_target_pairs={{16,0},{17,1},{18,2},{19,3},{20,4},{21,5},{22,6},{23,7},{24,8},{25... | collective-permute-start | bytes 7864328 | tf_op jit(solution)/shard_map/ppermute | solution.py:440
  1036.0 21.6 %collective-permute-start.8 = (bf16[512,256]{1,0:T(8,128)(2,1)S(1)}, bf16[512,256]{1,0:T(8,128)(2,1)S(1)}, u32[]{:S(2)}, u32[]{:S(2)}) collective-permute-start(bf16[512,256]{1,0:T(8,128)(2,1)S(1)} %broadcast_select_fusion.17), channel_id=1, source_target_pairs={{0,16},{16,0},{1,17},{17,1},{2,18},{18,2},{3,19},{19,3},{4,20},{20... | collective-permute-start | bytes 786440 | tf_op jit(solution)/shard_map/ppermute | solution.py:448
  1060.9 14.1 %collective-permute-start.7 = (bf16[256,640]{1,0:T(8,128)(2,1)S(1)}, bf16[256,640]{1,0:T(8,128)(2,1)S(1)}, u32[]{:S(2)}, u32[]{:S(2)}) collective-permute-start(bf16[256,640]{1,0:T(8,128)(2,1)S(1)} %broadcast_select_fusion.13), channel_id=1, source_target_pairs={{0,16},{16,0},{1,17},{17,1},{2,18},{18,2},{3,19},{19,3},{4,20},{20... | collective-permute-start | bytes 983048 | tf_op jit(solution)/shard_map/ppermute | solution.py:448
  1105.1 187.1 %collective-permute-start.10 = (bf16[1408,256]{1,0:T(8,128)(2,1)}, bf16[1408,256]{1,0:T(8,128)(2,1)}, u32[]{:S(2)}, u32[]{:S(2)}) collective-permute-start(bf16[1408,256]{1,0:T(8,128)(2,1)} %broadcast_select_fusion.7), channel_id=1, source_target_pairs={{0,16},{16,0},{1,17},{17,1},{2,18},{18,2},{3,19},{19,3},{4,20},{20... | collective-permute-start | bytes 2162696 | tf_op jit(solution)/shard_map/ppermute | solution.py:448
  1286.0 9.6 collective-permute-start.9
  (84 other events, 1990.6 us)
Sparse Core Ops, SparseCore 0:
  13.5 32.7 all-gather.8
  48.2 31.4 all-gather.10
  82.1 67.4 all-gather.12
  151.9 44.3 all-gather.14
  198.6 30.1 all-gather.16
  231.0 28.1 all-gather.18
  261.7 69.3 all-gather.20
  333.6 44.2 all-gather.22
  519.1 37.5 reduce-scatter.10
  763.5 27.5 reduce-scatter.12
  794.4 41.2 reduce-scatter.20
  839.2 41.2 reduce-scatter.18
  883.8 43.6 reduce-scatter.16
  930.7 47.1 reduce-scatter.14
  981.2 59.0 reduce-scatter.28
  1044.0 59.0 reduce-scatter.26
  1106.4 86.7 reduce-scatter.24
  1196.6 86.7 reduce-scatter.22

commit v2 on v1

v2 whole, which is shorter than its diff:
```python
import functools

import jax
import jax.numpy as jnp
from jax import lax
from jax.experimental import pallas as pl
from jax.experimental.pallas import tpu as pltpu
from jax.sharding import PartitionSpec as P

HEAD = 64
HALF = HEAD // 2
TRUNK = 1024
GROUP = 384
EPSILON = 1e-05
THETA = 10000.0
MASKED = -1e30
BF = jnp.bfloat16
F32 = jnp.float32
MESH = pl.DeviceIdType.MESH
BOTH = ("dp", "section")


def dot_f32(a, b, ca, cb):
    return lax.dot_general(a, b, (((ca,), (cb,)), ((), ())), preferred_element_type=F32)


BLOCK = 256
PIECE = 128
NO_COST = pl.CostEstimate(flops=1, transcendentals=0, bytes_accessed=1)


def product_sum_kernel(cfg, *refs):
    n_arrays, n_x, first_column, sides, stagger = cfg
    refs = list(refs)
    take = lambda n: [refs.pop(0) for _ in range(n)]
    from_hbm = take(n_arrays)
    (w_hbm,) = take(1)
    (o_ref,) = take(1)
    (g_hbm,) = take(1) if sides else (None,)
    arrays = take(n_arrays)
    load_sem, w_buf, p_buf, a_buf, s_buf, b_buf, c_buf, w_sem, sa, ra, sb, rb, sc, rc, so, turn = take(16)
    g_buf, g_sem = take(2) if sides else (None, None)
    pieces = p_buf.shape[0]
    per_block = BLOCK // PIECE
    blocks = pieces // per_block
    depth = w_buf.shape[2]

    t = lax.axis_index("tensor")
    sec = lax.axis_index("section")
    dat = lax.axis_index("dp")
    inner = (t == 1) | (t == 2)
    outer = jnp.logical_not(inner)
    pair = (sec, t + 1 - 2 * lax.rem(t, 2), dat)
    mid = (sec, 3 - t, dat)
    mate = (1 - sec, t, dat)

    def columns(j):
        return pl.ds(pl.multiple_of(j * BLOCK, BLOCK), BLOCK)

    def lanes(i):
        return pl.ds(pl.multiple_of(i * PIECE, PIECE), PIECE)

    def to_inner(i):
        return pltpu.make_async_remote_copy(
            p_buf.at[i], a_buf.at[i], sa.at[i], ra.at[i], device_id=pair, device_id_type=MESH
        )

    def across(i):
        return pltpu.make_async_remote_copy(
            s_buf.at[i], b_buf.at[i], sb.at[i], rb.at[i], device_id=mid, device_id_type=MESH
        )

    def to_outer(i):
        return pltpu.make_async_remote_copy(
            c_buf.at[i], c_buf.at[i], sc.at[i], rc.at[i], device_id=pair, device_id_type=MESH
        )

    def store(i):
        return pltpu.make_async_copy(c_buf.at[i], o_ref.at[:, lanes(i)], so.at[i])

    def load(k):
        return pltpu.make_async_copy(from_hbm[k], arrays[k], load_sem.at[k])

    def fetch(j, slot):
        return pltpu.make_async_copy(
            w_hbm.at[columns(j), pl.ds(first_column, depth)], w_buf.at[slot], w_sem.at[slot]
        )

    def flush(j, slot):
        return pltpu.make_async_copy(g_buf.at[slot], g_hbm.at[columns(j), :], g_sem.at[slot])

    for k in range(n_x):
        load(k).start()
    fetch(0, 0).start()
    for k in range(n_x, n_arrays):
        load(k).start()
    barrier = pltpu.get_barrier_semaphore()
    extra = 1 if stagger else 0
    pl.semaphore_signal(barrier, inc=1, device_id=pair, device_id_type=MESH)
    if stagger:
        pl.semaphore_signal(barrier, inc=1, device_id=mate, device_id_type=MESH)

    @pl.when(inner)
    def _():
        pl.semaphore_signal(barrier, inc=1, device_id=mid, device_id_type=MESH)
        pl.semaphore_wait(barrier, 2 + extra)

    @pl.when(outer)
    def _():
        pl.semaphore_wait(barrier, 1 + extra)

    if stagger:
        @pl.when(sec == 1)
        def _():
            pl.semaphore_wait(turn, 1)

    for k in range(n_x):
        load(k).wait()

    def first(i):
        to_inner(i).wait_recv()
        s_buf[i] = (p_buf[i].astype(F32) + a_buf[i].astype(F32)).astype(BF)
        across(i).start()

    def second(i):
        across(i).wait_recv()
        c_buf[i] = (s_buf[i].astype(F32) + b_buf[i].astype(F32)).astype(BF)
        to_outer(i).start()
        store(i).start()

    def step(j, _):
        slot = lax.rem(j, 2)
        fetch(j, slot).wait()

        @pl.when(j + 1 < blocks)
        def _():
            fetch(j + 1, 1 - slot).start()

        total, start = None, 0
        for x_ref in arrays[:n_x]:
            width = x_ref.shape[1]
            term = dot_f32(x_ref[...], w_buf[slot, :, start : start + width], 1, 1)
            total = term if total is None else total + term
            start += width
        total = total.astype(BF)
        for u in range(per_block):
            p_buf[per_block * j + u] = total[:, u * PIECE : (u + 1) * PIECE]

        @pl.when(outer)
        def _():
            for u in range(per_block):
                to_inner(per_block * j + u).start()

        @pl.when(inner)
        def _():
            for u in range(per_block):
                i = per_block * j + u
                first(i)

                @pl.when(j >= 1)
                def _():
                    second(i - per_block)

        if sides:

            @pl.when(j == 0)
            def _():
                for k in range(n_x, n_arrays):
                    load(k).wait()

            @pl.when(j >= 2)
            def _():
                flush(j - 2, slot).wait()

            start = 0
            for a, bs in sides:
                a_t = arrays[a][:, columns(j)].T
                for b in bs:
                    width = arrays[b].shape[1]
                    g_buf[slot, :, start : start + width] = jnp.dot(
                        a_t, arrays[b][...], preferred_element_type=F32
                    ).astype(BF)
                    start += width
            flush(j, slot).start()
        return 0

    lax.fori_loop(0, blocks, step, 0)

    @pl.when(inner)
    def _():
        for u in range(per_block):
            second(pieces - per_block + u)

        def last(i, _):
            across(i).wait_send()
            to_outer(i).wait_send()
            store(i).wait()
            return 0

        lax.fori_loop(0, pieces, last, 0)

    @pl.when(outer)
    def _():
        def arrive(i, _):
            to_outer(i).wait_recv()
            store(i).start()
            return 0

        def last(i, _):
            to_inner(i).wait_send()
            store(i).wait()
            return 0

        lax.fori_loop(0, pieces, arrive, 0)
        lax.fori_loop(0, pieces, last, 0)

    if sides:
        flush(blocks - 2, (blocks - 2) % 2).wait()
        flush(blocks - 1, (blocks - 1) % 2).wait()

    if stagger:

        @pl.when(sec == 0)
        def _():
            pl.semaphore_signal(turn, inc=1, device_id=mate, device_id_type=MESH)


def product_sum(xs, weights, first_column, others=(), sides=(), stagger=False, key=1):
    assert lax.axis_size("tensor") == 4
    arrays = (*xs, *others)
    rows, model = xs[0].shape[0], weights.shape[0]
    depth = sum(x.shape[1] for x in xs)
    pieces = model // PIECE
    anywhere = pl.BlockSpec(memory_space=pl.ANY)
    buf = pltpu.VMEM((pieces, rows, PIECE), BF)
    sem = pltpu.SemaphoreType.DMA((pieces,))
    two = pltpu.SemaphoreType.DMA((2,))
    out_shape = [jax.ShapeDtypeStruct((rows, model), BF)]
    out_specs = [anywhere]
    scratch = [pltpu.VMEM(x.shape, x.dtype) for x in arrays]
    scratch += [pltpu.SemaphoreType.DMA((len(arrays),)), pltpu.VMEM((2, BLOCK, depth), BF)]
    scratch += [buf, buf, buf, buf, buf, two, *[sem] * 7, pltpu.SemaphoreType.REGULAR]
    side_width = sum(arrays[b].shape[1] for _, bs in sides for b in bs)
    if sides:
        out_shape.append(jax.ShapeDtypeStruct((model, side_width), BF))
        out_specs.append(anywhere)
        scratch += [pltpu.VMEM((2, BLOCK, side_width), BF), two]
    cfg = (len(arrays), len(xs), first_column, tuple(sides), stagger)
    out = pl.pallas_call(
        functools.partial(product_sum_kernel, cfg),
        out_shape=out_shape,
        in_specs=[anywhere] * (len(arrays) + 1),
        out_specs=out_specs,
        scratch_shapes=scratch,
        compiler_params=pltpu.CompilerParams(
            collective_id=key, has_side_effects=True, vmem_limit_bytes=56 << 20
        ),
        cost_estimate=NO_COST,
        name=f"product_sum_{key}",
    )(*arrays, weights)
    return out if sides else out[0]


def dp_peers(count):
    me = lax.axis_index("dp")
    sec, t = lax.axis_index("section"), lax.axis_index("tensor")
    others = [lax.rem(me + k, count) for k in range(1, count)]
    return me, others, [(sec, t, other) for other in others]


def greet(ids):
    barrier = pltpu.get_barrier_semaphore()
    for device in ids:
        pl.semaphore_signal(barrier, inc=1, device_id=device, device_id_type=MESH)
    pl.semaphore_wait(barrier, len(ids))


def turn_rows(x, cos_ref, sin_ref):
    lane = lax.broadcasted_iota(jnp.int32, x.shape, 1)
    width = x.shape[1]
    partner = jnp.where(lane < HALF, pltpu.roll(x, width - HALF, 1), pltpu.roll(x, HALF, 1))
    return x * cos_ref[...] + partner * sin_ref[...]


def gather_kernel(count, raw_ref, cos_ref, sin_ref, o_ref, t_ref, x_ref, send, recv):
    me, _, ids = dp_peers(count)
    x_ref[...] = turn_rows(raw_ref[...], cos_ref, sin_ref).astype(BF)
    greet(ids)
    copies = [
        pltpu.make_async_remote_copy(
            x_ref, o_ref.at[me], send.at[k], recv.at[k], device_id=device, device_id_type=MESH
        )
        for k, device in enumerate(ids)
    ]
    for copy in copies:
        copy.start()
    o_ref[me] = x_ref[...]
    for copy in copies:
        copy.wait()
    t_ref[...] = o_ref[...].reshape(t_ref.shape[1], t_ref.shape[0]).T


def scatter_kernel(count, x_ref, cos_ref, sin_ref, o_ref, buf, send, recv):
    me, others, ids = dp_peers(count)
    greet(ids)
    copies = [
        pltpu.make_async_remote_copy(
            x_ref.at[others[k]], buf.at[k], send.at[k], recv.at[k], device_id=device, device_id_type=MESH
        )
        for k, device in enumerate(ids)
    ]
    for copy in copies:
        copy.start()
    total = x_ref[me].astype(F32)
    for k, copy in enumerate(copies):
        copy.wait()
        total = total + buf[k].astype(F32)
    o_ref[...] = turn_rows(total, cos_ref, sin_ref).astype(BF)


def gather_rows(raw, cos_rows, sin_rows):
    count = lax.axis_size("dp")
    rows, width = raw.shape
    in_vmem = pl.BlockSpec(memory_space=pltpu.VMEM)
    sem = pltpu.SemaphoreType.DMA((count - 1,))
    out, out_t = pl.pallas_call(
        functools.partial(gather_kernel, count),
        out_shape=(
            jax.ShapeDtypeStruct((count, rows, width), BF),
            jax.ShapeDtypeStruct((width, count * rows), BF),
        ),
        in_specs=[in_vmem] * 3,
        out_specs=(in_vmem, in_vmem),
        scratch_shapes=[pltpu.VMEM((rows, width), BF), sem, sem],
        compiler_params=pltpu.CompilerParams(collective_id=3, has_side_effects=True),
        cost_estimate=NO_COST,
        name="gather_rows",
    )(raw, cos_rows, sin_rows)
    return out.reshape(-1, width), out_t


def scatter_rows(x, cos_rows, sin_rows):
    count = lax.axis_size("dp")
    rows, width = x.shape[0] // count, x.shape[1]
    in_vmem = pl.BlockSpec(memory_space=pltpu.VMEM)
    sem = pltpu.SemaphoreType.DMA((count - 1,))
    return pl.pallas_call(
        functools.partial(scatter_kernel, count),
        out_shape=jax.ShapeDtypeStruct((rows, width), BF),
        in_specs=[in_vmem] * 3,
        out_specs=in_vmem,
        scratch_shapes=[pltpu.VMEM((count - 1, rows, width), x.dtype), sem, sem],
        compiler_params=pltpu.CompilerParams(collective_id=4, has_side_effects=True),
        cost_estimate=NO_COST,
        name="scatter_rows",
    )(x.reshape(count, rows, width), cos_rows, sin_rows)


def reduce_kernel(g_hbm, o_ref, mine, away, got, xs, ys, xr, yr, load_sem, send, recv):
    sec, t, dat = lax.axis_index("section"), lax.axis_index("tensor"), lax.axis_index("dp")
    flip_x = dat + 1 - 2 * lax.rem(dat, 2)
    flip_y = lax.rem(dat + 2, 4)
    across = lax.rem(flip_x + 2, 4)
    by_x, by_y, mate = (sec, t, flip_x), (sec, t, flip_y), (1 - sec, t, dat)
    rows = g_hbm.shape[1] // 2
    upper, lower = pl.ds(0, rows), pl.ds(rows, rows)
    order = (across, flip_x, flip_y, dat)
    loads = []
    for k, block in enumerate(order):
        loads.append(pltpu.make_async_copy(g_hbm.at[2 * block + 1 - sec], away.at[k], load_sem.at[k]))
        loads.append(pltpu.make_async_copy(g_hbm.at[2 * block + sec], mine.at[k], load_sem.at[4 + k]))
    for copy in loads:
        copy.start()
    greet([by_x, by_y, mate])

    def remote(src, dst, k, device):
        return pltpu.make_async_remote_copy(
            src, dst, send.at[k], recv.at[k], device_id=device, device_id_type=MESH
        )

    swaps = [remote(away.at[k], got.at[k], k, mate) for k in range(4)]
    for k in range(4):
        loads[2 * k].wait()
        swaps[k].start()
    outs = []
    for k in range(4):
        loads[2 * k + 1].wait()
        swaps[k].wait_recv()
        mine[k] = (mine[k].astype(F32) + got[k].astype(F32)).astype(BF)
        if k == 0:
            outs += [remote(mine.at[0, upper], xs.at[0], 4, by_x), remote(mine.at[0, lower], ys.at[0], 5, by_y)]
        if k == 1:
            outs += [remote(mine.at[1, upper], xs.at[1], 6, by_x)]
        if k == 2:
            outs += [remote(mine.at[2, lower], ys.at[1], 7, by_y)]
        for copy in outs[-(2 if k == 0 else 1) :]:
            if k < 3:
                copy.start()
    outs[0].wait_recv()
    mine[2, upper] = (mine[2, upper].astype(F32) + xs[0].astype(F32)).astype(BF)
    outs.append(remote(mine.at[2, upper], yr, 8, by_y))
    outs[4].start()
    outs[1].wait_recv()
    mine[1, lower] = (mine[1, lower].astype(F32) + ys[0].astype(F32)).astype(BF)
    outs.append(remote(mine.at[1, lower], xr, 9, by_x))
    outs[5].start()
    outs[2].wait_recv()
    outs[3].wait_recv()
    outs[4].wait_recv()
    o_ref[upper] = (mine[3, upper].astype(F32) + xs[1].astype(F32) + yr[...].astype(F32)).astype(BF)
    outs[5].wait_recv()
    o_ref[lower] = (mine[3, lower].astype(F32) + ys[1].astype(F32) + xr[...].astype(F32)).astype(BF)
    for copy in swaps + outs:
        copy.wait_send()


def reduce_now(g):
    if lax.axis_size("dp") != 4:
        return reduce_gradient(g)
    rows, width = g.shape[0] // 8, g.shape[1]
    part = pltpu.VMEM((2, rows // 2, width), BF)
    whole = pltpu.VMEM((4, rows, width), BF)
    end = pltpu.VMEM((rows // 2, width), BF)
    return pl.pallas_call(
        reduce_kernel,
        out_shape=jax.ShapeDtypeStruct((rows, width), BF),
        in_specs=[pl.BlockSpec(memory_space=pl.ANY)],
        out_specs=pl.BlockSpec(memory_space=pltpu.VMEM),
        scratch_shapes=[
            whole, whole, whole, part, part, end, end,
            pltpu.SemaphoreType.DMA((8,)), pltpu.SemaphoreType.DMA((10,)), pltpu.SemaphoreType.DMA((10,)),
        ],
        compiler_params=pltpu.CompilerParams(
            collective_id=12, has_side_effects=True, vmem_limit_bytes=40 << 20
        ),
        cost_estimate=NO_COST,
        name="reduce_now",
    )(g.reshape(8, rows, width))


def share_kernel(count, x_ref, o_ref, buf, send, recv):
    sec, t, dat = lax.axis_index("section"), lax.axis_index("tensor"), lax.axis_index("dp")
    peers = [
        (lax.rem(sec + k // count, 2), t, lax.rem(dat + k % count, count)) for k in range(1, 2 * count)
    ]
    greet(peers)
    copies = [
        pltpu.make_async_remote_copy(
            x_ref.at[peer[0], peer[2]], buf.at[k], send.at[k], recv.at[k], device_id=peer, device_id_type=MESH
        )
        for k, peer in enumerate(peers)
    ]
    for copy in copies:
        copy.start()
    total = x_ref[sec, dat]
    for k, copy in enumerate(copies):
        copy.wait()
        total = total + buf[k]
    o_ref[...] = total


def share_sums(x):
    count = lax.axis_size("dp")
    in_vmem = pl.BlockSpec(memory_space=pltpu.VMEM)
    sem = pltpu.SemaphoreType.DMA((2 * count - 1,))
    return pl.pallas_call(
        functools.partial(share_kernel, count),
        out_shape=jax.ShapeDtypeStruct(x.shape[2:], F32),
        in_specs=[in_vmem],
        out_specs=in_vmem,
        scratch_shapes=[pltpu.VMEM((2 * count - 1, *x.shape[2:]), F32), sem, sem],
        compiler_params=pltpu.CompilerParams(collective_id=8, has_side_effects=True),
        cost_estimate=NO_COST,
        name="share_sums",
    )(x)


def group_start(first_row):
    past = lax.max(first_row - TRUNK, 0)
    return pl.multiple_of(TRUNK + GROUP * lax.div(past, GROUP), 128)


def windows(tree_len, rows, tile, first_row):
    if tile % 128 == 0 and GROUP % tile == 0 and TRUNK % tile == 0 and rows % tile == 0:
        return (pl.ds(0, TRUNK), pl.ds(group_start(first_row), GROUP))
    return (pl.ds(0, tree_len),)


def beside(ref, head, count):
    parts = [ref[HEAD * (head + k) : HEAD * (head + k + 1), :] for k in range(count)]
    return parts[0] if count == 1 else jnp.concatenate(parts, axis=1)


def turned_beside(ref, cos, sin, head, count):
    parts = []
    for k in range(count):
        base = HEAD * (head + k)
        first, second = ref[base : base + HALF, :], ref[base + HALF : base + HEAD, :]
        parts.append(jnp.concatenate([first * cos - second * sin, second * cos + first * sin], axis=0))
    whole = parts[0] if count == 1 else jnp.concatenate(parts, axis=1)
    return (whole.astype(BF).astype(F32) * HEAD**-0.5).astype(BF)


def as_rows(x, tile, count):
    parts = [x[:, k * tile : (k + 1) * tile] for k in range(count)]
    return (parts[0] if count == 1 else jnp.concatenate(parts, axis=0)).T


def row_beside(ref, head, count):
    parts = [ref[head + k : head + k + 1, :] for k in range(count)]
    return parts[0] if count == 1 else jnp.concatenate(parts, axis=1)


def attend_kernel(
    rows, step, start_ref, q_ref, kv_ref, kvt_ref, bias_ref, cos_ref, sin_ref, o_ref, on_ref, lse_ref
):
    tile = q_ref.shape[1]
    heads = q_ref.shape[0] // HEAD
    first_row = start_ref[0] + pl.program_id(0) * tile
    wins = windows(kv_ref.shape[0], rows, tile, first_row)
    for head in range(0, heads, step):
        q = turned_beside(q_ref, cos_ref[...], sin_ref[...], head, step)
        scores = []
        for win in wins:
            bias = bias_ref[win, :].astype(F32)
            bias = bias if step == 1 else jnp.concatenate([bias] * step, axis=1)
            scores.append(dot_f32(kv_ref[win, :HEAD], q, 1, 0) + bias)
        top = functools.reduce(jnp.maximum, [jnp.max(s, 0, keepdims=True) for s in scores])
        expo = [jnp.exp(s - top) for s in scores]
        total = sum(jnp.sum(e, 0, keepdims=True) for e in expo)
        out = sum(dot_f32(kvt_ref[HEAD:, win], e.astype(BF), 1, 0) for win, e in zip(wins, expo))
        out = out / total
        on_ref[:, HEAD * head : HEAD * (head + step)] = as_rows(out, tile, step).astype(BF)
        out = out.astype(BF)
        lse = top + jnp.log(total)
        for k in range(step):
            o_ref[HEAD * (head + k) : HEAD * (head + k + 1), :] = out[:, k * tile : (k + 1) * tile]
            lse_ref[head + k : head + k + 1, :] = lse[:, k * tile : (k + 1) * tile]


def attend_back_kernel(
    rows, step, start_ref, q_ref, do_ref, o_ref, lse_ref, kv_ref, kvt_ref, bias_ref, cos_ref, sin_ref,
    dq_ref, dkv_ref, dk_acc, dv_acc,
):
    tile = q_ref.shape[1]
    heads = q_ref.shape[0] // HEAD
    first_row = start_ref[0] + pl.program_id(0) * tile
    wins = windows(kv_ref.shape[0], rows, tile, first_row)

    @pl.when(pl.program_id(0) == 0)
    def _():
        dk_acc[...] = jnp.zeros_like(dk_acc)
        dv_acc[...] = jnp.zeros_like(dv_acc)

    for head in range(0, heads, step):
        q = turned_beside(q_ref, cos_ref[...], sin_ref[...], head, step)
        do = beside(do_ref, head, step)
        out = beside(o_ref, head, step)
        lse = row_beside(lse_ref, head, step)
        delta = jnp.sum(do.astype(F32) * out.astype(F32), 0, keepdims=True)
        dq = jnp.zeros((HEAD, step * tile), F32)
        for win in wins:
            bias = bias_ref[win, :].astype(F32)
            bias = bias if step == 1 else jnp.concatenate([bias] * step, axis=1)
            p = jnp.exp(dot_f32(kv_ref[win, :HEAD], q, 1, 0) + bias - lse)
            dp = dot_f32(kv_ref[win, HEAD:], do, 1, 0)
            ds = (p * (dp - delta)).astype(BF)
            dk_acc[win, :] += dot_f32(ds, q, 1, 1)
            dv_acc[win, :] += dot_f32(p.astype(BF), do, 1, 1)
            dq = dq + dot_f32(kvt_ref[:HEAD, win], ds, 1, 0)
        dq = dq * HEAD**-0.5
        cos, sin = cos_ref[...], sin_ref[...]
        turned = []
        for k in range(step):
            first = dq[:HALF, k * tile : (k + 1) * tile]
            second = dq[HALF:, k * tile : (k + 1) * tile]
            turned += [first * cos + second * sin, second * cos - first * sin]
        dq_ref[:, HEAD * head : HEAD * (head + step)] = jnp.concatenate(turned, axis=0).T.astype(BF)

    @pl.when(pl.program_id(0) == pl.num_programs(0) - 1)
    def _():
        dkv_ref[...] = jnp.concatenate([dk_acc[...], dv_acc[...]], axis=1).astype(BF)


def row_tile(rows):
    return 128 if rows % 128 == 0 else rows


def attend(start, q_t, kv, kv_t, bias_t, cos_t, sin_t):
    width, rows = q_t.shape
    heads, tree_len, tile = width // HEAD, kv.shape[0], row_tile(rows)
    step = 2 if tile % 128 == 0 and heads % 2 == 0 else 1
    column = lambda i, s: (0, i)
    whole = lambda i, s: (0, 0)
    return pl.pallas_call(
        functools.partial(attend_kernel, rows, step),
        out_shape=(
            jax.ShapeDtypeStruct((width, rows), BF),
            jax.ShapeDtypeStruct((rows, width), BF),
            jax.ShapeDtypeStruct((heads, rows), F32),
        ),
        grid_spec=pltpu.PrefetchScalarGridSpec(
            num_scalar_prefetch=1,
            grid=(rows // tile,),
            in_specs=[
                pl.BlockSpec((width, tile), column),
                pl.BlockSpec((tree_len, 2 * HEAD), whole),
                pl.BlockSpec((2 * HEAD, tree_len), whole),
                pl.BlockSpec((tree_len, tile), column),
                pl.BlockSpec((HALF, tile), column),
                pl.BlockSpec((HALF, tile), column),
            ],
            out_specs=(
                pl.BlockSpec((width, tile), column),
                pl.BlockSpec((tile, width), lambda i, s: (i, 0)),
                pl.BlockSpec((heads, tile), column),
            ),
        ),
        compiler_params=pltpu.CompilerParams(vmem_limit_bytes=40 << 20),
        cost_estimate=NO_COST,
        name="attend",
    )(start, q_t, kv, kv_t, bias_t, cos_t, sin_t)


def attend_back(start, q_t, do_t, o_t, lse, kv, kv_t, bias_t, cos_t, sin_t):
    width, rows = q_t.shape
    heads, tree_len, tile = width // HEAD, kv.shape[0], row_tile(rows)
    step = 2 if tile % 128 == 0 and heads % 2 == 0 else 1
    column = lambda i, s: (0, i)
    whole = lambda i, s: (0, 0)
    return pl.pallas_call(
        functools.partial(attend_back_kernel, rows, step),
        out_shape=(
            jax.ShapeDtypeStruct((rows, width), BF),
            jax.ShapeDtypeStruct((tree_len, 2 * HEAD), BF),
        ),
        grid_spec=pltpu.PrefetchScalarGridSpec(
            num_scalar_prefetch=1,
            grid=(rows // tile,),
            in_specs=[
                pl.BlockSpec((width, tile), column),
                pl.BlockSpec((width, tile), column),
                pl.BlockSpec((width, tile), column),
                pl.BlockSpec((heads, tile), column),
                pl.BlockSpec((tree_len, 2 * HEAD), whole),
                pl.BlockSpec((2 * HEAD, tree_len), whole),
                pl.BlockSpec((tree_len, tile), column),
                pl.BlockSpec((HALF, tile), column),
                pl.BlockSpec((HALF, tile), column),
            ],
            out_specs=(
                pl.BlockSpec((tile, width), lambda i, s: (i, 0)),
                pl.BlockSpec((tree_len, 2 * HEAD), whole),
            ),
            scratch_shapes=[pltpu.VMEM((tree_len, HEAD), F32), pltpu.VMEM((tree_len, HEAD), F32)],
        ),
        compiler_params=pltpu.CompilerParams(vmem_limit_bytes=48 << 20),
        cost_estimate=NO_COST,
        name="attend_back",
    )(start, q_t, do_t, o_t, lse, kv, kv_t, bias_t, cos_t, sin_t)


def inverse_rms(hidden):
    return lax.rsqrt(jnp.mean(hidden * hidden, -1, keepdims=True) + EPSILON)


def norm_back(grad_normed, hidden, scale_rows, gain):
    unit = hidden * scale_rows
    grad_unit = grad_normed * gain
    grad_hidden = scale_rows * (grad_unit - unit * jnp.mean(grad_unit * unit, -1, keepdims=True))
    return grad_hidden, jnp.sum(grad_normed * unit, 0)


def layer_forward(hidden, weights, tables, stagger):
    gain_one, gain_two, w_attn, w_mlp, width, split, units = weights
    start, bias_t, cos_t, sin_t, cos_rows, sin_rows = tables
    scale_one = inverse_rms(hidden)
    normed_one = (hidden * scale_one * gain_one).astype(BF)
    q_t = dot_f32(w_attn[:, :width], normed_one, 0, 1)
    kv, kv_t = gather_rows(
        jnp.dot(normed_one, w_attn[:, width:split], preferred_element_type=F32), cos_rows, -sin_rows
    )
    o_t, o, lse = attend(start, q_t, kv, kv_t, bias_t, cos_t, sin_t)
    attn_sum = product_sum((o,), w_attn, split, stagger=stagger, key=1 if stagger else 2)
    middle = hidden + attn_sum.astype(F32)
    scale_two = inverse_rms(middle)
    normed_two = (middle * scale_two * gain_two).astype(BF)
    gate_up = jnp.dot(normed_two, w_mlp[:, : 2 * units], preferred_element_type=F32)
    gate, up = gate_up[:, :units], gate_up[:, units:]
    inner = (gate * jax.nn.sigmoid(gate) * up).astype(BF)
    return (hidden, scale_one, normed_one, q_t, kv, kv_t, o_t, o, lse, middle, scale_two, normed_two, gate, up, inner)


def units_backward(branch, weights, kept):
    gate, up = kept[12:14]
    units = weights[-1]
    d_inner = dot_f32(branch, weights[3][:, 2 * units :], 1, 0)
    sig = jax.nn.sigmoid(gate)
    d_gate = (d_inner * up * sig * (1.0 + gate * (1.0 - sig))).astype(BF)
    d_up = (d_inner * gate * sig).astype(BF)
    return d_gate, d_up


def middle_backward(grad_out, d_two, weights, tables, kept):
    gain_one, gain_two, w_attn, w_mlp, width, split, units = weights
    start, bias_t, cos_t, sin_t, cos_rows, sin_rows = tables
    hidden, scale_one, normed_one, q_t, kv, kv_t, o_t, o, lse, middle, scale_two = kept[:11]
    grad_norm, d_gain_two = norm_back(d_two.astype(F32), middle, scale_two, gain_two)
    grad_middle = grad_out + grad_norm
    grad_attn = grad_middle.astype(BF)
    do_t = dot_f32(w_attn[:, split : split + width], grad_attn, 0, 1).astype(BF)
    return grad_middle, grad_attn, do_t, d_gain_two


def attention_backward(do_t, tables, kept):
    start, bias_t, cos_t, sin_t, cos_rows, sin_rows = tables
    q_t, kv, kv_t, o_t, o, lse = kept[3:9]
    dq, dkv_part = attend_back(start, q_t, do_t, o_t, lse, kv, kv_t, bias_t, cos_t, sin_t)
    return dq, scatter_rows(dkv_part, cos_rows, sin_rows)


def first_backward(grad_middle, d_one, weights, kept):
    hidden, scale_one = kept[:2]
    grad_norm, d_gain_one = norm_back(d_one.astype(F32), hidden, scale_one, weights[0])
    return grad_middle + grad_norm, d_gain_one


def reduce_gradient(x):
    return lax.psum_scatter(x, BOTH, scatter_dimension=0, tiled=True)


def shards(
    inputs, cotangent, seg_ids, positions, parents, gain_attn, w_query, key_weight, value_weight,
    w_out, gain_mlp, w_gate, w_up, w_down,
):
    sec = lax.axis_index("section")
    data = lax.axis_index("dp")
    sections = lax.axis_size("section")
    devices = lax.axis_size("dp")
    assert sections == 2 and inputs.shape[0] == 2
    first_core = sec == 0
    rows, model = inputs.shape[1], inputs.shape[2]
    swap = [(0, 1), (1, 0)]

    hidden = lax.dynamic_index_in_dim(inputs, sec, 0, keepdims=False).astype(F32)
    cot = lax.dynamic_index_in_dim(cotangent, sec, 0, keepdims=False).astype(F32)
    segments = lax.dynamic_index_in_dim(seg_ids, sec, 0, keepdims=False)
    places = lax.dynamic_index_in_dim(positions, sec, 0, keepdims=False)
    parent = lax.dynamic_index_in_dim(parents, sec, 0, keepdims=False)

    width, span, units = w_query.shape[2], key_weight.shape[2], w_gate.shape[2]
    split = width + 2 * span
    shard_list = (
        jnp.concatenate(
            [w_query[0], key_weight[0], value_weight[0], w_out[0].T, gain_attn.T, gain_mlp.T], 1
        ).astype(BF),
        jnp.concatenate([w_gate[0], w_up[0], w_down[0].T], 1).astype(BF),
    )
    halves = []
    for shard in shard_list:
        half = shard.shape[0] // 2
        low, high = shard[:half], shard[half:]
        got = lax.ppermute(jnp.where(first_core, high, low), "section", swap)
        halves.append((jnp.where(first_core, low, got), jnp.where(first_core, got, high)))
    def gathered(halves):
        return [lax.all_gather(half, BOTH, axis=0, tiled=True) for half in halves]

    def with_gains(w_attn, w_mlp):
        gains = w_attn[:, split + width :].astype(F32).T
        return (gains[0:1], gains[1:2], w_attn, w_mlp, width, split, units)

    (attn_zero, attn_one), (mlp_zero, mlp_one) = halves
    zero = with_gains(*gathered((attn_zero, mlp_zero)))
    attn_one, mlp_one = gathered((attn_one, mlp_one))

    seg_count = parent.shape[0]
    labels = jnp.arange(seg_count, dtype=jnp.int32)
    parent_hot = (parent[:, None] == labels[None, :]).astype(F32)
    ancestry = jnp.eye(seg_count, dtype=F32) + parent_hot + jnp.dot(parent_hot, parent_hot)
    ancestry = (ancestry > 0.5).astype(F32)
    row_start = data * rows
    seg_rows = lax.dynamic_slice_in_dim(segments, row_start, rows, 0)
    pos_rows = lax.dynamic_slice_in_dim(places, row_start, rows, 0)
    key_hot = (segments[:, None] == labels[None, :]).astype(F32)
    query_hot = (labels[:, None] == seg_rows[None, :]).astype(F32)
    reach = jnp.dot(key_hot, jnp.dot(ancestry.T, query_hot))
    allowed = (reach > 0.5) & (places[:, None] <= pos_rows[None, :])
    bias_t = jnp.where(allowed, 0.0, MASKED).astype(BF)
    frequency = THETA ** (-(jnp.arange(HALF, dtype=F32) * 2.0 / HEAD))
    angles = frequency[:, None] * pos_rows.astype(F32)[None, :]
    cos_t, sin_t = jnp.cos(angles), jnp.sin(angles)
    ones = jnp.ones((rows, HEAD), F32)
    cos_rows = jnp.concatenate([cos_t.T, cos_t.T, ones], 1)
    sin_rows = jnp.concatenate([sin_t.T, -sin_t.T, 0 * ones], 1)
    tables = (row_start.astype(jnp.int32).reshape(1), bias_t, cos_t, sin_t, cos_rows, sin_rows)

    kept_zero = layer_forward(hidden, zero, tables, True)
    mlp_sum = product_sum(kept_zero[-1:], zero[3], 2 * units, key=5)
    out_zero = (kept_zero[9] + mlp_sum.astype(F32)).astype(BF)

    out_zero, attn_one = lax.optimization_barrier((out_zero, attn_one))
    one = with_gains(attn_one, mlp_one)
    kept_one = layer_forward(out_zero.astype(F32), one, tables, False)
    branch = cot.astype(BF)
    d_gate, d_up = units_backward(branch, one, kept_one)
    mlp_sum, d_mlp_one = product_sum(
        kept_one[-1:], one[3], 2 * units, (kept_one[11], branch, d_gate, d_up), ((1, (3, 4)), (2, (0,))), key=6
    )
    out_one = (kept_one[9] + mlp_sum.astype(F32)).astype(BF)
    g_mlp_one = reduce_gradient(d_mlp_one)
    d_gate, d_up, mlp_sum = lax.optimization_barrier((d_gate, d_up, mlp_sum))
    d_two = product_sum((d_gate, d_up), one[3], 0, key=7)
    grad_middle, grad_attn, do_t, d_gain_mlp_one = middle_backward(cot, d_two, one, tables, kept_one)
    dq, dkv = attention_backward(do_t, tables, kept_one)
    d_one, d_attn_one = product_sum(
        (dq, dkv), one[2], 0, (kept_one[2], grad_attn, kept_one[7]), ((2, (0, 1)), (3, (4,))), key=9
    )
    g_attn_one = reduce_gradient(d_attn_one)
    grad_one, d_gain_attn_one = first_backward(grad_middle, d_one, one, kept_one)

    branch = grad_one.astype(BF)
    d_gate, d_up = units_backward(branch, zero, kept_zero)
    d_gate, d_up, g_mlp_one = lax.optimization_barrier((d_gate, d_up, g_mlp_one))
    d_two, d_mlp_zero = product_sum(
        (d_gate, d_up), zero[3], 0, (kept_zero[11], branch, kept_zero[14]), ((2, (0, 1)), (3, (4,))), key=10
    )
    g_mlp_zero = reduce_gradient(d_mlp_zero)
    grad_middle, grad_attn, do_t, d_gain_mlp_zero = middle_backward(
        branch.astype(F32), d_two, zero, tables, kept_zero
    )
    do_t, g_attn_one = lax.optimization_barrier((do_t, g_attn_one))
    dq, dkv = attention_backward(do_t, tables, kept_zero)
    d_one, d_attn_zero = product_sum(
        (dq, dkv), zero[2], 0, (kept_zero[2], grad_attn, kept_zero[7]), ((2, (0, 1)), (3, (4,))), key=9
    )
    g_attn_zero = reduce_now(d_attn_zero)
    grad_zero, d_gain_attn_zero = first_backward(grad_middle, d_one, zero, kept_zero)

    grad_zero, grad_one, out_zero, out_one, g_mlp_zero, g_mlp_one, g_attn_one, d_gain_attn_zero = (
        lax.optimization_barrier(
            (grad_zero, grad_one, out_zero, out_one, g_mlp_zero, g_mlp_one, g_attn_one, d_gain_attn_zero)
        )
    )

    out_got = lax.ppermute(jnp.where(first_core, out_one, out_zero), "section", swap)
    layer_output = jnp.stack(
        [jnp.where(first_core, out_zero, out_got), jnp.where(first_core, out_got, out_one)]
    )
    one_got = lax.ppermute(grad_one.astype(BF), "section", [(0, 1)]).astype(F32)
    zero_got = lax.ppermute(grad_zero.astype(BF), "section", [(1, 0)]).astype(F32)
    input_grad = jnp.stack(
        [jnp.where(first_core, grad_zero, one_got), jnp.where(first_core, zero_got, grad_one)]
    )

    def own_shard(zero, one):
        got = lax.ppermute(jnp.where(first_core, one, zero), "section", swap)
        return jnp.where(first_core, zero, got), jnp.where(first_core, got, one)

    def joined(halves, start, stop):
        return jnp.concatenate([h[:, start:stop] for h in halves], 0).astype(F32)

    g_mlp = own_shard(g_mlp_zero, g_mlp_one)
    g_attn = own_shard(g_attn_zero, g_attn_one)
    d_gains = jnp.stack([d_gain_attn_zero, d_gain_mlp_zero, d_gain_attn_one, d_gain_mlp_one])
    d_gains = d_gains.reshape(2, 2, devices, -1).swapaxes(1, 2).reshape(2, devices, -1, 128)
    g_gain = share_sums(d_gains).reshape(2, -1)
    return (
        layer_output[None],
        input_grad[None],
        g_gain[0][None],
        joined(g_attn, 0, width)[None],
        joined(g_attn, width, width + span)[None],
        joined(g_attn, width + span, split)[None],
        joined(g_attn, split, split + width).T[None],
        g_gain[1][None],
        joined(g_mlp, 0, units)[None],
        joined(g_mlp, units, 2 * units)[None],
        joined(g_mlp, 2 * units, 3 * units).T[None],
    )


def solution(mesh):
    in_specs = (
        P(None, "dp", None),
        P(None, "dp", None),
        P(),
        P(),
        P(),
        P("section", "dp"),
        P("section", "dp", "tensor"),
        P("section", "dp", "tensor"),
        P("section", "dp", "tensor"),
        P("section", "tensor", "dp"),
        P("section", "dp"),
        P("section", "dp", "tensor"),
        P("section", "dp", "tensor"),
        P("section", "tensor", "dp"),
    )
    out_specs = (
        P("section", None, "dp", None),
        P("section", None, "dp", None),
        P("section", "dp"),
        P("section", "dp", "tensor"),
        P("section", "dp", "tensor"),
        P("section", "dp", "tensor"),
        P("section", "tensor", "dp"),
        P("section", "dp"),
        P("section", "dp", "tensor"),
        P("section", "dp", "tensor"),
        P("section", "tensor", "dp"),
    )
    return jax.shard_map(shards, mesh=mesh, in_specs=in_specs, out_specs=out_specs, check_vma=False)
```

time: 1310 us -> 943 us (0.72)
  waiting for transfers between devices: 263 us -> 28.9 us
  matrix products: 186 us -> 68.1 us
  blocking collectives: 66.7 us -> 0 us
  other arithmetic: 92.4 us -> 129 us
  local copies, waits for them, and re-layouts: 32.1 us -> 49.9 us
    reduce_scatter x10 -> x3, waiting for transfers between devices: 253 us -> 0.01 us  [reduce_gradient(): return lax.psum_scatter(x, BOTH, scatter_dimension=0, tiled=True)]
    dot_general x20 -> x6, matrix products: 141 us -> 37.1 us  [dot_f32(): lax.dot_general(a, b, (((ca,), (cb,)), ((), ())), preferred_element_type=...]
    all_gather x3 -> x0, blocking collectives: 46 us -> none  [the longest x2 24.2 us: layer_forward(): kv = lax.all_gather(kv_rows, 'dp', axis=0, tiled=True)]
    convert_element_type x9 -> x14, other arithmetic: 8.8 us -> 45.8 us  [the longest x1 9.63 us: shards(): branch = grad_one.astype(BF)]
    all_gather x8 -> x4, waiting for transfers between devices: 0.3 us -> 21.5 us  [gathered(): return [lax.all_gather(half, BOTH, axis=0, tiled=True) for half in halves]]
    psum x1 -> x0, blocking collectives: 20.7 us -> none  [shards(): lax.psum(jnp.stack([*d_gain_zero, *d_gain_one]).reshape(2, 2, model), both)]
    unnamed x178 -> x156, local copies, waits for them, and re-layouts: 23.5 us -> 37.6 us
    pallas_call x8 -> x14, Pallas kernels: 557 us -> 558 us  [the longest x8 462 us: product_sum(): pl.pallas_call(functools.partial(product_sum_kernel, cfg), out_shape=out_...]
  transfers between devices with their start and end apart: 29 -> 14, of which waited for: 10 -> 3; matrix products, arithmetic and copies ran while one was open for 16% -> 19% of each run, Pallas kernels for 30% -> 58%
where the time goes in v2:
time: 943 us; the launch traced here: 938 us
  Pallas kernels  636 us (67%)
  other arithmetic  129 us (14%)
  matrix products  68.1 us (7%)
  local copies, waits for them, and re-layouts  49.9 us (5%)
  waiting for transfers between devices  28.9 us (3%)
  between operations  15.6 us (2%)
  starting transfers between devices  10 us (1%)
    pallas_call x8, Pallas kernels, product_sum(): pl.pallas_call(functools.partial(product_sum_kernel, cfg), out_shape=out_...  462 us
    pallas_call x2, Pallas kernels, attend_back(): pl.pallas_call(functools.partial(attend_back_kernel, rows, step), out_sha...  46 us
    unnamed x156, local copies, waits for them, and re-layouts  37.6 us
    dot_general x6, matrix products, dot_f32(): lax.dot_general(a, b, (((ca,), (cb,)), ((), ())), preferred_element_type=...  37.1 us
    pallas_call x2, Pallas kernels, gather_rows(): pl.pallas_call(functools.partial(gather_kernel, count), out_shape=(jax.Sh...  34.9 us
    pallas_call x2, Pallas kernels, attend(): pl.pallas_call(functools.partial(attend_kernel, rows, step), out_shape=(j...  32.2 us
    pallas_call x2, Pallas kernels, scatter_rows(): pl.pallas_call(functools.partial(scatter_kernel, count), out_shape=jax.Sh...  28.8 us
    pallas_call x1, Pallas kernels, reduce_now(): pl.pallas_call(reduce_kernel, out_shape=jax.ShapeDtypeStruct((rows, width...  24.6 us
  transfers between devices with their start and end apart: 14, of which 3 were waited for; matrix products, arithmetic and copies ran while one was open for 19% of the time, Pallas kernels for 58%

profile of v2, /device:TPU:1, one launch (start us, length us, event | category | flops | bytes accessed | tf_op | source)
XLA Modules:
  0.0 937.6 jit_solution(13942787760411538108)
XLA Ops:
  41.6 21.5 %all-gather.5.cloned.1.call-done.refs_1_.refs_5_ = bf16[2048,1154]{1,0:T(8,128)(2,1)} async-done(((bf16[256,1154]{1,0:T(8,128)(2,1)}), bf16[2048,1154]{1,0:T(8,128)(2,1)}) %all-gather.5.cloned.1.call-update) | async-done | bytes 4726800 | tf_op jit(solution)/shard_map/all_gather | solution.py:766
  71.7 18.6 %gather_rows.2 = (bf16[4,640,128]{2,1,0:T(8,128)(2,1)}, bf16[128,2560]{1,0:T(8,128)(2,1)}) custom-call(f32[640,128]{1,0:T(8,128)} %fusion.61.raw_ref, f32[640,128]{1,0:T(8,128)} %maximum_maximum_fusion.cos_ref, f32[640,128]{1,0:T(8,128)} %get-tuple-element.158.sin_ref), custom_call_target="tpu_custom_call" | custom-call | flops 1 | bytes 1 | tf_op jit(solution)/shard_map/gather_rows/pallas_call | solution.py:326
  94.7 16.1 %attend.2 = (bf16[512,640]{1,0:T(8,128)(2,1)S(1)}, bf16[640,512]{1,0:T(8,128)(2,1)S(1)}, f32[8,640]{1,0:T(8,128)S(1)}) custom-call(s32[1]{0:T(128)} %bitcast.2.start_ref, f32[512,640]{1,0:T(8,128)S(1)} %fusion.46.q_ref, bf16[2560,128]{1,0:T(8,128)(2,1)S(1)} %bitcast.120, bf16[128,2560]{1,0:T(8,128)(2,1)S(1)} %copy-done.12, ...), custom_call_target="tpu_custom_call" | custom-call | flops 1 | bytes 1 | tf_op jit(solution)/shard_map/attend/pallas_call | solution.py:595
  113.5 85.1 %product_sum_1.1 = bf16[640,2048]{1,0:T(8,128)(2,1)} custom-call(bf16[640,512]{1,0:T(8,128)(2,1)} %copy-done.8, bf16[2048,1154]{1,0:T(8,128)(2,1)} %all-gather.5.cloned.1.call-done.refs_1_.refs_5_), custom_call_target="tpu_custom_call" | custom-call | flops 1 | bytes 1 | tf_op jit(solution)/shard_map/product_sum_1/pallas_call | solution.py:249
  206.8 11.9 %fusion.2 = f32[640,2816]{1,0:T(8,128)S(1)} fusion(bf16[640,2048]{1,0:T(8,128)(2,1)} %multiply_convert_fusion.1.refs_2_, bf16[2048,4224]{1,0:T(8,128)(2,1)} %all-gather.7.cloned.1.call-done.refs_1_.refs_5_), kind=kOutput, calls=%fused_computation.2 | convolution fusion | flops 7381975040 | bytes 21364736 | tf_op jit(solution)/shard_map/dot_general | solution.py:688
  224.3 43.3 %product_sum_5.1 = bf16[640,2048]{1,0:T(8,128)(2,1)} custom-call(bf16[640,1408]{1,0:T(8,128)(2,1)} %multiply_convert_fusion.7.refs_0_.refs_4_, bf16[2048,4224]{1,0:T(8,128)(2,1)} %all-gather.7.cloned.1.call-done.refs_1_.refs_5_), custom_call_target="tpu_custom_call" | custom-call | flops 1 | bytes 1 | tf_op jit(solution)/shard_map/product_sum_5/pallas_call | solution.py:249
  267.6 5.9 add_convert_fusion.1
  282.9 16.2 %gather_rows.3 = (bf16[4,640,128]{2,1,0:T(8,128)(2,1)}, bf16[128,2560]{1,0:T(8,128)(2,1)}) custom-call(f32[640,128]{1,0:T(8,128)} %fusion.63.raw_ref, f32[640,128]{1,0:T(8,128)} %maximum_maximum_fusion.cos_ref, f32[640,128]{1,0:T(8,128)} %get-tuple-element.158.sin_ref), custom_call_target="tpu_custom_call" | custom-call | flops 1 | bytes 1 | tf_op jit(solution)/shard_map/gather_rows/pallas_call | solution.py:326
  303.5 16.1 %attend.3 = (bf16[512,640]{1,0:T(8,128)(2,1)S(1)}, bf16[640,512]{1,0:T(8,128)(2,1)S(1)}, f32[8,640]{1,0:T(8,128)S(1)}) custom-call(s32[1]{0:T(128)} %bitcast.2.start_ref, f32[512,640]{1,0:T(8,128)S(1)} %fusion.50.q_ref, bf16[2560,128]{1,0:T(8,128)(2,1)S(1)} %bitcast.122, bf16[128,2560]{1,0:T(8,128)(2,1)S(1)} %copy-done.16, ...), custom_call_target="tpu_custom_call" | custom-call | flops 1 | bytes 1 | tf_op jit(solution)/shard_map/attend/pallas_call | solution.py:595
  321.3 40.3 %product_sum_2.1 = bf16[640,2048]{1,0:T(8,128)(2,1)} custom-call(bf16[640,512]{1,0:T(8,128)(2,1)} %copy-done.9, bf16[2048,1154]{1,0:T(8,128)(2,1)} %all-gather.9.cloned.1.call-done.refs_1_.refs_5_), custom_call_target="tpu_custom_call" | custom-call | flops 1 | bytes 1 | tf_op jit(solution)/shard_map/product_sum_2/pallas_call | solution.py:249
  367.5 12.1 %fusion = f32[640,2816]{1,0:T(8,128)S(1)} fusion(bf16[640,2048]{1,0:T(8,128)(2,1)} %multiply_convert_fusion.refs_1_, bf16[2048,4224]{1,0:T(8,128)(2,1)} %all-gather.11.cloned.1.call-done.refs_5_.refs_2_), kind=kOutput, calls=%fused_computation | convolution fusion | flops 7381975040 | bytes 21364736 | tf_op jit(solution)/shard_map/dot_general | solution.py:688
  379.6 9.7 %multiply_convert_fusion.5 = (bf16[640,1408]{1,0:T(8,128)(2,1)}, bf16[640,1408]{1,0:T(8,128)(2,1)}, bf16[640,1408]{1,0:T(8,128)(2,1)}) fusion(f32[640,2816]{1,0:T(8,128)S(1)} %fusion, bf16[640,2048]{1,0:T(8,128)(2,1)S(1)} %copy-done.50, bf16[2048,4224]{1,0:T(8,128)(2,1)} %all-gather.11.cloned.1.call-done.refs_5_.refs_2_), kind=kOutput, calls=%fused_computation.71 | convolution fusion | flops 3705405440 | bytes 21004288 | tf_op jit(solution)/shard_map/dot_general | solution.py:24
  389.3 62.6 %product_sum_6.1 = (bf16[640,2048]{1,0:T(8,128)(2,1)}, bf16[2048,4224]{1,0:T(8,128)(2,1)}) custom-call(bf16[640,1408]{1,0:T(8,128)(2,1)} %get-tuple-element.164.refs_0_, bf16[640,2048]{1,0:T(8,128)(2,1)} %multiply_convert_fusion.refs_1_, bf16[640,2048]{1,0:T(8,128)(2,1)} %dynamic-slice_bitcast_fusion.refs_2_, ...), custom_call_target="tpu_custom_call" | custom-call | flops 1 | bytes 1 | tf_op jit(solution)/shard_map/product_sum_6/pallas_call | solution.py:249
  452.0 44.8 %product_sum_7.1 = bf16[640,2048]{1,0:T(8,128)(2,1)} custom-call(bf16[640,1408]{1,0:T(8,128)(2,1)} %get-tuple-element.59.refs_3_.refs_0_, bf16[640,1408]{1,0:T(8,128)(2,1)} %get-tuple-element.60.refs_4_.refs_1_, bf16[2048,4224]{1,0:T(8,128)(2,1)} %all-gather.11.cloned.1.call-done.refs_5_.refs_2_), custom_call_target="tpu_custom_call" | custom-call | flops 1 | bytes 1 | tf_op jit(solution)/shard_map/product_sum_7/pallas_call | solution.py:249
  500.7 4.6 fusion.71.refs_3_
  505.4 4.6 fusion.52.do_ref
  510.0 23.0 %attend_back.2 = (bf16[640,512]{1,0:T(8,128)(2,1)S(1)}, bf16[2560,128]{1,0:T(8,128)(2,1)S(1)}) custom-call(s32[1]{0:T(128)} %bitcast.2.start_ref, f32[512,640]{1,0:T(8,128)S(1)} %copy-done.6, bf16[512,640]{1,0:T(8,128)(2,1)S(1)} %fusion.52.do_ref, bf16[512,640]{1,0:T(8,128)(2,1)S(1)} %copy-done.23, f32[8,640]{1,0:T(8,128)S(1)} %get-tuple-element.62.lse_ref, ...), custom_call_target="tpu_custom_call" | custom-call | flops 1 | bytes 1 | tf_op jit(solution)/shard_map/attend_back/pallas_call | solution.py:631
  534.7 11.4 %scatter_rows.2.refs_1_ = bf16[640,128]{1,0:T(8,128)(2,1)} custom-call(bf16[4,640,128]{2,1,0:T(8,128)(2,1)} %bitcast.125, f32[640,128]{1,0:T(8,128)} %maximum_maximum_fusion.cos_ref, f32[640,128]{1,0:T(8,128)} %get-tuple-element.159.sin_ref), custom_call_target="tpu_custom_call" | custom-call | flops 1 | bytes 1 | tf_op jit(solution)/shard_map/scatter_rows/pallas_call | solution.py:347
  546.1 55.9 %product_sum_9.2 = (bf16[640,2048]{1,0:T(8,128)(2,1)}, bf16[2048,1152]{1,0:T(8,128)(2,1)}) custom-call(bf16[640,512]{1,0:T(8,128)(2,1)} %copy-done.19, bf16[640,128]{1,0:T(8,128)(2,1)} %scatter_rows.2.refs_1_, bf16[640,2048]{1,0:T(8,128)(2,1)} %copy-done.49, bf16[640,2048]{1,0:T(8,128)(2,1)} %copy-done.47, bf16[640,512]{1,0:T(8,128)(2,1)} %copy-done.9, ...), custom_call_target="tpu_custom_call" | custom-call | flops 1 | bytes 1 | tf_op jit(solution)/shard_map/product_sum_9/pallas_call | solution.py:249
  605.8 9.6 %fusion.73 = (bf16[640,2048]{1,0:T(8,128)(2,1)S(1)}, f32[640,2048]{1,0:T(8,128)}, bf16[640,2048]{1,0:T(8,128)(2,1)}) fusion(f32[640]{0:T(1024)S(1)} %broadcast_multiply_fusion.2, f32[2048]{0:T(1024)S(1)} %get-tuple-element.153, bf16[640,2048]{1,0:T(8,128)(2,1)} %get-tuple-element.65, f32[640]{0:T(1024)S(1)} %add_rsqrt_fusion.1, ...), kind=kLoop, calls=%fused_computation.175 | loop fusion | flops 28835840 | bytes 26241028 | tf_op jit(solution)/shard_map/convert_element_type | solution.py:821
  616.9 9.3 multiply_convert_fusion.2
  626.2 70.4 %product_sum_10.1 = (bf16[640,2048]{1,0:T(8,128)(2,1)}, bf16[2048,4224]{1,0:T(8,128)(2,1)}) custom-call(bf16[640,1408]{1,0:T(8,128)(2,1)} %get-tuple-element.67.refs_0_, bf16[640,1408]{1,0:T(8,128)(2,1)} %get-tuple-element.68.refs_1_, bf16[640,2048]{1,0:T(8,128)(2,1)} %multiply_convert_fusion.1.refs_2_, bf16[640,2048]{1,0:T(8,128)(2,1)} %copy-done.39, ...), custom_call_target="tpu_custom_call" | custom-call | flops 1 | bytes 1 | tf_op jit(solution)/shard_map/product_sum_10/pallas_call | solution.py:249
  698.4 4.7 fusion.33
  709.0 4.8 fusion.55.do_ref
  715.1 23.0 %attend_back.3 = (bf16[640,512]{1,0:T(8,128)(2,1)S(1)}, bf16[2560,128]{1,0:T(8,128)(2,1)S(1)}) custom-call(s32[1]{0:T(128)} %bitcast.2.start_ref, f32[512,640]{1,0:T(8,128)S(1)} %copy-done.4, bf16[512,640]{1,0:T(8,128)(2,1)S(1)} %copy-done.24, bf16[512,640]{1,0:T(8,128)(2,1)S(1)} %copy-done.21, f32[8,640]{1,0:T(8,128)S(1)} %get-tuple-element.73.lse_ref, ...), custom_call_target="tpu_custom_call" | custom-call | flops 1 | bytes 1 | tf_op jit(solution)/shard_map/attend_back/pallas_call | solution.py:631
  739.7 17.5 %scatter_rows.3.refs_1_ = bf16[640,128]{1,0:T(8,128)(2,1)} custom-call(bf16[4,640,128]{2,1,0:T(8,128)(2,1)} %bitcast.124, f32[640,128]{1,0:T(8,128)} %maximum_maximum_fusion.cos_ref, f32[640,128]{1,0:T(8,128)} %get-tuple-element.159.sin_ref), custom_call_target="tpu_custom_call" | custom-call | flops 1 | bytes 1 | tf_op jit(solution)/shard_map/scatter_rows/pallas_call | solution.py:347
  757.2 59.3 %product_sum_9.3 = (bf16[640,2048]{1,0:T(8,128)(2,1)}, bf16[2048,1152]{1,0:T(8,128)(2,1)}) custom-call(bf16[640,512]{1,0:T(8,128)(2,1)} %copy-done.18, bf16[640,128]{1,0:T(8,128)(2,1)} %scatter_rows.3.refs_1_, bf16[640,2048]{1,0:T(8,128)(2,1)} %copy-done.48, bf16[640,2048]{1,0:T(8,128)(2,1)} %copy-done.46, bf16[640,512]{1,0:T(8,128)(2,1)} %copy-done.8, ...), custom_call_target="tpu_custom_call" | custom-call | flops 1 | bytes 1 | tf_op jit(solution)/shard_map/product_sum_9/pallas_call | solution.py:249
  821.1 7.5 fusion.23
  831.7 24.6 %reduce_now.1 = bf16[256,1152]{1,0:T(8,128)(2,1)S(1)} custom-call(bf16[8,256,1152]{2,1,0:T(8,128)(2,1)S(1)} %bitcast.119), custom_call_target="tpu_custom_call" | custom-call | flops 1 | bytes 1 | tf_op jit(solution)/shard_map/reduce_now/pallas_call | solution.py:424
  856.3 7.8 share_sums.1
  894.0 6.1 select_bitcast_fusion.1
  925.6 4.9 maximum_bitcast_fusion
  (281 shorter events, 168.8 us)
Async XLA Ops:
  7.2 29.1 %copy-start = (s32[2,13]{1,0:T(2,128)S(1)}, s32[2,13]{1,0:T(2,128)}, u32[]{:S(2)}) copy-start(s32[2,13]{1,0:T(2,128)} %param.18) | copy-start | bytes 316
  7.2 55.9 %all-gather.5.cloned.1.call-start = ((), (), s32[]{:S(2)}) async-start(), calls=%async_computation.3 | async-start | bytes 5898240 | tf_op jit(solution)/shard_map/all_gather | solution.py:766
  15.8 2.1 collective-permute-start
  19.3 187.5 %all-gather.7.cloned.1.call-start = ((), (), s32[]{:S(2)}) async-start(), calls=%async_computation.4 | async-start | bytes 19464192 | tf_op jit(solution)/shard_map/all_gather | solution.py:766
  25.1 4.3 collective-permute-start.1
  31.9 241.6 %all-gather.9.cloned.1.call-start = ((), (), s32[]{:S(2)}) async-start(), calls=%async_computation.5 | async-start | bytes 5898240 | tf_op jit(solution)/shard_map/all_gather | solution.py:766
  32.7 334.8 %all-gather.11.cloned.1.call-start = ((), (), s32[]{:S(2)}) async-start(), calls=%async_computation.6 | async-start | bytes 19464192 | tf_op jit(solution)/shard_map/all_gather | solution.py:766
  33.2 593.0 %reduce-scatter.4.cloned.1.call-start = ((), (), s32[]{:S(2)}) async-start(), calls=%async_computation.7 | async-start | bytes 19464192 | tf_op jit(solution)/shard_map/reduce_scatter | solution.py:729
  36.5 28.7 %copy-start.59 = (f32[640]{0:T(1024)}, f32[640]{0:T(1024)S(1)}, u32[]{:S(2)}) copy-start(f32[640]{0:T(1024)S(1)} %add_rsqrt_fusion.3) | copy-start | bytes 7684
  41.6 261.9 %copy-start.2 = (bf16[2560,640]{1,0:T(8,128)(2,1)}, bf16[2560,640]{1,0:T(8,128)(2,1)S(1)}, u32[]{:S(2)}) copy-start(bf16[2560,640]{1,0:T(8,128)(2,1)S(1)} %select_convert_fusion.bias_ref) | copy-start | bytes 9830404
  65.1 6.5 copy-start.57
  224.2 43.3 %copy-start.31 = (bf16[640,2048]{1,0:T(8,128)(2,1)S(1)}, bf16[640,2048]{1,0:T(8,128)(2,1)}, u32[]{:S(2)}) copy-start(bf16[640,2048]{1,0:T(8,128)(2,1)} %product_sum_1.1) | copy-start | bytes 7864324
  303.5 16.1 %copy-start.5 = (f32[512,640]{1,0:T(8,128)}, f32[512,640]{1,0:T(8,128)S(1)}, u32[]{:S(2)}) copy-start(f32[512,640]{1,0:T(8,128)S(1)} %fusion.50.q_ref) | copy-start | bytes 3932164
  321.3 40.3 %copy-start.28 = (bf16[640,2048]{1,0:T(8,128)(2,1)S(1)}, bf16[640,2048]{1,0:T(8,128)(2,1)}, u32[]{:S(2)}) copy-start(bf16[640,2048]{1,0:T(8,128)(2,1)} %add_convert_fusion.1) | copy-start | bytes 7864324
  367.5 12.1 %copy-start.50 = (bf16[640,2048]{1,0:T(8,128)(2,1)S(1)}, bf16[640,2048]{1,0:T(8,128)(2,1)}, u32[]{:S(2)}) copy-start(bf16[640,2048]{1,0:T(8,128)(2,1)} %dynamic-slice_bitcast_fusion.refs_2_) | copy-start | bytes 7864324
  451.9 261.9 %reduce-scatter.6.cloned.1.call-start = ((), (), s32[]{:S(2)}) async-start(), calls=%async_computation.8 | async-start | bytes 5308416 | tf_op jit(solution)/shard_map/reduce_scatter | solution.py:729
  452.0 44.8 %copy-start.35 = (bf16[640,2048]{1,0:T(8,128)(2,1)S(1)}, bf16[640,2048]{1,0:T(8,128)(2,1)}, u32[]{:S(2)}) copy-start(bf16[640,2048]{1,0:T(8,128)(2,1)} %product_sum_2.1) | copy-start | bytes 7864324
  602.0 226.6 %reduce-scatter.8.cloned.1.call-start = ((), (), s32[]{:S(2)}) async-start(), calls=%async_computation.9 | async-start | bytes 19464192 | tf_op jit(solution)/shard_map/reduce_scatter | solution.py:729
  602.1 14.8 %slice-start.8 = ((s8[7208960]{0:T(1024)(128)(4,1)}), s8[4194304]{0:T(1024)(128)(4,1)S(1)}, s32[]{:S(2)}) async-start(s8[7208960]{0:T(1024)(128)(4,1)} %bitcast.134), calls=%async_computation.18 | async-start | bytes 8388608
  605.8 11.2 %slice-start.9 = ((s8[7208960]{0:T(1024)(128)(4,1)}), s8[3014656]{0:T(1024)(128)(4,1)S(1)}, s32[]{:S(2)}) async-start(s8[7208960]{0:T(1024)(128)(4,1)} %bitcast.134), calls=%async_computation.19 | async-start | bytes 6029312
  757.2 59.4 %copy-start.58 = (f32[2048]{0:T(1024)S(1)}, f32[2048]{0:T(1024)}, u32[]{:S(2)}) copy-start(f32[2048]{0:T(1024)} %copy-done.57) | copy-start | bytes 24580
  757.2 59.4 %copy-start.60 = (f32[640]{0:T(1024)S(1)}, f32[640]{0:T(1024)}, u32[]{:S(2)}) copy-start(f32[640]{0:T(1024)} %copy-done.59) | copy-start | bytes 7684
  757.2 63.8 %copy-start.43 = (bf16[640,2048]{1,0:T(8,128)(2,1)S(1)}, bf16[640,2048]{1,0:T(8,128)(2,1)}, u32[]{:S(2)}) copy-start(bf16[640,2048]{1,0:T(8,128)(2,1)} %get-tuple-element.69) | copy-start | bytes 7864324
  831.7 34.0 %copy-start.51 = (bf16[256,4224]{1,0:T(8,128)(2,1)S(1)}, bf16[256,4224]{1,0:T(8,128)(2,1)}, u32[]{:S(2)}) copy-start(bf16[256,4224]{1,0:T(8,128)(2,1)} %reduce-scatter.4.cloned.1.call-done) | copy-start | bytes 6488068
  864.2 15.9 %collective-permute-start.5 = (bf16[256,1152]{1,0:T(8,128)(2,1)S(1)}, bf16[256,1152]{1,0:T(8,128)(2,1)S(1)}, u32[]{:S(2)}, u32[]{:S(2)}) collective-permute-start(bf16[256,1152]{1,0:T(8,128)(2,1)S(1)} %broadcast_select_fusion.12), channel_id=1, source_target_pairs={{0,16},{16,0},{1,17},{17,1},{2,18},{18,2},{3,19},{19,3},{4,20},{20... | collective-permute-start | bytes 1769480 | tf_op jit(solution)/shard_map/ppermute | solution.py:856
  869.0 6.0 copy-start.44
  869.0 20.6 %collective-permute-start.6 = (bf16[256,4224]{1,0:T(8,128)(2,1)}, bf16[256,4224]{1,0:T(8,128)(2,1)}, u32[]{:S(2)}, u32[]{:S(2)}) collective-permute-start(bf16[256,4224]{1,0:T(8,128)(2,1)} %broadcast_select_fusion.3), channel_id=1, source_target_pairs={{0,16},{16,0},{1,17},{17,1},{2,18},{18,2},{3,19},{19,3},{4,20},{20... | collective-permute-start | bytes 6488072 | tf_op jit(solution)/shard_map/ppermute | solution.py:856
  873.6 6.5 copy-start.56
  873.6 20.4 %collective-permute-start.3 = (bf16[640,2048]{1,0:T(8,128)(2,1)}, bf16[640,2048]{1,0:T(8,128)(2,1)}, u32[]{:S(2)}, u32[]{:S(2)}) collective-permute-start(bf16[640,2048]{1,0:T(8,128)(2,1)} %convert_element_type.209), channel_id=1, source_target_pairs={{0,16},{1,17},{2,18},{3,19},{4,20},{5,21},{6,22},{7,23},{8,24},{9,... | collective-permute-start | bytes 7864328 | tf_op jit(solution)/shard_map/ppermute | solution.py:849
  876.8 38.4 %collective-permute-start.2 = (bf16[640,2048]{1,0:T(8,128)(2,1)}, bf16[640,2048]{1,0:T(8,128)(2,1)}, u32[]{:S(2)}, u32[]{:S(2)}) collective-permute-start(bf16[640,2048]{1,0:T(8,128)(2,1)} %broadcast_select_fusion), channel_id=1, source_target_pairs={{0,16},{16,0},{1,17},{17,1},{2,18},{18,2},{3,19},{19,3},{4,20},{20... | collective-permute-start | bytes 7864328 | tf_op jit(solution)/shard_map/ppermute | solution.py:845
  900.1 20.7 %collective-permute-start.4 = (bf16[640,2048]{1,0:T(8,128)(2,1)}, bf16[640,2048]{1,0:T(8,128)(2,1)}, u32[]{:S(2)}, u32[]{:S(2)}) collective-permute-start(bf16[640,2048]{1,0:T(8,128)(2,1)} %get-tuple-element.168), channel_id=1, source_target_pairs={{16,0},{17,1},{18,2},{19,3},{20,4},{21,5},{22,6},{23,7},{24,8},{25... | collective-permute-start | bytes 7864328 | tf_op jit(solution)/shard_map/ppermute | solution.py:850
  917.6 7.9 slice-start.2
  (56 other events, 184.6 us)
Sparse Core Ops, SparseCore 0:
  19.4 43.6 all-gather.4
  65.6 98.2 all-gather.6
  166.3 41.1 all-gather.8
  209.2 97.0 all-gather.10
  452.0 124.9 reduce-scatter.3
  602.2 54.1 reduce-scatter.5
  696.8 121.7 reduce-scatter.7

commit v3 on v2

--- a/solution.py
+++ b/solution.py
@@ -29,21 +29,78 @@
 NO_COST = pl.CostEstimate(flops=1, transcendentals=0, bytes_accessed=1)
 
 
+def columns_of(i):
+    return pl.ds(pl.multiple_of(i * PIECE, PIECE), PIECE)
+
+
+def row_scale(squares, model):
+    return lax.rsqrt(jnp.sum(squares, 1, keepdims=True) * (1.0 / model) + EPSILON)
+
+
+def before_sum(job, arrays, keep):
+    kind, places = job[2]
+    if kind == "back":
+        value = arrays[places[0]]
+        model = value.shape[1]
+        squares = jnp.zeros(keep.shape, F32)
+        for i in range(model // PIECE):
+            x = value[:, i * PIECE : (i + 1) * PIECE].astype(F32)
+            squares += x * x
+        keep[...] = jnp.broadcast_to(row_scale(squares, model), keep.shape)
+
+
+def with_piece(job, i, total, arrays, outs, keep, sums):
+    kind, places = job[2]
+    at = columns_of(i)
+    if kind == "add":
+        y = (arrays[places[0]][:, at].astype(F32) + total).astype(outs[0].dtype)
+        outs[0][:, at] = y
+        if len(outs) > 1:
+            sums[...] += y.astype(F32) * y.astype(F32)
+    if kind == "back":
+        product = total * arrays[places[0]][:, at].astype(F32) * keep[...]
+        sums[...] += product * arrays[places[2]][:, at]
+        outs[2][:, at] = jnp.sum(product.reshape(-1, 8, PIECE), 0)
+
+
+def after_sum(job, rows, total, arrays, outs, keep, sums):
+    kind, places = job[2]
+    model = arrays[places[0]].shape[1]
+    at = lambda i: slice(i * PIECE, (i + 1) * PIECE)
+    if kind == "add" and len(outs) > 1:
+        scale = row_scale(sums[rows], model)
+        for i in range(model // PIECE):
+            y = outs[0][rows, at(i)].astype(F32)
+            outs[1][rows, at(i)] = (y * scale * arrays[places[1]][:, at(i)]).astype(BF)
+    if kind == "back":
+        mean = jnp.sum(sums[rows], 1, keepdims=True) * (1.0 / model)
+        scale = keep[rows]
+        for i in range(model // PIECE):
+            unit = arrays[places[0]][rows, at(i)].astype(F32) * scale
+            grad = total(i)[rows].astype(F32) * arrays[places[2]][:, at(i)]
+            out = arrays[places[1]][rows, at(i)].astype(F32) + scale * (grad - unit * mean)
+            outs[0][rows, at(i)] = out
+            outs[1][rows, at(i)] = out.astype(BF)
+
+
 def product_sum_kernel(cfg, *refs):
-    n_arrays, n_x, first_column, sides, stagger = cfg
+    n_arrays, job, sides, stagger = cfg
+    xs, first_column = job[:2]
     refs = list(refs)
     take = lambda n: [refs.pop(0) for _ in range(n)]
     from_hbm = take(n_arrays)
     (w_hbm,) = take(1)
-    (o_ref,) = take(1)
+    outs_hbm = take(len(job[3]))
     (g_hbm,) = take(1) if sides else (None,)
     arrays = take(n_arrays)
-    load_sem, w_buf, p_buf, a_buf, s_buf, b_buf, c_buf, w_sem, sa, ra, sb, rb, sc, rc, so, turn = take(16)
+    outs = take(len(job[3]))
+    load_sem, out_sem, w_buf, p_buf, a_buf, b_buf, w_sem, sa, ra, sb, rb, sc, rc, turn, keep, sums = take(16)
     g_buf, g_sem = take(2) if sides else (None, None)
+    per_block = BLOCK // PIECE
     pieces = p_buf.shape[0]
-    per_block = BLOCK // PIECE
     blocks = pieces // per_block
-    depth = w_buf.shape[2]
+    n_rows = p_buf.shape[1]
+    early = len(xs)
 
     t = lax.axis_index("tensor")
     sec = lax.axis_index("section")
@@ -57,9 +114,6 @@
     def columns(j):
         return pl.ds(pl.multiple_of(j * BLOCK, BLOCK), BLOCK)
 
-    def lanes(i):
-        return pl.ds(pl.multiple_of(i * PIECE, PIECE), PIECE)
-
     def to_inner(i):
         return pltpu.make_async_remote_copy(
             p_buf.at[i], a_buf.at[i], sa.at[i], ra.at[i], device_id=pair, device_id_type=MESH
@@ -67,66 +121,75 @@
 
     def across(i):
         return pltpu.make_async_remote_copy(
-            s_buf.at[i], b_buf.at[i], sb.at[i], rb.at[i], device_id=mid, device_id_type=MESH
+            p_buf.at[i], b_buf.at[i], sb.at[i], rb.at[i], device_id=mid, device_id_type=MESH
         )
 
     def to_outer(i):
         return pltpu.make_async_remote_copy(
-            c_buf.at[i], c_buf.at[i], sc.at[i], rc.at[i], device_id=pair, device_id_type=MESH
+            b_buf.at[i], b_buf.at[i], sc.at[i], rc.at[i], device_id=pair, device_id_type=MESH
         )
-
-    def store(i):
-        return pltpu.make_async_copy(c_buf.at[i], o_ref.at[:, lanes(i)], so.at[i])
 
     def load(k):
         return pltpu.make_async_copy(from_hbm[k], arrays[k], load_sem.at[k])
 
     def fetch(j, slot):
         return pltpu.make_async_copy(
-            w_hbm.at[columns(j), pl.ds(first_column, depth)], w_buf.at[slot], w_sem.at[slot]
+            w_hbm.at[columns(j), pl.ds(first_column, w_buf.shape[2])], w_buf.at[slot], w_sem.at[slot]
         )
 
     def flush(j, slot):
         return pltpu.make_async_copy(g_buf.at[slot], g_hbm.at[columns(j), :], g_sem.at[slot])
 
-    for k in range(n_x):
+    def every_piece(body):
+        def turn_of(i, _):
+            body(i)
+            return 0
+
+        lax.fori_loop(0, pieces, turn_of, 0)
+
+    for k in range(early):
         load(k).start()
     fetch(0, 0).start()
-    for k in range(n_x, n_arrays):
+    for k in range(early, n_arrays):
         load(k).start()
     barrier = pltpu.get_barrier_semaphore()
-    extra = 1 if stagger else 0
     pl.semaphore_signal(barrier, inc=1, device_id=pair, device_id_type=MESH)
-    if stagger:
-        pl.semaphore_signal(barrier, inc=1, device_id=mate, device_id_type=MESH)
+    sums[...] = jnp.zeros_like(sums)
 
     @pl.when(inner)
     def _():
         pl.semaphore_signal(barrier, inc=1, device_id=mid, device_id_type=MESH)
-        pl.semaphore_wait(barrier, 2 + extra)
+        pl.semaphore_wait(barrier, 2)
 
     @pl.when(outer)
     def _():
-        pl.semaphore_wait(barrier, 1 + extra)
-
-    if stagger:
-        @pl.when(sec == 1)
-        def _():
-            pl.semaphore_wait(turn, 1)
-
-    for k in range(n_x):
+        if stagger:
+            pl.semaphore_signal(barrier, inc=1, device_id=mate, device_id_type=MESH)
+            pl.semaphore_wait(barrier, 2)
+
+            @pl.when(sec == 1)
+            def _():
+                pl.semaphore_wait(turn, 1)
+
+        else:
+            pl.semaphore_wait(barrier, 1)
+
+    for k in range(early):
         load(k).wait()
+
+    def done(i):
+        with_piece(job, i, b_buf[i].astype(F32), arrays, outs, keep, sums)
 
     def first(i):
         to_inner(i).wait_recv()
-        s_buf[i] = (p_buf[i].astype(F32) + a_buf[i].astype(F32)).astype(BF)
+        p_buf[i] = (p_buf[i].astype(F32) + a_buf[i].astype(F32)).astype(BF)
         across(i).start()
 
     def second(i):
         across(i).wait_recv()
-        c_buf[i] = (s_buf[i].astype(F32) + b_buf[i].astype(F32)).astype(BF)
+        b_buf[i] = (p_buf[i].astype(F32) + b_buf[i].astype(F32)).astype(BF)
         to_outer(i).start()
-        store(i).start()
+        done(i)
 
     def step(j, _):
         slot = lax.rem(j, 2)
@@ -137,9 +200,9 @@
             fetch(j + 1, 1 - slot).start()
 
         total, start = None, 0
-        for x_ref in arrays[:n_x]:
-            width = x_ref.shape[1]
-            term = dot_f32(x_ref[...], w_buf[slot, :, start : start + width], 1, 1)
+        for x in xs:
+            width = arrays[x].shape[1]
+            term = dot_f32(arrays[x][...], w_buf[slot, :, start : start + width], 1, 1)
             total = term if total is None else total + term
             start += width
         total = total.astype(BF)
@@ -151,6 +214,12 @@
             for u in range(per_block):
                 to_inner(per_block * j + u).start()
 
+        @pl.when(j == 0)
+        def _():
+            for k in range(early, n_arrays):
+                load(k).wait()
+            before_sum(job, arrays, keep)
+
         @pl.when(inner)
         def _():
             for u in range(per_block):
@@ -162,11 +231,6 @@
                     second(i - per_block)
 
         if sides:
-
-            @pl.when(j == 0)
-            def _():
-                for k in range(n_x, n_arrays):
-                    load(k).wait()
 
             @pl.when(j >= 2)
             def _():
@@ -182,6 +246,7 @@
                     ).astype(BF)
                     start += width
             flush(j, slot).start()
+
         return 0
 
     lax.fori_loop(0, blocks, step, 0)
@@ -191,74 +256,97 @@
         for u in range(per_block):
             second(pieces - per_block + u)
 
-        def last(i, _):
+    @pl.when(outer)
+    def _():
+        every_piece(lambda i: to_inner(i).wait_send())
+        if stagger:
+
+            @pl.when(sec == 0)
+            def _():
+                pl.semaphore_signal(turn, inc=1, device_id=mate, device_id_type=MESH)
+
+        def arrive(i):
+            to_outer(i).wait_recv()
+            done(i)
+
+        every_piece(arrive)
+
+    chunks = 5 if n_rows % (5 * 32) == 0 else 1
+    chunk = n_rows // chunks
+    block = 32 if chunk % 32 == 0 else 16
+    height = lambda m: 8 if job[2][0] == "back" and m == 2 else n_rows
+    stores = []
+
+    def store(m, rows):
+        copy = pltpu.make_async_copy(outs[m].at[rows], outs_hbm[m].at[rows], out_sem.at[len(stores)])
+        copy.start()
+        stores.append(copy)
+
+    for c in range(chunks):
+
+        def turn_rows(r, _):
+            rows = pl.ds(pl.multiple_of(c * chunk + r * block, block), block)
+            after_sum(job, rows, lambda i: b_buf.at[i], arrays, outs, keep, sums)
+            return 0
+
+        if job[2][0] == "back" or len(outs) > 1:
+            lax.fori_loop(0, chunk // block, turn_rows, 0)
+        for m in range(len(outs)):
+            if height(m) == n_rows:
+                store(m, pl.ds(c * chunk, chunk))
+    for m in range(len(outs)):
+        if height(m) != n_rows:
+            store(m, pl.ds(0, height(m)))
+
+    @pl.when(inner)
+    def _():
+        def sent(i):
             across(i).wait_send()
             to_outer(i).wait_send()
-            store(i).wait()
-            return 0
-
-        lax.fori_loop(0, pieces, last, 0)
-
-    @pl.when(outer)
-    def _():
-        def arrive(i, _):
-            to_outer(i).wait_recv()
-            store(i).start()
-            return 0
-
-        def last(i, _):
-            to_inner(i).wait_send()
-            store(i).wait()
-            return 0
-
-        lax.fori_loop(0, pieces, arrive, 0)
-        lax.fori_loop(0, pieces, last, 0)
+
+        every_piece(sent)
 
     if sides:
         flush(blocks - 2, (blocks - 2) % 2).wait()
         flush(blocks - 1, (blocks - 1) % 2).wait()
-
-    if stagger:
-
-        @pl.when(sec == 0)
-        def _():
-            pl.semaphore_signal(turn, inc=1, device_id=mate, device_id_type=MESH)
-
-
-def product_sum(xs, weights, first_column, others=(), sides=(), stagger=False, key=1):
+    for copy in stores:
+        copy.wait()
+
+
+def product_sum(arrays, job, weights, sides=(), stagger=False, key=1):
     assert lax.axis_size("tensor") == 4
-    arrays = (*xs, *others)
-    rows, model = xs[0].shape[0], weights.shape[0]
-    depth = sum(x.shape[1] for x in xs)
+    rows, model = arrays[0].shape[0], weights.shape[0]
     pieces = model // PIECE
+    depth = sum(arrays[x].shape[1] for x in job[0])
     anywhere = pl.BlockSpec(memory_space=pl.ANY)
     buf = pltpu.VMEM((pieces, rows, PIECE), BF)
     sem = pltpu.SemaphoreType.DMA((pieces,))
     two = pltpu.SemaphoreType.DMA((2,))
-    out_shape = [jax.ShapeDtypeStruct((rows, model), BF)]
-    out_specs = [anywhere]
-    scratch = [pltpu.VMEM(x.shape, x.dtype) for x in arrays]
-    scratch += [pltpu.SemaphoreType.DMA((len(arrays),)), pltpu.VMEM((2, BLOCK, depth), BF)]
-    scratch += [buf, buf, buf, buf, buf, two, *[sem] * 7, pltpu.SemaphoreType.REGULAR]
-    side_width = sum(arrays[b].shape[1] for _, bs in sides for b in bs)
+    out_shape = []
+    for m, dtype in enumerate(job[3]):
+        height = 8 if job[2][0] == "back" and m == 2 else rows
+        out_shape.append(jax.ShapeDtypeStruct((height, model), dtype))
+    scratch = [pltpu.VMEM(x.shape, x.dtype) for x in (*arrays, *out_shape)]
+    scratch += [pltpu.SemaphoreType.DMA((len(arrays),)), pltpu.SemaphoreType.DMA((16,))]
+    scratch += [pltpu.VMEM((2, BLOCK, depth), BF), buf, buf, buf, two, *[sem] * 6, pltpu.SemaphoreType.REGULAR]
+    scratch += [pltpu.VMEM((rows, PIECE), F32)] * 2
     if sides:
+        side_width = sum(arrays[b].shape[1] for _, bs in sides for b in bs)
         out_shape.append(jax.ShapeDtypeStruct((model, side_width), BF))
-        out_specs.append(anywhere)
         scratch += [pltpu.VMEM((2, BLOCK, side_width), BF), two]
-    cfg = (len(arrays), len(xs), first_column, tuple(sides), stagger)
     out = pl.pallas_call(
-        functools.partial(product_sum_kernel, cfg),
+        functools.partial(product_sum_kernel, (len(arrays), job, tuple(sides), stagger)),
         out_shape=out_shape,
         in_specs=[anywhere] * (len(arrays) + 1),
-        out_specs=out_specs,
+        out_specs=[anywhere] * len(out_shape),
         scratch_shapes=scratch,
         compiler_params=pltpu.CompilerParams(
-            collective_id=key, has_side_effects=True, vmem_limit_bytes=56 << 20
+            collective_id=key, has_side_effects=True, vmem_limit_bytes=62 << 20
         ),
         cost_estimate=NO_COST,
         name=f"product_sum_{key}",
     )(*arrays, weights)
-    return out if sides else out[0]
+    return out if len(out) > 1 else out[0]
 
 
 def dp_peers(count):
@@ -356,12 +444,20 @@
     )(x.reshape(count, rows, width), cos_rows, sin_rows)
 
 
-def reduce_kernel(g_hbm, o_ref, mine, away, got, xs, ys, xr, yr, load_sem, send, recv):
+def finish_kernel(
+    g_hbm, gain_ref, out_zero, out_one, in_zero, in_one, mlp_zero, mlp_one, attn_one,
+    o_ref, gain_out, got_out, got_in, got_mlp, got_attn,
+    mine, away, got, xs, ys, xr, yr, gains, load_sem, send, recv, mate_send, mate_recv, gain_send, gain_recv,
+):
     sec, t, dat = lax.axis_index("section"), lax.axis_index("tensor"), lax.axis_index("dp")
     flip_x = dat + 1 - 2 * lax.rem(dat, 2)
     flip_y = lax.rem(dat + 2, 4)
     across = lax.rem(flip_x + 2, 4)
     by_x, by_y, mate = (sec, t, flip_x), (sec, t, flip_y), (1 - sec, t, dat)
+    peers = [
+        mate, by_x, by_y, (sec, t, across),
+        (1 - sec, t, flip_x), (1 - sec, t, flip_y), (1 - sec, t, across),
+    ]
     rows = g_hbm.shape[1] // 2
     upper, lower = pl.ds(0, rows), pl.ds(rows, rows)
     order = (across, flip_x, flip_y, dat)
@@ -371,17 +467,31 @@
         loads.append(pltpu.make_async_copy(g_hbm.at[2 * block + sec], mine.at[k], load_sem.at[4 + k]))
     for copy in loads:
         copy.start()
-    greet([by_x, by_y, mate])
+    greet(peers)
 
     def remote(src, dst, k, device):
         return pltpu.make_async_remote_copy(
             src, dst, send.at[k], recv.at[k], device_id=device, device_id_type=MESH
         )
 
+    def to_mate(src, dst, k):
+        return pltpu.make_async_remote_copy(
+            src, dst, mate_send.at[k], mate_recv.at[k], device_id=mate, device_id_type=MESH
+        )
+
     swaps = [remote(away.at[k], got.at[k], k, mate) for k in range(4)]
     for k in range(4):
         loads[2 * k].wait()
         swaps[k].start()
+    gain_copies = [
+        pltpu.make_async_remote_copy(
+            gain_ref.at[peer[0], peer[2]], gains.at[k], gain_send.at[k], gain_recv.at[k],
+            device_id=peer, device_id_type=MESH,
+        )
+        for k, peer in enumerate(peers)
+    ]
+    for copy in gain_copies:
+        copy.start()
     outs = []
     for k in range(4):
         loads[2 * k + 1].wait()
@@ -396,6 +506,20 @@
         for copy in outs[-(2 if k == 0 else 1) :]:
             if k < 3:
                 copy.start()
+
+    @pl.when(sec == 0)
+    def _():
+        to_mate(in_one, got_in, 0).start()
+        to_mate(out_one, got_out, 1).start()
+        to_mate(mlp_one, got_mlp, 2).start()
+        to_mate(attn_one, got_attn, 3).start()
+
+    @pl.when(sec == 1)
+    def _():
+        to_mate(in_zero, got_in, 0).start()
+        to_mate(out_zero, got_out, 1).start()
+        to_mate(mlp_zero, got_mlp, 2).start()
+
     outs[0].wait_recv()
     mine[2, upper] = (mine[2, upper].astype(F32) + xs[0].astype(F32)).astype(BF)
     outs.append(remote(mine.at[2, upper], yr, 8, by_y))
@@ -404,38 +528,184 @@
     mine[1, lower] = (mine[1, lower].astype(F32) + ys[0].astype(F32)).astype(BF)
     outs.append(remote(mine.at[1, lower], xr, 9, by_x))
     outs[5].start()
+    total = gain_ref[sec, dat]
+    for k, copy in enumerate(gain_copies):
+        copy.wait()
+        total = total + gains[k]
+    gain_out[...] = total
     outs[2].wait_recv()
     outs[3].wait_recv()
     outs[4].wait_recv()
     o_ref[upper] = (mine[3, upper].astype(F32) + xs[1].astype(F32) + yr[...].astype(F32)).astype(BF)
     outs[5].wait_recv()
     o_ref[lower] = (mine[3, lower].astype(F32) + ys[1].astype(F32) + xr[...].astype(F32)).astype(BF)
+
+    @pl.when(sec == 1)
+    def _():
+        to_mate(o_ref, got_attn, 3).start()
+
     for copy in swaps + outs:
         copy.wait_send()
-
-
-def reduce_now(g):
-    if lax.axis_size("dp") != 4:
-        return reduce_gradient(g)
+    to_mate(in_one, got_in, 0).wait()
+    to_mate(out_one, got_out, 1).wait()
+    to_mate(mlp_one, got_mlp, 2).wait()
+    to_mate(attn_one, got_attn, 3).wait()
+
+
+def finish(g, gains, out_zero, out_one, in_zero, in_one, mlp_zero, mlp_one, attn_one):
     rows, width = g.shape[0] // 8, g.shape[1]
     part = pltpu.VMEM((2, rows // 2, width), BF)
     whole = pltpu.VMEM((4, rows, width), BF)
     end = pltpu.VMEM((rows // 2, width), BF)
+    in_vmem, anywhere = pl.BlockSpec(memory_space=pltpu.VMEM), pl.BlockSpec(memory_space=pl.ANY)
+    like = lambda x: jax.ShapeDtypeStruct(x.shape, x.dtype)
+    dma = lambda n: pltpu.SemaphoreType.DMA((n,))
     return pl.pallas_call(
-        reduce_kernel,
-        out_shape=jax.ShapeDtypeStruct((rows, width), BF),
-        in_specs=[pl.BlockSpec(memory_space=pl.ANY)],
-        out_specs=pl.BlockSpec(memory_space=pltpu.VMEM),
+        finish_kernel,
+        out_shape=(
+            jax.ShapeDtypeStruct((rows, width), BF),
+            jax.ShapeDtypeStruct(gains.shape[2:], F32),
+            like(out_zero), like(in_zero), like(mlp_zero), like(attn_one),
+        ),
+        in_specs=[anywhere, in_vmem, *[anywhere] * 7],
+        out_specs=(in_vmem, in_vmem, *[anywhere] * 4),
         scratch_shapes=[
-            whole, whole, whole, part, part, end, end,
-            pltpu.SemaphoreType.DMA((8,)), pltpu.SemaphoreType.DMA((10,)), pltpu.SemaphoreType.DMA((10,)),
+            whole, whole, whole, part, part, end, end, pltpu.VMEM((7, *gains.shape[2:]), F32),
+            dma(8), dma(10), dma(10), dma(4), dma(4), dma(7), dma(7),
         ],
         compiler_params=pltpu.CompilerParams(
             collective_id=12, has_side_effects=True, vmem_limit_bytes=40 << 20
         ),
         cost_estimate=NO_COST,
-        name="reduce_now",
-    )(g.reshape(8, rows, width))
+        name="finish",
+    )(g.reshape(8, rows, width), gains, out_zero, out_one, in_zero, in_one, mlp_zero, mlp_one, attn_one)
+
+
+def finish_apart(g, gains, out_zero, out_one, in_zero, in_one, mlp_zero, mlp_one, attn_one):
+    first_core = lax.axis_index("section") == 0
+    half = reduce_gradient(g)
+    swap = lambda zero, one: lax.ppermute(jnp.where(first_core, one, zero), "section", [(0, 1), (1, 0)])
+    return (
+        half, share_sums(gains), swap(out_zero, out_one), swap(in_zero, in_one), swap(mlp_zero, mlp_one),
+        swap(half, attn_one),
+    )
+
+
+def write_kernel(
+    split, out_zero, out_one, got_out, in_zero, in_one, got_in, mlp_zero, mlp_one, got_mlp, attn_zero, attn_one, got_attn,
+    out_hbm, in_hbm, q_hbm, k_hbm, v_hbm, o_hbm, gate_hbm, up_hbm, down_hbm,
+    mlp, attn, got_narrow, got_wide, q_buf, k_buf, v_buf, o_buf, gate_buf, up_buf, down_buf, load_sem, store_sem,
+):
+    sec = lax.axis_index("section")
+    half = mlp_zero.shape[0]
+    low, high = pl.ds(0, half), pl.ds(half, half)
+
+    def start(own_out, own_in, mlp_low, mlp_high, attn_low, attn_high):
+        pltpu.make_async_copy(mlp_low, mlp.at[low], load_sem.at[0]).start()
+        pltpu.make_async_copy(mlp_high, mlp.at[high], load_sem.at[1]).start()
+        pltpu.make_async_copy(attn_low, attn.at[low], load_sem.at[2]).start()
+        pltpu.make_async_copy(attn_high, attn.at[high], load_sem.at[3]).start()
+        pltpu.make_async_copy(own_out, out_hbm.at[sec], store_sem.at[0]).start()
+        pltpu.make_async_copy(own_in, in_hbm.at[sec], store_sem.at[1]).start()
+
+    load_in = pltpu.make_async_copy(got_in, got_narrow, load_sem.at[4])
+    load_in.start()
+
+    @pl.when(sec == 0)
+    def _():
+        start(out_zero, in_zero, mlp_zero, got_mlp, attn_zero, got_attn)
+
+    @pl.when(sec == 1)
+    def _():
+        start(out_one, in_one, got_mlp, mlp_one, got_attn, attn_one)
+
+    other = pltpu.make_async_copy(got_out, out_hbm.at[1 - sec], store_sem.at[2])
+    other.start()
+    stores = [other]
+
+    def store(src, dst, k):
+        stores.append(pltpu.make_async_copy(src, dst, store_sem.at[k]))
+        stores[-1].start()
+
+    def in_rows(count, block, body):
+        def turn(r, _):
+            body(pl.ds(pl.multiple_of(r * block, block), block))
+            return 0
+
+        lax.fori_loop(0, count // block, turn, 0)
+
+    def widen(rows):
+        got_wide[rows] = got_narrow[rows].astype(F32)
+
+    load_in.wait()
+    in_rows(got_narrow.shape[0], 32, widen)
+    store(got_wide, in_hbm.at[1 - sec], 3)
+    units = gate_buf.shape[1]
+    width = q_buf.shape[1]
+    span = k_buf.shape[1]
+    pltpu.make_async_copy(mlp_zero, mlp.at[low], load_sem.at[0]).wait()
+    pltpu.make_async_copy(mlp_zero, mlp.at[high], load_sem.at[1]).wait()
+
+    def gates(rows):
+        gate_buf[rows] = mlp[rows, :units].astype(F32)
+        up_buf[rows] = mlp[rows, units : 2 * units].astype(F32)
+
+    in_rows(2 * half, 32, gates)
+    store(gate_buf, gate_hbm, 4)
+    store(up_buf, up_hbm, 5)
+    for c in range(0, units, 128):
+        down_buf[c : c + 128] = mlp[:, 2 * units + c : 2 * units + c + 128].astype(F32).T
+    store(down_buf, down_hbm, 6)
+    pltpu.make_async_copy(attn_one, attn.at[low], load_sem.at[2]).wait()
+    pltpu.make_async_copy(attn_one, attn.at[high], load_sem.at[3]).wait()
+
+    def projections(rows):
+        q_buf[rows] = attn[rows, :width].astype(F32)
+        k_buf[rows] = attn[rows, width : width + span].astype(F32)
+        v_buf[rows] = attn[rows, width + span : split].astype(F32)
+
+    in_rows(2 * half, 32, projections)
+    for c in range(0, width, 128):
+        o_buf[c : c + 128] = attn[:, split + c : split + c + 128].astype(F32).T
+    store(q_buf, q_hbm, 7)
+    store(k_buf, k_hbm, 8)
+    store(v_buf, v_hbm, 9)
+    store(o_buf, o_hbm, 10)
+    for copy in stores:
+        copy.wait()
+    pltpu.make_async_copy(out_zero, out_hbm.at[sec], store_sem.at[0]).wait()
+    pltpu.make_async_copy(in_zero, in_hbm.at[sec], store_sem.at[1]).wait()
+
+
+def write_results(outs, ins, mlps, attns, width, span, units):
+    rows, model = outs[0].shape
+    shard = 2 * mlps[0].shape[0]
+    anywhere = pl.BlockSpec(memory_space=pl.ANY)
+    shapes = [
+        (shard, width), (shard, span), (shard, span), (width, shard), (shard, units), (shard, units), (units, shard),
+    ]
+    return pl.pallas_call(
+        functools.partial(write_kernel, width + 2 * span),
+        out_shape=[
+            jax.ShapeDtypeStruct((2, rows, model), BF),
+            jax.ShapeDtypeStruct((2, rows, model), F32),
+            *[jax.ShapeDtypeStruct(shape, F32) for shape in shapes],
+        ],
+        in_specs=[anywhere] * 12,
+        out_specs=[anywhere] * 9,
+        scratch_shapes=[
+            pltpu.VMEM((shard, mlps[0].shape[1]), BF),
+            pltpu.VMEM((shard, attns[0].shape[1]), BF),
+            pltpu.VMEM((rows, model), BF),
+            pltpu.VMEM((rows, model), F32),
+            *[pltpu.VMEM(shape, F32) for shape in shapes],
+            pltpu.SemaphoreType.DMA((5,)),
+            pltpu.SemaphoreType.DMA((11,)),
+        ],
+        compiler_params=pltpu.CompilerParams(vmem_limit_bytes=56 << 20),
+        cost_estimate=NO_COST,
+        name="write_results",
+    )(*outs, *ins, *mlps, *attns)
 
 
 def share_kernel(count, x_ref, o_ref, buf, send, recv):
@@ -469,7 +739,7 @@
         in_specs=[in_vmem],
         out_specs=in_vmem,
         scratch_shapes=[pltpu.VMEM((2 * count - 1, *x.shape[2:]), F32), sem, sem],
-        compiler_params=pltpu.CompilerParams(collective_id=8, has_side_effects=True),
+        compiler_params=pltpu.CompilerParams(collective_id=13, has_side_effects=True),
         cost_estimate=NO_COST,
         name="share_sums",
     )(x)
@@ -486,16 +756,20 @@
     return (pl.ds(0, tree_len),)
 
 
+def head_rows(ref, head):
+    return ref[head * HEAD : (head + 1) * HEAD, :]
+
+
 def beside(ref, head, count):
-    parts = [ref[HEAD * (head + k) : HEAD * (head + k + 1), :] for k in range(count)]
+    parts = [head_rows(ref, head + k) for k in range(count)]
     return parts[0] if count == 1 else jnp.concatenate(parts, axis=1)
 
 
 def turned_beside(ref, cos, sin, head, count):
     parts = []
     for k in range(count):
-        base = HEAD * (head + k)
-        first, second = ref[base : base + HALF, :], ref[base + HALF : base + HEAD, :]
+        rows = head_rows(ref, head + k)
+        first, second = rows[:HALF], rows[HALF:]
         parts.append(jnp.concatenate([first * cos - second * sin, second * cos + first * sin], axis=0))
     whole = parts[0] if count == 1 else jnp.concatenate(parts, axis=1)
     return (whole.astype(BF).astype(F32) * HEAD**-0.5).astype(BF)
@@ -506,9 +780,9 @@
     return (parts[0] if count == 1 else jnp.concatenate(parts, axis=0)).T
 
 
-def row_beside(ref, head, count):
-    parts = [ref[head + k : head + k + 1, :] for k in range(count)]
-    return parts[0] if count == 1 else jnp.concatenate(parts, axis=1)
+def over_groups(groups, step, body):
+    for group in range(groups):
+        body(group, slice(group * step * HEAD, (group + 1) * step * HEAD))
 
 
 def attend_kernel(
@@ -518,7 +792,9 @@
     heads = q_ref.shape[0] // HEAD
     first_row = start_ref[0] + pl.program_id(0) * tile
     wins = windows(kv_ref.shape[0], rows, tile, first_row)
-    for head in range(0, heads, step):
+
+    def body(group, lanes):
+        head = group * step
         q = turned_beside(q_ref, cos_ref[...], sin_ref[...], head, step)
         scores = []
         for win in wins:
@@ -530,12 +806,13 @@
         total = sum(jnp.sum(e, 0, keepdims=True) for e in expo)
         out = sum(dot_f32(kvt_ref[HEAD:, win], e.astype(BF), 1, 0) for win, e in zip(wins, expo))
         out = out / total
-        on_ref[:, HEAD * head : HEAD * (head + step)] = as_rows(out, tile, step).astype(BF)
+        on_ref[:, lanes] = as_rows(out, tile, step).astype(BF)
+        lse_ref[group, 0] = top + jnp.log(total)
         out = out.astype(BF)
-        lse = top + jnp.log(total)
         for k in range(step):
-            o_ref[HEAD * (head + k) : HEAD * (head + k + 1), :] = out[:, k * tile : (k + 1) * tile]
-            lse_ref[head + k : head + k + 1, :] = lse[:, k * tile : (k + 1) * tile]
+            o_ref[(head + k) * HEAD : (head + k + 1) * HEAD, :] = out[:, k * tile : (k + 1) * tile]
+
+    over_groups(heads // step, step, body)
 
 
 def attend_back_kernel(
@@ -552,11 +829,13 @@
         dk_acc[...] = jnp.zeros_like(dk_acc)
         dv_acc[...] = jnp.zeros_like(dv_acc)
 
-    for head in range(0, heads, step):
-        q = turned_beside(q_ref, cos_ref[...], sin_ref[...], head, step)
+    def body(group, lanes):
+        head = group * step
+        cos, sin = cos_ref[...], sin_ref[...]
+        q = turned_beside(q_ref, cos, sin, head, step)
         do = beside(do_ref, head, step)
         out = beside(o_ref, head, step)
-        lse = row_beside(lse_ref, head, step)
+        lse = lse_ref[group, 0]
         delta = jnp.sum(do.astype(F32) * out.astype(F32), 0, keepdims=True)
         dq = jnp.zeros((HEAD, step * tile), F32)
         for win in wins:
@@ -569,13 +848,14 @@
             dv_acc[win, :] += dot_f32(p.astype(BF), do, 1, 1)
             dq = dq + dot_f32(kvt_ref[:HEAD, win], ds, 1, 0)
         dq = dq * HEAD**-0.5
-        cos, sin = cos_ref[...], sin_ref[...]
         turned = []
         for k in range(step):
             first = dq[:HALF, k * tile : (k + 1) * tile]
             second = dq[HALF:, k * tile : (k + 1) * tile]
             turned += [first * cos + second * sin, second * cos - first * sin]
-        dq_ref[:, HEAD * head : HEAD * (head + step)] = jnp.concatenate(turned, axis=0).T.astype(BF)
+        dq_ref[:, lanes] = jnp.concatenate(turned, axis=0).T.astype(BF)
+
+    over_groups(heads // step, step, body)
 
     @pl.when(pl.program_id(0) == pl.num_programs(0) - 1)
     def _():
@@ -597,7 +877,7 @@
         out_shape=(
             jax.ShapeDtypeStruct((width, rows), BF),
             jax.ShapeDtypeStruct((rows, width), BF),
-            jax.ShapeDtypeStruct((heads, rows), F32),
+            jax.ShapeDtypeStruct((heads // step, rows // tile, 1, step * tile), F32),
         ),
         grid_spec=pltpu.PrefetchScalarGridSpec(
             num_scalar_prefetch=1,
@@ -613,7 +893,7 @@
             out_specs=(
                 pl.BlockSpec((width, tile), column),
                 pl.BlockSpec((tile, width), lambda i, s: (i, 0)),
-                pl.BlockSpec((heads, tile), column),
+                pl.BlockSpec((heads // step, 1, 1, step * tile), lambda i, s: (0, i, 0, 0)),
             ),
         ),
         compiler_params=pltpu.CompilerParams(vmem_limit_bytes=40 << 20),
@@ -641,7 +921,7 @@
                 pl.BlockSpec((width, tile), column),
                 pl.BlockSpec((width, tile), column),
                 pl.BlockSpec((width, tile), column),
-                pl.BlockSpec((heads, tile), column),
+                pl.BlockSpec((heads // step, 1, 1, step * tile), lambda i, s: (0, i, 0, 0)),
                 pl.BlockSpec((tree_len, 2 * HEAD), whole),
                 pl.BlockSpec((2 * HEAD, tree_len), whole),
                 pl.BlockSpec((tree_len, tile), column),
@@ -660,69 +940,40 @@
     )(start, q_t, do_t, o_t, lse, kv, kv_t, bias_t, cos_t, sin_t)
 
 
-def inverse_rms(hidden):
-    return lax.rsqrt(jnp.mean(hidden * hidden, -1, keepdims=True) + EPSILON)
-
-
-def norm_back(grad_normed, hidden, scale_rows, gain):
-    unit = hidden * scale_rows
-    grad_unit = grad_normed * gain
-    grad_hidden = scale_rows * (grad_unit - unit * jnp.mean(grad_unit * unit, -1, keepdims=True))
-    return grad_hidden, jnp.sum(grad_normed * unit, 0)
-
-
-def layer_forward(hidden, weights, tables, stagger):
+def layer_attention(normed, weights, tables):
     gain_one, gain_two, w_attn, w_mlp, width, split, units = weights
     start, bias_t, cos_t, sin_t, cos_rows, sin_rows = tables
-    scale_one = inverse_rms(hidden)
-    normed_one = (hidden * scale_one * gain_one).astype(BF)
-    q_t = dot_f32(w_attn[:, :width], normed_one, 0, 1)
+    q_t = dot_f32(w_attn[:, :width], normed, 0, 1)
     kv, kv_t = gather_rows(
-        jnp.dot(normed_one, w_attn[:, width:split], preferred_element_type=F32), cos_rows, -sin_rows
+        jnp.dot(normed, w_attn[:, width:split], preferred_element_type=F32), cos_rows, -sin_rows
     )
     o_t, o, lse = attend(start, q_t, kv, kv_t, bias_t, cos_t, sin_t)
-    attn_sum = product_sum((o,), w_attn, split, stagger=stagger, key=1 if stagger else 2)
-    middle = hidden + attn_sum.astype(F32)
-    scale_two = inverse_rms(middle)
-    normed_two = (middle * scale_two * gain_two).astype(BF)
-    gate_up = jnp.dot(normed_two, w_mlp[:, : 2 * units], preferred_element_type=F32)
+    return (q_t, kv, kv_t, o_t, lse), o
+
+
+def attention_backward(grad_attn, weights, tables, kept):
+    gain_one, gain_two, w_attn, w_mlp, width, split, units = weights
+    start, bias_t, cos_t, sin_t, cos_rows, sin_rows = tables
+    q_t, kv, kv_t, o_t, lse = kept
+    do_t = dot_f32(w_attn[:, split : split + width], grad_attn, 0, 1).astype(BF)
+    dq, dkv_part = attend_back(start, q_t, do_t, o_t, lse, kv, kv_t, bias_t, cos_t, sin_t)
+    return dq, scatter_rows(dkv_part, cos_rows, sin_rows)
+
+
+def layer_units(normed, weights):
+    units = weights[-1]
+    gate_up = jnp.dot(normed, weights[3][:, : 2 * units], preferred_element_type=F32)
     gate, up = gate_up[:, :units], gate_up[:, units:]
-    inner = (gate * jax.nn.sigmoid(gate) * up).astype(BF)
-    return (hidden, scale_one, normed_one, q_t, kv, kv_t, o_t, o, lse, middle, scale_two, normed_two, gate, up, inner)
-
-
-def units_backward(branch, weights, kept):
-    gate, up = kept[12:14]
+    return gate, up, (gate * jax.nn.sigmoid(gate) * up).astype(BF)
+
+
+def units_backward(branch, weights, gate, up):
     units = weights[-1]
     d_inner = dot_f32(branch, weights[3][:, 2 * units :], 1, 0)
     sig = jax.nn.sigmoid(gate)
     d_gate = (d_inner * up * sig * (1.0 + gate * (1.0 - sig))).astype(BF)
     d_up = (d_inner * gate * sig).astype(BF)
     return d_gate, d_up
-
-
-def middle_backward(grad_out, d_two, weights, tables, kept):
-    gain_one, gain_two, w_attn, w_mlp, width, split, units = weights
-    start, bias_t, cos_t, sin_t, cos_rows, sin_rows = tables
-    hidden, scale_one, normed_one, q_t, kv, kv_t, o_t, o, lse, middle, scale_two = kept[:11]
-    grad_norm, d_gain_two = norm_back(d_two.astype(F32), middle, scale_two, gain_two)
-    grad_middle = grad_out + grad_norm
-    grad_attn = grad_middle.astype(BF)
-    do_t = dot_f32(w_attn[:, split : split + width], grad_attn, 0, 1).astype(BF)
-    return grad_middle, grad_attn, do_t, d_gain_two
-
-
-def attention_backward(do_t, tables, kept):
-    start, bias_t, cos_t, sin_t, cos_rows, sin_rows = tables
-    q_t, kv, kv_t, o_t, o, lse = kept[3:9]
-    dq, dkv_part = attend_back(start, q_t, do_t, o_t, lse, kv, kv_t, bias_t, cos_t, sin_t)
-    return dq, scatter_rows(dkv_part, cos_rows, sin_rows)
-
-
-def first_backward(grad_middle, d_one, weights, kept):
-    hidden, scale_one = kept[:2]
-    grad_norm, d_gain_one = norm_back(d_one.astype(F32), hidden, scale_one, weights[0])
-    return grad_middle + grad_norm, d_gain_one
 
 
 def reduce_gradient(x):
@@ -742,8 +993,8 @@
     rows, model = inputs.shape[1], inputs.shape[2]
     swap = [(0, 1), (1, 0)]
 
-    hidden = lax.dynamic_index_in_dim(inputs, sec, 0, keepdims=False).astype(F32)
-    cot = lax.dynamic_index_in_dim(cotangent, sec, 0, keepdims=False).astype(F32)
+    tree = lax.dynamic_index_in_dim(inputs, sec, 0, keepdims=False)
+    hidden = tree.astype(F32)
     segments = lax.dynamic_index_in_dim(seg_ids, sec, 0, keepdims=False)
     places = lax.dynamic_index_in_dim(positions, sec, 0, keepdims=False)
     parent = lax.dynamic_index_in_dim(parents, sec, 0, keepdims=False)
@@ -770,8 +1021,11 @@
         return (gains[0:1], gains[1:2], w_attn, w_mlp, width, split, units)
 
     (attn_zero, attn_one), (mlp_zero, mlp_one) = halves
-    zero = with_gains(*gathered((attn_zero, mlp_zero)))
+    attn_zero = jnp.concatenate([attn_zero, attn_one[:, split + width : split + width + 1]], 1)
+    attn_zero, mlp_zero = gathered((attn_zero, mlp_zero))
+    zero = with_gains(attn_zero, mlp_zero)
     attn_one, mlp_one = gathered((attn_one, mlp_one))
+    one_gain = attn_zero[:, split + width + 2 :].astype(F32).T
 
     seg_count = parent.shape[0]
     labels = jnp.arange(seg_count, dtype=jnp.int32)
@@ -794,88 +1048,81 @@
     sin_rows = jnp.concatenate([sin_t.T, -sin_t.T, 0 * ones], 1)
     tables = (row_start.astype(jnp.int32).reshape(1), bias_t, cos_t, sin_t, cos_rows, sin_rows)
 
-    kept_zero = layer_forward(hidden, zero, tables, True)
-    mlp_sum = product_sum(kept_zero[-1:], zero[3], 2 * units, key=5)
-    out_zero = (kept_zero[9] + mlp_sum.astype(F32)).astype(BF)
-
-    out_zero, attn_one = lax.optimization_barrier((out_zero, attn_one))
+    split_out, split_down = split, 2 * units
+    wide, narrow = (F32, BF), (BF, BF)
+    back = (F32, BF, F32)
+
+    normed_zero = (hidden * lax.rsqrt(jnp.mean(hidden * hidden, -1, keepdims=True) + EPSILON) * zero[0]).astype(BF)
+    kept_zero, o_zero = layer_attention(normed_zero, zero, tables)
+    middle_zero, r_zero = product_sum(
+        (o_zero, tree, zero[1]), ((0,), split_out, ("add", (1, 2)), wide), zero[2], stagger=True, key=1
+    )
+    gate_zero, up_zero, inner_zero = layer_units(r_zero, zero)
+    out_zero, normed_one = product_sum(
+        (inner_zero, middle_zero, one_gain), ((0,), split_down, ("add", (1, 2)), narrow), zero[3], key=5
+    )
+
+    out_zero, normed_one, attn_one = lax.optimization_barrier((out_zero, normed_one, attn_one))
     one = with_gains(attn_one, mlp_one)
-    kept_one = layer_forward(out_zero.astype(F32), one, tables, False)
-    branch = cot.astype(BF)
-    d_gate, d_up = units_backward(branch, one, kept_one)
-    mlp_sum, d_mlp_one = product_sum(
-        kept_one[-1:], one[3], 2 * units, (kept_one[11], branch, d_gate, d_up), ((1, (3, 4)), (2, (0,))), key=6
-    )
-    out_one = (kept_one[9] + mlp_sum.astype(F32)).astype(BF)
+    kept_one, o_one = layer_attention(normed_one, one, tables)
+    middle_one, r_one = product_sum(
+        (o_one, out_zero, one[1]), ((0,), split_out, ("add", (1, 2)), wide), one[2], key=2
+    )
+    gate_one, up_one, inner_one = layer_units(r_one, one)
+    branch = lax.dynamic_index_in_dim(cotangent, sec, 0, keepdims=False)
+    d_gate, d_up = units_backward(branch, one, gate_one, up_one)
+    out_one, d_mlp_one = product_sum(
+        (inner_one, middle_one, r_one, branch, d_gate, d_up), ((0,), split_down, ("add", (1,)), (BF,)),
+        one[3], ((2, (4, 5)), (3, (0,))), key=6,
+    )
+    d_gate, out_one = lax.optimization_barrier((d_gate, out_one))
+    grad_middle, grad_attn, d_gain_mlp_one = product_sum(
+        (d_gate, d_up, middle_one, branch, one[1]), ((0, 1), 0, ("back", (2, 3, 4)), back), one[3], key=8
+    )
     g_mlp_one = reduce_gradient(d_mlp_one)
-    d_gate, d_up, mlp_sum = lax.optimization_barrier((d_gate, d_up, mlp_sum))
-    d_two = product_sum((d_gate, d_up), one[3], 0, key=7)
-    grad_middle, grad_attn, do_t, d_gain_mlp_one = middle_backward(cot, d_two, one, tables, kept_one)
-    dq, dkv = attention_backward(do_t, tables, kept_one)
-    d_one, d_attn_one = product_sum(
-        (dq, dkv), one[2], 0, (kept_one[2], grad_attn, kept_one[7]), ((2, (0, 1)), (3, (4,))), key=9
+    dq, dkv = attention_backward(grad_attn, one, tables, kept_one)
+    grad_one, branch, d_gain_attn_one, d_attn_one = product_sum(
+        (dq, dkv, out_zero, grad_middle, one[0], normed_one, grad_attn, o_one),
+        ((0, 1), 0, ("back", (2, 3, 4)), back),
+        one[2], ((5, (0, 1)), (6, (7,))), key=7,
     )
     g_attn_one = reduce_gradient(d_attn_one)
-    grad_one, d_gain_attn_one = first_backward(grad_middle, d_one, one, kept_one)
-
-    branch = grad_one.astype(BF)
-    d_gate, d_up = units_backward(branch, zero, kept_zero)
-    d_gate, d_up, g_mlp_one = lax.optimization_barrier((d_gate, d_up, g_mlp_one))
-    d_two, d_mlp_zero = product_sum(
-        (d_gate, d_up), zero[3], 0, (kept_zero[11], branch, kept_zero[14]), ((2, (0, 1)), (3, (4,))), key=10
+
+    d_gate, d_up = units_backward(branch, zero, gate_zero, up_zero)
+    grad_middle, grad_attn, d_gain_mlp_zero, d_mlp_zero = product_sum(
+        (d_gate, d_up, inner_zero, middle_zero, branch, r_zero, zero[1]),
+        ((0, 1), 0, ("back", (3, 4, 6)), back),
+        zero[3], ((5, (0, 1)), (4, (2,))), key=9,
     )
     g_mlp_zero = reduce_gradient(d_mlp_zero)
-    grad_middle, grad_attn, do_t, d_gain_mlp_zero = middle_backward(
-        branch.astype(F32), d_two, zero, tables, kept_zero
-    )
-    do_t, g_attn_one = lax.optimization_barrier((do_t, g_attn_one))
-    dq, dkv = attention_backward(do_t, tables, kept_zero)
-    d_one, d_attn_zero = product_sum(
-        (dq, dkv), zero[2], 0, (kept_zero[2], grad_attn, kept_zero[7]), ((2, (0, 1)), (3, (4,))), key=9
-    )
-    g_attn_zero = reduce_now(d_attn_zero)
-    grad_zero, d_gain_attn_zero = first_backward(grad_middle, d_one, zero, kept_zero)
-
-    grad_zero, grad_one, out_zero, out_one, g_mlp_zero, g_mlp_one, g_attn_one, d_gain_attn_zero = (
-        lax.optimization_barrier(
-            (grad_zero, grad_one, out_zero, out_one, g_mlp_zero, g_mlp_one, g_attn_one, d_gain_attn_zero)
-        )
-    )
-
-    out_got = lax.ppermute(jnp.where(first_core, out_one, out_zero), "section", swap)
-    layer_output = jnp.stack(
-        [jnp.where(first_core, out_zero, out_got), jnp.where(first_core, out_got, out_one)]
-    )
-    one_got = lax.ppermute(grad_one.astype(BF), "section", [(0, 1)]).astype(F32)
-    zero_got = lax.ppermute(grad_zero.astype(BF), "section", [(1, 0)]).astype(F32)
-    input_grad = jnp.stack(
-        [jnp.where(first_core, grad_zero, one_got), jnp.where(first_core, zero_got, grad_one)]
-    )
-
-    def own_shard(zero, one):
-        got = lax.ppermute(jnp.where(first_core, one, zero), "section", swap)
-        return jnp.where(first_core, zero, got), jnp.where(first_core, got, one)
-
-    def joined(halves, start, stop):
-        return jnp.concatenate([h[:, start:stop] for h in halves], 0).astype(F32)
-
-    g_mlp = own_shard(g_mlp_zero, g_mlp_one)
-    g_attn = own_shard(g_attn_zero, g_attn_one)
+    grad_attn, g_mlp_one = lax.optimization_barrier((grad_attn, g_mlp_one))
+    dq, dkv = attention_backward(grad_attn, zero, tables, kept_zero)
+    dq, g_attn_one = lax.optimization_barrier((dq, g_attn_one))
+    grad_zero, send_zero, d_gain_attn_zero, d_attn_zero = product_sum(
+        (dq, dkv, tree, grad_middle, zero[0], normed_zero, grad_attn, o_zero),
+        ((0, 1), 0, ("back", (2, 3, 4)), back),
+        zero[2], ((5, (0, 1)), (6, (7,))), key=11,
+    )
+    d_gain_attn_zero, d_gain_mlp_zero, d_gain_attn_one, d_gain_mlp_one = [
+        jnp.sum(x, 0) for x in (d_gain_attn_zero, d_gain_mlp_zero, d_gain_attn_one, d_gain_mlp_one)
+    ]
     d_gains = jnp.stack([d_gain_attn_zero, d_gain_mlp_zero, d_gain_attn_one, d_gain_mlp_one])
     d_gains = d_gains.reshape(2, 2, devices, -1).swapaxes(1, 2).reshape(2, devices, -1, 128)
-    g_gain = share_sums(d_gains).reshape(2, -1)
+
+    ending = finish if devices == 4 else finish_apart
+    g_attn_zero, g_gain, got_out, got_in, got_mlp, got_attn = ending(
+        d_attn_zero, d_gains, out_zero, out_one, send_zero, branch,
+        g_mlp_zero, g_mlp_one, g_attn_one,
+    )
+
+    layer_output, input_grad, *grads = write_results(
+        (out_zero, out_one, got_out), (grad_zero, grad_one, got_in), (g_mlp_zero, g_mlp_one, got_mlp),
+        (g_attn_zero, g_attn_one, got_attn), width, span, units,
+    )
+    g_query, g_key, g_value, g_out, g_gate, g_up, g_down = [grad[None] for grad in grads]
+    g_gain = g_gain.reshape(2, 1, -1)
     return (
-        layer_output[None],
-        input_grad[None],
-        g_gain[0][None],
-        joined(g_attn, 0, width)[None],
-        joined(g_attn, width, width + span)[None],
-        joined(g_attn, width + span, split)[None],
-        joined(g_attn, split, split + width).T[None],
-        g_gain[1][None],
-        joined(g_mlp, 0, units)[None],
-        joined(g_mlp, units, 2 * units)[None],
-        joined(g_mlp, 2 * units, 3 * units).T[None],
+        layer_output[None], input_grad[None], g_gain[0], g_query, g_key, g_value, g_out, g_gain[1], g_gate, g_up, g_down,
     )
 
 

time: 943 us -> 1180 us (1.25)
  Pallas kernels: 636 us -> 983 us
  other arithmetic: 129 us -> 26 us
    pallas_call x10, Pallas kernels: 494 us -> 849 us  [the longest x8 503 us: product_sum(): pl.pallas_call(functools.partial(product_sum_kernel, (len(arrays), job, t...]
    convert_element_type x15 -> x2, other arithmetic: 48.2 us -> 3.44 us  [the longest x1 2.78 us: layer_units(): return (gate, up, (gate * jax.nn.sigmoid(gate) * up).astype(BF))]
    reduce_sum x8 -> x5, other arithmetic: 26 us -> 4.66 us  [the longest x1 3.74 us: shards(): jnp.mean(hidden * hidden, -1, keepdims=True) + EPSILON]
    another operation x3 -> x0, other arithmetic: 12.1 us -> none  [the longest x2 9.66 us: shards(): jnp.stack([jnp.where(first_core, grad_zero, one_got), jnp.where(first_cor...]
    unnamed x156 -> x110, local copies, waits for them, and re-layouts: 37.6 us -> 30.2 us
  transfers between devices with their start and end apart: 14 -> 9, of which waited for: 3 -> 4; matrix products, arithmetic and copies ran while one was open for 19% -> 7% of each run, Pallas kernels for 58% -> 49%
where the time goes in v3:
time: 1180 us; the launch traced here: 1170 us
  Pallas kernels  983 us (83%)
  matrix products  70.1 us (6%)
  local copies, waits for them, and re-layouts  45.3 us (4%)
  waiting for transfers between devices  28.7 us (2%)
  other arithmetic  26 us (2%)
  between operations  15.4 us (1%)
    pallas_call x8, Pallas kernels, product_sum(): pl.pallas_call(functools.partial(product_sum_kernel, (len(arrays), job, t...  503 us
    pallas_call x1, Pallas kernels, write_results(): pl.pallas_call(functools.partial(write_kernel, width + 2 * span), out_sha...  319 us
    pallas_call x2, Pallas kernels, attend_back(): pl.pallas_call(functools.partial(attend_back_kernel, rows, step), out_sha...  45.8 us
    dot_general x6, matrix products, dot_f32(): lax.dot_general(a, b, (((ca,), (cb,)), ((), ())), preferred_element_type=...  38.2 us
    pallas_call x2, Pallas kernels, gather_rows(): pl.pallas_call(functools.partial(gather_kernel, count), out_shape=(jax.Sh...  33.9 us
    pallas_call x2, Pallas kernels, attend(): pl.pallas_call(functools.partial(attend_kernel, rows, step), out_shape=(j...  31.2 us
    unnamed x110, local copies, waits for them, and re-layouts  30.2 us
    pallas_call x1, Pallas kernels, finish(): pl.pallas_call(finish_kernel, out_shape=(jax.ShapeDtypeStruct((rows, widt...  27.1 us
  transfers between devices with their start and end apart: 9, of which 4 were waited for; matrix products, arithmetic and copies ran while one was open for 7% of the time, Pallas kernels for 49%

profile of v3, /device:TPU:1, one launch (start us, length us, event | category | flops | bytes accessed | tf_op | source)
XLA Modules:
  0.0 1169.6 jit_solution(17783636873027516485)
XLA Ops:
  21.6 3.0 convert_bitcast_fusion.1
  25.4 4.1 collective-permute-done.1
  34.4 3.7 fusion.8
  43.5 19.8 %all-gather.5.cloned.1.call-done.refs_3_.refs_8_ = bf16[2048,1155]{1,0:T(8,128)(2,1)} async-done(((bf16[256,1155]{1,0:T(8,128)(2,1)}), bf16[2048,1155]{1,0:T(8,128)(2,1)}) %all-gather.5.cloned.1.call-update) | async-done | bytes 4730896 | tf_op jit(solution)/shard_map/all_gather | solution.py:1017
  71.1 17.4 %gather_rows.2 = (bf16[4,640,128]{2,1,0:T(8,128)(2,1)}, bf16[128,2560]{1,0:T(8,128)(2,1)}) custom-call(f32[640,128]{1,0:T(8,128)} %fusion.28.raw_ref, f32[640,128]{1,0:T(8,128)} %maximum_maximum_fusion.cos_ref, f32[640,128]{1,0:T(8,128)} %get-tuple-element.188.sin_ref), custom_call_target="tpu_custom_call" | custom-call | flops 1 | bytes 1 | tf_op jit(solution)/shard_map/gather_rows/pallas_call | solution.py:414
  88.5 4.3 fusion.13.q_ref
  92.9 15.6 %attend.2 = (bf16[512,640]{1,0:T(8,128)(2,1)S(1)}, bf16[640,512]{1,0:T(8,128)(2,1)S(1)}, f32[4,5,1,256]{3,2,1,0:T(1,128)S(1)}) custom-call(s32[1]{0:T(128)} %bitcast.start_ref, f32[512,640]{1,0:T(8,128)S(1)} %fusion.13.q_ref, bf16[2560,128]{1,0:T(8,128)(2,1)S(1)} %bitcast.71, bf16[128,2560]{1,0:T(8,128)(2,1)S(1)} %copy-done.14, ...), custom_call_target="tpu_custom_call" | custom-call | flops 1 | bytes 1 | tf_op jit(solution)/shard_map/attend/pallas_call | solution.py:875
  112.3 78.4 %product_sum_1.1 = (f32[640,2048]{1,0:T(8,128)}, bf16[640,2048]{1,0:T(8,128)(2,1)}) custom-call(bf16[640,512]{1,0:T(8,128)(2,1)} %copy-done.8, bf16[640,2048]{1,0:T(8,128)(2,1)} %get-tuple-element.191.refs_1_.refs_2_, f32[1,2048]{1,0:T(1,128)} %copy.97.refs_2_.refs_6_, bf16[2048,1155]{1,0:T(8,128)(2,1)} %all-gather.5.cloned.1.call-done.refs_3_.refs_8_), custom_call_target="tpu_custom_call" | custom-call | flops 1 | bytes 1 | tf_op jit(solution)/shard_map/product_sum_1/pallas_call | solution.py:337
  192.8 12.0 %fusion.2 = f32[640,2816]{1,0:T(8,128)S(1)} fusion(bf16[640,2048]{1,0:T(8,128)(2,1)} %get-tuple-element.75.refs_5_, bf16[2048,4224]{1,0:T(8,128)(2,1)} %all-gather.7.cloned.1.call-done.refs_3_.refs_7_), kind=kOutput, calls=%fused_computation.2 | convolution fusion | flops 7381975040 | bytes 21364736 | tf_op jit(solution)/shard_map/dot_general | solution.py:965
  208.4 49.0 %product_sum_5.1 = (bf16[640,2048]{1,0:T(8,128)(2,1)}, bf16[640,2048]{1,0:T(8,128)(2,1)}) custom-call(bf16[640,1408]{1,0:T(8,128)(2,1)} %multiply_convert_fusion.5.refs_0_.refs_2_, f32[640,2048]{1,0:T(8,128)} %get-tuple-element.76.refs_1_.refs_3_, f32[1,2048]{1,0:T(1,128)} %bitcast.85, bf16[2048,4224]{1,0:T(8,128)(2,1)} %all-gather.7.cloned.1.call-done.refs_3_.refs_7_), custom_call_target="tpu_custom_call" | custom-call | flops 1 | bytes 1 | tf_op jit(solution)/shard_map/product_sum_5/pallas_call | solution.py:337
  257.4 3.4 fusion.30.raw_ref
  260.8 3.6 dynamic-slice_bitcast_fusion.refs_3_
  264.4 16.5 %gather_rows.3 = (bf16[4,640,128]{2,1,0:T(8,128)(2,1)}, bf16[128,2560]{1,0:T(8,128)(2,1)}) custom-call(f32[640,128]{1,0:T(8,128)} %fusion.30.raw_ref, f32[640,128]{1,0:T(8,128)} %maximum_maximum_fusion.cos_ref, f32[640,128]{1,0:T(8,128)} %get-tuple-element.188.sin_ref), custom_call_target="tpu_custom_call" | custom-call | flops 1 | bytes 1 | tf_op jit(solution)/shard_map/gather_rows/pallas_call | solution.py:414
  280.9 4.6 fusion.17.q_ref
  285.5 15.6 %attend.3 = (bf16[512,640]{1,0:T(8,128)(2,1)S(1)}, bf16[640,512]{1,0:T(8,128)(2,1)S(1)}, f32[4,5,1,256]{3,2,1,0:T(1,128)S(1)}) custom-call(s32[1]{0:T(128)} %bitcast.start_ref, f32[512,640]{1,0:T(8,128)S(1)} %fusion.17.q_ref, bf16[2560,128]{1,0:T(8,128)(2,1)S(1)} %bitcast.73, bf16[128,2560]{1,0:T(8,128)(2,1)S(1)} %copy-done.17, ...), custom_call_target="tpu_custom_call" | custom-call | flops 1 | bytes 1 | tf_op jit(solution)/shard_map/attend/pallas_call | solution.py:875
  306.3 43.7 %product_sum_2.1 = (f32[640,2048]{1,0:T(8,128)}, bf16[640,2048]{1,0:T(8,128)(2,1)}) custom-call(bf16[640,512]{1,0:T(8,128)(2,1)} %copy-done.9, bf16[640,2048]{1,0:T(8,128)(2,1)} %get-tuple-element.79.refs_1_.refs_2_.out_zero, f32[1,2048]{1,0:T(1,128)} %copy.99.refs_2_.refs_4_, bf16[2048,1154]{1,0:T(8,128)(2,1)} %all-gather.9.cloned.1.call-done.refs_3_.refs_8_), custom_call_target="tpu_custom_call" | custom-call | flops 1 | bytes 1 | tf_op jit(solution)/shard_map/product_sum_2/pallas_call | solution.py:337
  350.0 12.1 %fusion = f32[640,2816]{1,0:T(8,128)S(1)} fusion(bf16[640,2048]{1,0:T(8,128)(2,1)} %get-tuple-element.85.refs_2_, bf16[2048,4224]{1,0:T(8,128)(2,1)} %all-gather.11.cloned.1.call-done.refs_6_.refs_5_), kind=kOutput, calls=%fused_computation | convolution fusion | flops 7381975040 | bytes 21364736 | tf_op jit(solution)/shard_map/dot_general | solution.py:965
  362.1 9.7 multiply_convert_fusion.2
  371.8 66.2 %product_sum_6.1 = (bf16[640,2048]{1,0:T(8,128)(2,1)}, bf16[2048,4224]{1,0:T(8,128)(2,1)}) custom-call(bf16[640,1408]{1,0:T(8,128)(2,1)} %get-tuple-element.196.refs_0_, f32[640,2048]{1,0:T(8,128)} %get-tuple-element.86.refs_1_.refs_2_, bf16[640,2048]{1,0:T(8,128)(2,1)} %get-tuple-element.85.refs_2_, bf16[640,2048]{1,0:T(8,128)(2,1)} %dynamic-slice_bitcast_fusion.refs_3_, ...), custom_call_target="tpu_custom_call" | custom-call | flops 1 | bytes 1 | tf_op jit(solution)/shard_map/product_sum_6/pallas_call | solution.py:337
  438.1 54.4 %product_sum_8.1 = (f32[640,2048]{1,0:T(8,128)}, bf16[640,2048]{1,0:T(8,128)(2,1)}, f32[8,2048]{1,0:T(8,128)}) custom-call(bf16[640,1408]{1,0:T(8,128)(2,1)} %get-tuple-element.89.refs_4_.refs_0_, bf16[640,1408]{1,0:T(8,128)(2,1)} %get-tuple-element.194.refs_5_.refs_1_, f32[640,2048]{1,0:T(8,128)} %get-tuple-element.86.refs_1_.refs_2_, ...), custom_call_target="tpu_custom_call" | custom-call | flops 1 | bytes 1 | tf_op jit(solution)/shard_map/product_sum_8/pallas_call | solution.py:337
  492.5 4.4 fusion.19.do_ref
  496.9 22.9 %attend_back.2 = (bf16[640,512]{1,0:T(8,128)(2,1)S(1)}, bf16[2560,128]{1,0:T(8,128)(2,1)S(1)}) custom-call(s32[1]{0:T(128)} %bitcast.start_ref, f32[512,640]{1,0:T(8,128)S(1)} %fusion.17.q_ref, bf16[512,640]{1,0:T(8,128)(2,1)S(1)} %fusion.19.do_ref, bf16[512,640]{1,0:T(8,128)(2,1)S(1)} %copy-done.34, f32[4,5,1,256]{3,2,1,0:T(1,128)S(1)} %get-tuple-element.92.lse_ref, ...), custom_call_target="tpu_custom_call" | custom-call | flops 1 | bytes 1 | tf_op jit(solution)/shard_map/attend_back/pallas_call | solution.py:911
  521.5 9.1 scatter_rows.2.refs_1_
  531.6 66.2 %product_sum_7.1 = (f32[640,2048]{1,0:T(8,128)}, bf16[640,2048]{1,0:T(8,128)(2,1)}, f32[8,2048]{1,0:T(8,128)}, bf16[2048,1152]{1,0:T(8,128)(2,1)}) custom-call(bf16[640,512]{1,0:T(8,128)(2,1)} %copy-done.30, bf16[640,128]{1,0:T(8,128)(2,1)} %scatter_rows.2.refs_1_, bf16[640,2048]{1,0:T(8,128)(2,1)} %get-tuple-element.79.refs_1_.refs_2_.out_zero, ...), custom_call_target="tpu_custom_call" | custom-call | flops 1 | bytes 1 | tf_op jit(solution)/shard_map/product_sum_7/pallas_call | solution.py:337
  599.6 10.3 multiply_convert_fusion
  609.9 75.1 %product_sum_9.1 = (f32[640,2048]{1,0:T(8,128)}, bf16[640,2048]{1,0:T(8,128)(2,1)}, f32[8,2048]{1,0:T(8,128)}, bf16[2048,4224]{1,0:T(8,128)(2,1)}) custom-call(bf16[640,1408]{1,0:T(8,128)(2,1)} %get-tuple-element.193.refs_0_, bf16[640,1408]{1,0:T(8,128)(2,1)} %get-tuple-element.192.refs_1_, bf16[640,1408]{1,0:T(8,128)(2,1)} %multiply_convert_fusion.5.refs_0_.refs_2_, ...), custom_call_target="tpu_custom_call" | custom-call | flops 1 | bytes 1 | tf_op jit(solution)/shard_map/product_sum_9/pallas_call | solution.py:337
  687.4 4.8 fusion.22.do_ref
  692.3 23.0 %attend_back.3 = (bf16[640,512]{1,0:T(8,128)(2,1)S(1)}, bf16[2560,128]{1,0:T(8,128)(2,1)S(1)}) custom-call(s32[1]{0:T(128)} %bitcast.start_ref, f32[512,640]{1,0:T(8,128)S(1)} %copy-done.7, bf16[512,640]{1,0:T(8,128)(2,1)S(1)} %fusion.22.do_ref, bf16[512,640]{1,0:T(8,128)(2,1)S(1)} %copy-done.32, f32[4,5,1,256]{3,2,1,0:T(1,128)S(1)} %get-tuple-element.101.lse_ref, ...), custom_call_target="tpu_custom_call" | custom-call | flops 1 | bytes 1 | tf_op jit(solution)/shard_map/attend_back/pallas_call | solution.py:911
  717.0 13.6 %scatter_rows.3.refs_1_ = bf16[640,128]{1,0:T(8,128)(2,1)} custom-call(bf16[4,640,128]{2,1,0:T(8,128)(2,1)} %bitcast.75, f32[640,128]{1,0:T(8,128)} %maximum_maximum_fusion.cos_ref, f32[640,128]{1,0:T(8,128)} %get-tuple-element.189.sin_ref), custom_call_target="tpu_custom_call" | custom-call | flops 1 | bytes 1 | tf_op jit(solution)/shard_map/scatter_rows/pallas_call | solution.py:435
  730.6 70.0 %product_sum_11.1 = (f32[640,2048]{1,0:T(8,128)}, bf16[640,2048]{1,0:T(8,128)(2,1)}, f32[8,2048]{1,0:T(8,128)}, bf16[2048,1152]{1,0:T(8,128)(2,1)}) custom-call(bf16[640,512]{1,0:T(8,128)(2,1)} %copy-done.29, bf16[640,128]{1,0:T(8,128)(2,1)} %scatter_rows.3.refs_1_, bf16[640,2048]{1,0:T(8,128)(2,1)} %get-tuple-element.191.refs_1_.refs_2_, ...), custom_call_target="tpu_custom_call" | custom-call | flops 1 | bytes 1 | tf_op jit(solution)/shard_map/product_sum_11/pallas_call | solution.py:337
  806.5 27.1 %finish.1 = (bf16[256,1152]{1,0:T(8,128)(2,1)S(1)}, f32[8,128]{1,0:T(8,128)S(1)}, bf16[640,2048]{1,0:T(8,128)(2,1)S(1)}, bf16[640,2048]{1,0:T(8,128)(2,1)S(1)}, ...) custom-call(bf16[8,256,1152]{2,1,0:T(8,128)(2,1)} %bitcast.78, f32[2,4,8,128]{3,2,1,0:T(8,128)S(1)} %reshape.82.gain_ref, ...), custom_call_target="tpu_custom_call" | custom-call | flops 1 | bytes 1 | tf_op jit(solution)/shard_map/finish/pallas_call | solution.py:563
  840.2 318.9 %write_results.1 = (bf16[2,640,2048]{2,1,0:T(8,128)(2,1)}, f32[2,640,2048]{2,1,0:T(8,128)}, f32[512,512]{1,0:T(8,128)}, f32[512,64]{1,0:T(8,128)}, f32[512,64]{1...) custom-call(bf16[640,2048]{1,0:T(8,128)(2,1)} %get-tuple-element.79.refs_1_.r, ...), custom_call_target="tpu_custom_call" | custom-call | flops 1 | bytes 1 | tf_op jit(solution)/shard_map/write_results/pallas_call | solution.py:687
  (185 shorter events, 71.7 us)
Async XLA Ops:
  7.2 27.2 %copy-start = (s32[2,13]{1,0:T(2,128)S(1)}, s32[2,13]{1,0:T(2,128)}, u32[]{:S(2)}) copy-start(s32[2,13]{1,0:T(2,128)} %param.18) | copy-start | bytes 316
  7.2 56.1 %all-gather.5.cloned.1.call-start = ((), (), s32[]{:S(2)}) async-start(), calls=%async_computation.3 | async-start | bytes 5898240 | tf_op jit(solution)/shard_map/all_gather | solution.py:1017
  15.8 2.1 collective-permute-start
  18.3 6.3 copy-start.46
  19.4 173.4 %all-gather.7.cloned.1.call-start = ((), (), s32[]{:S(2)}) async-start(), calls=%async_computation.4 | async-start | bytes 19464192 | tf_op jit(solution)/shard_map/all_gather | solution.py:1017
  25.2 4.3 collective-permute-start.1
  32.0 225.4 %all-gather.9.cloned.1.call-start = ((), (), s32[]{:S(2)}) async-start(), calls=%async_computation.5 | async-start | bytes 5898240 | tf_op jit(solution)/shard_map/all_gather | solution.py:1017
  32.7 317.3 %all-gather.11.cloned.1.call-start = ((), (), s32[]{:S(2)}) async-start(), calls=%async_computation.6 | async-start | bytes 19464192 | tf_op jit(solution)/shard_map/all_gather | solution.py:1017
  33.3 654.1 %reduce-scatter.4.cloned.1.call-start = ((), (), s32[]{:S(2)}) async-start(), calls=%async_computation.7 | async-start | bytes 19464192 | tf_op jit(solution)/shard_map/reduce_scatter | solution.py:980
  38.7 54.1 %copy-start.21 = (f32[32,640]{1,0:T(8,128)}, f32[32,640]{1,0:T(8,128)S(1)}, u32[]{:S(2)}) copy-start(f32[32,640]{1,0:T(8,128)S(1)} %get-tuple-element.206.sin_ref) | copy-start | bytes 245764
  38.7 54.1 %copy-start.25 = (f32[32,640]{1,0:T(8,128)}, f32[32,640]{1,0:T(8,128)S(1)}, u32[]{:S(2)}) copy-start(f32[32,640]{1,0:T(8,128)S(1)} %get-tuple-element.207.cos_ref) | copy-start | bytes 245764
  43.5 49.4 %copy-start.2 = (bf16[2560,640]{1,0:T(8,128)(2,1)}, bf16[2560,640]{1,0:T(8,128)(2,1)S(1)}, u32[]{:S(2)}) copy-start(bf16[2560,640]{1,0:T(8,128)(2,1)S(1)} %select_convert_fusion.bias_ref) | copy-start | bytes 9830404
  92.8 15.6 %copy-start.6 = (f32[512,640]{1,0:T(8,128)}, f32[512,640]{1,0:T(8,128)S(1)}, u32[]{:S(2)}) copy-start(f32[512,640]{1,0:T(8,128)S(1)} %fusion.13.q_ref) | copy-start | bytes 3932164
  280.9 4.6 copy-start.3
  280.9 4.6 copy-start.16
  280.9 4.6 copy-start.17
  280.9 4.6 copy-start.22
  280.9 4.6 copy-start.26
  350.0 12.1 %copy-start.40 = (bf16[640,2048]{1,0:T(8,128)(2,1)S(1)}, bf16[640,2048]{1,0:T(8,128)(2,1)}, u32[]{:S(2)}) copy-start(bf16[640,2048]{1,0:T(8,128)(2,1)} %dynamic-slice_bitcast_fusion.refs_3_) | copy-start | bytes 7864324
  438.0 292.6 %reduce-scatter.6.cloned.1.call-start = ((), (), s32[]{:S(2)}) async-start(), calls=%async_computation.8 | async-start | bytes 5308416 | tf_op jit(solution)/shard_map/reduce_scatter | solution.py:980
  492.5 4.4 copy-start.18
  492.5 4.4 copy-start.23
  496.9 33.8 %copy-start.45 = (f32[1,2048]{0,1:T(8,128)S(1)}, f32[1,2048]{0,1:T(8,128)}, u32[]{:S(2)}) copy-start(f32[1,2048]{0,1:T(8,128)} %get-tuple-element.204) | copy-start | bytes 24580
  597.9 205.4 %reduce-scatter.8.cloned.1.call-start = ((), (), s32[]{:S(2)}) async-start(), calls=%async_computation.9 | async-start | bytes 19464192 | tf_op jit(solution)/shard_map/reduce_scatter | solution.py:980
  687.4 4.9 copy-start.7
  687.4 4.9 copy-start.13
  687.4 4.9 copy-start.15
  687.4 4.9 copy-start.24
  687.4 4.9 copy-start.28
  687.4 4.9 copy-start.32
  730.6 72.6 %copy-start.19 = (bf16[256,1152]{1,0:T(8,128)(2,1)S(1)}, bf16[256,1152]{1,0:T(8,128)(2,1)}, u32[]{:S(2)}) copy-start(bf16[256,1152]{1,0:T(8,128)(2,1)} %reduce-scatter.6.cloned.1.call-done.attn_one) | copy-start | bytes 1769476
  840.2 322.4 %copy-start.1 = (s32[2,13]{1,0:T(2,128)S(1)}, s32[2,13]{1,0:T(2,128)}, u32[]{:S(2)}) copy-start(s32[2,13]{1,0:T(2,128)} %param.18) | copy-start | bytes 316
  (29 other events, 55.7 us)
Sparse Core Ops, SparseCore 0:
  19.5 43.7 all-gather.4
  65.7 97.3 all-gather.6
  165.0 41.1 all-gather.8
  207.9 98.8 all-gather.10
  438.2 120.6 reduce-scatter.3
  598.0 52.2 reduce-scatter.5
  685.3 117.9 reduce-scatter.7

commit v4 on v3

--- a/solution.py
+++ b/solution.py
@@ -33,6 +33,10 @@
     return pl.ds(pl.multiple_of(i * PIECE, PIECE), PIECE)
 
 
+def gain_row(arrays, place, at):
+    return arrays[place[0]][place[1] : place[1] + 1, at]
+
+
 def row_scale(squares, model):
     return lax.rsqrt(jnp.sum(squares, 1, keepdims=True) * (1.0 / model) + EPSILON)
 
@@ -59,7 +63,7 @@
             sums[...] += y.astype(F32) * y.astype(F32)
     if kind == "back":
         product = total * arrays[places[0]][:, at].astype(F32) * keep[...]
-        sums[...] += product * arrays[places[2]][:, at]
+        sums[...] += product * gain_row(arrays, places[2], at)
         outs[2][:, at] = jnp.sum(product.reshape(-1, 8, PIECE), 0)
 
 
@@ -71,13 +75,13 @@
         scale = row_scale(sums[rows], model)
         for i in range(model // PIECE):
             y = outs[0][rows, at(i)].astype(F32)
-            outs[1][rows, at(i)] = (y * scale * arrays[places[1]][:, at(i)]).astype(BF)
+            outs[1][rows, at(i)] = (y * scale * gain_row(arrays, places[1], at(i))).astype(BF)
     if kind == "back":
         mean = jnp.sum(sums[rows], 1, keepdims=True) * (1.0 / model)
         scale = keep[rows]
         for i in range(model // PIECE):
             unit = arrays[places[0]][rows, at(i)].astype(F32) * scale
-            grad = total(i)[rows].astype(F32) * arrays[places[2]][:, at(i)]
+            grad = total(i)[rows].astype(F32) * gain_row(arrays, places[2], at(i))
             out = arrays[places[1]][rows, at(i)].astype(F32) + scale * (grad - unit * mean)
             outs[0][rows, at(i)] = out
             outs[1][rows, at(i)] = out.astype(BF)
@@ -182,12 +186,12 @@
 
     def first(i):
         to_inner(i).wait_recv()
-        p_buf[i] = (p_buf[i].astype(F32) + a_buf[i].astype(F32)).astype(BF)
+        p_buf[i] = p_buf[i] + a_buf[i]
         across(i).start()
 
     def second(i):
         across(i).wait_recv()
-        b_buf[i] = (p_buf[i].astype(F32) + b_buf[i].astype(F32)).astype(BF)
+        b_buf[i] = p_buf[i] + b_buf[i]
         to_outer(i).start()
         done(i)
 
@@ -445,7 +449,7 @@
 
 
 def finish_kernel(
-    g_hbm, gain_ref, out_zero, out_one, in_zero, in_one, mlp_zero, mlp_one, attn_one,
+    g_hbm, gain_ref, out_zero, out_one, in_zero, in_one, mlp_one, attn_one,
     o_ref, gain_out, got_out, got_in, got_mlp, got_attn,
     mine, away, got, xs, ys, xr, yr, gains, load_sem, send, recv, mate_send, mate_recv, gain_send, gain_recv,
 ):
@@ -518,7 +522,6 @@
     def _():
         to_mate(in_zero, got_in, 0).start()
         to_mate(out_zero, got_out, 1).start()
-        to_mate(mlp_zero, got_mlp, 2).start()
 
     outs[0].wait_recv()
     mine[2, upper] = (mine[2, upper].astype(F32) + xs[0].astype(F32)).astype(BF)
@@ -548,11 +551,18 @@
         copy.wait_send()
     to_mate(in_one, got_in, 0).wait()
     to_mate(out_one, got_out, 1).wait()
-    to_mate(mlp_one, got_mlp, 2).wait()
     to_mate(attn_one, got_attn, 3).wait()
 
-
-def finish(g, gains, out_zero, out_one, in_zero, in_one, mlp_zero, mlp_one, attn_one):
+    @pl.when(sec == 0)
+    def _():
+        to_mate(mlp_one, got_mlp, 2).wait_send()
+
+    @pl.when(sec == 1)
+    def _():
+        to_mate(mlp_one, got_mlp, 2).wait_recv()
+
+
+def finish(g, gains, out_zero, out_one, in_zero, in_one, mlp_one, attn_one):
     rows, width = g.shape[0] // 8, g.shape[1]
     part = pltpu.VMEM((2, rows // 2, width), BF)
     whole = pltpu.VMEM((4, rows, width), BF)
@@ -565,9 +575,9 @@
         out_shape=(
             jax.ShapeDtypeStruct((rows, width), BF),
             jax.ShapeDtypeStruct(gains.shape[2:], F32),
-            like(out_zero), like(in_zero), like(mlp_zero), like(attn_one),
+            like(out_zero), like(in_zero), like(mlp_one), like(attn_one),
         ),
-        in_specs=[anywhere, in_vmem, *[anywhere] * 7],
+        in_specs=[anywhere, in_vmem, *[anywhere] * 6],
         out_specs=(in_vmem, in_vmem, *[anywhere] * 4),
         scratch_shapes=[
             whole, whole, whole, part, part, end, end, pltpu.VMEM((7, *gains.shape[2:]), F32),
@@ -578,86 +588,133 @@
         ),
         cost_estimate=NO_COST,
         name="finish",
-    )(g.reshape(8, rows, width), gains, out_zero, out_one, in_zero, in_one, mlp_zero, mlp_one, attn_one)
-
-
-def finish_apart(g, gains, out_zero, out_one, in_zero, in_one, mlp_zero, mlp_one, attn_one):
+    )(g.reshape(8, rows, width), gains, out_zero, out_one, in_zero, in_one, mlp_one, attn_one)
+
+
+def finish_apart(g, gains, out_zero, out_one, in_zero, in_one, mlp_one, attn_one):
     first_core = lax.axis_index("section") == 0
     half = reduce_gradient(g)
     swap = lambda zero, one: lax.ppermute(jnp.where(first_core, one, zero), "section", [(0, 1), (1, 0)])
     return (
-        half, share_sums(gains), swap(out_zero, out_one), swap(in_zero, in_one), swap(mlp_zero, mlp_one),
-        swap(half, attn_one),
-    )
-
-
-def write_kernel(
-    split, out_zero, out_one, got_out, in_zero, in_one, got_in, mlp_zero, mlp_one, got_mlp, attn_zero, attn_one, got_attn,
-    out_hbm, in_hbm, q_hbm, k_hbm, v_hbm, o_hbm, gate_hbm, up_hbm, down_hbm,
-    mlp, attn, got_narrow, got_wide, q_buf, k_buf, v_buf, o_buf, gate_buf, up_buf, down_buf, load_sem, store_sem,
+        half, share_sums(gains), swap(out_zero, out_one), swap(in_zero, in_one),
+        lax.ppermute(mlp_one, "section", [(0, 1)]), swap(half, attn_one),
+    )
+
+
+def in_rows(count, block, body):
+    def turn(r, _):
+        body(pl.ds(pl.multiple_of(r * block, block), block))
+        return 0
+
+    lax.fori_loop(0, count // block, turn, 0)
+
+
+def widen_turned(dst, src, start, width):
+    for c in range(0, width, 128):
+        dst[c : c + 128] = src[:, start + c : start + c + 128].astype(F32).T
+
+
+def write_mlp_kernel(
+    zero, one, from_one, from_zero, gate_hbm, up_hbm, down_hbm, mlp, gate_buf, up_buf, down_buf, load_sem, store_sem
 ):
     sec = lax.axis_index("section")
-    half = mlp_zero.shape[0]
+    half, units = zero.shape[0], gate_buf.shape[1]
     low, high = pl.ds(0, half), pl.ds(half, half)
-
-    def start(own_out, own_in, mlp_low, mlp_high, attn_low, attn_high):
-        pltpu.make_async_copy(mlp_low, mlp.at[low], load_sem.at[0]).start()
-        pltpu.make_async_copy(mlp_high, mlp.at[high], load_sem.at[1]).start()
-        pltpu.make_async_copy(attn_low, attn.at[low], load_sem.at[2]).start()
-        pltpu.make_async_copy(attn_high, attn.at[high], load_sem.at[3]).start()
-        pltpu.make_async_copy(own_out, out_hbm.at[sec], store_sem.at[0]).start()
-        pltpu.make_async_copy(own_in, in_hbm.at[sec], store_sem.at[1]).start()
-
-    load_in = pltpu.make_async_copy(got_in, got_narrow, load_sem.at[4])
-    load_in.start()
+    load = lambda src, at, k: pltpu.make_async_copy(src, mlp.at[at], load_sem.at[k])
+    store = lambda src, dst, k: pltpu.make_async_copy(src, dst, store_sem.at[k])
 
     @pl.when(sec == 0)
     def _():
-        start(out_zero, in_zero, mlp_zero, got_mlp, attn_zero, got_attn)
+        load(zero, low, 0).start()
+        load(from_one, high, 1).start()
 
     @pl.when(sec == 1)
     def _():
-        start(out_one, in_one, got_mlp, mlp_one, got_attn, attn_one)
-
-    other = pltpu.make_async_copy(got_out, out_hbm.at[1 - sec], store_sem.at[2])
-    other.start()
-    stores = [other]
-
-    def store(src, dst, k):
-        stores.append(pltpu.make_async_copy(src, dst, store_sem.at[k]))
-        stores[-1].start()
-
-    def in_rows(count, block, body):
-        def turn(r, _):
-            body(pl.ds(pl.multiple_of(r * block, block), block))
-            return 0
-
-        lax.fori_loop(0, count // block, turn, 0)
-
-    def widen(rows):
-        got_wide[rows] = got_narrow[rows].astype(F32)
-
-    load_in.wait()
-    in_rows(got_narrow.shape[0], 32, widen)
-    store(got_wide, in_hbm.at[1 - sec], 3)
-    units = gate_buf.shape[1]
-    width = q_buf.shape[1]
-    span = k_buf.shape[1]
-    pltpu.make_async_copy(mlp_zero, mlp.at[low], load_sem.at[0]).wait()
-    pltpu.make_async_copy(mlp_zero, mlp.at[high], load_sem.at[1]).wait()
+        load(from_zero, low, 0).start()
+        load(one, high, 1).start()
+
+    load(zero, low, 0).wait()
+    load(zero, high, 1).wait()
 
     def gates(rows):
         gate_buf[rows] = mlp[rows, :units].astype(F32)
         up_buf[rows] = mlp[rows, units : 2 * units].astype(F32)
 
     in_rows(2 * half, 32, gates)
-    store(gate_buf, gate_hbm, 4)
-    store(up_buf, up_hbm, 5)
-    for c in range(0, units, 128):
-        down_buf[c : c + 128] = mlp[:, 2 * units + c : 2 * units + c + 128].astype(F32).T
-    store(down_buf, down_hbm, 6)
-    pltpu.make_async_copy(attn_one, attn.at[low], load_sem.at[2]).wait()
-    pltpu.make_async_copy(attn_one, attn.at[high], load_sem.at[3]).wait()
+    stores = [store(gate_buf, gate_hbm, 0), store(up_buf, up_hbm, 1), store(down_buf, down_hbm, 2)]
+    stores[0].start()
+    stores[1].start()
+    widen_turned(down_buf, mlp, 2 * units, units)
+    stores[2].start()
+    for copy in stores:
+        copy.wait()
+
+
+def write_mlp(zero, one, from_one, from_zero, units):
+    shard = 2 * zero.shape[0]
+    anywhere = pl.BlockSpec(memory_space=pl.ANY)
+    shapes = [(shard, units), (shard, units), (units, shard)]
+    return pl.pallas_call(
+        write_mlp_kernel,
+        out_shape=[jax.ShapeDtypeStruct(shape, F32) for shape in shapes],
+        in_specs=[anywhere] * 4,
+        out_specs=[anywhere] * 3,
+        scratch_shapes=[
+            pltpu.VMEM((shard, zero.shape[1]), BF),
+            *[pltpu.VMEM(shape, F32) for shape in shapes],
+            pltpu.SemaphoreType.DMA((2,)),
+            pltpu.SemaphoreType.DMA((3,)),
+        ],
+        compiler_params=pltpu.CompilerParams(vmem_limit_bytes=40 << 20),
+        cost_estimate=NO_COST,
+        name="write_mlp",
+    )(zero, one, from_one, from_zero)
+
+
+def write_kernel(
+    split, out_zero, out_one, got_out, in_zero, in_one, got_in, attn_zero, attn_one, got_attn,
+    out_hbm, in_hbm, q_hbm, k_hbm, v_hbm, o_hbm,
+    outs, wides, attn, narrow, q_buf, k_buf, v_buf, o_buf, load_sem, store_sem,
+):
+    sec = lax.axis_index("section")
+    half = attn_zero.shape[0]
+    low, high = pl.ds(0, half), pl.ds(half, half)
+    load = lambda src, dst, k: pltpu.make_async_copy(src, dst, load_sem.at[k])
+    store = lambda src, dst, k: pltpu.make_async_copy(src, dst, store_sem.at[k])
+
+    def start(own_out, own_in, attn_low, attn_high):
+        load(own_out, outs.at[0], 0).start()
+        load(own_in, wides.at[0], 1).start()
+        load(attn_low, attn.at[low], 2).start()
+        load(attn_high, attn.at[high], 3).start()
+
+    @pl.when(sec == 0)
+    def _():
+        start(out_zero, in_zero, attn_zero, got_attn)
+
+    @pl.when(sec == 1)
+    def _():
+        start(out_one, in_one, got_attn, attn_one)
+
+    load(got_in, narrow, 4).start()
+    load(got_out, outs.at[1], 5).start()
+    stores = [
+        store(outs.at[0], out_hbm.at[sec], 0),
+        store(wides.at[0], in_hbm.at[sec], 1),
+        store(outs.at[1], out_hbm.at[1 - sec], 2),
+        store(wides.at[1], in_hbm.at[1 - sec], 3),
+        store(q_buf, q_hbm, 4),
+        store(k_buf, k_hbm, 5),
+        store(v_buf, v_hbm, 6),
+        store(o_buf, o_hbm, 7),
+    ]
+    load(out_zero, outs.at[0], 0).wait()
+    stores[0].start()
+    load(in_zero, wides.at[0], 1).wait()
+    stores[1].start()
+    width, span = q_buf.shape[1], k_buf.shape[1]
+    load(attn_one, attn.at[low], 2).wait()
+    load(attn_one, attn.at[high], 3).wait()
 
     def projections(rows):
         q_buf[rows] = attn[rows, :width].astype(F32)
@@ -665,25 +722,28 @@
         v_buf[rows] = attn[rows, width + span : split].astype(F32)
 
     in_rows(2 * half, 32, projections)
-    for c in range(0, width, 128):
-        o_buf[c : c + 128] = attn[:, split + c : split + c + 128].astype(F32).T
-    store(q_buf, q_hbm, 7)
-    store(k_buf, k_hbm, 8)
-    store(v_buf, v_hbm, 9)
-    store(o_buf, o_hbm, 10)
+    for k in (4, 5, 6):
+        stores[k].start()
+    widen_turned(o_buf, attn, split, width)
+    stores[7].start()
+    load(got_in, narrow, 4).wait()
+
+    def widen(rows):
+        wides[1, rows] = narrow[rows].astype(F32)
+
+    in_rows(narrow.shape[0], 32, widen)
+    stores[3].start()
+    load(got_out, outs.at[1], 5).wait()
+    stores[2].start()
     for copy in stores:
         copy.wait()
-    pltpu.make_async_copy(out_zero, out_hbm.at[sec], store_sem.at[0]).wait()
-    pltpu.make_async_copy(in_zero, in_hbm.at[sec], store_sem.at[1]).wait()
-
-
-def write_results(outs, ins, mlps, attns, width, span, units):
-    rows, model = outs[0].shape
-    shard = 2 * mlps[0].shape[0]
+
+
+def write_results(results, ins, attns, width, span):
+    rows, model = results[0].shape
+    shard = 2 * attns[0].shape[0]
     anywhere = pl.BlockSpec(memory_space=pl.ANY)
-    shapes = [
-        (shard, width), (shard, span), (shard, span), (width, shard), (shard, units), (shard, units), (units, shard),
-    ]
+    shapes = [(shard, width), (shard, span), (shard, span), (width, shard)]
     return pl.pallas_call(
         functools.partial(write_kernel, width + 2 * span),
         out_shape=[
@@ -691,21 +751,21 @@
             jax.ShapeDtypeStruct((2, rows, model), F32),
             *[jax.ShapeDtypeStruct(shape, F32) for shape in shapes],
         ],
-        in_specs=[anywhere] * 12,
-        out_specs=[anywhere] * 9,
+        in_specs=[anywhere] * 9,
+        out_specs=[anywhere] * 6,
         scratch_shapes=[
-            pltpu.VMEM((shard, mlps[0].shape[1]), BF),
+            pltpu.VMEM((2, rows, model), BF),
+            pltpu.VMEM((2, rows, model), F32),
             pltpu.VMEM((shard, attns[0].shape[1]), BF),
             pltpu.VMEM((rows, model), BF),
-            pltpu.VMEM((rows, model), F32),
             *[pltpu.VMEM(shape, F32) for shape in shapes],
-            pltpu.SemaphoreType.DMA((5,)),
-            pltpu.SemaphoreType.DMA((11,)),
+            pltpu.SemaphoreType.DMA((6,)),
+            pltpu.SemaphoreType.DMA((8,)),
         ],
-        compiler_params=pltpu.CompilerParams(vmem_limit_bytes=56 << 20),
+        compiler_params=pltpu.CompilerParams(vmem_limit_bytes=40 << 20),
         cost_estimate=NO_COST,
         name="write_results",
-    )(*outs, *ins, *mlps, *attns)
+    )(*results, *ins, *attns)
 
 
 def share_kernel(count, x_ref, o_ref, buf, send, recv):
@@ -941,7 +1001,7 @@
 
 
 def layer_attention(normed, weights, tables):
-    gain_one, gain_two, w_attn, w_mlp, width, split, units = weights
+    gains, w_attn, w_mlp, width, split, units = weights
     start, bias_t, cos_t, sin_t, cos_rows, sin_rows = tables
     q_t = dot_f32(w_attn[:, :width], normed, 0, 1)
     kv, kv_t = gather_rows(
@@ -952,7 +1012,7 @@
 
 
 def attention_backward(grad_attn, weights, tables, kept):
-    gain_one, gain_two, w_attn, w_mlp, width, split, units = weights
+    gains, w_attn, w_mlp, width, split, units = weights
     start, bias_t, cos_t, sin_t, cos_rows, sin_rows = tables
     q_t, kv, kv_t, o_t, lse = kept
     do_t = dot_f32(w_attn[:, split : split + width], grad_attn, 0, 1).astype(BF)
@@ -962,14 +1022,14 @@
 
 def layer_units(normed, weights):
     units = weights[-1]
-    gate_up = jnp.dot(normed, weights[3][:, : 2 * units], preferred_element_type=F32)
+    gate_up = jnp.dot(normed, weights[2][:, : 2 * units], preferred_element_type=F32)
     gate, up = gate_up[:, :units], gate_up[:, units:]
     return gate, up, (gate * jax.nn.sigmoid(gate) * up).astype(BF)
 
 
 def units_backward(branch, weights, gate, up):
     units = weights[-1]
-    d_inner = dot_f32(branch, weights[3][:, 2 * units :], 1, 0)
+    d_inner = dot_f32(branch, weights[2][:, 2 * units :], 1, 0)
     sig = jax.nn.sigmoid(gate)
     d_gate = (d_inner * up * sig * (1.0 + gate * (1.0 - sig))).astype(BF)
     d_up = (d_inner * gate * sig).astype(BF)
@@ -1017,15 +1077,15 @@
         return [lax.all_gather(half, BOTH, axis=0, tiled=True) for half in halves]
 
     def with_gains(w_attn, w_mlp):
-        gains = w_attn[:, split + width :].astype(F32).T
-        return (gains[0:1], gains[1:2], w_attn, w_mlp, width, split, units)
+        return (w_attn[:, split + width :].astype(F32).T, w_attn, w_mlp, width, split, units)
 
     (attn_zero, attn_one), (mlp_zero, mlp_one) = halves
     attn_zero = jnp.concatenate([attn_zero, attn_one[:, split + width : split + width + 1]], 1)
     attn_zero, mlp_zero = gathered((attn_zero, mlp_zero))
+    cot = lax.dynamic_index_in_dim(cotangent, sec, 0, keepdims=False)
+    attn_zero, cot = lax.optimization_barrier((attn_zero, cot))
     zero = with_gains(attn_zero, mlp_zero)
     attn_one, mlp_one = gathered((attn_one, mlp_one))
-    one_gain = attn_zero[:, split + width + 2 :].astype(F32).T
 
     seg_count = parent.shape[0]
     labels = jnp.arange(seg_count, dtype=jnp.int32)
@@ -1052,47 +1112,47 @@
     wide, narrow = (F32, BF), (BF, BF)
     back = (F32, BF, F32)
 
-    normed_zero = (hidden * lax.rsqrt(jnp.mean(hidden * hidden, -1, keepdims=True) + EPSILON) * zero[0]).astype(BF)
+    normed_zero = (hidden * lax.rsqrt(jnp.mean(hidden * hidden, -1, keepdims=True) + EPSILON) * zero[0][:1]).astype(BF)
     kept_zero, o_zero = layer_attention(normed_zero, zero, tables)
     middle_zero, r_zero = product_sum(
-        (o_zero, tree, zero[1]), ((0,), split_out, ("add", (1, 2)), wide), zero[2], stagger=True, key=1
+        (o_zero, tree, zero[0]), ((0,), split_out, ("add", (1, (2, 1))), wide), zero[1], stagger=True, key=1
     )
     gate_zero, up_zero, inner_zero = layer_units(r_zero, zero)
     out_zero, normed_one = product_sum(
-        (inner_zero, middle_zero, one_gain), ((0,), split_down, ("add", (1, 2)), narrow), zero[3], key=5
+        (inner_zero, middle_zero, zero[0]), ((0,), split_down, ("add", (1, (2, 2))), narrow), zero[2], key=5
     )
 
     out_zero, normed_one, attn_one = lax.optimization_barrier((out_zero, normed_one, attn_one))
     one = with_gains(attn_one, mlp_one)
     kept_one, o_one = layer_attention(normed_one, one, tables)
     middle_one, r_one = product_sum(
-        (o_one, out_zero, one[1]), ((0,), split_out, ("add", (1, 2)), wide), one[2], key=2
+        (o_one, out_zero, one[0]), ((0,), split_out, ("add", (1, (2, 1))), wide), one[1], key=2
     )
     gate_one, up_one, inner_one = layer_units(r_one, one)
-    branch = lax.dynamic_index_in_dim(cotangent, sec, 0, keepdims=False)
+    branch = cot
     d_gate, d_up = units_backward(branch, one, gate_one, up_one)
     out_one, d_mlp_one = product_sum(
         (inner_one, middle_one, r_one, branch, d_gate, d_up), ((0,), split_down, ("add", (1,)), (BF,)),
-        one[3], ((2, (4, 5)), (3, (0,))), key=6,
+        one[2], ((2, (4, 5)), (3, (0,))), key=6,
     )
     d_gate, out_one = lax.optimization_barrier((d_gate, out_one))
     grad_middle, grad_attn, d_gain_mlp_one = product_sum(
-        (d_gate, d_up, middle_one, branch, one[1]), ((0, 1), 0, ("back", (2, 3, 4)), back), one[3], key=8
+        (d_gate, d_up, middle_one, branch, one[0]), ((0, 1), 0, ("back", (2, 3, (4, 1))), back), one[2], key=8
     )
     g_mlp_one = reduce_gradient(d_mlp_one)
     dq, dkv = attention_backward(grad_attn, one, tables, kept_one)
     grad_one, branch, d_gain_attn_one, d_attn_one = product_sum(
         (dq, dkv, out_zero, grad_middle, one[0], normed_one, grad_attn, o_one),
-        ((0, 1), 0, ("back", (2, 3, 4)), back),
-        one[2], ((5, (0, 1)), (6, (7,))), key=7,
+        ((0, 1), 0, ("back", (2, 3, (4, 0))), back),
+        one[1], ((5, (0, 1)), (6, (7,))), stagger=True, key=7,
     )
     g_attn_one = reduce_gradient(d_attn_one)
 
     d_gate, d_up = units_backward(branch, zero, gate_zero, up_zero)
     grad_middle, grad_attn, d_gain_mlp_zero, d_mlp_zero = product_sum(
-        (d_gate, d_up, inner_zero, middle_zero, branch, r_zero, zero[1]),
-        ((0, 1), 0, ("back", (3, 4, 6)), back),
-        zero[3], ((5, (0, 1)), (4, (2,))), key=9,
+        (d_gate, d_up, inner_zero, middle_zero, branch, r_zero, zero[0]),
+        ((0, 1), 0, ("back", (3, 4, (6, 1))), back),
+        zero[2], ((5, (0, 1)), (4, (2,))), key=9,
     )
     g_mlp_zero = reduce_gradient(d_mlp_zero)
     grad_attn, g_mlp_one = lax.optimization_barrier((grad_attn, g_mlp_one))
@@ -1100,8 +1160,8 @@
     dq, g_attn_one = lax.optimization_barrier((dq, g_attn_one))
     grad_zero, send_zero, d_gain_attn_zero, d_attn_zero = product_sum(
         (dq, dkv, tree, grad_middle, zero[0], normed_zero, grad_attn, o_zero),
-        ((0, 1), 0, ("back", (2, 3, 4)), back),
-        zero[2], ((5, (0, 1)), (6, (7,))), key=11,
+        ((0, 1), 0, ("back", (2, 3, (4, 0))), back),
+        zero[1], ((5, (0, 1)), (6, (7,))), key=11,
     )
     d_gain_attn_zero, d_gain_mlp_zero, d_gain_attn_one, d_gain_mlp_one = [
         jnp.sum(x, 0) for x in (d_gain_attn_zero, d_gain_mlp_zero, d_gain_attn_one, d_gain_mlp_one)
@@ -1112,12 +1172,15 @@
     ending = finish if devices == 4 else finish_apart
     g_attn_zero, g_gain, got_out, got_in, got_mlp, got_attn = ending(
         d_attn_zero, d_gains, out_zero, out_one, send_zero, branch,
-        g_mlp_zero, g_mlp_one, g_attn_one,
+        g_mlp_one, g_attn_one,
     )
 
     layer_output, input_grad, *grads = write_results(
-        (out_zero, out_one, got_out), (grad_zero, grad_one, got_in), (g_mlp_zero, g_mlp_one, got_mlp),
-        (g_attn_zero, g_attn_one, got_attn), width, span, units,
+        (out_zero, out_one, got_out), (grad_zero, grad_one, got_in), (g_attn_zero, g_attn_one, got_attn), width, span
+    )
+    input_grad, g_mlp_zero = lax.optimization_barrier((input_grad, g_mlp_zero))
+    grads += write_mlp(
+        g_mlp_zero, g_mlp_one, lax.ppermute(g_mlp_zero, "section", [(1, 0)]), got_mlp, units
     )
     g_query, g_key, g_value, g_out, g_gate, g_up, g_down = [grad[None] for grad in grads]
     g_gain = g_gain.reshape(2, 1, -1)

time: 1180 us -> 871 us (0.74)
  Pallas kernels: 983 us -> 684 us
    pallas_call x1, Pallas kernels: 319 us -> 9.16 us  [write_results(): pl.pallas_call(functools.partial(write_kernel, width + 2 * span), out_sha...]
    unnamed x110 -> x118, local copies, waits for them, and re-layouts: 30.2 us -> 33.9 us
  transfers between devices with their start and end apart: 9 -> 10, of which waited for: 4 -> 4; matrix products, arithmetic and copies ran while one was open for 7% -> 9% of each run, Pallas kernels for 49% -> 71%
where the time goes in v4:
time: 871 us; the launch traced here: 866 us
  Pallas kernels  684 us (79%)
  matrix products  69 us (8%)
  local copies, waits for them, and re-layouts  42.5 us (5%)
  waiting for transfers between devices  27.5 us (3%)
  other arithmetic  24.2 us (3%)
  between operations  15.4 us (2%)
    pallas_call x8, Pallas kernels, product_sum(): pl.pallas_call(functools.partial(product_sum_kernel, (len(arrays), job, t...  514 us
    pallas_call x2, Pallas kernels, attend_back(): pl.pallas_call(functools.partial(attend_back_kernel, rows, step), out_sha...  45.8 us
    dot_general x6, matrix products, dot_f32(): lax.dot_general(a, b, (((ca,), (cb,)), ((), ())), preferred_element_type=...  37.2 us
    unnamed x118, local copies, waits for them, and re-layouts  33.9 us
    pallas_call x2, Pallas kernels, gather_rows(): pl.pallas_call(functools.partial(gather_kernel, count), out_shape=(jax.Sh...  32.9 us
    pallas_call x2, Pallas kernels, attend(): pl.pallas_call(functools.partial(attend_kernel, rows, step), out_shape=(j...  31.2 us
    pallas_call x1, Pallas kernels, finish(): pl.pallas_call(finish_kernel, out_shape=(jax.ShapeDtypeStruct((rows, widt...  27.5 us
    dot_general x2, matrix products, layer_units(): jnp.dot(normed, weights[2][:, :2 * units], preferred_element_type=F32)  24 us
  transfers between devices with their start and end apart: 10, of which 4 were waited for; matrix products, arithmetic and copies ran while one was open for 9% of the time, Pallas kernels for 71%

profile of v4, /device:TPU:1, one launch (start us, length us, event | category | flops | bytes accessed | tf_op | source)
XLA Modules:
  0.0 865.7 jit_solution(3001549547503367251)
XLA Ops:
  21.6 3.0 convert_bitcast_fusion.1
  25.4 4.1 collective-permute-done.1
  34.0 3.9 fusion.8
  44.9 18.2 %all-gather.5.cloned.1.call-done.refs_3_.refs_8_ = bf16[2048,1155]{1,0:T(8,128)(2,1)} async-done(((bf16[256,1155]{1,0:T(8,128)(2,1)}), bf16[2048,1155]{1,0:T(8,128)(2,1)}) %all-gather.5.cloned.1.call-update) | async-done | bytes 4730896 | tf_op jit(solution)/shard_map/all_gather | solution.py:1077
  70.2 16.5 %gather_rows.2 = (bf16[4,640,128]{2,1,0:T(8,128)(2,1)}, bf16[128,2560]{1,0:T(8,128)(2,1)}) custom-call(f32[640,128]{1,0:T(8,128)} %fusion.30.raw_ref, f32[640,128]{1,0:T(8,128)} %maximum_maximum_fusion.cos_ref, f32[640,128]{1,0:T(8,128)} %get-tuple-element.196.sin_ref), custom_call_target="tpu_custom_call" | custom-call | flops 1 | bytes 1 | tf_op jit(solution)/shard_map/gather_rows/pallas_call | solution.py:418
  86.7 4.3 fusion.17.q_ref
  91.1 15.6 %attend.2 = (bf16[512,640]{1,0:T(8,128)(2,1)S(1)}, bf16[640,512]{1,0:T(8,128)(2,1)S(1)}, f32[4,5,1,256]{3,2,1,0:T(1,128)S(1)}) custom-call(s32[1]{0:T(128)} %bitcast.start_ref, f32[512,640]{1,0:T(8,128)S(1)} %fusion.17.q_ref, bf16[2560,128]{1,0:T(8,128)(2,1)S(1)} %bitcast.70, bf16[128,2560]{1,0:T(8,128)(2,1)S(1)} %copy-done.14, ...), custom_call_target="tpu_custom_call" | custom-call | flops 1 | bytes 1 | tf_op jit(solution)/shard_map/attend/pallas_call | solution.py:935
  111.6 78.3 %product_sum_1.1 = (f32[640,2048]{1,0:T(8,128)}, bf16[640,2048]{1,0:T(8,128)(2,1)}) custom-call(bf16[640,512]{1,0:T(8,128)(2,1)} %copy-done.10, bf16[640,2048]{1,0:T(8,128)(2,1)} %get-tuple-element.199.refs_1_.refs_2_, f32[3,2048]{1,0:T(4,128)} %copy.101.refs_2_.refs_6_.refs_4_, bf16[2048,1155]{1,0:T(8,128)(2,1)} %all-gather.5.cloned.1.call-done.refs_3_.refs_8_), custom_call_target="tpu_custom_call" | custom-call | flops 1 | bytes 1 | tf_op jit(solution)/shard_map/product_sum_1/pallas_call | solution.py:341
  189.9 12.0 %fusion.2 = f32[640,2816]{1,0:T(8,128)S(1)} fusion(bf16[640,2048]{1,0:T(8,128)(2,1)} %get-tuple-element.80.refs_5_, bf16[2048,4224]{1,0:T(8,128)(2,1)} %all-gather.7.cloned.1.call-done.refs_3_.refs_7_), kind=kOutput, calls=%fused_computation.2 | convolution fusion | flops 7381975040 | bytes 21364736 | tf_op jit(solution)/shard_map/dot_general | solution.py:1025
  205.4 51.2 %product_sum_5.1 = (bf16[640,2048]{1,0:T(8,128)(2,1)}, bf16[640,2048]{1,0:T(8,128)(2,1)}) custom-call(bf16[640,1408]{1,0:T(8,128)(2,1)} %multiply_convert_fusion.5.refs_0_.refs_2_, f32[640,2048]{1,0:T(8,128)} %get-tuple-element.81.refs_1_.refs_3_, f32[3,2048]{1,0:T(4,128)} %copy.101.refs_2_.refs_6_.refs_4_, ...), custom_call_target="tpu_custom_call" | custom-call | flops 1 | bytes 1 | tf_op jit(solution)/shard_map/product_sum_5/pallas_call | solution.py:341
  256.7 3.4 fusion.28.raw_ref
  260.1 16.4 %gather_rows.3 = (bf16[4,640,128]{2,1,0:T(8,128)(2,1)}, bf16[128,2560]{1,0:T(8,128)(2,1)}) custom-call(f32[640,128]{1,0:T(8,128)} %fusion.28.raw_ref, f32[640,128]{1,0:T(8,128)} %maximum_maximum_fusion.cos_ref, f32[640,128]{1,0:T(8,128)} %get-tuple-element.196.sin_ref), custom_call_target="tpu_custom_call" | custom-call | flops 1 | bytes 1 | tf_op jit(solution)/shard_map/gather_rows/pallas_call | solution.py:418
  276.5 4.4 fusion.15.q_ref
  280.9 15.6 %attend.3 = (bf16[512,640]{1,0:T(8,128)(2,1)S(1)}, bf16[640,512]{1,0:T(8,128)(2,1)S(1)}, f32[4,5,1,256]{3,2,1,0:T(1,128)S(1)}) custom-call(s32[1]{0:T(128)} %bitcast.start_ref, f32[512,640]{1,0:T(8,128)S(1)} %fusion.15.q_ref, bf16[2560,128]{1,0:T(8,128)(2,1)S(1)} %bitcast.72, bf16[128,2560]{1,0:T(8,128)(2,1)S(1)} %copy-done.17, ...), custom_call_target="tpu_custom_call" | custom-call | flops 1 | bytes 1 | tf_op jit(solution)/shard_map/attend/pallas_call | solution.py:935
  300.3 47.0 %product_sum_2.1 = (f32[640,2048]{1,0:T(8,128)}, bf16[640,2048]{1,0:T(8,128)(2,1)}) custom-call(bf16[640,512]{1,0:T(8,128)(2,1)} %copy-done.11, bf16[640,2048]{1,0:T(8,128)(2,1)} %get-tuple-element.84.refs_1_.refs_2_.out_zero, f32[2,2048]{1,0:T(2,128)} %copy.104.refs_2_.refs_4_, bf16[2048,1154]{1,0:T(8,128)(2,1)} %all-gather.9.cloned.1.call-done.refs_3_.refs_8_), custom_call_target="tpu_custom_call" | custom-call | flops 1 | bytes 1 | tf_op jit(solution)/shard_map/product_sum_2/pallas_call | solution.py:341
  347.3 12.1 %fusion = f32[640,2816]{1,0:T(8,128)S(1)} fusion(bf16[640,2048]{1,0:T(8,128)(2,1)} %get-tuple-element.91.refs_2_, bf16[2048,4224]{1,0:T(8,128)(2,1)} %all-gather.11.cloned.1.call-done.refs_6_.refs_5_), kind=kOutput, calls=%fused_computation | convolution fusion | flops 7381975040 | bytes 21364736 | tf_op jit(solution)/shard_map/dot_general | solution.py:1025
  359.4 9.7 %multiply_convert_fusion.2 = (bf16[640,1408]{1,0:T(8,128)(2,1)}, bf16[640,1408]{1,0:T(8,128)(2,1)}, bf16[640,1408]{1,0:T(8,128)(2,1)}) fusion(f32[640,2816]{1,0:T(8,128)S(1)} %fusion, bf16[640,2048]{1,0:T(8,128)(2,1)S(1)} %copy-done.42, bf16[2048,4224]{1,0:T(8,128)(2,1)} %all-gather.11.cloned.1.call-done.refs_6_.refs_5_), kind=kOutput, calls=%fused_computation.17 | convolution fusion | flops 3705405440 | bytes 21004288 | tf_op jit(solution)/shard_map/dot_general | solution.py:24
  369.1 65.6 %product_sum_6.1 = (bf16[640,2048]{1,0:T(8,128)(2,1)}, bf16[2048,4224]{1,0:T(8,128)(2,1)}) custom-call(bf16[640,1408]{1,0:T(8,128)(2,1)} %get-tuple-element.204.refs_0_, f32[640,2048]{1,0:T(8,128)} %get-tuple-element.92.refs_1_.refs_2_, bf16[640,2048]{1,0:T(8,128)(2,1)} %get-tuple-element.91.refs_2_, bf16[640,2048]{1,0:T(8,128)(2,1)} %dynamic-slice_bitcast_fusion.1.refs_3_, ...), custom_call_target="tpu_custom_call" | custom-call | flops 1 | bytes 1 | tf_op jit(solution)/shard_map/product_sum_6/pallas_call | solution.py:341
  434.8 58.2 %product_sum_8.1 = (f32[640,2048]{1,0:T(8,128)}, bf16[640,2048]{1,0:T(8,128)(2,1)}, f32[8,2048]{1,0:T(8,128)}) custom-call(bf16[640,1408]{1,0:T(8,128)(2,1)} %get-tuple-element.95.refs_4_.refs_0_, bf16[640,1408]{1,0:T(8,128)(2,1)} %get-tuple-element.202.refs_5_.refs_1_, f32[640,2048]{1,0:T(8,128)} %get-tuple-element.92.refs_1_.refs_2_, ...), custom_call_target="tpu_custom_call" | custom-call | flops 1 | bytes 1 | tf_op jit(solution)/shard_map/product_sum_8/pallas_call | solution.py:341
  493.0 4.6 fusion.22.do_ref
  497.6 22.8 %attend_back.2 = (bf16[640,512]{1,0:T(8,128)(2,1)S(1)}, bf16[2560,128]{1,0:T(8,128)(2,1)S(1)}) custom-call(s32[1]{0:T(128)} %bitcast.start_ref, f32[512,640]{1,0:T(8,128)S(1)} %fusion.15.q_ref, bf16[512,640]{1,0:T(8,128)(2,1)S(1)} %fusion.22.do_ref, bf16[512,640]{1,0:T(8,128)(2,1)S(1)} %copy-done.38, f32[4,5,1,256]{3,2,1,0:T(1,128)S(1)} %get-tuple-element.98.lse_ref, ...), custom_call_target="tpu_custom_call" | custom-call | flops 1 | bytes 1 | tf_op jit(solution)/shard_map/attend_back/pallas_call | solution.py:971
  522.2 8.9 %scatter_rows.2.refs_1_ = bf16[640,128]{1,0:T(8,128)(2,1)} custom-call(bf16[4,640,128]{2,1,0:T(8,128)(2,1)} %bitcast.75, f32[640,128]{1,0:T(8,128)} %maximum_maximum_fusion.cos_ref, f32[640,128]{1,0:T(8,128)} %get-tuple-element.197.sin_ref), custom_call_target="tpu_custom_call" | custom-call | flops 1 | bytes 1 | tf_op jit(solution)/shard_map/scatter_rows/pallas_call | solution.py:439
  531.1 76.2 %product_sum_7.1 = (f32[640,2048]{1,0:T(8,128)}, bf16[640,2048]{1,0:T(8,128)(2,1)}, f32[8,2048]{1,0:T(8,128)}, bf16[2048,1152]{1,0:T(8,128)(2,1)}) custom-call(bf16[640,512]{1,0:T(8,128)(2,1)} %copy-done.34, bf16[640,128]{1,0:T(8,128)(2,1)} %scatter_rows.2.refs_1_, bf16[640,2048]{1,0:T(8,128)(2,1)} %get-tuple-element.84.refs_1_.refs_2_.out_zero, ...), custom_call_target="tpu_custom_call" | custom-call | flops 1 | bytes 1 | tf_op jit(solution)/shard_map/product_sum_7/pallas_call | solution.py:341
  609.1 10.7 %multiply_convert_fusion = (bf16[640,1408]{1,0:T(8,128)(2,1)}, bf16[640,1408]{1,0:T(8,128)(2,1)}) fusion(f32[640,2816]{1,0:T(8,128)} %copy-done.46, bf16[640,2048]{1,0:T(8,128)(2,1)S(1)} %copy-done.43, bf16[2048,4224]{1,0:T(8,128)(2,1)} %all-gather.7.cloned.1.call-done.refs_3_.refs_7_), kind=kOutput, calls=%fused_computation.15 | convolution fusion | flops 3702702080 | bytes 19202048 | tf_op jit(solution)/shard_map/dot_general | solution.py:24
  619.7 72.8 %product_sum_9.1 = (f32[640,2048]{1,0:T(8,128)}, bf16[640,2048]{1,0:T(8,128)(2,1)}, f32[8,2048]{1,0:T(8,128)}, bf16[2048,4224]{1,0:T(8,128)(2,1)}) custom-call(bf16[640,1408]{1,0:T(8,128)(2,1)} %get-tuple-element.201.refs_0_, bf16[640,1408]{1,0:T(8,128)(2,1)} %get-tuple-element.200.refs_1_, bf16[640,1408]{1,0:T(8,128)(2,1)} %multiply_convert_fusion.5.refs_0_.refs_2_, ...), custom_call_target="tpu_custom_call" | custom-call | flops 1 | bytes 1 | tf_op jit(solution)/shard_map/product_sum_9/pallas_call | solution.py:341
  694.5 3.6 fusion.19.do_ref
  698.1 22.9 %attend_back.3 = (bf16[640,512]{1,0:T(8,128)(2,1)S(1)}, bf16[2560,128]{1,0:T(8,128)(2,1)S(1)}) custom-call(s32[1]{0:T(128)} %bitcast.start_ref, f32[512,640]{1,0:T(8,128)S(1)} %copy-done.9, bf16[512,640]{1,0:T(8,128)(2,1)S(1)} %fusion.19.do_ref, bf16[512,640]{1,0:T(8,128)(2,1)S(1)} %copy-done.36, f32[4,5,1,256]{3,2,1,0:T(1,128)S(1)} %get-tuple-element.107.lse_ref, ...), custom_call_target="tpu_custom_call" | custom-call | flops 1 | bytes 1 | tf_op jit(solution)/shard_map/attend_back/pallas_call | solution.py:971
  722.7 10.1 %scatter_rows.3.refs_1_ = bf16[640,128]{1,0:T(8,128)(2,1)} custom-call(bf16[4,640,128]{2,1,0:T(8,128)(2,1)} %bitcast.74, f32[640,128]{1,0:T(8,128)} %maximum_maximum_fusion.cos_ref, f32[640,128]{1,0:T(8,128)} %get-tuple-element.197.sin_ref), custom_call_target="tpu_custom_call" | custom-call | flops 1 | bytes 1 | tf_op jit(solution)/shard_map/scatter_rows/pallas_call | solution.py:439
  732.9 64.7 %product_sum_11.1 = (f32[640,2048]{1,0:T(8,128)}, bf16[640,2048]{1,0:T(8,128)(2,1)}, f32[8,2048]{1,0:T(8,128)}, bf16[2048,1152]{1,0:T(8,128)(2,1)}) custom-call(bf16[640,512]{1,0:T(8,128)(2,1)} %copy-done.33, bf16[640,128]{1,0:T(8,128)(2,1)} %scatter_rows.3.refs_1_, bf16[640,2048]{1,0:T(8,128)(2,1)} %get-tuple-element.199.refs_1_.refs_2_, ...), custom_call_target="tpu_custom_call" | custom-call | flops 1 | bytes 1 | tf_op jit(solution)/shard_map/product_sum_11/pallas_call | solution.py:341
  802.0 27.5 %finish.1 = (bf16[256,1152]{1,0:T(8,128)(2,1)S(1)}, f32[8,128]{1,0:T(8,128)S(1)}, bf16[640,2048]{1,0:T(8,128)(2,1)S(1)}, bf16[640,2048]{1,0:T(8,128)(2,1)S(1)}, ...) custom-call(bf16[8,256,1152]{2,1,0:T(8,128)(2,1)} %bitcast.79, f32[2,4,8,128]{3,2,1,0:T(8,128)S(1)} %reshape.82.gain_ref, ...), custom_call_target="tpu_custom_call" | custom-call | flops 1 | bytes 1 | tf_op jit(solution)/shard_map/finish/pallas_call | solution.py:573
  830.8 9.2 %write_results.1 = (bf16[2,640,2048]{2,1,0:T(8,128)(2,1)}, f32[2,640,2048]{2,1,0:T(8,128)}, f32[512,512]{1,0:T(8,128)}, f32[512,64]{1,0:T(8,128)S(1)}, f32[512,64]{1,0:T(8,128)S(1)}, /*index=5*/f32[512,512]{1,0:T(8,128)}) custom-call(bf16[640,2048]{1,0:T(8,128)(2,1)S(1)} %copy-done.4, bf16[640,2048]{1,0:T(8,128)(2,1)S(1)} %copy-done.5, ...), custom_call_target="tpu_custom_call" | custom-call | flops 1 | bytes 1 | tf_op jit(solution)/shard_map/write_results/pallas_call | solution.py:747
  854.2 4.4 write_mlp.1
  (193 shorter events, 72.6 us)
Async XLA Ops:
  7.2 26.8 %copy-start = (s32[2,13]{1,0:T(2,128)S(1)}, s32[2,13]{1,0:T(2,128)}, u32[]{:S(2)}) copy-start(s32[2,13]{1,0:T(2,128)} %param.18) | copy-start | bytes 316
  7.2 56.0 %all-gather.5.cloned.1.call-start = ((), (), s32[]{:S(2)}) async-start(), calls=%async_computation.3 | async-start | bytes 5898240 | tf_op jit(solution)/shard_map/all_gather | solution.py:1077
  15.8 2.1 collective-permute-start
  18.3 6.3 copy-start.47
  19.4 170.5 %all-gather.7.cloned.1.call-start = ((), (), s32[]{:S(2)}) async-start(), calls=%async_computation.4 | async-start | bytes 19464192 | tf_op jit(solution)/shard_map/all_gather | solution.py:1077
  25.2 4.3 collective-permute-start.1
  32.0 224.7 %all-gather.9.cloned.1.call-start = ((), (), s32[]{:S(2)}) async-start(), calls=%async_computation.5 | async-start | bytes 5898240 | tf_op jit(solution)/shard_map/all_gather | solution.py:1077
  32.7 314.6 %all-gather.11.cloned.1.call-start = ((), (), s32[]{:S(2)}) async-start(), calls=%async_computation.6 | async-start | bytes 19464192 | tf_op jit(solution)/shard_map/all_gather | solution.py:1077
  32.8 8.9 %slice-start = ((s8[5242880]{0:T(1024)(128)(4,1)}), s8[1048576]{0:T(1024)(128)(4,1)S(1)}, s32[]{:S(2)}) async-start(s8[5242880]{0:T(1024)(128)(4,1)} %bitcast.81), calls=%async_computation.10 | async-start | bytes 2097152
  33.3 660.3 %reduce-scatter.4.cloned.1.call-start = ((), (), s32[]{:S(2)}) async-start(), calls=%async_computation.7 | async-start | bytes 19464192 | tf_op jit(solution)/shard_map/reduce_scatter | solution.py:1040
  34.0 7.6 slice-start.1
  38.5 52.5 %copy-start.25 = (f32[32,640]{1,0:T(8,128)}, f32[32,640]{1,0:T(8,128)S(1)}, u32[]{:S(2)}) copy-start(f32[32,640]{1,0:T(8,128)S(1)} %get-tuple-element.209.sin_ref) | copy-start | bytes 245764
  38.5 52.5 %copy-start.29 = (f32[32,640]{1,0:T(8,128)}, f32[32,640]{1,0:T(8,128)S(1)}, u32[]{:S(2)}) copy-start(f32[32,640]{1,0:T(8,128)S(1)} %get-tuple-element.210.cos_ref) | copy-start | bytes 245764
  44.9 46.1 %copy-start.2 = (bf16[2560,640]{1,0:T(8,128)(2,1)}, bf16[2560,640]{1,0:T(8,128)(2,1)S(1)}, u32[]{:S(2)}) copy-start(bf16[2560,640]{1,0:T(8,128)(2,1)S(1)} %select_convert_fusion.bias_ref) | copy-start | bytes 9830404
  86.7 4.4 copy-start.12
  86.7 4.4 copy-start.14
  276.5 4.4 copy-start.3
  276.5 4.4 copy-start.16
  276.5 4.4 copy-start.17
  276.5 4.4 copy-start.26
  276.5 4.4 copy-start.30
  347.3 12.1 %copy-start.42 = (bf16[640,2048]{1,0:T(8,128)(2,1)S(1)}, bf16[640,2048]{1,0:T(8,128)(2,1)}, u32[]{:S(2)}) copy-start(bf16[640,2048]{1,0:T(8,128)(2,1)} %dynamic-slice_bitcast_fusion.1.refs_3_) | copy-start | bytes 7864324
  434.7 298.2 %reduce-scatter.6.cloned.1.call-start = ((), (), s32[]{:S(2)}) async-start(), calls=%async_computation.8 | async-start | bytes 5308416 | tf_op jit(solution)/shard_map/reduce_scatter | solution.py:1040
  493.0 4.6 copy-start.18
  493.0 4.6 copy-start.27
  493.0 4.6 copy-start.31
  493.0 4.6 copy-start.38
  607.4 232.7 %reduce-scatter.8.cloned.1.call-start = ((), (), s32[]{:S(2)}) async-start(), calls=%async_computation.9 | async-start | bytes 19464192 | tf_op jit(solution)/shard_map/reduce_scatter | solution.py:1040
  732.9 65.7 %copy-start.19 = (bf16[256,1152]{1,0:T(8,128)(2,1)S(1)}, bf16[256,1152]{1,0:T(8,128)(2,1)}, u32[]{:S(2)}) copy-start(bf16[256,1152]{1,0:T(8,128)(2,1)} %reduce-scatter.6.cloned.1.call-done.attn_one) | copy-start | bytes 1769476
  802.0 28.8 %copy-start.5 = (bf16[640,2048]{1,0:T(8,128)(2,1)S(1)}, bf16[640,2048]{1,0:T(8,128)(2,1)}, u32[]{:S(2)}) copy-start(bf16[640,2048]{1,0:T(8,128)(2,1)} %get-tuple-element.94.out_one) | copy-start | bytes 7864324
  840.0 6.4 collective-permute-start.2
  847.7 10.9 %copy-start.1 = (s32[2,13]{1,0:T(2,128)S(1)}, s32[2,13]{1,0:T(2,128)}, u32[]{:S(2)}) copy-start(s32[2,13]{1,0:T(2,128)} %param.18) | copy-start | bytes 316
  (34 other events, 60.1 us)
Sparse Core Ops, SparseCore 0:
  19.5 43.6 all-gather.4
  65.6 96.5 all-gather.6
  164.1 41.1 all-gather.8
  207.0 99.0 all-gather.10
  434.8 121.8 reduce-scatter.3
  607.5 51.1 reduce-scatter.5
  692.8 117.7 reduce-scatter.7

commit v5 on v4

--- a/solution.py
+++ b/solution.py
@@ -88,11 +88,12 @@
 
 
 def product_sum_kernel(cfg, *refs):
-    n_arrays, job, sides, stagger = cfg
+    n_join, n_arrays, job, sides, stagger = cfg
     xs, first_column = job[:2]
     refs = list(refs)
     take = lambda n: [refs.pop(0) for _ in range(n)]
-    from_hbm = take(n_arrays)
+    joined = take(n_join)
+    from_hbm = [None, *take(n_arrays - 1)]
     (w_hbm,) = take(1)
     outs_hbm = take(len(job[3]))
     (g_hbm,) = take(1) if sides else (None,)
@@ -105,6 +106,8 @@
     blocks = pieces // per_block
     n_rows = p_buf.shape[1]
     early = len(xs)
+    lag = 2
+    assert xs[0] == 0
 
     t = lax.axis_index("tensor")
     sec = lax.axis_index("section")
@@ -136,6 +139,14 @@
     def load(k):
         return pltpu.make_async_copy(from_hbm[k], arrays[k], load_sem.at[k])
 
+    def join():
+        copies, start = [], 0
+        for m, src in enumerate(joined):
+            at = pl.ds(start, src.shape[1])
+            copies.append(pltpu.make_async_copy(src, arrays[0].at[:, at], load_sem.at[n_arrays + m]))
+            start += src.shape[1]
+        return copies
+
     def fetch(j, slot):
         return pltpu.make_async_copy(
             w_hbm.at[columns(j), pl.ds(first_column, w_buf.shape[2])], w_buf.at[slot], w_sem.at[slot]
@@ -151,7 +162,9 @@
 
         lax.fori_loop(0, pieces, turn_of, 0)
 
-    for k in range(early):
+    for copy in join():
+        copy.start()
+    for k in range(1, early):
         load(k).start()
     fetch(0, 0).start()
     for k in range(early, n_arrays):
@@ -178,7 +191,9 @@
         else:
             pl.semaphore_wait(barrier, 1)
 
-    for k in range(early):
+    for copy in join():
+        copy.wait()
+    for k in range(1, early):
         load(k).wait()
 
     def done(i):
@@ -194,6 +209,25 @@
         b_buf[i] = p_buf[i] + b_buf[i]
         to_outer(i).start()
         done(i)
+
+    def side(j):
+        slot = lax.rem(j, 2)
+
+        @pl.when(j >= 2)
+        def _():
+            flush(j - 2, slot).wait()
+
+        start = 0
+        for a, bs in sides:
+            a_t = arrays[a][:, columns(j)].T
+            for b in bs:
+                width = arrays[b].shape[1]
+                g_buf[slot, :, start : start + width] = jnp.dot(
+                    a_t, arrays[b][...], preferred_element_type=F32
+                ).astype(BF)
+                start += width
+        flush(j, slot).start()
+        return 0
 
     def step(j, _):
         slot = lax.rem(j, 2)
@@ -218,11 +252,17 @@
             for u in range(per_block):
                 to_inner(per_block * j + u).start()
 
-        @pl.when(j == 0)
+        @pl.when(j == 1)
         def _():
             for k in range(early, n_arrays):
                 load(k).wait()
             before_sum(job, arrays, keep)
+
+        if sides:
+
+            @pl.when(j >= lag)
+            def _():
+                side(j - lag)
 
         @pl.when(inner)
         def _():
@@ -234,23 +274,6 @@
                 def _():
                     second(i - per_block)
 
-        if sides:
-
-            @pl.when(j >= 2)
-            def _():
-                flush(j - 2, slot).wait()
-
-            start = 0
-            for a, bs in sides:
-                a_t = arrays[a][:, columns(j)].T
-                for b in bs:
-                    width = arrays[b].shape[1]
-                    g_buf[slot, :, start : start + width] = jnp.dot(
-                        a_t, arrays[b][...], preferred_element_type=F32
-                    ).astype(BF)
-                    start += width
-            flush(j, slot).start()
-
         return 0
 
     lax.fori_loop(0, blocks, step, 0)
@@ -260,14 +283,23 @@
         for u in range(per_block):
             second(pieces - per_block + u)
 
-    @pl.when(outer)
-    def _():
-        every_piece(lambda i: to_inner(i).wait_send())
-        if stagger:
+    if stagger:
+
+        @pl.when(outer)
+        def _():
+            every_piece(lambda i: to_inner(i).wait_send())
 
             @pl.when(sec == 0)
             def _():
                 pl.semaphore_signal(turn, inc=1, device_id=mate, device_id_type=MESH)
+
+    if sides:
+        lax.fori_loop(blocks - lag, blocks, lambda j, _: side(j), 0)
+
+    @pl.when(outer)
+    def _():
+        if not stagger:
+            every_piece(lambda i: to_inner(i).wait_send())
 
         def arrive(i):
             to_outer(i).wait_recv()
@@ -319,7 +351,10 @@
 
 def product_sum(arrays, job, weights, sides=(), stagger=False, key=1):
     assert lax.axis_size("tensor") == 4
-    rows, model = arrays[0].shape[0], weights.shape[0]
+    first = arrays[0] if isinstance(arrays[0], tuple) else (arrays[0],)
+    given = (*first, *arrays[1:])
+    rows, model = first[0].shape[0], weights.shape[0]
+    arrays = (jax.ShapeDtypeStruct((rows, sum(x.shape[1] for x in first)), BF), *arrays[1:])
     pieces = model // PIECE
     depth = sum(arrays[x].shape[1] for x in job[0])
     anywhere = pl.BlockSpec(memory_space=pl.ANY)
@@ -331,7 +366,7 @@
         height = 8 if job[2][0] == "back" and m == 2 else rows
         out_shape.append(jax.ShapeDtypeStruct((height, model), dtype))
     scratch = [pltpu.VMEM(x.shape, x.dtype) for x in (*arrays, *out_shape)]
-    scratch += [pltpu.SemaphoreType.DMA((len(arrays),)), pltpu.SemaphoreType.DMA((16,))]
+    scratch += [pltpu.SemaphoreType.DMA((len(arrays) + len(first),)), pltpu.SemaphoreType.DMA((16,))]
     scratch += [pltpu.VMEM((2, BLOCK, depth), BF), buf, buf, buf, two, *[sem] * 6, pltpu.SemaphoreType.REGULAR]
     scratch += [pltpu.VMEM((rows, PIECE), F32)] * 2
     if sides:
@@ -339,9 +374,9 @@
         out_shape.append(jax.ShapeDtypeStruct((model, side_width), BF))
         scratch += [pltpu.VMEM((2, BLOCK, side_width), BF), two]
     out = pl.pallas_call(
-        functools.partial(product_sum_kernel, (len(arrays), job, tuple(sides), stagger)),
+        functools.partial(product_sum_kernel, (len(first), len(arrays), job, tuple(sides), stagger)),
         out_shape=out_shape,
-        in_specs=[anywhere] * (len(arrays) + 1),
+        in_specs=[anywhere] * (len(given) + 1),
         out_specs=[anywhere] * len(out_shape),
         scratch_shapes=scratch,
         compiler_params=pltpu.CompilerParams(
@@ -349,7 +384,7 @@
         ),
         cost_estimate=NO_COST,
         name=f"product_sum_{key}",
-    )(*arrays, weights)
+    )(*given, weights)
     return out if len(out) > 1 else out[0]
 
 
@@ -584,7 +619,7 @@
             dma(8), dma(10), dma(10), dma(4), dma(4), dma(7), dma(7),
         ],
         compiler_params=pltpu.CompilerParams(
-            collective_id=12, has_side_effects=True, vmem_limit_bytes=40 << 20
+            collective_id=12, has_side_effects=True, vmem_limit_bytes=62 << 20
         ),
         cost_estimate=NO_COST,
         name="finish",
@@ -665,7 +700,7 @@
             pltpu.SemaphoreType.DMA((2,)),
             pltpu.SemaphoreType.DMA((3,)),
         ],
-        compiler_params=pltpu.CompilerParams(vmem_limit_bytes=40 << 20),
+        compiler_params=pltpu.CompilerParams(vmem_limit_bytes=62 << 20),
         cost_estimate=NO_COST,
         name="write_mlp",
     )(zero, one, from_one, from_zero)
@@ -762,7 +797,7 @@
             pltpu.SemaphoreType.DMA((6,)),
             pltpu.SemaphoreType.DMA((8,)),
         ],
-        compiler_params=pltpu.CompilerParams(vmem_limit_bytes=40 << 20),
+        compiler_params=pltpu.CompilerParams(vmem_limit_bytes=62 << 20),
         cost_estimate=NO_COST,
         name="write_results",
     )(*results, *ins, *attns)
@@ -810,10 +845,24 @@
     return pl.multiple_of(TRUNK + GROUP * lax.div(past, GROUP), 128)
 
 
-def windows(tree_len, rows, tile, first_row):
+def over_windows(tree_len, rows, tile, first_row, run):
     if tile % 128 == 0 and GROUP % tile == 0 and TRUNK % tile == 0 and rows % tile == 0:
-        return (pl.ds(0, TRUNK), pl.ds(group_start(first_row), GROUP))
-    return (pl.ds(0, tree_len),)
+
+        @pl.when(first_row < TRUNK)
+        def _():
+            run(((pl.ds(0, TRUNK), True),))
+
+        @pl.when(first_row >= TRUNK)
+        def _():
+            run(((pl.ds(0, TRUNK), False), (pl.ds(group_start(first_row), GROUP), True)))
+
+    else:
+        run(((pl.ds(0, tree_len), True),))
+
+
+def masked(scores, bias_ref, win, step):
+    bias = bias_ref[win, :].astype(F32)
+    return scores + (bias if step == 1 else jnp.concatenate([bias] * step, axis=1))
 
 
 def head_rows(ref, head):
@@ -851,20 +900,18 @@
     tile = q_ref.shape[1]
     heads = q_ref.shape[0] // HEAD
     first_row = start_ref[0] + pl.program_id(0) * tile
-    wins = windows(kv_ref.shape[0], rows, tile, first_row)
-
-    def body(group, lanes):
+
+    def body(wins, group, lanes):
         head = group * step
         q = turned_beside(q_ref, cos_ref[...], sin_ref[...], head, step)
         scores = []
-        for win in wins:
-            bias = bias_ref[win, :].astype(F32)
-            bias = bias if step == 1 else jnp.concatenate([bias] * step, axis=1)
-            scores.append(dot_f32(kv_ref[win, :HEAD], q, 1, 0) + bias)
+        for win, mask in wins:
+            score = dot_f32(kv_ref[win, :HEAD], q, 1, 0)
+            scores.append(masked(score, bias_ref, win, step) if mask else score)
         top = functools.reduce(jnp.maximum, [jnp.max(s, 0, keepdims=True) for s in scores])
         expo = [jnp.exp(s - top) for s in scores]
         total = sum(jnp.sum(e, 0, keepdims=True) for e in expo)
-        out = sum(dot_f32(kvt_ref[HEAD:, win], e.astype(BF), 1, 0) for win, e in zip(wins, expo))
+        out = sum(dot_f32(kvt_ref[HEAD:, win], e.astype(BF), 1, 0) for (win, _), e in zip(wins, expo))
         out = out / total
         on_ref[:, lanes] = as_rows(out, tile, step).astype(BF)
         lse_ref[group, 0] = top + jnp.log(total)
@@ -872,7 +919,10 @@
         for k in range(step):
             o_ref[(head + k) * HEAD : (head + k + 1) * HEAD, :] = out[:, k * tile : (k + 1) * tile]
 
-    over_groups(heads // step, step, body)
+    over_windows(
+        kv_ref.shape[0], rows, tile, first_row,
+        lambda wins: over_groups(heads // step, step, functools.partial(body, wins)),
+    )
 
 
 def attend_back_kernel(
@@ -882,14 +932,13 @@
     tile = q_ref.shape[1]
     heads = q_ref.shape[0] // HEAD
     first_row = start_ref[0] + pl.program_id(0) * tile
-    wins = windows(kv_ref.shape[0], rows, tile, first_row)
 
     @pl.when(pl.program_id(0) == 0)
     def _():
         dk_acc[...] = jnp.zeros_like(dk_acc)
         dv_acc[...] = jnp.zeros_like(dv_acc)
 
-    def body(group, lanes):
+    def body(wins, group, lanes):
         head = group * step
         cos, sin = cos_ref[...], sin_ref[...]
         q = turned_beside(q_ref, cos, sin, head, step)
@@ -898,10 +947,9 @@
         lse = lse_ref[group, 0]
         delta = jnp.sum(do.astype(F32) * out.astype(F32), 0, keepdims=True)
         dq = jnp.zeros((HEAD, step * tile), F32)
-        for win in wins:
-            bias = bias_ref[win, :].astype(F32)
-            bias = bias if step == 1 else jnp.concatenate([bias] * step, axis=1)
-            p = jnp.exp(dot_f32(kv_ref[win, :HEAD], q, 1, 0) + bias - lse)
+        for win, mask in wins:
+            score = dot_f32(kv_ref[win, :HEAD], q, 1, 0)
+            p = jnp.exp((masked(score, bias_ref, win, step) if mask else score) - lse)
             dp = dot_f32(kv_ref[win, HEAD:], do, 1, 0)
             ds = (p * (dp - delta)).astype(BF)
             dk_acc[win, :] += dot_f32(ds, q, 1, 1)
@@ -915,7 +963,10 @@
             turned += [first * cos + second * sin, second * cos - first * sin]
         dq_ref[:, lanes] = jnp.concatenate(turned, axis=0).T.astype(BF)
 
-    over_groups(heads // step, step, body)
+    over_windows(
+        kv_ref.shape[0], rows, tile, first_row,
+        lambda wins: over_groups(heads // step, step, functools.partial(body, wins)),
+    )
 
     @pl.when(pl.program_id(0) == pl.num_programs(0) - 1)
     def _():
@@ -956,7 +1007,7 @@
                 pl.BlockSpec((heads // step, 1, 1, step * tile), lambda i, s: (0, i, 0, 0)),
             ),
         ),
-        compiler_params=pltpu.CompilerParams(vmem_limit_bytes=40 << 20),
+        compiler_params=pltpu.CompilerParams(vmem_limit_bytes=62 << 20),
         cost_estimate=NO_COST,
         name="attend",
     )(start, q_t, kv, kv_t, bias_t, cos_t, sin_t)
@@ -994,7 +1045,7 @@
             ),
             scratch_shapes=[pltpu.VMEM((tree_len, HEAD), F32), pltpu.VMEM((tree_len, HEAD), F32)],
         ),
-        compiler_params=pltpu.CompilerParams(vmem_limit_bytes=48 << 20),
+        compiler_params=pltpu.CompilerParams(vmem_limit_bytes=62 << 20),
         cost_estimate=NO_COST,
         name="attend_back",
     )(start, q_t, do_t, o_t, lse, kv, kv_t, bias_t, cos_t, sin_t)
@@ -1137,31 +1188,31 @@
     )
     d_gate, out_one = lax.optimization_barrier((d_gate, out_one))
     grad_middle, grad_attn, d_gain_mlp_one = product_sum(
-        (d_gate, d_up, middle_one, branch, one[0]), ((0, 1), 0, ("back", (2, 3, (4, 1))), back), one[2], key=8
+        ((d_gate, d_up), middle_one, branch, one[0]), ((0,), 0, ("back", (1, 2, (3, 1))), back), one[2], key=8
     )
     g_mlp_one = reduce_gradient(d_mlp_one)
     dq, dkv = attention_backward(grad_attn, one, tables, kept_one)
     grad_one, branch, d_gain_attn_one, d_attn_one = product_sum(
-        (dq, dkv, out_zero, grad_middle, one[0], normed_one, grad_attn, o_one),
-        ((0, 1), 0, ("back", (2, 3, (4, 0))), back),
-        one[1], ((5, (0, 1)), (6, (7,))), stagger=True, key=7,
+        ((dq, dkv), out_zero, grad_middle, one[0], normed_one, grad_attn, o_one),
+        ((0,), 0, ("back", (1, 2, (3, 0))), back),
+        one[1], ((4, (0,)), (5, (6,))), stagger=True, key=7,
     )
     g_attn_one = reduce_gradient(d_attn_one)
 
     d_gate, d_up = units_backward(branch, zero, gate_zero, up_zero)
     grad_middle, grad_attn, d_gain_mlp_zero, d_mlp_zero = product_sum(
-        (d_gate, d_up, inner_zero, middle_zero, branch, r_zero, zero[0]),
-        ((0, 1), 0, ("back", (3, 4, (6, 1))), back),
-        zero[2], ((5, (0, 1)), (4, (2,))), key=9,
+        ((d_gate, d_up), inner_zero, middle_zero, branch, r_zero, zero[0]),
+        ((0,), 0, ("back", (2, 3, (5, 1))), back),
+        zero[2], ((4, (0,)), (3, (1,))), key=9,
     )
     g_mlp_zero = reduce_gradient(d_mlp_zero)
     grad_attn, g_mlp_one = lax.optimization_barrier((grad_attn, g_mlp_one))
     dq, dkv = attention_backward(grad_attn, zero, tables, kept_zero)
     dq, g_attn_one = lax.optimization_barrier((dq, g_attn_one))
     grad_zero, send_zero, d_gain_attn_zero, d_attn_zero = product_sum(
-        (dq, dkv, tree, grad_middle, zero[0], normed_zero, grad_attn, o_zero),
-        ((0, 1), 0, ("back", (2, 3, (4, 0))), back),
-        zero[1], ((5, (0, 1)), (6, (7,))), key=11,
+        ((dq, dkv), tree, grad_middle, zero[0], normed_zero, grad_attn, o_zero),
+        ((0,), 0, ("back", (1, 2, (3, 0))), back),
+        zero[1], ((4, (0,)), (5, (6,))), key=11,
     )
     d_gain_attn_zero, d_gain_mlp_zero, d_gain_attn_one, d_gain_mlp_one = [
         jnp.sum(x, 0) for x in (d_gain_attn_zero, d_gain_mlp_zero, d_gain_attn_one, d_gain_mlp_one)

time: 871 us -> 868 us (level)
  local copies, waits for them, and re-layouts: 42.5 us -> 25.3 us
  Pallas kernels: 684 us -> 695 us
    pallas_call x2, Pallas kernels: 19 us -> 41.6 us  [scatter_rows(): pl.pallas_call(functools.partial(scatter_kernel, count), out_shape=jax.Sh...]
    unnamed x118 -> x42, local copies, waits for them, and re-layouts: 33.9 us -> 15.4 us
    pallas_call x8, Pallas kernels: 514 us -> 502 us  [product_sum(): pl.pallas_call(functools.partial(product_sum_kernel, (len(first), len(arr...]
    pallas_call x2, Pallas kernels: 45.8 us -> 35.6 us  [attend_back(): pl.pallas_call(functools.partial(attend_back_kernel, rows, step), out_sha...]
  transfers between devices with their start and end apart: 10 -> 10, of which waited for: 4 -> 3; matrix products, arithmetic and copies ran while one was open for 9% -> 10% of each run, Pallas kernels for 71% -> 73%
where the time goes in v5:
time: 868 us; the launch traced here: 860 us
  Pallas kernels  695 us (80%)
  matrix products  74.1 us (9%)
  local copies, waits for them, and re-layouts  25.3 us (3%)
  other arithmetic  23.3 us (3%)
  waiting for transfers between devices  22.7 us (3%)
  between operations  15.2 us (2%)
    pallas_call x8, Pallas kernels, product_sum(): pl.pallas_call(functools.partial(product_sum_kernel, (len(first), len(arr...  502 us
    pallas_call x2, Pallas kernels, scatter_rows(): pl.pallas_call(functools.partial(scatter_kernel, count), out_shape=jax.Sh...  41.6 us
    dot_general x6, matrix products, dot_f32(): lax.dot_general(a, b, (((ca,), (cb,)), ((), ())), preferred_element_type=...  39.9 us
    pallas_call x2, Pallas kernels, attend_back(): pl.pallas_call(functools.partial(attend_back_kernel, rows, step), out_sha...  35.6 us
    pallas_call x2, Pallas kernels, attend(): pl.pallas_call(functools.partial(attend_kernel, rows, step), out_shape=(j...  34.5 us
    pallas_call x2, Pallas kernels, gather_rows(): pl.pallas_call(functools.partial(gather_kernel, count), out_shape=(jax.Sh...  33 us
    pallas_call x1, Pallas kernels, finish(): pl.pallas_call(finish_kernel, out_shape=(jax.ShapeDtypeStruct((rows, widt...  31.8 us
    dot_general x2, matrix products, layer_units(): jnp.dot(normed, weights[2][:, :2 * units], preferred_element_type=F32)  24.2 us
  transfers between devices with their start and end apart: 10, of which 3 were waited for; matrix products, arithmetic and copies ran while one was open for 10% of the time, Pallas kernels for 73%

profile of v5, /device:TPU:1, one launch (start us, length us, event | category | flops | bytes accessed | tf_op | source)
XLA Modules:
  0.0 860.0 jit_solution(13399824163233670036)
XLA Ops:
  25.3 4.1 collective-permute-done.1
  40.7 3.6 dynamic-slice_bitcast_fusion.1.refs_3_
  44.3 3.6 select_convert_fusion.bias_ref
  47.9 15.2 %all-gather.5.cloned.1.call-done.refs_3_.refs_8_ = bf16[2048,1155]{1,0:T(8,128)(2,1)} async-done(((bf16[256,1155]{1,0:T(8,128)(2,1)}), bf16[2048,1155]{1,0:T(8,128)(2,1)}) %all-gather.5.cloned.1.call-update) | async-done | bytes 4730896 | tf_op jit(solution)/shard_map/all_gather | solution.py:1128
  70.0 16.5 %gather_rows.2 = (bf16[4,640,128]{2,1,0:T(8,128)(2,1)}, bf16[128,2560]{1,0:T(8,128)(2,1)}) custom-call(f32[640,128]{1,0:T(8,128)} %fusion.30.raw_ref, f32[640,128]{1,0:T(8,128)} %maximum_maximum_fusion.cos_ref, f32[640,128]{1,0:T(8,128)} %get-tuple-element.196.sin_ref), custom_call_target="tpu_custom_call" | custom-call | flops 1 | bytes 1 | tf_op jit(solution)/shard_map/gather_rows/pallas_call | solution.py:453
  86.5 5.3 fusion.17.q_ref
  91.8 17.2 %attend.2 = (bf16[512,640]{1,0:T(8,128)(2,1)}, bf16[640,512]{1,0:T(8,128)(2,1)}, f32[4,5,1,256]{3,2,1,0:T(1,128)}) custom-call(s32[1]{0:T(128)} %bitcast.start_ref, f32[512,640]{1,0:T(8,128)} %fusion.17.q_ref, bf16[2560,128]{1,0:T(8,128)(2,1)} %bitcast.72, bf16[128,2560]{1,0:T(8,128)(2,1)} %get-tuple-element.78.kvt_ref, ...), custom_call_target="tpu_custom_call" | custom-call | flops 1 | bytes 1 | tf_op jit(solution)/shard_map/attend/pallas_call | solution.py:986
  109.9 78.6 %product_sum_1.1 = (f32[640,2048]{1,0:T(8,128)}, bf16[640,2048]{1,0:T(8,128)(2,1)}) custom-call(bf16[640,512]{1,0:T(8,128)(2,1)} %get-tuple-element.79.refs_0_.refs_7_, bf16[640,2048]{1,0:T(8,128)(2,1)} %copy-done.2, f32[3,2048]{1,0:T(4,128)} %copy.101.refs_2_.refs_6_.refs_4_, bf16[2048,1155]{1,0:T(8,128)(2,1)} %all-gather.5.cloned.1.call-done.refs_3_.refs_8_), custom_call_target="tpu_custom_call" | custom-call | flops 1 | bytes 1 | tf_op jit(solution)/shard_map/product_sum_1/pallas_call | solution.py:376
  188.5 12.1 %fusion.2 = f32[640,2816]{1,0:T(8,128)S(1)} fusion(bf16[640,2048]{1,0:T(8,128)(2,1)} %get-tuple-element.80.refs_5_, bf16[2048,4224]{1,0:T(8,128)(2,1)} %all-gather.7.cloned.1.call-done.refs_3_.refs_7_), kind=kOutput, calls=%fused_computation.2 | convolution fusion | flops 7381975040 | bytes 21364736 | tf_op jit(solution)/shard_map/dot_general | solution.py:1076
  204.2 52.5 %product_sum_5.1 = (bf16[640,2048]{1,0:T(8,128)(2,1)}, bf16[640,2048]{1,0:T(8,128)(2,1)}) custom-call(bf16[640,1408]{1,0:T(8,128)(2,1)} %multiply_convert_fusion.5.refs_0_.refs_2_, f32[640,2048]{1,0:T(8,128)} %get-tuple-element.81.refs_1_.refs_3_, f32[3,2048]{1,0:T(4,128)} %copy.101.refs_2_.refs_6_.refs_4_, ...), custom_call_target="tpu_custom_call" | custom-call | flops 1 | bytes 1 | tf_op jit(solution)/shard_map/product_sum_5/pallas_call | solution.py:376
  260.4 16.5 %gather_rows.3 = (bf16[4,640,128]{2,1,0:T(8,128)(2,1)}, bf16[128,2560]{1,0:T(8,128)(2,1)}) custom-call(f32[640,128]{1,0:T(8,128)} %fusion.28.raw_ref, f32[640,128]{1,0:T(8,128)} %maximum_maximum_fusion.cos_ref, f32[640,128]{1,0:T(8,128)} %get-tuple-element.196.sin_ref), custom_call_target="tpu_custom_call" | custom-call | flops 1 | bytes 1 | tf_op jit(solution)/shard_map/gather_rows/pallas_call | solution.py:453
  276.9 4.6 fusion.15.q_ref
  281.4 17.3 %attend.3 = (bf16[512,640]{1,0:T(8,128)(2,1)}, bf16[640,512]{1,0:T(8,128)(2,1)}, f32[4,5,1,256]{3,2,1,0:T(1,128)}) custom-call(s32[1]{0:T(128)} %bitcast.start_ref, f32[512,640]{1,0:T(8,128)} %fusion.15.q_ref, bf16[2560,128]{1,0:T(8,128)(2,1)} %bitcast.74, bf16[128,2560]{1,0:T(8,128)(2,1)} %get-tuple-element.89.kvt_ref, ...), custom_call_target="tpu_custom_call" | custom-call | flops 1 | bytes 1 | tf_op jit(solution)/shard_map/attend/pallas_call | solution.py:986
  300.8 48.0 %product_sum_2.1 = (f32[640,2048]{1,0:T(8,128)}, bf16[640,2048]{1,0:T(8,128)(2,1)}) custom-call(bf16[640,512]{1,0:T(8,128)(2,1)} %get-tuple-element.90.refs_0_.refs_7_, bf16[640,2048]{1,0:T(8,128)(2,1)} %get-tuple-element.84.refs_1_.refs_2_.out_zero, f32[2,2048]{1,0:T(2,128)} %copy.104.refs_2_.refs_4_, ...), custom_call_target="tpu_custom_call" | custom-call | flops 1 | bytes 1 | tf_op jit(solution)/shard_map/product_sum_2/pallas_call | solution.py:376
  348.8 12.1 %fusion = f32[640,2816]{1,0:T(8,128)S(1)} fusion(bf16[640,2048]{1,0:T(8,128)(2,1)} %get-tuple-element.91.refs_2_, bf16[2048,4224]{1,0:T(8,128)(2,1)} %all-gather.11.cloned.1.call-done.refs_6_.refs_5_), kind=kOutput, calls=%fused_computation | convolution fusion | flops 7381975040 | bytes 21364736 | tf_op jit(solution)/shard_map/dot_general | solution.py:1076
  360.9 9.8 %multiply_convert_fusion.2 = (bf16[640,1408]{1,0:T(8,128)(2,1)}, bf16[640,1408]{1,0:T(8,128)(2,1)}, bf16[640,1408]{1,0:T(8,128)(2,1)}) fusion(f32[640,2816]{1,0:T(8,128)S(1)} %fusion, bf16[640,2048]{1,0:T(8,128)(2,1)S(1)} %copy-done.3, bf16[2048,4224]{1,0:T(8,128)(2,1)} %all-gather.11.cloned.1.call-done.refs_6_.refs_5_), kind=kOutput, calls=%fused_computation.17 | convolution fusion | flops 3705405440 | bytes 21004288 | tf_op jit(solution)/shard_map/dot_general | solution.py:24
  370.7 61.9 %product_sum_6.1 = (bf16[640,2048]{1,0:T(8,128)(2,1)}, bf16[2048,4224]{1,0:T(8,128)(2,1)}) custom-call(bf16[640,1408]{1,0:T(8,128)(2,1)} %get-tuple-element.204.refs_0_, f32[640,2048]{1,0:T(8,128)} %get-tuple-element.92.refs_1_.refs_2_, bf16[640,2048]{1,0:T(8,128)(2,1)} %get-tuple-element.91.refs_2_, bf16[640,2048]{1,0:T(8,128)(2,1)} %dynamic-slice_bitcast_fusion.1.refs_3_, ...), custom_call_target="tpu_custom_call" | custom-call | flops 1 | bytes 1 | tf_op jit(solution)/shard_map/product_sum_6/pallas_call | solution.py:376
  432.6 58.4 %product_sum_8.1 = (f32[640,2048]{1,0:T(8,128)}, bf16[640,2048]{1,0:T(8,128)(2,1)}, f32[8,2048]{1,0:T(8,128)}) custom-call(bf16[640,1408]{1,0:T(8,128)(2,1)} %get-tuple-element.95.refs_4_.refs_0_, bf16[640,1408]{1,0:T(8,128)(2,1)} %get-tuple-element.202.refs_5_.refs_1_, f32[640,2048]{1,0:T(8,128)} %get-tuple-element.92.refs_1_.refs_2_, ...), custom_call_target="tpu_custom_call" | custom-call | flops 1 | bytes 1 | tf_op jit(solution)/shard_map/product_sum_8/pallas_call | solution.py:376
  491.0 5.3 fusion.22.do_ref
  496.4 17.7 %attend_back.2 = (bf16[640,512]{1,0:T(8,128)(2,1)}, bf16[2560,128]{1,0:T(8,128)(2,1)}) custom-call(s32[1]{0:T(128)} %bitcast.start_ref, f32[512,640]{1,0:T(8,128)} %fusion.15.q_ref, bf16[512,640]{1,0:T(8,128)(2,1)} %fusion.22.do_ref, bf16[512,640]{1,0:T(8,128)(2,1)} %get-tuple-element.97.o_ref, f32[4,5,1,256]{3,2,1,0:T(1,128)} %get-tuple-element.98.lse_ref, ...), custom_call_target="tpu_custom_call" | custom-call | flops 1 | bytes 1 | tf_op jit(solution)/shard_map/attend_back/pallas_call | solution.py:1022
  514.0 20.7 %scatter_rows.2.refs_1_ = bf16[640,128]{1,0:T(8,128)(2,1)} custom-call(bf16[4,640,128]{2,1,0:T(8,128)(2,1)} %bitcast.78, f32[640,128]{1,0:T(8,128)} %maximum_maximum_fusion.cos_ref, f32[640,128]{1,0:T(8,128)} %get-tuple-element.197.sin_ref), custom_call_target="tpu_custom_call" | custom-call | flops 1 | bytes 1 | tf_op jit(solution)/shard_map/scatter_rows/pallas_call | solution.py:474
  534.8 77.6 %product_sum_7.1 = (f32[640,2048]{1,0:T(8,128)}, bf16[640,2048]{1,0:T(8,128)(2,1)}, f32[8,2048]{1,0:T(8,128)}, bf16[2048,1152]{1,0:T(8,128)(2,1)}) custom-call(bf16[640,512]{1,0:T(8,128)(2,1)} %get-tuple-element.99.refs_0_, bf16[640,128]{1,0:T(8,128)(2,1)} %scatter_rows.2.refs_1_, bf16[640,2048]{1,0:T(8,128)(2,1)} %get-tuple-element.84.refs_1_.refs_2_.out_zero, ...), custom_call_target="tpu_custom_call" | custom-call | flops 1 | bytes 1 | tf_op jit(solution)/shard_map/product_sum_7/pallas_call | solution.py:376
  614.2 10.6 %multiply_convert_fusion = (bf16[640,1408]{1,0:T(8,128)(2,1)}, bf16[640,1408]{1,0:T(8,128)(2,1)}) fusion(f32[640,2816]{1,0:T(8,128)} %copy-done.8, bf16[640,2048]{1,0:T(8,128)(2,1)S(1)} %copy-done.4, bf16[2048,4224]{1,0:T(8,128)(2,1)} %all-gather.7.cloned.1.call-done.refs_3_.refs_7_), kind=kOutput, calls=%fused_computation.15 | convolution fusion | flops 3702702080 | bytes 19202048 | tf_op jit(solution)/shard_map/dot_general | solution.py:24
  624.8 63.4 %product_sum_9.1 = (f32[640,2048]{1,0:T(8,128)}, bf16[640,2048]{1,0:T(8,128)(2,1)}, f32[8,2048]{1,0:T(8,128)}, bf16[2048,4224]{1,0:T(8,128)(2,1)}) custom-call(bf16[640,1408]{1,0:T(8,128)(2,1)} %get-tuple-element.201.refs_0_, bf16[640,1408]{1,0:T(8,128)(2,1)} %get-tuple-element.200.refs_1_, bf16[640,1408]{1,0:T(8,128)(2,1)} %multiply_convert_fusion.5.refs_0_.refs_2_, ...), custom_call_target="tpu_custom_call" | custom-call | flops 1 | bytes 1 | tf_op jit(solution)/shard_map/product_sum_9/pallas_call | solution.py:376
  690.1 4.3 fusion.19.do_ref
  694.4 18.0 %attend_back.3 = (bf16[640,512]{1,0:T(8,128)(2,1)}, bf16[2560,128]{1,0:T(8,128)(2,1)}) custom-call(s32[1]{0:T(128)} %bitcast.start_ref, f32[512,640]{1,0:T(8,128)} %fusion.17.q_ref, bf16[512,640]{1,0:T(8,128)(2,1)} %fusion.19.do_ref, bf16[512,640]{1,0:T(8,128)(2,1)} %get-tuple-element.106.o_ref, f32[4,5,1,256]{3,2,1,0:T(1,128)} %get-tuple-element.107.lse_ref, ...), custom_call_target="tpu_custom_call" | custom-call | flops 1 | bytes 1 | tf_op jit(solution)/shard_map/attend_back/pallas_call | solution.py:1022
  712.4 20.9 %scatter_rows.3.refs_1_ = bf16[640,128]{1,0:T(8,128)(2,1)} custom-call(bf16[4,640,128]{2,1,0:T(8,128)(2,1)} %bitcast.77, f32[640,128]{1,0:T(8,128)} %maximum_maximum_fusion.cos_ref, f32[640,128]{1,0:T(8,128)} %get-tuple-element.197.sin_ref), custom_call_target="tpu_custom_call" | custom-call | flops 1 | bytes 1 | tf_op jit(solution)/shard_map/scatter_rows/pallas_call | solution.py:474
  733.4 61.6 %product_sum_11.1 = (f32[640,2048]{1,0:T(8,128)}, bf16[640,2048]{1,0:T(8,128)(2,1)}, f32[8,2048]{1,0:T(8,128)}, bf16[2048,1152]{1,0:T(8,128)(2,1)}) custom-call(bf16[640,512]{1,0:T(8,128)(2,1)} %get-tuple-element.110.refs_0_, bf16[640,128]{1,0:T(8,128)(2,1)} %scatter_rows.3.refs_1_, bf16[640,2048]{1,0:T(8,128)(2,1)} %copy-done.2, ...), custom_call_target="tpu_custom_call" | custom-call | flops 1 | bytes 1 | tf_op jit(solution)/shard_map/product_sum_11/pallas_call | solution.py:376
  796.6 31.8 %finish.1 = (bf16[256,1152]{1,0:T(8,128)(2,1)}, f32[8,128]{1,0:T(8,128)}, bf16[640,2048]{1,0:T(8,128)(2,1)}, bf16[640,2048]{1,0:T(8,128)(2,1)}, bf16[256,4224]{1,0:T(8,128)(2,1)}, /*index=5*/bf16[256,1152]{1,0:T(8,128)(2,1)}) custom-call(bf16[8,256,1152]{2,1,0:T(8,128)(2,1)} %bitcast.71, f32[2,4,8,128]{3,2,1,0:T(8,128)} %reshape.82.gain_ref, ...), custom_call_target="tpu_custom_call" | custom-call | flops 1 | bytes 1 | tf_op jit(solution)/shard_map/finish/pallas_call | solution.py:608
  828.5 10.3 %write_results.1 = (bf16[2,640,2048]{2,1,0:T(8,128)(2,1)}, f32[2,640,2048]{2,1,0:T(8,128)}, f32[512,512]{1,0:T(8,128)}, f32[512,64]{1,0:T(8,128)}, f32[512,64]{1,0:T(8,128)}, /*index=5*/f32[512,512]{1,0:T(8,128)}) custom-call(bf16[640,2048]{1,0:T(8,128)(2,1)} %get-tuple-element.84.refs_1_.refs_2_.out_zero, bf16[640,2048]{1,0:T(8,128)(2,1)} %get-tuple-element.94.out_one, ...), custom_call_target="tpu_custom_call" | custom-call | flops 1 | bytes 1 | tf_op jit(solution)/shard_map/write_results/pallas_call | solution.py:782
  838.8 3.7 collective-permute-start.2
  846.5 6.2 write_mlp.1
  (116 shorter events, 55.4 us)
Async XLA Ops:
  7.2 26.6 %copy-start = (s32[2,13]{1,0:T(2,128)S(1)}, s32[2,13]{1,0:T(2,128)}, u32[]{:S(2)}) copy-start(s32[2,13]{1,0:T(2,128)} %param.18) | copy-start | bytes 316
  7.2 55.9 %all-gather.5.cloned.1.call-start = ((), (), s32[]{:S(2)}) async-start(), calls=%async_computation.3 | async-start | bytes 5898240 | tf_op jit(solution)/shard_map/all_gather | solution.py:1128
  15.8 2.1 collective-permute-start
  18.3 6.3 copy-start.9
  19.3 169.2 %all-gather.7.cloned.1.call-start = ((), (), s32[]{:S(2)}) async-start(), calls=%async_computation.4 | async-start | bytes 19464192 | tf_op jit(solution)/shard_map/all_gather | solution.py:1128
  25.1 4.3 collective-permute-start.1
  31.9 1.6 copy-start.15
  31.9 1.7 copy-start.16
  31.9 224.9 %all-gather.9.cloned.1.call-start = ((), (), s32[]{:S(2)}) async-start(), calls=%async_computation.5 | async-start | bytes 5898240 | tf_op jit(solution)/shard_map/all_gather | solution.py:1128
  32.7 316.1 %all-gather.11.cloned.1.call-start = ((), (), s32[]{:S(2)}) async-start(), calls=%async_computation.6 | async-start | bytes 19464192 | tf_op jit(solution)/shard_map/all_gather | solution.py:1128
  33.2 655.9 %reduce-scatter.4.cloned.1.call-start = ((), (), s32[]{:S(2)}) async-start(), calls=%async_computation.7 | async-start | bytes 19464192 | tf_op jit(solution)/shard_map/reduce_scatter | solution.py:1091
  36.1 29.1 %copy-start.2 = (bf16[640,2048]{1,0:T(8,128)(2,1)}, bf16[640,2048]{1,0:T(8,128)(2,1)S(1)}, u32[]{:S(2)}) copy-start(bf16[640,2048]{1,0:T(8,128)(2,1)S(1)} %get-tuple-element.199.refs_1_.refs_2_) | copy-start | bytes 7864324
  64.2 1.0 copy-start.6
  65.9 1.5 copy-start.5
  91.8 17.2 %copy-start.7 = (f32[3,2048]{0,1:T(8,128)S(1)}, f32[3,2048]{0,1:T(8,128)}, u32[]{:S(2)}) copy-start(f32[3,2048]{0,1:T(8,128)} %copy-done.6) | copy-start | bytes 73732
  200.7 3.5 copy-start.8
  256.8 20.1 %copy-start.11 = (bf16[640,2048]{1,0:T(8,128)(2,1)S(1)}, bf16[640,2048]{1,0:T(8,128)(2,1)}, u32[]{:S(2)}) copy-start(bf16[640,2048]{1,0:T(8,128)(2,1)} %get-tuple-element.87.refs_5_) | copy-start | bytes 7864324
  348.8 12.1 %copy-start.3 = (bf16[640,2048]{1,0:T(8,128)(2,1)S(1)}, bf16[640,2048]{1,0:T(8,128)(2,1)}, u32[]{:S(2)}) copy-start(bf16[640,2048]{1,0:T(8,128)(2,1)} %dynamic-slice_bitcast_fusion.1.refs_3_) | copy-start | bytes 7864324
  432.6 300.8 %reduce-scatter.6.cloned.1.call-start = ((), (), s32[]{:S(2)}) async-start(), calls=%async_computation.8 | async-start | bytes 5308416 | tf_op jit(solution)/shard_map/reduce_scatter | solution.py:1091
  612.4 1.7 copy-start.4
  612.5 226.3 %reduce-scatter.8.cloned.1.call-start = ((), (), s32[]{:S(2)}) async-start(), calls=%async_computation.9 | async-start | bytes 19464192 | tf_op jit(solution)/shard_map/reduce_scatter | solution.py:1091
  688.2 0.8 copy-start.12
  688.2 0.9 copy-start.13
  688.2 0.9 copy-start.14
  688.3 1.8 copy-start.10
  828.5 17.4 %copy-start.17 = (f32[8,128]{1,0:T(8,128)S(1)}, f32[8,128]{1,0:T(8,128)}, u32[]{:S(2)}) copy-start(f32[8,128]{1,0:T(8,128)} %get-tuple-element.131) | copy-start | bytes 12292
  838.8 7.7 collective-permute-start.2
  846.5 6.2 copy-start.1
Sparse Core Ops, SparseCore 0:
  19.4 43.6 all-gather.4
  65.6 96.3 all-gather.6
  163.9 41.1 all-gather.8
  206.8 99.0 all-gather.10
  432.7 120.9 reduce-scatter.3
  612.6 52.3 reduce-scatter.5
  688.4 121.5 reduce-scatter.7

commit v6 on v5

--- a/solution.py
+++ b/solution.py
@@ -88,19 +88,22 @@
 
 
 def product_sum_kernel(cfg, *refs):
-    n_join, n_arrays, job, sides, stagger = cfg
+    n_join, n_arrays, job, sides, stagger, extra = cfg
     xs, first_column = job[:2]
     refs = list(refs)
     take = lambda n: [refs.pop(0) for _ in range(n)]
     joined = take(n_join)
     from_hbm = [None, *take(n_arrays - 1)]
     (w_hbm,) = take(1)
+    extra_in = take(extra[0]) if extra else []
     outs_hbm = take(len(job[3]))
     (g_hbm,) = take(1) if sides else (None,)
+    extra_out = take(extra[1]) if extra else []
     arrays = take(n_arrays)
     outs = take(len(job[3]))
     load_sem, out_sem, w_buf, p_buf, a_buf, b_buf, w_sem, sa, ra, sb, rb, sc, rc, turn, keep, sums = take(16)
     g_buf, g_sem = take(2) if sides else (None, None)
+    begin, peers, steps, end = extra[2](extra_in, extra_out, refs) if extra else (None, [], [], None)
     per_block = BLOCK // PIECE
     pieces = p_buf.shape[0]
     blocks = pieces // per_block
@@ -169,14 +172,17 @@
     fetch(0, 0).start()
     for k in range(early, n_arrays):
         load(k).start()
+    if extra:
+        begin()
     barrier = pltpu.get_barrier_semaphore()
-    pl.semaphore_signal(barrier, inc=1, device_id=pair, device_id_type=MESH)
+    for device in [pair, *peers]:
+        pl.semaphore_signal(barrier, inc=1, device_id=device, device_id_type=MESH)
     sums[...] = jnp.zeros_like(sums)
 
     @pl.when(inner)
     def _():
         pl.semaphore_signal(barrier, inc=1, device_id=mid, device_id_type=MESH)
-        pl.semaphore_wait(barrier, 2)
+        pl.semaphore_wait(barrier, 2 + len(peers))
 
     @pl.when(outer)
     def _():
@@ -189,7 +195,7 @@
                 pl.semaphore_wait(turn, 1)
 
         else:
-            pl.semaphore_wait(barrier, 1)
+            pl.semaphore_wait(barrier, 1 + len(peers))
 
     for copy in join():
         copy.wait()
@@ -274,6 +280,9 @@
                 def _():
                     second(i - per_block)
 
+        for at, body in steps:
+            pl.when(j == at)(body)
+
         return 0
 
     lax.fori_loop(0, blocks, step, 0)
@@ -307,6 +316,8 @@
 
         every_piece(arrive)
 
+    if extra:
+        end(outs[0])
     chunks = 5 if n_rows % (5 * 32) == 0 else 1
     chunk = n_rows // chunks
     block = 32 if chunk % 32 == 0 else 16
@@ -349,7 +360,7 @@
         copy.wait()
 
 
-def product_sum(arrays, job, weights, sides=(), stagger=False, key=1):
+def product_sum(arrays, job, weights, sides=(), stagger=False, key=1, extra=None):
     assert lax.axis_size("tensor") == 4
     first = arrays[0] if isinstance(arrays[0], tuple) else (arrays[0],)
     given = (*first, *arrays[1:])
@@ -373,10 +384,16 @@
         side_width = sum(arrays[b].shape[1] for _, bs in sides for b in bs)
         out_shape.append(jax.ShapeDtypeStruct((model, side_width), BF))
         scratch += [pltpu.VMEM((2, BLOCK, side_width), BF), two]
+    more, plan = (), None
+    if extra:
+        more, shapes, buffers, steps = extra
+        out_shape += shapes
+        scratch += buffers
+        plan = (len(more), len(shapes), steps)
     out = pl.pallas_call(
-        functools.partial(product_sum_kernel, (len(first), len(arrays), job, tuple(sides), stagger)),
+        functools.partial(product_sum_kernel, (len(first), len(arrays), job, tuple(sides), stagger, plan)),
         out_shape=out_shape,
-        in_specs=[anywhere] * (len(given) + 1),
+        in_specs=[anywhere] * (len(given) + 1 + len(more)),
         out_specs=[anywhere] * len(out_shape),
         scratch_shapes=scratch,
         compiler_params=pltpu.CompilerParams(
@@ -384,7 +401,7 @@
         ),
         cost_estimate=NO_COST,
         name=f"product_sum_{key}",
-    )(*given, weights)
+    )(*given, weights, *more)
     return out if len(out) > 1 else out[0]
 
 
@@ -483,11 +500,13 @@
     )(x.reshape(count, rows, width), cos_rows, sin_rows)
 
 
-def finish_kernel(
-    g_hbm, gain_ref, out_zero, out_one, in_zero, in_one, mlp_one, attn_one,
-    o_ref, gain_out, got_out, got_in, got_mlp, got_attn,
-    mine, away, got, xs, ys, xr, yr, gains, load_sem, send, recv, mate_send, mate_recv, gain_send, gain_recv,
-):
+def finish_steps(ins, outs, scratch):
+    g_hbm, gain_hbm, out_zero, in_zero, in_one, mlp_one, attn_one = ins
+    o_hbm, gain_out, got_out, got_in, got_mlp, got_attn = outs
+    (
+        mine, away, got, xs, ys, xr, yr, o_buf, gain, gains, gain_sum,
+        load_sem, store_sem, send, recv, mate_send, mate_recv, gain_send, gain_recv,
+    ) = scratch
     sec, t, dat = lax.axis_index("section"), lax.axis_index("tensor"), lax.axis_index("dp")
     flip_x = dat + 1 - 2 * lax.rem(dat, 2)
     flip_y = lax.rem(dat + 2, 4)
@@ -500,13 +519,11 @@
     rows = g_hbm.shape[1] // 2
     upper, lower = pl.ds(0, rows), pl.ds(rows, rows)
     order = (across, flip_x, flip_y, dat)
-    loads = []
-    for k, block in enumerate(order):
-        loads.append(pltpu.make_async_copy(g_hbm.at[2 * block + 1 - sec], away.at[k], load_sem.at[k]))
-        loads.append(pltpu.make_async_copy(g_hbm.at[2 * block + sec], mine.at[k], load_sem.at[4 + k]))
-    for copy in loads:
-        copy.start()
-    greet(peers)
+    load_away = lambda k: pltpu.make_async_copy(g_hbm.at[2 * order[k] + 1 - sec], away.at[k], load_sem.at[k])
+    load_mine = lambda k: pltpu.make_async_copy(g_hbm.at[2 * order[k] + sec], mine.at[k], load_sem.at[4 + k])
+    load_gain = lambda: pltpu.make_async_copy(gain_hbm, gain, load_sem.at[8])
+    store_o = lambda: pltpu.make_async_copy(o_buf, o_hbm, store_sem.at[0])
+    store_gain = lambda: pltpu.make_async_copy(gain_sum, gain_out, store_sem.at[1])
 
     def remote(src, dst, k, device):
         return pltpu.make_async_remote_copy(
@@ -518,112 +535,144 @@
             src, dst, mate_send.at[k], mate_recv.at[k], device_id=mate, device_id_type=MESH
         )
 
-    swaps = [remote(away.at[k], got.at[k], k, mate) for k in range(4)]
-    for k in range(4):
-        loads[2 * k].wait()
-        swaps[k].start()
-    gain_copies = [
-        pltpu.make_async_remote_copy(
-            gain_ref.at[peer[0], peer[2]], gains.at[k], gain_send.at[k], gain_recv.at[k],
-            device_id=peer, device_id_type=MESH,
+    def share(k):
+        return pltpu.make_async_remote_copy(
+            gain.at[peers[k][0], peers[k][2]], gains.at[k], gain_send.at[k], gain_recv.at[k],
+            device_id=peers[k], device_id_type=MESH,
         )
-        for k, peer in enumerate(peers)
+
+    swap = lambda k: remote(away.at[k], got.at[k], k, mate)
+    hops = (
+        lambda: remote(mine.at[0, upper], xs.at[0], 4, by_x),
+        lambda: remote(mine.at[0, lower], ys.at[0], 5, by_y),
+        lambda: remote(mine.at[1, upper], xs.at[1], 6, by_x),
+        lambda: remote(mine.at[2, lower], ys.at[1], 7, by_y),
+        lambda: remote(mine.at[2, upper], yr, 8, by_y),
+        lambda: remote(mine.at[1, lower], xr, 9, by_x),
+    )
+
+    def begin():
+        for k in range(4):
+            load_away(k).start()
+        for k in range(4):
+            load_mine(k).start()
+        load_gain().start()
+
+    def exchange():
+        for k in range(4):
+            load_away(k).wait()
+            swap(k).start()
+        load_gain().wait()
+        for k in range(7):
+            share(k).start()
+
+    def add(k):
+        load_mine(k).wait()
+        swap(k).wait_recv()
+        mine[k] = mine[k] + got[k]
+
+    def first_hops():
+        add(0)
+        hops[0]().start()
+        hops[1]().start()
+        add(1)
+        hops[2]().start()
+
+    def more_hops():
+        add(2)
+        hops[3]().start()
+        add(3)
+
+    def swap_results():
+        @pl.when(sec == 0)
+        def _():
+            to_mate(in_one, got_in, 0).start()
+            to_mate(mlp_one, got_mlp, 2).start()
+            to_mate(attn_one, got_attn, 3).start()
+
+        @pl.when(sec == 1)
+        def _():
+            to_mate(in_zero, got_in, 0).start()
+            to_mate(out_zero, got_out, 1).start()
+
+    def second_hops():
+        hops[0]().wait_recv()
+        mine[2, upper] = mine[2, upper] + xs[0]
+        hops[4]().start()
+        hops[1]().wait_recv()
+        mine[1, lower] = mine[1, lower] + ys[0]
+        hops[5]().start()
+
+    def gain_sums():
+        total = gain[sec, dat]
+        for k in range(7):
+            share(k).wait()
+            total = total + gains[k]
+        gain_sum[...] = total
+        store_gain().start()
+
+    def last_adds():
+        for k in (2, 3, 4, 5):
+            hops[k]().wait_recv()
+        o_buf[upper] = (mine[3, upper].astype(F32) + xs[1].astype(F32) + yr[...].astype(F32)).astype(BF)
+        o_buf[lower] = (mine[3, lower].astype(F32) + ys[1].astype(F32) + xr[...].astype(F32)).astype(BF)
+        store_o().start()
+
+        @pl.when(sec == 1)
+        def _():
+            to_mate(o_buf, got_attn, 3).start()
+
+    def end(out_one):
+        @pl.when(sec == 0)
+        def _():
+            to_mate(out_one, got_out, 1).start()
+
+        for k in range(4):
+            swap(k).wait_send()
+        for hop in hops:
+            hop().wait_send()
+        store_o().wait()
+        store_gain().wait()
+        to_mate(in_one, got_in, 0).wait()
+        to_mate(out_one, got_out, 1).wait()
+        to_mate(attn_one, got_attn, 3).wait()
+
+        @pl.when(sec == 0)
+        def _():
+            to_mate(mlp_one, got_mlp, 2).wait_send()
+
+        @pl.when(sec == 1)
+        def _():
+            to_mate(mlp_one, got_mlp, 2).wait_recv()
+
+    steps = [
+        (0, exchange), (1, first_hops), (2, more_hops), (3, swap_results), (4, second_hops), (5, gain_sums),
+        (6, last_adds),
     ]
-    for copy in gain_copies:
-        copy.start()
-    outs = []
-    for k in range(4):
-        loads[2 * k + 1].wait()
-        swaps[k].wait_recv()
-        mine[k] = (mine[k].astype(F32) + got[k].astype(F32)).astype(BF)
-        if k == 0:
-            outs += [remote(mine.at[0, upper], xs.at[0], 4, by_x), remote(mine.at[0, lower], ys.at[0], 5, by_y)]
-        if k == 1:
-            outs += [remote(mine.at[1, upper], xs.at[1], 6, by_x)]
-        if k == 2:
-            outs += [remote(mine.at[2, lower], ys.at[1], 7, by_y)]
-        for copy in outs[-(2 if k == 0 else 1) :]:
-            if k < 3:
-                copy.start()
-
-    @pl.when(sec == 0)
-    def _():
-        to_mate(in_one, got_in, 0).start()
-        to_mate(out_one, got_out, 1).start()
-        to_mate(mlp_one, got_mlp, 2).start()
-        to_mate(attn_one, got_attn, 3).start()
-
-    @pl.when(sec == 1)
-    def _():
-        to_mate(in_zero, got_in, 0).start()
-        to_mate(out_zero, got_out, 1).start()
-
-    outs[0].wait_recv()
-    mine[2, upper] = (mine[2, upper].astype(F32) + xs[0].astype(F32)).astype(BF)
-    outs.append(remote(mine.at[2, upper], yr, 8, by_y))
-    outs[4].start()
-    outs[1].wait_recv()
-    mine[1, lower] = (mine[1, lower].astype(F32) + ys[0].astype(F32)).astype(BF)
-    outs.append(remote(mine.at[1, lower], xr, 9, by_x))
-    outs[5].start()
-    total = gain_ref[sec, dat]
-    for k, copy in enumerate(gain_copies):
-        copy.wait()
-        total = total + gains[k]
-    gain_out[...] = total
-    outs[2].wait_recv()
-    outs[3].wait_recv()
-    outs[4].wait_recv()
-    o_ref[upper] = (mine[3, upper].astype(F32) + xs[1].astype(F32) + yr[...].astype(F32)).astype(BF)
-    outs[5].wait_recv()
-    o_ref[lower] = (mine[3, lower].astype(F32) + ys[1].astype(F32) + xr[...].astype(F32)).astype(BF)
-
-    @pl.when(sec == 1)
-    def _():
-        to_mate(o_ref, got_attn, 3).start()
-
-    for copy in swaps + outs:
-        copy.wait_send()
-    to_mate(in_one, got_in, 0).wait()
-    to_mate(out_one, got_out, 1).wait()
-    to_mate(attn_one, got_attn, 3).wait()
-
-    @pl.when(sec == 0)
-    def _():
-        to_mate(mlp_one, got_mlp, 2).wait_send()
-
-    @pl.when(sec == 1)
-    def _():
-        to_mate(mlp_one, got_mlp, 2).wait_recv()
-
-
-def finish(g, gains, out_zero, out_one, in_zero, in_one, mlp_one, attn_one):
+    return begin, peers, steps, end
+
+
+def finishing(g, gains, out_zero, in_zero, in_one, mlp_one, attn_one):
     rows, width = g.shape[0] // 8, g.shape[1]
     part = pltpu.VMEM((2, rows // 2, width), BF)
     whole = pltpu.VMEM((4, rows, width), BF)
     end = pltpu.VMEM((rows // 2, width), BF)
-    in_vmem, anywhere = pl.BlockSpec(memory_space=pltpu.VMEM), pl.BlockSpec(memory_space=pl.ANY)
     like = lambda x: jax.ShapeDtypeStruct(x.shape, x.dtype)
     dma = lambda n: pltpu.SemaphoreType.DMA((n,))
-    return pl.pallas_call(
-        finish_kernel,
-        out_shape=(
-            jax.ShapeDtypeStruct((rows, width), BF),
-            jax.ShapeDtypeStruct(gains.shape[2:], F32),
+    shape = gains.shape[2:]
+    return (
+        (g.reshape(8, rows, width), gains, out_zero, in_zero, in_one, mlp_one, attn_one),
+        [
+            jax.ShapeDtypeStruct((rows, width), BF), jax.ShapeDtypeStruct(shape, F32),
             like(out_zero), like(in_zero), like(mlp_one), like(attn_one),
-        ),
-        in_specs=[anywhere, in_vmem, *[anywhere] * 6],
-        out_specs=(in_vmem, in_vmem, *[anywhere] * 4),
-        scratch_shapes=[
-            whole, whole, whole, part, part, end, end, pltpu.VMEM((7, *gains.shape[2:]), F32),
-            dma(8), dma(10), dma(10), dma(4), dma(4), dma(7), dma(7),
         ],
-        compiler_params=pltpu.CompilerParams(
-            collective_id=12, has_side_effects=True, vmem_limit_bytes=62 << 20
-        ),
-        cost_estimate=NO_COST,
-        name="finish",
-    )(g.reshape(8, rows, width), gains, out_zero, out_one, in_zero, in_one, mlp_one, attn_one)
+        [
+            whole, whole, whole, part, part, end, end, pltpu.VMEM((rows, width), BF),
+            pltpu.VMEM(gains.shape, F32), pltpu.VMEM((7, *shape), F32), pltpu.VMEM(shape, F32),
+            dma(9), dma(2), dma(10), dma(10), dma(4), dma(4), dma(7), dma(7),
+        ],
+        finish_steps,
+    )
 
 
 def finish_apart(g, gains, out_zero, out_one, in_zero, in_one, mlp_one, attn_one):
@@ -1182,13 +1231,9 @@
     gate_one, up_one, inner_one = layer_units(r_one, one)
     branch = cot
     d_gate, d_up = units_backward(branch, one, gate_one, up_one)
-    out_one, d_mlp_one = product_sum(
-        (inner_one, middle_one, r_one, branch, d_gate, d_up), ((0,), split_down, ("add", (1,)), (BF,)),
-        one[2], ((2, (4, 5)), (3, (0,))), key=6,
-    )
-    d_gate, out_one = lax.optimization_barrier((d_gate, out_one))
-    grad_middle, grad_attn, d_gain_mlp_one = product_sum(
-        ((d_gate, d_up), middle_one, branch, one[0]), ((0,), 0, ("back", (1, 2, (3, 1))), back), one[2], key=8
+    grad_middle, grad_attn, d_gain_mlp_one, d_mlp_one = product_sum(
+        ((d_gate, d_up), inner_one, middle_one, branch, r_one, one[0]), ((0,), 0, ("back", (2, 3, (5, 1))), back),
+        one[2], ((4, (0,)), (3, (1,))), key=8,
     )
     g_mlp_one = reduce_gradient(d_mlp_one)
     dq, dkv = attention_backward(grad_attn, one, tables, kept_one)
@@ -1220,11 +1265,19 @@
     d_gains = jnp.stack([d_gain_attn_zero, d_gain_mlp_zero, d_gain_attn_one, d_gain_mlp_one])
     d_gains = d_gains.reshape(2, 2, devices, -1).swapaxes(1, 2).reshape(2, devices, -1, 128)
 
-    ending = finish if devices == 4 else finish_apart
-    g_attn_zero, g_gain, got_out, got_in, got_mlp, got_attn = ending(
-        d_attn_zero, d_gains, out_zero, out_one, send_zero, branch,
-        g_mlp_one, g_attn_one,
-    )
+    inner_one, send_zero = lax.optimization_barrier((inner_one, send_zero))
+    last_sum = functools.partial(
+        product_sum, (inner_one, middle_one), ((0,), split_down, ("add", (1,)), (BF,)), one[2], key=6
+    )
+    if devices == 4:
+        out_one, g_attn_zero, g_gain, got_out, got_in, got_mlp, got_attn = last_sum(
+            extra=finishing(d_attn_zero, d_gains, out_zero, send_zero, branch, g_mlp_one, g_attn_one)
+        )
+    else:
+        out_one = last_sum()
+        g_attn_zero, g_gain, got_out, got_in, got_mlp, got_attn = finish_apart(
+            d_attn_zero, d_gains, out_zero, out_one, send_zero, branch, g_mlp_one, g_attn_one
+        )
 
     layer_output, input_grad, *grads = write_results(
         (out_zero, out_one, got_out), (grad_zero, grad_one, got_in), (g_attn_zero, g_attn_one, got_attn), width, span

time: 868 us -> 856 us (0.986)
  Pallas kernels: 695 us -> 683 us
    pallas_call x1 -> x0, Pallas kernels: 31.8 us -> none  [finish(): pl.pallas_call(finish_kernel, out_shape=(jax.ShapeDtypeStruct((rows, widt...]
    pallas_call x8, Pallas kernels: 502 us -> 524 us  [product_sum(): pl.pallas_call(functools.partial(product_sum_kernel, (len(first), len(arr...]
where the time goes in v6:
time: 856 us; the launch traced here: 848 us
  Pallas kernels  683 us (80%)
  matrix products  72.7 us (8%)
  local copies, waits for them, and re-layouts  26.9 us (3%)
  other arithmetic  23.3 us (3%)
  waiting for transfers between devices  22.6 us (3%)
  between operations  15.2 us (2%)
    pallas_call x8, Pallas kernels, product_sum(): pl.pallas_call(functools.partial(product_sum_kernel, (len(first), len(arr...  524 us
    pallas_call x2, Pallas kernels, scatter_rows(): pl.pallas_call(functools.partial(scatter_kernel, count), out_shape=jax.Sh...  39.3 us
    dot_general x6, matrix products, dot_f32(): lax.dot_general(a, b, (((ca,), (cb,)), ((), ())), preferred_element_type=...  38.5 us
    pallas_call x2, Pallas kernels, attend_back(): pl.pallas_call(functools.partial(attend_back_kernel, rows, step), out_sha...  36.8 us
    pallas_call x2, Pallas kernels, attend(): pl.pallas_call(functools.partial(attend_kernel, rows, step), out_shape=(j...  34.5 us
    pallas_call x2, Pallas kernels, gather_rows(): pl.pallas_call(functools.partial(gather_kernel, count), out_shape=(jax.Sh...  32.8 us
    dot_general x2, matrix products, layer_units(): jnp.dot(normed, weights[2][:, :2 * units], preferred_element_type=F32)  24.2 us
  transfers between devices with their start and end apart: 10, of which 3 were waited for; matrix products, arithmetic and copies ran while one was open for 10% of the time, Pallas kernels for 73%

profile of v6, /device:TPU:1, one launch (start us, length us, event | category | flops | bytes accessed | tf_op | source)
XLA Modules:
  0.0 848.3 jit_solution(8010133633032607908)
XLA Ops:
  25.3 4.1 collective-permute-done.1
  40.7 3.6 dynamic-slice_bitcast_fusion.1.refs_4_
  44.3 3.6 select_convert_fusion.bias_ref
  47.9 15.2 %all-gather.5.cloned.1.call-done.refs_3_.refs_8_ = bf16[2048,1155]{1,0:T(8,128)(2,1)} async-done(((bf16[256,1155]{1,0:T(8,128)(2,1)}), bf16[2048,1155]{1,0:T(8,128)(2,1)}) %all-gather.5.cloned.1.call-update) | async-done | bytes 4730896 | tf_op jit(solution)/shard_map/all_gather | solution.py:1177
  70.0 16.5 %gather_rows.2 = (bf16[4,640,128]{2,1,0:T(8,128)(2,1)}, bf16[128,2560]{1,0:T(8,128)(2,1)}) custom-call(f32[640,128]{1,0:T(8,128)} %fusion.30.raw_ref, f32[640,128]{1,0:T(8,128)} %maximum_maximum_fusion.cos_ref, f32[640,128]{1,0:T(8,128)} %get-tuple-element.196.sin_ref), custom_call_target="tpu_custom_call" | custom-call | flops 1 | bytes 1 | tf_op jit(solution)/shard_map/gather_rows/pallas_call | solution.py:470
  86.5 5.3 fusion.17.q_ref
  91.7 17.2 %attend.2 = (bf16[512,640]{1,0:T(8,128)(2,1)}, bf16[640,512]{1,0:T(8,128)(2,1)}, f32[4,5,1,256]{3,2,1,0:T(1,128)}) custom-call(s32[1]{0:T(128)} %bitcast.start_ref, f32[512,640]{1,0:T(8,128)} %fusion.17.q_ref, bf16[2560,128]{1,0:T(8,128)(2,1)} %bitcast.72, bf16[128,2560]{1,0:T(8,128)(2,1)} %get-tuple-element.78.kvt_ref, ...), custom_call_target="tpu_custom_call" | custom-call | flops 1 | bytes 1 | tf_op jit(solution)/shard_map/attend/pallas_call | solution.py:1035
  109.9 78.6 %product_sum_1.1 = (f32[640,2048]{1,0:T(8,128)}, bf16[640,2048]{1,0:T(8,128)(2,1)}) custom-call(bf16[640,512]{1,0:T(8,128)(2,1)} %get-tuple-element.79.refs_0_.refs_7_, bf16[640,2048]{1,0:T(8,128)(2,1)} %copy-done.2, f32[3,2048]{1,0:T(4,128)} %copy.101.refs_2_.refs_6_.refs_4_, bf16[2048,1155]{1,0:T(8,128)(2,1)} %all-gather.5.cloned.1.call-done.refs_3_.refs_8_), custom_call_target="tpu_custom_call" | custom-call | flops 1 | bytes 1 | tf_op jit(solution)/shard_map/product_sum_1/pallas_call | solution.py:393
  188.5 12.1 %fusion.2 = f32[640,2816]{1,0:T(8,128)S(1)} fusion(bf16[640,2048]{1,0:T(8,128)(2,1)} %get-tuple-element.80.refs_5_, bf16[2048,4224]{1,0:T(8,128)(2,1)} %all-gather.7.cloned.1.call-done.refs_3_.refs_7_), kind=kOutput, calls=%fused_computation.2 | convolution fusion | flops 7381975040 | bytes 21364736 | tf_op jit(solution)/shard_map/dot_general | solution.py:1125
  204.2 52.6 %product_sum_5.1 = (bf16[640,2048]{1,0:T(8,128)(2,1)}, bf16[640,2048]{1,0:T(8,128)(2,1)}) custom-call(bf16[640,1408]{1,0:T(8,128)(2,1)} %multiply_convert_fusion.5.refs_0_.refs_2_, f32[640,2048]{1,0:T(8,128)} %get-tuple-element.81.refs_1_.refs_3_, f32[3,2048]{1,0:T(4,128)} %copy.101.refs_2_.refs_6_.refs_4_, ...), custom_call_target="tpu_custom_call" | custom-call | flops 1 | bytes 1 | tf_op jit(solution)/shard_map/product_sum_5/pallas_call | solution.py:393
  256.8 3.6 fusion.28.raw_ref
  260.4 16.3 %gather_rows.3 = (bf16[4,640,128]{2,1,0:T(8,128)(2,1)}, bf16[128,2560]{1,0:T(8,128)(2,1)}) custom-call(f32[640,128]{1,0:T(8,128)} %fusion.28.raw_ref, f32[640,128]{1,0:T(8,128)} %maximum_maximum_fusion.cos_ref, f32[640,128]{1,0:T(8,128)} %get-tuple-element.196.sin_ref), custom_call_target="tpu_custom_call" | custom-call | flops 1 | bytes 1 | tf_op jit(solution)/shard_map/gather_rows/pallas_call | solution.py:470
  276.7 4.6 fusion.15.q_ref
  281.3 17.3 %attend.3 = (bf16[512,640]{1,0:T(8,128)(2,1)}, bf16[640,512]{1,0:T(8,128)(2,1)}, f32[4,5,1,256]{3,2,1,0:T(1,128)}) custom-call(s32[1]{0:T(128)} %bitcast.start_ref, f32[512,640]{1,0:T(8,128)} %fusion.15.q_ref, bf16[2560,128]{1,0:T(8,128)(2,1)} %bitcast.74, bf16[128,2560]{1,0:T(8,128)(2,1)} %get-tuple-element.88.kvt_ref, ...), custom_call_target="tpu_custom_call" | custom-call | flops 1 | bytes 1 | tf_op jit(solution)/shard_map/attend/pallas_call | solution.py:1035
  300.7 48.2 %product_sum_2.1 = (f32[640,2048]{1,0:T(8,128)}, bf16[640,2048]{1,0:T(8,128)(2,1)}) custom-call(bf16[640,512]{1,0:T(8,128)(2,1)} %get-tuple-element.89.refs_0_.refs_7_, bf16[640,2048]{1,0:T(8,128)(2,1)} %get-tuple-element.84.refs_1_.refs_2_.refs_5_.out_zero, f32[2,2048]{1,0:T(2,128)} %copy.104.refs_2_.refs_6_.refs_4_, ...), custom_call_target="tpu_custom_call" | custom-call | flops 1 | bytes 1 | tf_op jit(solution)/shard_map/product_sum_2/pallas_call | solution.py:393
  348.9 12.1 %fusion = f32[640,2816]{1,0:T(8,128)S(1)} fusion(bf16[640,2048]{1,0:T(8,128)(2,1)} %get-tuple-element.90.refs_5_, bf16[2048,4224]{1,0:T(8,128)(2,1)} %all-gather.11.cloned.1.call-done.refs_7_.refs_2_), kind=kOutput, calls=%fused_computation | convolution fusion | flops 7381975040 | bytes 21364736 | tf_op jit(solution)/shard_map/dot_general | solution.py:1125
  361.0 9.8 %multiply_convert_fusion.2 = (bf16[640,1408]{1,0:T(8,128)(2,1)}, bf16[640,1408]{1,0:T(8,128)(2,1)}, bf16[640,1408]{1,0:T(8,128)(2,1)}) fusion(f32[640,2816]{1,0:T(8,128)S(1)} %fusion, bf16[640,2048]{1,0:T(8,128)(2,1)S(1)} %copy-done.4, bf16[2048,4224]{1,0:T(8,128)(2,1)} %all-gather.11.cloned.1.call-done.refs_7_.refs_2_), kind=kOutput, calls=%fused_computation.17 | convolution fusion | flops 3705405440 | bytes 21004288 | tf_op jit(solution)/shard_map/dot_general | solution.py:24
  370.8 61.9 %product_sum_8.1 = (f32[640,2048]{1,0:T(8,128)}, bf16[640,2048]{1,0:T(8,128)(2,1)}, f32[8,2048]{1,0:T(8,128)}, bf16[2048,4224]{1,0:T(8,128)(2,1)}) custom-call(bf16[640,1408]{1,0:T(8,128)(2,1)} %get-tuple-element.203.refs_0_, bf16[640,1408]{1,0:T(8,128)(2,1)} %get-tuple-element.202.refs_1_, bf16[640,1408]{1,0:T(8,128)(2,1)} %get-tuple-element.111.refs_2_.refs_0_, ...), custom_call_target="tpu_custom_call" | custom-call | flops 1 | bytes 1 | tf_op jit(solution)/shard_map/product_sum_8/pallas_call | solution.py:393
  434.4 4.3 fusion.22.do_ref
  438.7 18.4 %attend_back.2 = (bf16[640,512]{1,0:T(8,128)(2,1)}, bf16[2560,128]{1,0:T(8,128)(2,1)}) custom-call(s32[1]{0:T(128)} %bitcast.start_ref, f32[512,640]{1,0:T(8,128)} %fusion.15.q_ref, bf16[512,640]{1,0:T(8,128)(2,1)} %fusion.22.do_ref, bf16[512,640]{1,0:T(8,128)(2,1)} %get-tuple-element.94.o_ref, f32[4,5,1,256]{3,2,1,0:T(1,128)} %get-tuple-element.95.lse_ref, ...), custom_call_target="tpu_custom_call" | custom-call | flops 1 | bytes 1 | tf_op jit(solution)/shard_map/attend_back/pallas_call | solution.py:1071
  457.1 19.4 %scatter_rows.2.refs_1_ = bf16[640,128]{1,0:T(8,128)(2,1)} custom-call(bf16[4,640,128]{2,1,0:T(8,128)(2,1)} %bitcast.78, f32[640,128]{1,0:T(8,128)} %maximum_maximum_fusion.cos_ref, f32[640,128]{1,0:T(8,128)} %get-tuple-element.197.sin_ref), custom_call_target="tpu_custom_call" | custom-call | flops 1 | bytes 1 | tf_op jit(solution)/shard_map/scatter_rows/pallas_call | solution.py:491
  476.5 76.9 %product_sum_7.1 = (f32[640,2048]{1,0:T(8,128)}, bf16[640,2048]{1,0:T(8,128)(2,1)}, f32[8,2048]{1,0:T(8,128)}, bf16[2048,1152]{1,0:T(8,128)(2,1)}) custom-call(bf16[640,512]{1,0:T(8,128)(2,1)} %get-tuple-element.96.refs_0_, bf16[640,128]{1,0:T(8,128)(2,1)} %scatter_rows.2.refs_1_, bf16[640,2048]{1,0:T(8,128)(2,1)} %get-tuple-element.84.refs_1_.refs_2_.refs_5_.out_zero, ...), custom_call_target="tpu_custom_call" | custom-call | flops 1 | bytes 1 | tf_op jit(solution)/shard_map/product_sum_7/pallas_call | solution.py:393
  555.2 10.2 %multiply_convert_fusion = (bf16[640,1408]{1,0:T(8,128)(2,1)}, bf16[640,1408]{1,0:T(8,128)(2,1)}) fusion(f32[640,2816]{1,0:T(8,128)} %copy-done.8, bf16[640,2048]{1,0:T(8,128)(2,1)S(1)} %copy-done.3, bf16[2048,4224]{1,0:T(8,128)(2,1)} %all-gather.7.cloned.1.call-done.refs_3_.refs_7_), kind=kOutput, calls=%fused_computation.15 | convolution fusion | flops 3702702080 | bytes 19202048 | tf_op jit(solution)/shard_map/dot_general | solution.py:24
  565.4 63.0 %product_sum_9.1 = (f32[640,2048]{1,0:T(8,128)}, bf16[640,2048]{1,0:T(8,128)(2,1)}, f32[8,2048]{1,0:T(8,128)}, bf16[2048,4224]{1,0:T(8,128)(2,1)}) custom-call(bf16[640,1408]{1,0:T(8,128)(2,1)} %get-tuple-element.201.refs_0_, bf16[640,1408]{1,0:T(8,128)(2,1)} %get-tuple-element.200.refs_1_, bf16[640,1408]{1,0:T(8,128)(2,1)} %multiply_convert_fusion.5.refs_0_.refs_2_, ...), custom_call_target="tpu_custom_call" | custom-call | flops 1 | bytes 1 | tf_op jit(solution)/shard_map/product_sum_9/pallas_call | solution.py:393
  630.3 4.3 fusion.19.do_ref
  634.6 18.3 %attend_back.3 = (bf16[640,512]{1,0:T(8,128)(2,1)}, bf16[2560,128]{1,0:T(8,128)(2,1)}) custom-call(s32[1]{0:T(128)} %bitcast.start_ref, f32[512,640]{1,0:T(8,128)} %fusion.17.q_ref, bf16[512,640]{1,0:T(8,128)(2,1)} %fusion.19.do_ref, bf16[512,640]{1,0:T(8,128)(2,1)} %get-tuple-element.103.o_ref, f32[4,5,1,256]{3,2,1,0:T(1,128)} %get-tuple-element.104.lse_ref, ...), custom_call_target="tpu_custom_call" | custom-call | flops 1 | bytes 1 | tf_op jit(solution)/shard_map/attend_back/pallas_call | solution.py:1071
  652.9 19.9 %scatter_rows.3.refs_1_ = bf16[640,128]{1,0:T(8,128)(2,1)} custom-call(bf16[4,640,128]{2,1,0:T(8,128)(2,1)} %bitcast.77, f32[640,128]{1,0:T(8,128)} %maximum_maximum_fusion.cos_ref, f32[640,128]{1,0:T(8,128)} %get-tuple-element.197.sin_ref), custom_call_target="tpu_custom_call" | custom-call | flops 1 | bytes 1 | tf_op jit(solution)/shard_map/scatter_rows/pallas_call | solution.py:491
  672.8 60.6 %product_sum_11.1 = (f32[640,2048]{1,0:T(8,128)}, bf16[640,2048]{1,0:T(8,128)(2,1)}, f32[8,2048]{1,0:T(8,128)}, bf16[2048,1152]{1,0:T(8,128)(2,1)}) custom-call(bf16[640,512]{1,0:T(8,128)(2,1)} %get-tuple-element.107.refs_0_, bf16[640,128]{1,0:T(8,128)(2,1)} %scatter_rows.3.refs_1_, bf16[640,2048]{1,0:T(8,128)(2,1)} %copy-done.2, ...), custom_call_target="tpu_custom_call" | custom-call | flops 1 | bytes 1 | tf_op jit(solution)/shard_map/product_sum_11/pallas_call | solution.py:393
  735.1 81.9 %product_sum_6.1 = (bf16[640,2048]{1,0:T(8,128)(2,1)}, bf16[256,1152]{1,0:T(8,128)(2,1)}, f32[8,128]{1,0:T(8,128)}, bf16[640,2048]{1,0:T(8,128)(2,1)}, bf16[640,...) custom-call(bf16[640,1408]{1,0:T(8,128)(2,1)} %get-tuple-element.111.refs_2_.refs_0_, ...), custom_call_target="tpu_custom_call" | custom-call | flops 1 | bytes 1 | tf_op jit(solution)/shard_map/product_sum_6/pallas_call | solution.py:393
  817.0 10.3 %write_results.1 = (bf16[2,640,2048]{2,1,0:T(8,128)(2,1)}, f32[2,640,2048]{2,1,0:T(8,128)}, f32[512,512]{1,0:T(8,128)}, f32[512,64]{1,0:T(8,128)}, f32[512,64]{1,0:T(8,128)}, /*index=5*/f32[512,512]{1,0:T(8,128)}) custom-call(bf16[640,2048]{1,0:T(8,128)(2,1)} %get-tuple-element.84.refs_1_.refs_2_.refs_5_.out_zero, ...), custom_call_target="tpu_custom_call" | custom-call | flops 1 | bytes 1 | tf_op jit(solution)/shard_map/write_results/pallas_call | solution.py:831
  827.3 3.4 collective-permute-start.2
  834.7 6.2 write_mlp.1
  (117 shorter events, 53.5 us)
Async XLA Ops:
  7.2 26.6 %copy-start = (s32[2,13]{1,0:T(2,128)S(1)}, s32[2,13]{1,0:T(2,128)}, u32[]{:S(2)}) copy-start(s32[2,13]{1,0:T(2,128)} %param.18) | copy-start | bytes 316
  7.2 55.9 %all-gather.5.cloned.1.call-start = ((), (), s32[]{:S(2)}) async-start(), calls=%async_computation.3 | async-start | bytes 5898240 | tf_op jit(solution)/shard_map/all_gather | solution.py:1177
  15.8 2.1 collective-permute-start
  18.3 6.3 copy-start.9
  19.3 169.2 %all-gather.7.cloned.1.call-start = ((), (), s32[]{:S(2)}) async-start(), calls=%async_computation.4 | async-start | bytes 19464192 | tf_op jit(solution)/shard_map/all_gather | solution.py:1177
  25.1 4.3 collective-permute-start.1
  31.9 1.6 copy-start.16
  31.9 1.7 copy-start.17
  31.9 224.9 %all-gather.9.cloned.1.call-start = ((), (), s32[]{:S(2)}) async-start(), calls=%async_computation.5 | async-start | bytes 5898240 | tf_op jit(solution)/shard_map/all_gather | solution.py:1177
  32.7 316.2 %all-gather.11.cloned.1.call-start = ((), (), s32[]{:S(2)}) async-start(), calls=%async_computation.6 | async-start | bytes 19464192 | tf_op jit(solution)/shard_map/all_gather | solution.py:1177
  33.2 596.1 %reduce-scatter.4.cloned.1.call-start = ((), (), s32[]{:S(2)}) async-start(), calls=%async_computation.7 | async-start | bytes 19464192 | tf_op jit(solution)/shard_map/reduce_scatter | solution.py:1140
  36.1 29.1 %copy-start.2 = (bf16[640,2048]{1,0:T(8,128)(2,1)}, bf16[640,2048]{1,0:T(8,128)(2,1)S(1)}, u32[]{:S(2)}) copy-start(bf16[640,2048]{1,0:T(8,128)(2,1)S(1)} %get-tuple-element.199.refs_1_.refs_2_) | copy-start | bytes 7864324
  64.2 1.0 copy-start.6
  65.9 1.5 copy-start.5
  91.7 17.2 %copy-start.7 = (f32[3,2048]{0,1:T(8,128)S(1)}, f32[3,2048]{0,1:T(8,128)}, u32[]{:S(2)}) copy-start(f32[3,2048]{0,1:T(8,128)} %copy-done.6) | copy-start | bytes 73732
  200.6 3.5 copy-start.8
  256.8 19.9 %copy-start.11 = (bf16[640,2048]{1,0:T(8,128)(2,1)S(1)}, bf16[640,2048]{1,0:T(8,128)(2,1)}, u32[]{:S(2)}) copy-start(bf16[640,2048]{1,0:T(8,128)(2,1)} %get-tuple-element.86.refs_5_) | copy-start | bytes 7864324
  348.9 12.1 %copy-start.4 = (bf16[640,2048]{1,0:T(8,128)(2,1)S(1)}, bf16[640,2048]{1,0:T(8,128)(2,1)}, u32[]{:S(2)}) copy-start(bf16[640,2048]{1,0:T(8,128)(2,1)} %dynamic-slice_bitcast_fusion.1.refs_4_) | copy-start | bytes 7864324
  432.7 1.7 copy-start.12
  432.7 240.1 %reduce-scatter.6.cloned.1.call-start = ((), (), s32[]{:S(2)}) async-start(), calls=%async_computation.8 | async-start | bytes 5308416 | tf_op jit(solution)/shard_map/reduce_scatter | solution.py:1140
  553.5 1.7 copy-start.3
  553.5 273.7 %reduce-scatter.8.cloned.1.call-start = ((), (), s32[]{:S(2)}) async-start(), calls=%async_computation.9 | async-start | bytes 19464192 | tf_op jit(solution)/shard_map/reduce_scatter | solution.py:1140
  628.4 0.8 copy-start.13
  628.4 0.9 copy-start.14
  628.4 0.9 copy-start.15
  628.4 1.8 copy-start.10
  817.0 17.2 %copy-start.18 = (f32[8,128]{1,0:T(8,128)S(1)}, f32[8,128]{1,0:T(8,128)}, u32[]{:S(2)}) copy-start(f32[8,128]{1,0:T(8,128)} %get-tuple-element.131) | copy-start | bytes 12292
  827.3 7.5 collective-permute-start.2
  834.7 6.2 copy-start.1
Sparse Core Ops, SparseCore 0:
  19.4 43.6 all-gather.4
  65.6 96.3 all-gather.6
  163.8 41.1 all-gather.8
  206.8 98.9 all-gather.10
  432.8 117.0 reduce-scatter.3
  553.6 53.9 reduce-scatter.5
  628.6 121.3 reduce-scatter.7

commit v7 on v5

--- a/solution.py
+++ b/solution.py
@@ -1182,20 +1182,16 @@
     gate_one, up_one, inner_one = layer_units(r_one, one)
     branch = cot
     d_gate, d_up = units_backward(branch, one, gate_one, up_one)
-    out_one, d_mlp_one = product_sum(
-        (inner_one, middle_one, r_one, branch, d_gate, d_up), ((0,), split_down, ("add", (1,)), (BF,)),
-        one[2], ((2, (4, 5)), (3, (0,))), key=6,
-    )
-    d_gate, out_one = lax.optimization_barrier((d_gate, out_one))
-    grad_middle, grad_attn, d_gain_mlp_one = product_sum(
-        ((d_gate, d_up), middle_one, branch, one[0]), ((0,), 0, ("back", (1, 2, (3, 1))), back), one[2], key=8
+    grad_middle, grad_attn, d_gain_mlp_one, d_mlp_one = product_sum(
+        ((d_gate, d_up), inner_one, middle_one, branch, r_one, one[0]), ((0,), 0, ("back", (2, 3, (5, 1))), back),
+        one[2], ((4, (0,)), (3, (1,))), key=8,
     )
     g_mlp_one = reduce_gradient(d_mlp_one)
     dq, dkv = attention_backward(grad_attn, one, tables, kept_one)
     grad_one, branch, d_gain_attn_one, d_attn_one = product_sum(
         ((dq, dkv), out_zero, grad_middle, one[0], normed_one, grad_attn, o_one),
         ((0,), 0, ("back", (1, 2, (3, 0))), back),
-        one[1], ((4, (0,)), (5, (6,))), stagger=True, key=7,
+        one[1], ((4, (0,)), (5, (6,))), key=7,
     )
     g_attn_one = reduce_gradient(d_attn_one)
 
@@ -1220,6 +1216,10 @@
     d_gains = jnp.stack([d_gain_attn_zero, d_gain_mlp_zero, d_gain_attn_one, d_gain_mlp_one])
     d_gains = d_gains.reshape(2, 2, devices, -1).swapaxes(1, 2).reshape(2, devices, -1, 128)
 
+    inner_one, send_zero = lax.optimization_barrier((inner_one, send_zero))
+    out_one = product_sum(
+        (inner_one, middle_one), ((0,), split_down, ("add", (1,)), (BF,)), one[2], key=6
+    )
     ending = finish if devices == 4 else finish_apart
     g_attn_zero, g_gain, got_out, got_in, got_mlp, got_attn = ending(
         d_attn_zero, d_gains, out_zero, out_one, send_zero, branch,

time: 868 us -> 854 us (0.984)
  Pallas kernels: 695 us -> 682 us
    pallas_call x8, Pallas kernels: 502 us -> 492 us  [product_sum(): pl.pallas_call(functools.partial(product_sum_kernel, (len(first), len(arr...]
where the time goes in v7:
time: 854 us; the launch traced here: 847 us
  Pallas kernels  682 us (80%)
  matrix products  72.8 us (9%)
  local copies, waits for them, and re-layouts  27.1 us (3%)
  waiting for transfers between devices  22.7 us (3%)
  other arithmetic  22.5 us (3%)
  between operations  15.3 us (2%)
    pallas_call x8, Pallas kernels, product_sum(): pl.pallas_call(functools.partial(product_sum_kernel, (len(first), len(arr...  492 us
    pallas_call x2, Pallas kernels, scatter_rows(): pl.pallas_call(functools.partial(scatter_kernel, count), out_shape=jax.Sh...  40 us
    dot_general x6, matrix products, dot_f32(): lax.dot_general(a, b, (((ca,), (cb,)), ((), ())), preferred_element_type=...  38.6 us
    pallas_call x2, Pallas kernels, attend_back(): pl.pallas_call(functools.partial(attend_back_kernel, rows, step), out_sha...  36.7 us
    pallas_call x2, Pallas kernels, attend(): pl.pallas_call(functools.partial(attend_kernel, rows, step), out_shape=(j...  34.5 us
    pallas_call x2, Pallas kernels, gather_rows(): pl.pallas_call(functools.partial(gather_kernel, count), out_shape=(jax.Sh...  32.8 us
    pallas_call x1, Pallas kernels, finish(): pl.pallas_call(finish_kernel, out_shape=(jax.ShapeDtypeStruct((rows, widt...  29.1 us
    dot_general x2, matrix products, layer_units(): jnp.dot(normed, weights[2][:, :2 * units], preferred_element_type=F32)  24.2 us
  transfers between devices with their start and end apart: 10, of which 3 were waited for; matrix products, arithmetic and copies ran while one was open for 10% of the time, Pallas kernels for 73%

profile of v7, /device:TPU:1, one launch (start us, length us, event | category | flops | bytes accessed | tf_op | source)
XLA Modules:
  0.0 846.6 jit_solution(6638873580296215882)
XLA Ops:
  25.3 4.1 collective-permute-done.1
  40.7 3.6 dynamic-slice_bitcast_fusion.1.refs_4_
  44.3 3.6 select_convert_fusion.bias_ref
  47.9 15.2 %all-gather.5.cloned.1.call-done.refs_3_.refs_8_ = bf16[2048,1155]{1,0:T(8,128)(2,1)} async-done(((bf16[256,1155]{1,0:T(8,128)(2,1)}), bf16[2048,1155]{1,0:T(8,128)(2,1)}) %all-gather.5.cloned.1.call-update) | async-done | bytes 4730896 | tf_op jit(solution)/shard_map/all_gather | solution.py:1128
  70.0 16.5 %gather_rows.2 = (bf16[4,640,128]{2,1,0:T(8,128)(2,1)}, bf16[128,2560]{1,0:T(8,128)(2,1)}) custom-call(f32[640,128]{1,0:T(8,128)} %fusion.30.raw_ref, f32[640,128]{1,0:T(8,128)} %maximum_maximum_fusion.cos_ref, f32[640,128]{1,0:T(8,128)} %get-tuple-element.194.sin_ref), custom_call_target="tpu_custom_call" | custom-call | flops 1 | bytes 1 | tf_op jit(solution)/shard_map/gather_rows/pallas_call | solution.py:453
  86.5 5.3 fusion.17.q_ref
  91.7 17.2 %attend.2 = (bf16[512,640]{1,0:T(8,128)(2,1)}, bf16[640,512]{1,0:T(8,128)(2,1)}, f32[4,5,1,256]{3,2,1,0:T(1,128)}) custom-call(s32[1]{0:T(128)} %bitcast.start_ref, f32[512,640]{1,0:T(8,128)} %fusion.17.q_ref, bf16[2560,128]{1,0:T(8,128)(2,1)} %bitcast.72, bf16[128,2560]{1,0:T(8,128)(2,1)} %get-tuple-element.77.kvt_ref, ...), custom_call_target="tpu_custom_call" | custom-call | flops 1 | bytes 1 | tf_op jit(solution)/shard_map/attend/pallas_call | solution.py:986
  109.9 78.5 %product_sum_1.1 = (f32[640,2048]{1,0:T(8,128)}, bf16[640,2048]{1,0:T(8,128)(2,1)}) custom-call(bf16[640,512]{1,0:T(8,128)(2,1)} %get-tuple-element.78.refs_0_.refs_7_, bf16[640,2048]{1,0:T(8,128)(2,1)} %copy-done.2, f32[3,2048]{1,0:T(4,128)} %copy.101.refs_2_.refs_6_.refs_4_, bf16[2048,1155]{1,0:T(8,128)(2,1)} %all-gather.5.cloned.1.call-done.refs_3_.refs_8_), custom_call_target="tpu_custom_call" | custom-call | flops 1 | bytes 1 | tf_op jit(solution)/shard_map/product_sum_1/pallas_call | solution.py:376
  188.5 12.1 %fusion.2 = f32[640,2816]{1,0:T(8,128)S(1)} fusion(bf16[640,2048]{1,0:T(8,128)(2,1)} %get-tuple-element.79.refs_5_, bf16[2048,4224]{1,0:T(8,128)(2,1)} %all-gather.7.cloned.1.call-done.refs_3_.refs_7_), kind=kOutput, calls=%fused_computation.2 | convolution fusion | flops 7381975040 | bytes 21364736 | tf_op jit(solution)/shard_map/dot_general | solution.py:1076
  204.2 52.6 %product_sum_5.1 = (bf16[640,2048]{1,0:T(8,128)(2,1)}, bf16[640,2048]{1,0:T(8,128)(2,1)}) custom-call(bf16[640,1408]{1,0:T(8,128)(2,1)} %multiply_convert_fusion.5.refs_0_.refs_2_, f32[640,2048]{1,0:T(8,128)} %get-tuple-element.80.refs_1_.refs_3_, f32[3,2048]{1,0:T(4,128)} %copy.101.refs_2_.refs_6_.refs_4_, ...), custom_call_target="tpu_custom_call" | custom-call | flops 1 | bytes 1 | tf_op jit(solution)/shard_map/product_sum_5/pallas_call | solution.py:376
  260.4 16.3 %gather_rows.3 = (bf16[4,640,128]{2,1,0:T(8,128)(2,1)}, bf16[128,2560]{1,0:T(8,128)(2,1)}) custom-call(f32[640,128]{1,0:T(8,128)} %fusion.28.raw_ref, f32[640,128]{1,0:T(8,128)} %maximum_maximum_fusion.cos_ref, f32[640,128]{1,0:T(8,128)} %get-tuple-element.194.sin_ref), custom_call_target="tpu_custom_call" | custom-call | flops 1 | bytes 1 | tf_op jit(solution)/shard_map/gather_rows/pallas_call | solution.py:453
  276.7 4.6 fusion.15.q_ref
  281.3 17.3 %attend.3 = (bf16[512,640]{1,0:T(8,128)(2,1)}, bf16[640,512]{1,0:T(8,128)(2,1)}, f32[4,5,1,256]{3,2,1,0:T(1,128)}) custom-call(s32[1]{0:T(128)} %bitcast.start_ref, f32[512,640]{1,0:T(8,128)} %fusion.15.q_ref, bf16[2560,128]{1,0:T(8,128)(2,1)} %bitcast.74, bf16[128,2560]{1,0:T(8,128)(2,1)} %get-tuple-element.87.kvt_ref, ...), custom_call_target="tpu_custom_call" | custom-call | flops 1 | bytes 1 | tf_op jit(solution)/shard_map/attend/pallas_call | solution.py:986
  300.6 48.2 %product_sum_2.1 = (f32[640,2048]{1,0:T(8,128)}, bf16[640,2048]{1,0:T(8,128)(2,1)}) custom-call(bf16[640,512]{1,0:T(8,128)(2,1)} %get-tuple-element.88.refs_0_.refs_7_, bf16[640,2048]{1,0:T(8,128)(2,1)} %get-tuple-element.83.refs_1_.refs_2_.out_zero, f32[2,2048]{1,0:T(2,128)} %copy.104.refs_2_.refs_6_.refs_4_, ...), custom_call_target="tpu_custom_call" | custom-call | flops 1 | bytes 1 | tf_op jit(solution)/shard_map/product_sum_2/pallas_call | solution.py:376
  348.9 12.1 %fusion = f32[640,2816]{1,0:T(8,128)S(1)} fusion(bf16[640,2048]{1,0:T(8,128)(2,1)} %get-tuple-element.89.refs_5_, bf16[2048,4224]{1,0:T(8,128)(2,1)} %all-gather.11.cloned.1.call-done.refs_7_.refs_2_), kind=kOutput, calls=%fused_computation | convolution fusion | flops 7381975040 | bytes 21364736 | tf_op jit(solution)/shard_map/dot_general | solution.py:1076
  361.0 9.8 %multiply_convert_fusion.2 = (bf16[640,1408]{1,0:T(8,128)(2,1)}, bf16[640,1408]{1,0:T(8,128)(2,1)}, bf16[640,1408]{1,0:T(8,128)(2,1)}) fusion(f32[640,2816]{1,0:T(8,128)S(1)} %fusion, bf16[640,2048]{1,0:T(8,128)(2,1)S(1)} %copy-done.4, bf16[2048,4224]{1,0:T(8,128)(2,1)} %all-gather.11.cloned.1.call-done.refs_7_.refs_2_), kind=kOutput, calls=%fused_computation.17 | convolution fusion | flops 3705405440 | bytes 21004288 | tf_op jit(solution)/shard_map/dot_general | solution.py:24
  370.8 61.9 %product_sum_8.1 = (f32[640,2048]{1,0:T(8,128)}, bf16[640,2048]{1,0:T(8,128)(2,1)}, f32[8,2048]{1,0:T(8,128)}, bf16[2048,4224]{1,0:T(8,128)(2,1)}) custom-call(bf16[640,1408]{1,0:T(8,128)(2,1)} %get-tuple-element.201.refs_0_, bf16[640,1408]{1,0:T(8,128)(2,1)} %get-tuple-element.200.refs_1_, bf16[640,1408]{1,0:T(8,128)(2,1)} %get-tuple-element.110.refs_2_.refs_0_, ...), custom_call_target="tpu_custom_call" | custom-call | flops 1 | bytes 1 | tf_op jit(solution)/shard_map/product_sum_8/pallas_call | solution.py:376
  434.4 4.3 fusion.22.do_ref
  438.8 18.4 %attend_back.2 = (bf16[640,512]{1,0:T(8,128)(2,1)}, bf16[2560,128]{1,0:T(8,128)(2,1)}) custom-call(s32[1]{0:T(128)} %bitcast.start_ref, f32[512,640]{1,0:T(8,128)} %fusion.15.q_ref, bf16[512,640]{1,0:T(8,128)(2,1)} %fusion.22.do_ref, bf16[512,640]{1,0:T(8,128)(2,1)} %get-tuple-element.93.o_ref, f32[4,5,1,256]{3,2,1,0:T(1,128)} %get-tuple-element.94.lse_ref, ...), custom_call_target="tpu_custom_call" | custom-call | flops 1 | bytes 1 | tf_op jit(solution)/shard_map/attend_back/pallas_call | solution.py:1022
  457.2 19.1 %scatter_rows.2.refs_1_ = bf16[640,128]{1,0:T(8,128)(2,1)} custom-call(bf16[4,640,128]{2,1,0:T(8,128)(2,1)} %bitcast.78, f32[640,128]{1,0:T(8,128)} %maximum_maximum_fusion.cos_ref, f32[640,128]{1,0:T(8,128)} %get-tuple-element.195.sin_ref), custom_call_target="tpu_custom_call" | custom-call | flops 1 | bytes 1 | tf_op jit(solution)/shard_map/scatter_rows/pallas_call | solution.py:474
  476.3 60.9 %product_sum_7.1 = (f32[640,2048]{1,0:T(8,128)}, bf16[640,2048]{1,0:T(8,128)(2,1)}, f32[8,2048]{1,0:T(8,128)}, bf16[2048,1152]{1,0:T(8,128)(2,1)}) custom-call(bf16[640,512]{1,0:T(8,128)(2,1)} %get-tuple-element.95.refs_0_, bf16[640,128]{1,0:T(8,128)(2,1)} %scatter_rows.2.refs_1_, bf16[640,2048]{1,0:T(8,128)(2,1)} %get-tuple-element.83.refs_1_.refs_2_.out_zero, ...), custom_call_target="tpu_custom_call" | custom-call | flops 1 | bytes 1 | tf_op jit(solution)/shard_map/product_sum_7/pallas_call | solution.py:376
  539.1 10.3 %multiply_convert_fusion = (bf16[640,1408]{1,0:T(8,128)(2,1)}, bf16[640,1408]{1,0:T(8,128)(2,1)}) fusion(f32[640,2816]{1,0:T(8,128)} %copy-done.8, bf16[640,2048]{1,0:T(8,128)(2,1)S(1)} %copy-done.3, bf16[2048,4224]{1,0:T(8,128)(2,1)} %all-gather.7.cloned.1.call-done.refs_3_.refs_7_), kind=kOutput, calls=%fused_computation.15 | convolution fusion | flops 3702702080 | bytes 19202048 | tf_op jit(solution)/shard_map/dot_general | solution.py:24
  549.4 67.3 %product_sum_9.1 = (f32[640,2048]{1,0:T(8,128)}, bf16[640,2048]{1,0:T(8,128)(2,1)}, f32[8,2048]{1,0:T(8,128)}, bf16[2048,4224]{1,0:T(8,128)(2,1)}) custom-call(bf16[640,1408]{1,0:T(8,128)(2,1)} %get-tuple-element.199.refs_0_, bf16[640,1408]{1,0:T(8,128)(2,1)} %get-tuple-element.198.refs_1_, bf16[640,1408]{1,0:T(8,128)(2,1)} %multiply_convert_fusion.5.refs_0_.refs_2_, ...), custom_call_target="tpu_custom_call" | custom-call | flops 1 | bytes 1 | tf_op jit(solution)/shard_map/product_sum_9/pallas_call | solution.py:376
  618.6 4.3 fusion.19.do_ref
  622.9 18.3 %attend_back.3 = (bf16[640,512]{1,0:T(8,128)(2,1)}, bf16[2560,128]{1,0:T(8,128)(2,1)}) custom-call(s32[1]{0:T(128)} %bitcast.start_ref, f32[512,640]{1,0:T(8,128)} %fusion.17.q_ref, bf16[512,640]{1,0:T(8,128)(2,1)} %fusion.19.do_ref, bf16[512,640]{1,0:T(8,128)(2,1)} %get-tuple-element.102.o_ref, f32[4,5,1,256]{3,2,1,0:T(1,128)} %get-tuple-element.103.lse_ref, ...), custom_call_target="tpu_custom_call" | custom-call | flops 1 | bytes 1 | tf_op jit(solution)/shard_map/attend_back/pallas_call | solution.py:1022
  641.2 20.9 %scatter_rows.3.refs_1_ = bf16[640,128]{1,0:T(8,128)(2,1)} custom-call(bf16[4,640,128]{2,1,0:T(8,128)(2,1)} %bitcast.77, f32[640,128]{1,0:T(8,128)} %maximum_maximum_fusion.cos_ref, f32[640,128]{1,0:T(8,128)} %get-tuple-element.195.sin_ref), custom_call_target="tpu_custom_call" | custom-call | flops 1 | bytes 1 | tf_op jit(solution)/shard_map/scatter_rows/pallas_call | solution.py:474
  662.2 63.1 %product_sum_11.1 = (f32[640,2048]{1,0:T(8,128)}, bf16[640,2048]{1,0:T(8,128)(2,1)}, f32[8,2048]{1,0:T(8,128)}, bf16[2048,1152]{1,0:T(8,128)(2,1)}) custom-call(bf16[640,512]{1,0:T(8,128)(2,1)} %get-tuple-element.106.refs_0_, bf16[640,128]{1,0:T(8,128)(2,1)} %scatter_rows.3.refs_1_, bf16[640,2048]{1,0:T(8,128)(2,1)} %copy-done.2, ...), custom_call_target="tpu_custom_call" | custom-call | flops 1 | bytes 1 | tf_op jit(solution)/shard_map/product_sum_11/pallas_call | solution.py:376
  725.3 59.8 %product_sum_6.1.out_one = bf16[640,2048]{1,0:T(8,128)(2,1)} custom-call(bf16[640,1408]{1,0:T(8,128)(2,1)} %get-tuple-element.110.refs_2_.refs_0_, f32[640,2048]{1,0:T(8,128)} %get-tuple-element.91.refs_3_.refs_1_, bf16[2048,4224]{1,0:T(8,128)(2,1)} %all-gather.11.cloned.1.call-done.refs_7_.refs_2_), custom_call_target="tpu_custom_call" | custom-call | flops 1 | bytes 1 | tf_op jit(solution)/shard_map/product_sum_6/pallas_call | solution.py:376
  785.9 29.1 %finish.1 = (bf16[256,1152]{1,0:T(8,128)(2,1)}, f32[8,128]{1,0:T(8,128)}, bf16[640,2048]{1,0:T(8,128)(2,1)}, bf16[640,2048]{1,0:T(8,128)(2,1)}, bf16[256,4224]{1,0:T(8,128)(2,1)}, /*index=5*/bf16[256,1152]{1,0:T(8,128)(2,1)}) custom-call(bf16[8,256,1152]{2,1,0:T(8,128)(2,1)} %bitcast.71, f32[2,4,8,128]{3,2,1,0:T(8,128)} %reshape.82.gain_ref, ...), custom_call_target="tpu_custom_call" | custom-call | flops 1 | bytes 1 | tf_op jit(solution)/shard_map/finish/pallas_call | solution.py:608
  815.1 10.3 %write_results.1 = (bf16[2,640,2048]{2,1,0:T(8,128)(2,1)}, f32[2,640,2048]{2,1,0:T(8,128)}, f32[512,512]{1,0:T(8,128)}, f32[512,64]{1,0:T(8,128)}, f32[512,64]{1,0:T(8,128)}, /*index=5*/f32[512,512]{1,0:T(8,128)}) custom-call(bf16[640,2048]{1,0:T(8,128)(2,1)} %get-tuple-element.83.refs_1_.refs_2_.out_zero, bf16[640,2048]{1,0:T(8,128)(2,1)} %product_sum_6.1.out_one, ...), custom_call_target="tpu_custom_call" | custom-call | flops 1 | bytes 1 | tf_op jit(solution)/shard_map/write_results/pallas_call | solution.py:782
  825.4 3.7 collective-permute-start.2
  833.0 6.2 write_mlp.1
  (120 shorter events, 56.4 us)
Async XLA Ops:
  7.2 26.6 %copy-start = (s32[2,13]{1,0:T(2,128)S(1)}, s32[2,13]{1,0:T(2,128)}, u32[]{:S(2)}) copy-start(s32[2,13]{1,0:T(2,128)} %param.18) | copy-start | bytes 316
  7.2 55.9 %all-gather.5.cloned.1.call-start = ((), (), s32[]{:S(2)}) async-start(), calls=%async_computation.3 | async-start | bytes 5898240 | tf_op jit(solution)/shard_map/all_gather | solution.py:1128
  15.8 2.1 collective-permute-start
  18.3 6.3 copy-start.9
  19.3 169.1 %all-gather.7.cloned.1.call-start = ((), (), s32[]{:S(2)}) async-start(), calls=%async_computation.4 | async-start | bytes 19464192 | tf_op jit(solution)/shard_map/all_gather | solution.py:1128
  25.1 4.3 collective-permute-start.1
  31.9 1.6 copy-start.17
  31.9 1.7 copy-start.18
  31.9 224.9 %all-gather.9.cloned.1.call-start = ((), (), s32[]{:S(2)}) async-start(), calls=%async_computation.5 | async-start | bytes 5898240 | tf_op jit(solution)/shard_map/all_gather | solution.py:1128
  32.7 316.2 %all-gather.11.cloned.1.call-start = ((), (), s32[]{:S(2)}) async-start(), calls=%async_computation.6 | async-start | bytes 19464192 | tf_op jit(solution)/shard_map/all_gather | solution.py:1128
  33.2 584.4 %reduce-scatter.4.cloned.1.call-start = ((), (), s32[]{:S(2)}) async-start(), calls=%async_computation.7 | async-start | bytes 19464192 | tf_op jit(solution)/shard_map/reduce_scatter | solution.py:1091
  36.1 29.1 %copy-start.2 = (bf16[640,2048]{1,0:T(8,128)(2,1)}, bf16[640,2048]{1,0:T(8,128)(2,1)S(1)}, u32[]{:S(2)}) copy-start(bf16[640,2048]{1,0:T(8,128)(2,1)S(1)} %get-tuple-element.197.refs_1_.refs_2_) | copy-start | bytes 7864324
  64.2 1.0 copy-start.6
  65.9 1.5 copy-start.5
  91.7 17.2 %copy-start.7 = (f32[3,2048]{0,1:T(8,128)S(1)}, f32[3,2048]{0,1:T(8,128)}, u32[]{:S(2)}) copy-start(f32[3,2048]{0,1:T(8,128)} %copy-done.6) | copy-start | bytes 73732
  200.6 3.5 copy-start.8
  256.8 19.9 %copy-start.11 = (bf16[640,2048]{1,0:T(8,128)(2,1)S(1)}, bf16[640,2048]{1,0:T(8,128)(2,1)}, u32[]{:S(2)}) copy-start(bf16[640,2048]{1,0:T(8,128)(2,1)} %get-tuple-element.85.refs_5_) | copy-start | bytes 7864324
  348.9 12.1 %copy-start.4 = (bf16[640,2048]{1,0:T(8,128)(2,1)S(1)}, bf16[640,2048]{1,0:T(8,128)(2,1)}, u32[]{:S(2)}) copy-start(bf16[640,2048]{1,0:T(8,128)(2,1)} %dynamic-slice_bitcast_fusion.1.refs_4_) | copy-start | bytes 7864324
  432.7 1.7 copy-start.12
  432.7 229.4 %reduce-scatter.6.cloned.1.call-start = ((), (), s32[]{:S(2)}) async-start(), calls=%async_computation.8 | async-start | bytes 5308416 | tf_op jit(solution)/shard_map/reduce_scatter | solution.py:1091
  537.2 1.9 copy-start.3
  537.2 288.1 %reduce-scatter.8.cloned.1.call-start = ((), (), s32[]{:S(2)}) async-start(), calls=%async_computation.9 | async-start | bytes 19464192 | tf_op jit(solution)/shard_map/reduce_scatter | solution.py:1091
  616.7 0.8 copy-start.13
  616.7 0.9 copy-start.14
  616.8 0.9 copy-start.15
  616.8 1.8 copy-start.10
  725.3 59.8 %copy-start.16 = (f32[8,2048]{1,0:T(8,128)S(1)}, f32[8,2048]{1,0:T(8,128)}, u32[]{:S(2)}) copy-start(f32[8,2048]{1,0:T(8,128)} %get-tuple-element.112) | copy-start | bytes 196612
  815.0 17.4 %copy-start.19 = (f32[8,128]{1,0:T(8,128)S(1)}, f32[8,128]{1,0:T(8,128)}, u32[]{:S(2)}) copy-start(f32[8,128]{1,0:T(8,128)} %get-tuple-element.129) | copy-start | bytes 12292
  825.4 7.7 collective-permute-start.2
  833.0 6.2 copy-start.1
Sparse Core Ops, SparseCore 0:
  19.4 43.6 all-gather.4
  65.6 96.3 all-gather.6
  163.9 41.1 all-gather.8
  206.8 98.9 all-gather.10
  432.9 117.1 reduce-scatter.3
  553.7 53.9 reduce-scatter.5
  616.9 117.4 reduce-scatter.7

commit v8 on v7

--- a/solution.py
+++ b/solution.py
@@ -409,9 +409,16 @@
     return x * cos_ref[...] + partner * sin_ref[...]
 
 
-def gather_kernel(count, raw_ref, cos_ref, sin_ref, o_ref, t_ref, x_ref, send, recv):
+def gather_kernel(
+    count, normed_ref, w_hbm, cos_ref, sin_ref, o_ref, t_ref, q_ref, x_ref, w_buf, load_sem, send, recv
+):
     me, _, ids = dp_peers(count)
-    x_ref[...] = turn_rows(raw_ref[...], cos_ref, sin_ref).astype(BF)
+    load = pltpu.make_async_copy(w_hbm.at[:, pl.ds(0, w_buf.shape[1])], w_buf, load_sem)
+    load.start()
+    load.wait()
+    width = q_ref.shape[0]
+    raw = jnp.dot(normed_ref[...], w_buf[:, width:], preferred_element_type=F32)
+    x_ref[...] = turn_rows(raw, cos_ref, sin_ref).astype(BF)
     greet(ids)
     copies = [
         pltpu.make_async_remote_copy(
@@ -422,6 +429,7 @@
     for copy in copies:
         copy.start()
     o_ref[me] = x_ref[...]
+    q_ref[...] = jnp.dot(normed_ref[...], w_buf[:, :width], preferred_element_type=F32).T
     for copy in copies:
         copy.wait()
     t_ref[...] = o_ref[...].reshape(t_ref.shape[1], t_ref.shape[0]).T
@@ -445,25 +453,31 @@
     o_ref[...] = turn_rows(total, cos_ref, sin_ref).astype(BF)
 
 
-def gather_rows(raw, cos_rows, sin_rows):
+def gather_rows(normed, w_attn, width, split, cos_rows, sin_rows, key):
     count = lax.axis_size("dp")
-    rows, width = raw.shape
+    rows, span = normed.shape[0], split - width
     in_vmem = pl.BlockSpec(memory_space=pltpu.VMEM)
     sem = pltpu.SemaphoreType.DMA((count - 1,))
-    out, out_t = pl.pallas_call(
+    out, out_t, q_t = pl.pallas_call(
         functools.partial(gather_kernel, count),
         out_shape=(
-            jax.ShapeDtypeStruct((count, rows, width), BF),
-            jax.ShapeDtypeStruct((width, count * rows), BF),
+            jax.ShapeDtypeStruct((count, rows, span), BF),
+            jax.ShapeDtypeStruct((span, count * rows), BF),
+            jax.ShapeDtypeStruct((width, rows), F32),
         ),
-        in_specs=[in_vmem] * 3,
-        out_specs=(in_vmem, in_vmem),
-        scratch_shapes=[pltpu.VMEM((rows, width), BF), sem, sem],
-        compiler_params=pltpu.CompilerParams(collective_id=3, has_side_effects=True),
+        in_specs=[in_vmem, pl.BlockSpec(memory_space=pl.ANY), in_vmem, in_vmem],
+        out_specs=(in_vmem, in_vmem, in_vmem),
+        scratch_shapes=[
+            pltpu.VMEM((rows, span), BF), pltpu.VMEM((normed.shape[1], split), BF),
+            pltpu.SemaphoreType.DMA, sem, sem,
+        ],
+        compiler_params=pltpu.CompilerParams(
+            collective_id=key, has_side_effects=True, vmem_limit_bytes=40 << 20
+        ),
         cost_estimate=NO_COST,
         name="gather_rows",
-    )(raw, cos_rows, sin_rows)
-    return out.reshape(-1, width), out_t
+    )(normed, w_attn, cos_rows, sin_rows)
+    return out.reshape(-1, span), out_t, q_t
 
 
 def scatter_rows(x, cos_rows, sin_rows):
@@ -847,15 +861,7 @@
 
 def over_windows(tree_len, rows, tile, first_row, run):
     if tile % 128 == 0 and GROUP % tile == 0 and TRUNK % tile == 0 and rows % tile == 0:
-
-        @pl.when(first_row < TRUNK)
-        def _():
-            run(((pl.ds(0, TRUNK), True),))
-
-        @pl.when(first_row >= TRUNK)
-        def _():
-            run(((pl.ds(0, TRUNK), False), (pl.ds(group_start(first_row), GROUP), True)))
-
+        run(((pl.ds(0, TRUNK), True), (pl.ds(group_start(first_row), GROUP), True)))
     else:
         run(((pl.ds(0, tree_len), True),))
 
@@ -1051,13 +1057,10 @@
     )(start, q_t, do_t, o_t, lse, kv, kv_t, bias_t, cos_t, sin_t)
 
 
-def layer_attention(normed, weights, tables):
+def layer_attention(normed, weights, tables, key):
     gains, w_attn, w_mlp, width, split, units = weights
     start, bias_t, cos_t, sin_t, cos_rows, sin_rows = tables
-    q_t = dot_f32(w_attn[:, :width], normed, 0, 1)
-    kv, kv_t = gather_rows(
-        jnp.dot(normed, w_attn[:, width:split], preferred_element_type=F32), cos_rows, -sin_rows
-    )
+    kv, kv_t, q_t = gather_rows(normed, w_attn, width, split, cos_rows, -sin_rows, key)
     o_t, o, lse = attend(start, q_t, kv, kv_t, bias_t, cos_t, sin_t)
     return (q_t, kv, kv_t, o_t, lse), o
 
@@ -1164,7 +1167,7 @@
     back = (F32, BF, F32)
 
     normed_zero = (hidden * lax.rsqrt(jnp.mean(hidden * hidden, -1, keepdims=True) + EPSILON) * zero[0][:1]).astype(BF)
-    kept_zero, o_zero = layer_attention(normed_zero, zero, tables)
+    kept_zero, o_zero = layer_attention(normed_zero, zero, tables, 3)
     middle_zero, r_zero = product_sum(
         (o_zero, tree, zero[0]), ((0,), split_out, ("add", (1, (2, 1))), wide), zero[1], stagger=True, key=1
     )
@@ -1175,7 +1178,7 @@
 
     out_zero, normed_one, attn_one = lax.optimization_barrier((out_zero, normed_one, attn_one))
     one = with_gains(attn_one, mlp_one)
-    kept_one, o_one = layer_attention(normed_one, one, tables)
+    kept_one, o_one = layer_attention(normed_one, one, tables, 14)
     middle_one, r_one = product_sum(
         (o_one, out_zero, one[0]), ((0,), split_out, ("add", (1, (2, 1))), wide), one[1], key=2
     )

time: 854 us -> 887 us (1.039)
  Pallas kernels: 682 us -> 724 us
  matrix products: 72.8 us -> 55.9 us
    pallas_call x8, Pallas kernels: 492 us -> 540 us  [product_sum(): pl.pallas_call(functools.partial(product_sum_kernel, (len(first), len(arr...]
    pallas_call x2, Pallas kernels: 40 us -> 26.4 us  [scatter_rows(): pl.pallas_call(functools.partial(scatter_kernel, count), out_shape=jax.Sh...]
    pallas_call x2, Pallas kernels: 36.7 us -> 49.8 us  [attend_back(): pl.pallas_call(functools.partial(attend_back_kernel, rows, step), out_sha...]
    dot_general x6 -> x4, matrix products: 38.6 us -> 28.6 us  [dot_f32(): lax.dot_general(a, b, (((ca,), (cb,)), ((), ())), preferred_element_type=...]
    unnamed x46 -> x62, local copies, waits for them, and re-layouts: 17.2 us -> 24.2 us
  transfers between devices with their start and end apart: 10 -> 10, of which waited for: 3 -> 3; matrix products, arithmetic and copies ran while one was open for 10% -> 8% of each run, Pallas kernels for 73% -> 74%
where the time goes in v8:
time: 887 us; the launch traced here: 882 us
  Pallas kernels  724 us (82%)
  matrix products  55.9 us (6%)
  local copies, waits for them, and re-layouts  32.2 us (4%)
  other arithmetic  25 us (3%)
  waiting for transfers between devices  24.4 us (3%)
  between operations  15.3 us (2%)
    pallas_call x8, Pallas kernels, product_sum(): pl.pallas_call(functools.partial(product_sum_kernel, (len(first), len(arr...  540 us
    pallas_call x2, Pallas kernels, attend_back(): pl.pallas_call(functools.partial(attend_back_kernel, rows, step), out_sha...  49.8 us
    pallas_call x2, Pallas kernels, attend(): pl.pallas_call(functools.partial(attend_kernel, rows, step), out_shape=(j...  35.2 us
    dot_general x4, matrix products, dot_f32(): lax.dot_general(a, b, (((ca,), (cb,)), ((), ())), preferred_element_type=...  28.6 us
    pallas_call x1, Pallas kernels, finish(): pl.pallas_call(finish_kernel, out_shape=(jax.ShapeDtypeStruct((rows, widt...  28.3 us
    pallas_call x2, Pallas kernels, gather_rows(): pl.pallas_call(functools.partial(gather_kernel, count), out_shape=(jax.Sh...  28 us
    pallas_call x2, Pallas kernels, scatter_rows(): pl.pallas_call(functools.partial(scatter_kernel, count), out_shape=jax.Sh...  26.4 us
    unnamed x62, local copies, waits for them, and re-layouts  24.2 us
  transfers between devices with their start and end apart: 10, of which 3 were waited for; matrix products, arithmetic and copies ran while one was open for 8% of the time, Pallas kernels for 74%

profile of v8, /device:TPU:1, one launch (start us, length us, event | category | flops | bytes accessed | tf_op | source)
XLA Modules:
  0.0 882.0 jit_solution(6565807059478521944)
XLA Ops:
  21.5 3.0 convert_bitcast_fusion.1
  25.3 4.1 collective-permute-done.1
  34.0 3.9 fusion.8
  43.1 3.1 select_convert_fusion.bias_ref
  46.2 17.0 %all-gather.5.cloned.1.call-done.w_hbm.refs_3_.refs_8_ = bf16[2048,1155]{1,0:T(8,128)(2,1)} async-done(((bf16[256,1155]{1,0:T(8,128)(2,1)}), bf16[2048,1155]{1,0:T(8,128)(2,1)}) %all-gather.5.cloned.1.call-update) | async-done | bytes 4730896 | tf_op jit(solution)/shard_map/all_gather | solution.py:1131
  67.3 13.2 %gather_rows.2 = (bf16[4,640,128]{2,1,0:T(8,128)(2,1)S(1)}, bf16[128,2560]{1,0:T(8,128)(2,1)S(1)}, f32[512,640]{1,0:T(8,128)S(1)}) custom-call(bf16[640,2048]{1,0:T(8,128)(2,1)S(1)} %fusion.10.normed_ref.refs_5_, bf16[2048,1155]{1,0:T(8,128)(2,1)S(1)} %copy-done.2, f32[640,128]{1,0:T(8,128)S(1)} %maximum_maximum_fusion.cos_ref, ...), custom_call_target="tpu_custom_call" | custom-call | flops 1 | bytes 1 | tf_op jit(solution)/shard_map/gather_rows/pallas_call | solution.py:461
  83.2 17.6 %attend.2 = (bf16[512,640]{1,0:T(8,128)(2,1)}, bf16[640,512]{1,0:T(8,128)(2,1)}, f32[4,5,1,256]{3,2,1,0:T(1,128)}) custom-call(s32[1]{0:T(128)} %bitcast.start_ref, f32[512,640]{1,0:T(8,128)} %copy-done.7, bf16[2560,128]{1,0:T(8,128)(2,1)} %bitcast.66, bf16[128,2560]{1,0:T(8,128)(2,1)} %copy-done.10, bf16[2560,640]{1,0:T(8,128)(2,1)} %select_convert_fusion.bias_ref, ...), custom_call_target="tpu_custom_call" | custom-call | flops 1 | bytes 1 | tf_op jit(solution)/shard_map/attend/pallas_call | solution.py:992
  101.8 77.1 %product_sum_1.1 = (f32[640,2048]{1,0:T(8,128)}, bf16[640,2048]{1,0:T(8,128)(2,1)}) custom-call(bf16[640,512]{1,0:T(8,128)(2,1)} %get-tuple-element.81.refs_0_.refs_7_, bf16[640,2048]{1,0:T(8,128)(2,1)} %get-tuple-element.201.refs_1_.refs_2_, f32[3,2048]{1,0:T(4,128)} %copy.101.refs_2_.refs_6_.refs_4_, ...), custom_call_target="tpu_custom_call" | custom-call | flops 1 | bytes 1 | tf_op jit(solution)/shard_map/product_sum_1/pallas_call | solution.py:376
  178.9 11.9 %fusion.2 = f32[640,2816]{1,0:T(8,128)S(1)} fusion(bf16[640,2048]{1,0:T(8,128)(2,1)} %get-tuple-element.82.refs_5_, bf16[2048,4224]{1,0:T(8,128)(2,1)} %all-gather.7.cloned.1.call-done.refs_3_.refs_7_), kind=kOutput, calls=%fused_computation.2 | convolution fusion | flops 7381975040 | bytes 21364736 | tf_op jit(solution)/shard_map/dot_general | solution.py:1079
  190.9 2.8 multiply_convert_fusion.5.refs_0_.refs_2_
  194.4 60.4 %product_sum_5.1 = (bf16[640,2048]{1,0:T(8,128)(2,1)}, bf16[640,2048]{1,0:T(8,128)(2,1)}) custom-call(bf16[640,1408]{1,0:T(8,128)(2,1)} %multiply_convert_fusion.5.refs_0_.refs_2_, f32[640,2048]{1,0:T(8,128)} %get-tuple-element.83.refs_1_.refs_3_, f32[3,2048]{1,0:T(4,128)} %copy.101.refs_2_.refs_6_.refs_4_, ...), custom_call_target="tpu_custom_call" | custom-call | flops 1 | bytes 1 | tf_op jit(solution)/shard_map/product_sum_5/pallas_call | solution.py:376
  259.0 14.7 %gather_rows.3 = (bf16[4,640,128]{2,1,0:T(8,128)(2,1)S(1)}, bf16[128,2560]{1,0:T(8,128)(2,1)S(1)}, f32[512,640]{1,0:T(8,128)S(1)}) custom-call(bf16[640,2048]{1,0:T(8,128)(2,1)S(1)} %copy-done.5, bf16[2048,1154]{1,0:T(8,128)(2,1)S(1)} %copy-done.3, f32[640,128]{1,0:T(8,128)S(1)} %maximum_maximum_fusion.cos_ref, f32[640,128]{1,0:T(8,128)S(1)} %get-tuple-element.198.sin_ref), custom_call_target="tpu_custom_call" | custom-call | flops 1 | bytes 1 | tf_op jit(solution)/shard_map/gather_rows/pallas_call | solution.py:461
  276.5 17.6 %attend.3 = (bf16[512,640]{1,0:T(8,128)(2,1)}, bf16[640,512]{1,0:T(8,128)(2,1)}, f32[4,5,1,256]{3,2,1,0:T(1,128)}) custom-call(s32[1]{0:T(128)} %bitcast.start_ref, f32[512,640]{1,0:T(8,128)} %copy-done.8, bf16[2560,128]{1,0:T(8,128)(2,1)} %bitcast.68, bf16[128,2560]{1,0:T(8,128)(2,1)} %copy-done.12, bf16[2560,640]{1,0:T(8,128)(2,1)} %select_convert_fusion.bias_ref, ...), custom_call_target="tpu_custom_call" | custom-call | flops 1 | bytes 1 | tf_op jit(solution)/shard_map/attend/pallas_call | solution.py:992
  296.2 61.6 %product_sum_2.1 = (f32[640,2048]{1,0:T(8,128)}, bf16[640,2048]{1,0:T(8,128)(2,1)}) custom-call(bf16[640,512]{1,0:T(8,128)(2,1)} %get-tuple-element.92.refs_0_.refs_7_, bf16[640,2048]{1,0:T(8,128)(2,1)} %get-tuple-element.86.refs_1_.refs_2_.out_zero, f32[2,2048]{1,0:T(2,128)} %copy.104.refs_2_.refs_6_.refs_4_, ...), custom_call_target="tpu_custom_call" | custom-call | flops 1 | bytes 1 | tf_op jit(solution)/shard_map/product_sum_2/pallas_call | solution.py:376
  357.9 12.1 %fusion = f32[640,2816]{1,0:T(8,128)S(1)} fusion(bf16[640,2048]{1,0:T(8,128)(2,1)} %get-tuple-element.93.refs_5_, bf16[2048,4224]{1,0:T(8,128)(2,1)} %all-gather.11.cloned.1.call-done.refs_7_.refs_2_), kind=kOutput, calls=%fused_computation | convolution fusion | flops 7381975040 | bytes 21364736 | tf_op jit(solution)/shard_map/dot_general | solution.py:1079
  369.9 9.8 %multiply_convert_fusion.2 = (bf16[640,1408]{1,0:T(8,128)(2,1)}, bf16[640,1408]{1,0:T(8,128)(2,1)}, bf16[640,1408]{1,0:T(8,128)(2,1)}) fusion(f32[640,2816]{1,0:T(8,128)S(1)} %fusion, bf16[640,2048]{1,0:T(8,128)(2,1)S(1)} %copy-done.14, bf16[2048,4224]{1,0:T(8,128)(2,1)} %all-gather.11.cloned.1.call-done.refs_7_.refs_2_), kind=kOutput, calls=%fused_computation.17 | convolution fusion | flops 3705405440 | bytes 21004288 | tf_op jit(solution)/shard_map/dot_general | solution.py:24
  379.7 68.5 %product_sum_8.1 = (f32[640,2048]{1,0:T(8,128)}, bf16[640,2048]{1,0:T(8,128)(2,1)}, f32[8,2048]{1,0:T(8,128)}, bf16[2048,4224]{1,0:T(8,128)(2,1)}) custom-call(bf16[640,1408]{1,0:T(8,128)(2,1)} %get-tuple-element.205.refs_0_, bf16[640,1408]{1,0:T(8,128)(2,1)} %get-tuple-element.204.refs_1_, bf16[640,1408]{1,0:T(8,128)(2,1)} %get-tuple-element.114.refs_2_.refs_0_, ...), custom_call_target="tpu_custom_call" | custom-call | flops 1 | bytes 1 | tf_op jit(solution)/shard_map/product_sum_8/pallas_call | solution.py:376
  450.0 4.3 fusion.18.do_ref
  454.3 24.9 %attend_back.2 = (bf16[640,512]{1,0:T(8,128)(2,1)}, bf16[2560,128]{1,0:T(8,128)(2,1)}) custom-call(s32[1]{0:T(128)} %bitcast.start_ref, f32[512,640]{1,0:T(8,128)} %copy-done.8, bf16[512,640]{1,0:T(8,128)(2,1)} %fusion.18.do_ref, bf16[512,640]{1,0:T(8,128)(2,1)} %get-tuple-element.97.o_ref, f32[4,5,1,256]{3,2,1,0:T(1,128)} %get-tuple-element.98.lse_ref, ...), custom_call_target="tpu_custom_call" | custom-call | flops 1 | bytes 1 | tf_op jit(solution)/shard_map/attend_back/pallas_call | solution.py:1028
  479.3 13.8 %scatter_rows.2.refs_1_ = bf16[640,128]{1,0:T(8,128)(2,1)} custom-call(bf16[4,640,128]{2,1,0:T(8,128)(2,1)} %bitcast.76, f32[640,128]{1,0:T(8,128)} %copy-done.6, f32[640,128]{1,0:T(8,128)} %get-tuple-element.199.sin_ref), custom_call_target="tpu_custom_call" | custom-call | flops 1 | bytes 1 | tf_op jit(solution)/shard_map/scatter_rows/pallas_call | solution.py:488
  493.0 68.0 %product_sum_7.1 = (f32[640,2048]{1,0:T(8,128)}, bf16[640,2048]{1,0:T(8,128)(2,1)}, f32[8,2048]{1,0:T(8,128)}, bf16[2048,1152]{1,0:T(8,128)(2,1)}) custom-call(bf16[640,512]{1,0:T(8,128)(2,1)} %get-tuple-element.99.refs_0_, bf16[640,128]{1,0:T(8,128)(2,1)} %scatter_rows.2.refs_1_, bf16[640,2048]{1,0:T(8,128)(2,1)} %get-tuple-element.86.refs_1_.refs_2_.out_zero, ...), custom_call_target="tpu_custom_call" | custom-call | flops 1 | bytes 1 | tf_op jit(solution)/shard_map/product_sum_7/pallas_call | solution.py:376
  562.8 10.1 %multiply_convert_fusion = (bf16[640,1408]{1,0:T(8,128)(2,1)}, bf16[640,1408]{1,0:T(8,128)(2,1)}) fusion(f32[640,2816]{1,0:T(8,128)} %copy-done.15, bf16[640,2048]{1,0:T(8,128)(2,1)S(1)} %copy-done.13, bf16[2048,4224]{1,0:T(8,128)(2,1)} %all-gather.7.cloned.1.call-done.refs_3_.refs_7_), kind=kOutput, calls=%fused_computation.15 | convolution fusion | flops 3702702080 | bytes 19202048 | tf_op jit(solution)/shard_map/dot_general | solution.py:24
  572.9 71.4 %product_sum_9.1 = (f32[640,2048]{1,0:T(8,128)}, bf16[640,2048]{1,0:T(8,128)(2,1)}, f32[8,2048]{1,0:T(8,128)}, bf16[2048,4224]{1,0:T(8,128)(2,1)}) custom-call(bf16[640,1408]{1,0:T(8,128)(2,1)} %get-tuple-element.203.refs_0_, bf16[640,1408]{1,0:T(8,128)(2,1)} %get-tuple-element.202.refs_1_, bf16[640,1408]{1,0:T(8,128)(2,1)} %multiply_convert_fusion.5.refs_0_.refs_2_, ...), custom_call_target="tpu_custom_call" | custom-call | flops 1 | bytes 1 | tf_op jit(solution)/shard_map/product_sum_9/pallas_call | solution.py:376
  646.1 4.3 fusion.15.do_ref
  650.5 24.9 %attend_back.3 = (bf16[640,512]{1,0:T(8,128)(2,1)}, bf16[2560,128]{1,0:T(8,128)(2,1)}) custom-call(s32[1]{0:T(128)} %bitcast.start_ref, f32[512,640]{1,0:T(8,128)} %copy-done.7, bf16[512,640]{1,0:T(8,128)(2,1)} %fusion.15.do_ref, bf16[512,640]{1,0:T(8,128)(2,1)} %get-tuple-element.106.o_ref, f32[4,5,1,256]{3,2,1,0:T(1,128)} %get-tuple-element.107.lse_ref, ...), custom_call_target="tpu_custom_call" | custom-call | flops 1 | bytes 1 | tf_op jit(solution)/shard_map/attend_back/pallas_call | solution.py:1028
  675.4 12.7 %scatter_rows.3.refs_1_ = bf16[640,128]{1,0:T(8,128)(2,1)} custom-call(bf16[4,640,128]{2,1,0:T(8,128)(2,1)} %bitcast.75, f32[640,128]{1,0:T(8,128)} %copy-done.6, f32[640,128]{1,0:T(8,128)} %get-tuple-element.199.sin_ref), custom_call_target="tpu_custom_call" | custom-call | flops 1 | bytes 1 | tf_op jit(solution)/shard_map/scatter_rows/pallas_call | solution.py:488
  688.1 68.7 %product_sum_11.1 = (f32[640,2048]{1,0:T(8,128)}, bf16[640,2048]{1,0:T(8,128)(2,1)}, f32[8,2048]{1,0:T(8,128)}, bf16[2048,1152]{1,0:T(8,128)(2,1)}) custom-call(bf16[640,512]{1,0:T(8,128)(2,1)} %get-tuple-element.110.refs_0_, bf16[640,128]{1,0:T(8,128)(2,1)} %scatter_rows.3.refs_1_, bf16[640,2048]{1,0:T(8,128)(2,1)} %get-tuple-element.201.refs_1_.refs_2_, ...), custom_call_target="tpu_custom_call" | custom-call | flops 1 | bytes 1 | tf_op jit(solution)/shard_map/product_sum_11/pallas_call | solution.py:376
  756.8 64.4 %product_sum_6.1.out_one = bf16[640,2048]{1,0:T(8,128)(2,1)} custom-call(bf16[640,1408]{1,0:T(8,128)(2,1)} %get-tuple-element.114.refs_2_.refs_0_, f32[640,2048]{1,0:T(8,128)} %get-tuple-element.95.refs_3_.refs_1_, bf16[2048,4224]{1,0:T(8,128)(2,1)} %all-gather.11.cloned.1.call-done.refs_7_.refs_2_), custom_call_target="tpu_custom_call" | custom-call | flops 1 | bytes 1 | tf_op jit(solution)/shard_map/product_sum_6/pallas_call | solution.py:376
  822.0 28.3 %finish.1 = (bf16[256,1152]{1,0:T(8,128)(2,1)}, f32[8,128]{1,0:T(8,128)}, bf16[640,2048]{1,0:T(8,128)(2,1)}, bf16[640,2048]{1,0:T(8,128)(2,1)}, bf16[256,4224]{1,0:T(8,128)(2,1)}, /*index=5*/bf16[256,1152]{1,0:T(8,128)(2,1)}) custom-call(bf16[8,256,1152]{2,1,0:T(8,128)(2,1)} %bitcast.71, f32[2,4,8,128]{3,2,1,0:T(8,128)} %reshape.82.gain_ref, ...), custom_call_target="tpu_custom_call" | custom-call | flops 1 | bytes 1 | tf_op jit(solution)/shard_map/finish/pallas_call | solution.py:622
  850.4 10.3 %write_results.1 = (bf16[2,640,2048]{2,1,0:T(8,128)(2,1)}, f32[2,640,2048]{2,1,0:T(8,128)}, f32[512,512]{1,0:T(8,128)}, f32[512,64]{1,0:T(8,128)}, f32[512,64]{1,0:T(8,128)}, /*index=5*/f32[512,512]{1,0:T(8,128)}) custom-call(bf16[640,2048]{1,0:T(8,128)(2,1)} %get-tuple-element.86.refs_1_.refs_2_.out_zero, bf16[640,2048]{1,0:T(8,128)(2,1)} %product_sum_6.1.out_one, ...), custom_call_target="tpu_custom_call" | custom-call | flops 1 | bytes 1 | tf_op jit(solution)/shard_map/write_results/pallas_call | solution.py:796
  860.7 3.7 collective-permute-start.2
  868.4 6.2 write_mlp.1
  (133 shorter events, 52.2 us)
Async XLA Ops:
  7.2 26.8 %copy-start = (s32[2,13]{1,0:T(2,128)S(1)}, s32[2,13]{1,0:T(2,128)}, u32[]{:S(2)}) copy-start(s32[2,13]{1,0:T(2,128)} %param.18) | copy-start | bytes 316
  7.2 55.9 %all-gather.5.cloned.1.call-start = ((), (), s32[]{:S(2)}) async-start(), calls=%async_computation.3 | async-start | bytes 5898240 | tf_op jit(solution)/shard_map/all_gather | solution.py:1131
  15.8 2.1 collective-permute-start
  18.3 6.3 copy-start.16
  19.3 159.6 %all-gather.7.cloned.1.call-start = ((), (), s32[]{:S(2)}) async-start(), calls=%async_computation.4 | async-start | bytes 19464192 | tf_op jit(solution)/shard_map/all_gather | solution.py:1131
  25.1 4.3 collective-permute-start.1
  31.9 1.7 copy-start.23
  31.9 1.8 copy-start.24
  31.9 222.9 %all-gather.9.cloned.1.call-start = ((), (), s32[]{:S(2)}) async-start(), calls=%async_computation.5 | async-start | bytes 5898240 | tf_op jit(solution)/shard_map/all_gather | solution.py:1131
  32.7 325.2 %all-gather.11.cloned.1.call-start = ((), (), s32[]{:S(2)}) async-start(), calls=%async_computation.6 | async-start | bytes 19464192 | tf_op jit(solution)/shard_map/all_gather | solution.py:1131
  32.7 8.7 slice-start
  33.2 612.0 %reduce-scatter.4.cloned.1.call-start = ((), (), s32[]{:S(2)}) async-start(), calls=%async_computation.7 | async-start | bytes 19464192 | tf_op jit(solution)/shard_map/reduce_scatter | solution.py:1094
  34.0 7.4 slice-start.1
  40.5 214.3 %copy-start.6 = (f32[640,128]{1,0:T(8,128)}, f32[640,128]{1,0:T(8,128)S(1)}, u32[]{:S(2)}) copy-start(f32[640,128]{1,0:T(8,128)S(1)} %maximum_maximum_fusion.cos_ref) | copy-start | bytes 983044
  63.1 4.1 copy-start.2
  67.2 13.2 %copy-start.4 = (bf16[640,2048]{1,0:T(8,128)(2,1)}, bf16[640,2048]{1,0:T(8,128)(2,1)S(1)}, u32[]{:S(2)}) copy-start(bf16[640,2048]{1,0:T(8,128)(2,1)S(1)} %fusion.10.normed_ref.refs_5_) | copy-start | bytes 7864324
  80.5 1.1 copy-start.7
  190.9 3.5 copy-start.15
  254.8 2.5 copy-start.3
  257.3 1.7 copy-start.5
  273.8 1.1 copy-start.8
  357.8 12.1 %copy-start.14 = (bf16[640,2048]{1,0:T(8,128)(2,1)S(1)}, bf16[640,2048]{1,0:T(8,128)(2,1)}, u32[]{:S(2)}) copy-start(bf16[640,2048]{1,0:T(8,128)(2,1)} %dynamic-slice_bitcast_fusion.refs_4_) | copy-start | bytes 7864324
  448.3 1.7 copy-start.18
  448.3 239.7 %reduce-scatter.6.cloned.1.call-start = ((), (), s32[]{:S(2)}) async-start(), calls=%async_computation.8 | async-start | bytes 5308416 | tf_op jit(solution)/shard_map/reduce_scatter | solution.py:1094
  561.0 1.7 copy-start.13
  561.1 299.6 %reduce-scatter.8.cloned.1.call-start = ((), (), s32[]{:S(2)}) async-start(), calls=%async_computation.9 | async-start | bytes 19464192 | tf_op jit(solution)/shard_map/reduce_scatter | solution.py:1094
  644.3 0.9 copy-start.21
  644.3 1.8 copy-start.17
  756.8 64.5 %copy-start.22 = (f32[8,2048]{1,0:T(8,128)S(1)}, f32[8,2048]{1,0:T(8,128)}, u32[]{:S(2)}) copy-start(f32[8,2048]{1,0:T(8,128)} %get-tuple-element.116) | copy-start | bytes 196612
  850.4 17.4 %copy-start.25 = (f32[8,128]{1,0:T(8,128)S(1)}, f32[8,128]{1,0:T(8,128)}, u32[]{:S(2)}) copy-start(f32[8,128]{1,0:T(8,128)} %get-tuple-element.133) | copy-start | bytes 12292
  860.7 7.7 collective-permute-start.2
  868.4 6.2 copy-start.1
  (6 other events, 5.0 us)
Sparse Core Ops, SparseCore 0:
  19.4 43.6 all-gather.4
  65.6 93.5 all-gather.6
  161.1 41.1 all-gather.8
  204.0 99.0 all-gather.10
  448.4 117.4 reduce-scatter.3
  569.6 53.9 reduce-scatter.5
  644.5 116.3 reduce-scatter.7

commit v9 on v8

--- a/solution.py
+++ b/solution.py
@@ -283,29 +283,23 @@
         for u in range(per_block):
             second(pieces - per_block + u)
 
-    if stagger:
-
-        @pl.when(outer)
-        def _():
-            every_piece(lambda i: to_inner(i).wait_send())
+    if sides:
+        lax.fori_loop(blocks - lag, blocks, lambda j, _: side(j), 0)
+
+    @pl.when(outer)
+    def _():
+        every_piece(lambda i: to_inner(i).wait_send())
+
+        def arrive(i):
+            to_outer(i).wait_recv()
+            done(i)
+
+        every_piece(arrive)
+        if stagger:
 
             @pl.when(sec == 0)
             def _():
                 pl.semaphore_signal(turn, inc=1, device_id=mate, device_id_type=MESH)
-
-    if sides:
-        lax.fori_loop(blocks - lag, blocks, lambda j, _: side(j), 0)
-
-    @pl.when(outer)
-    def _():
-        if not stagger:
-            every_piece(lambda i: to_inner(i).wait_send())
-
-        def arrive(i):
-            to_outer(i).wait_recv()
-            done(i)
-
-        every_piece(arrive)
 
     chunks = 5 if n_rows % (5 * 32) == 0 else 1
     chunk = n_rows // chunks

time: 887 us -> 845 us (0.953)
  Pallas kernels: 724 us -> 682 us
    pallas_call x8, Pallas kernels: 540 us -> 496 us  [product_sum(): pl.pallas_call(functools.partial(product_sum_kernel, (len(first), len(arr...]
  transfers between devices with their start and end apart: 10 -> 10, of which waited for: 3 -> 3; matrix products, arithmetic and copies ran while one was open for 8% -> 8% of each run, Pallas kernels for 74% -> 73%
where the time goes in v9:
time: 845 us; the launch traced here: 840 us
  Pallas kernels  682 us (81%)
  matrix products  55.9 us (7%)
  local copies, waits for them, and re-layouts  32.5 us (4%)
  other arithmetic  25 us (3%)
  waiting for transfers between devices  24.4 us (3%)
  between operations  15.3 us (2%)
    pallas_call x8, Pallas kernels, product_sum(): pl.pallas_call(functools.partial(product_sum_kernel, (len(first), len(arr...  496 us
    pallas_call x2, Pallas kernels, attend_back(): pl.pallas_call(functools.partial(attend_back_kernel, rows, step), out_sha...  49.4 us
    pallas_call x2, Pallas kernels, attend(): pl.pallas_call(functools.partial(attend_kernel, rows, step), out_shape=(j...  35.2 us
    pallas_call x2, Pallas kernels, gather_rows(): pl.pallas_call(functools.partial(gather_kernel, count), out_shape=(jax.Sh...  29 us
    dot_general x4, matrix products, dot_f32(): lax.dot_general(a, b, (((ca,), (cb,)), ((), ())), preferred_element_type=...  28.6 us
    pallas_call x2, Pallas kernels, scatter_rows(): pl.pallas_call(functools.partial(scatter_kernel, count), out_shape=jax.Sh...  28.2 us
    pallas_call x1, Pallas kernels, finish(): pl.pallas_call(finish_kernel, out_shape=(jax.ShapeDtypeStruct((rows, widt...  28 us
    unnamed x62, local copies, waits for them, and re-layouts  24.5 us
  transfers between devices with their start and end apart: 10, of which 3 were waited for; matrix products, arithmetic and copies ran while one was open for 8% of the time, Pallas kernels for 73%

profile of v9, /device:TPU:1, one launch (start us, length us, event | category | flops | bytes accessed | tf_op | source)
XLA Modules:
  0.0 839.9 jit_solution(11475993528678867260)
XLA Ops:
  21.5 3.0 convert_bitcast_fusion.1
  25.3 4.1 collective-permute-done.1
  34.0 3.9 fusion.8
  43.1 3.1 select_convert_fusion.bias_ref
  46.2 17.0 %all-gather.5.cloned.1.call-done.w_hbm.refs_3_.refs_8_ = bf16[2048,1155]{1,0:T(8,128)(2,1)} async-done(((bf16[256,1155]{1,0:T(8,128)(2,1)}), bf16[2048,1155]{1,0:T(8,128)(2,1)}) %all-gather.5.cloned.1.call-update) | async-done | bytes 4730896 | tf_op jit(solution)/shard_map/all_gather | solution.py:1125
  67.3 13.2 %gather_rows.2 = (bf16[4,640,128]{2,1,0:T(8,128)(2,1)S(1)}, bf16[128,2560]{1,0:T(8,128)(2,1)S(1)}, f32[512,640]{1,0:T(8,128)S(1)}) custom-call(bf16[640,2048]{1,0:T(8,128)(2,1)S(1)} %fusion.10.normed_ref.refs_5_, bf16[2048,1155]{1,0:T(8,128)(2,1)S(1)} %copy-done.2, f32[640,128]{1,0:T(8,128)S(1)} %maximum_maximum_fusion.cos_ref, ...), custom_call_target="tpu_custom_call" | custom-call | flops 1 | bytes 1 | tf_op jit(solution)/shard_map/gather_rows/pallas_call | solution.py:455
  83.2 17.6 %attend.2 = (bf16[512,640]{1,0:T(8,128)(2,1)}, bf16[640,512]{1,0:T(8,128)(2,1)}, f32[4,5,1,256]{3,2,1,0:T(1,128)}) custom-call(s32[1]{0:T(128)} %bitcast.start_ref, f32[512,640]{1,0:T(8,128)} %copy-done.7, bf16[2560,128]{1,0:T(8,128)(2,1)} %bitcast.66, bf16[128,2560]{1,0:T(8,128)(2,1)} %copy-done.10, bf16[2560,640]{1,0:T(8,128)(2,1)} %select_convert_fusion.bias_ref, ...), custom_call_target="tpu_custom_call" | custom-call | flops 1 | bytes 1 | tf_op jit(solution)/shard_map/attend/pallas_call | solution.py:986
  101.8 86.6 %product_sum_1.1 = (f32[640,2048]{1,0:T(8,128)}, bf16[640,2048]{1,0:T(8,128)(2,1)}) custom-call(bf16[640,512]{1,0:T(8,128)(2,1)} %get-tuple-element.81.refs_0_.refs_7_, bf16[640,2048]{1,0:T(8,128)(2,1)} %get-tuple-element.201.refs_1_.refs_2_, f32[3,2048]{1,0:T(4,128)} %copy.101.refs_2_.refs_6_.refs_4_, ...), custom_call_target="tpu_custom_call" | custom-call | flops 1 | bytes 1 | tf_op jit(solution)/shard_map/product_sum_1/pallas_call | solution.py:370
  188.5 12.0 %fusion.2 = f32[640,2816]{1,0:T(8,128)S(1)} fusion(bf16[640,2048]{1,0:T(8,128)(2,1)} %get-tuple-element.82.refs_5_, bf16[2048,4224]{1,0:T(8,128)(2,1)} %all-gather.7.cloned.1.call-done.refs_3_.refs_7_), kind=kOutput, calls=%fused_computation.2 | convolution fusion | flops 7381975040 | bytes 21364736 | tf_op jit(solution)/shard_map/dot_general | solution.py:1073
  200.5 2.8 multiply_convert_fusion.5.refs_0_.refs_2_
  204.0 48.3 %product_sum_5.1 = (bf16[640,2048]{1,0:T(8,128)(2,1)}, bf16[640,2048]{1,0:T(8,128)(2,1)}) custom-call(bf16[640,1408]{1,0:T(8,128)(2,1)} %multiply_convert_fusion.5.refs_0_.refs_2_, f32[640,2048]{1,0:T(8,128)} %get-tuple-element.83.refs_1_.refs_3_, f32[3,2048]{1,0:T(4,128)} %copy.101.refs_2_.refs_6_.refs_4_, ...), custom_call_target="tpu_custom_call" | custom-call | flops 1 | bytes 1 | tf_op jit(solution)/shard_map/product_sum_5/pallas_call | solution.py:370
  256.7 15.8 %gather_rows.3 = (bf16[4,640,128]{2,1,0:T(8,128)(2,1)S(1)}, bf16[128,2560]{1,0:T(8,128)(2,1)S(1)}, f32[512,640]{1,0:T(8,128)S(1)}) custom-call(bf16[640,2048]{1,0:T(8,128)(2,1)S(1)} %copy-done.5, bf16[2048,1154]{1,0:T(8,128)(2,1)S(1)} %copy-done.3, f32[640,128]{1,0:T(8,128)S(1)} %maximum_maximum_fusion.cos_ref, f32[640,128]{1,0:T(8,128)S(1)} %get-tuple-element.198.sin_ref), custom_call_target="tpu_custom_call" | custom-call | flops 1 | bytes 1 | tf_op jit(solution)/shard_map/gather_rows/pallas_call | solution.py:455
  275.2 17.6 %attend.3 = (bf16[512,640]{1,0:T(8,128)(2,1)}, bf16[640,512]{1,0:T(8,128)(2,1)}, f32[4,5,1,256]{3,2,1,0:T(1,128)}) custom-call(s32[1]{0:T(128)} %bitcast.start_ref, f32[512,640]{1,0:T(8,128)} %copy-done.8, bf16[2560,128]{1,0:T(8,128)(2,1)} %bitcast.68, bf16[128,2560]{1,0:T(8,128)(2,1)} %copy-done.12, bf16[2560,640]{1,0:T(8,128)(2,1)} %select_convert_fusion.bias_ref, ...), custom_call_target="tpu_custom_call" | custom-call | flops 1 | bytes 1 | tf_op jit(solution)/shard_map/attend/pallas_call | solution.py:986
  294.9 47.5 %product_sum_2.1 = (f32[640,2048]{1,0:T(8,128)}, bf16[640,2048]{1,0:T(8,128)(2,1)}) custom-call(bf16[640,512]{1,0:T(8,128)(2,1)} %get-tuple-element.92.refs_0_.refs_7_, bf16[640,2048]{1,0:T(8,128)(2,1)} %get-tuple-element.86.refs_1_.refs_2_.out_zero, f32[2,2048]{1,0:T(2,128)} %copy.104.refs_2_.refs_6_.refs_4_, ...), custom_call_target="tpu_custom_call" | custom-call | flops 1 | bytes 1 | tf_op jit(solution)/shard_map/product_sum_2/pallas_call | solution.py:370
  342.4 12.1 %fusion = f32[640,2816]{1,0:T(8,128)S(1)} fusion(bf16[640,2048]{1,0:T(8,128)(2,1)} %get-tuple-element.93.refs_5_, bf16[2048,4224]{1,0:T(8,128)(2,1)} %all-gather.11.cloned.1.call-done.refs_7_.refs_2_), kind=kOutput, calls=%fused_computation | convolution fusion | flops 7381975040 | bytes 21364736 | tf_op jit(solution)/shard_map/dot_general | solution.py:1073
  354.5 9.8 %multiply_convert_fusion.2 = (bf16[640,1408]{1,0:T(8,128)(2,1)}, bf16[640,1408]{1,0:T(8,128)(2,1)}, bf16[640,1408]{1,0:T(8,128)(2,1)}) fusion(f32[640,2816]{1,0:T(8,128)S(1)} %fusion, bf16[640,2048]{1,0:T(8,128)(2,1)S(1)} %copy-done.14, bf16[2048,4224]{1,0:T(8,128)(2,1)} %all-gather.11.cloned.1.call-done.refs_7_.refs_2_), kind=kOutput, calls=%fused_computation.17 | convolution fusion | flops 3705405440 | bytes 21004288 | tf_op jit(solution)/shard_map/dot_general | solution.py:24
  364.3 61.8 %product_sum_8.1 = (f32[640,2048]{1,0:T(8,128)}, bf16[640,2048]{1,0:T(8,128)(2,1)}, f32[8,2048]{1,0:T(8,128)}, bf16[2048,4224]{1,0:T(8,128)(2,1)}) custom-call(bf16[640,1408]{1,0:T(8,128)(2,1)} %get-tuple-element.205.refs_0_, bf16[640,1408]{1,0:T(8,128)(2,1)} %get-tuple-element.204.refs_1_, bf16[640,1408]{1,0:T(8,128)(2,1)} %get-tuple-element.114.refs_2_.refs_0_, ...), custom_call_target="tpu_custom_call" | custom-call | flops 1 | bytes 1 | tf_op jit(solution)/shard_map/product_sum_8/pallas_call | solution.py:370
  427.8 4.3 fusion.18.do_ref
  432.2 25.0 %attend_back.2 = (bf16[640,512]{1,0:T(8,128)(2,1)}, bf16[2560,128]{1,0:T(8,128)(2,1)}) custom-call(s32[1]{0:T(128)} %bitcast.start_ref, f32[512,640]{1,0:T(8,128)} %copy-done.8, bf16[512,640]{1,0:T(8,128)(2,1)} %fusion.18.do_ref, bf16[512,640]{1,0:T(8,128)(2,1)} %get-tuple-element.97.o_ref, f32[4,5,1,256]{3,2,1,0:T(1,128)} %get-tuple-element.98.lse_ref, ...), custom_call_target="tpu_custom_call" | custom-call | flops 1 | bytes 1 | tf_op jit(solution)/shard_map/attend_back/pallas_call | solution.py:1022
  457.2 13.8 %scatter_rows.2.refs_1_ = bf16[640,128]{1,0:T(8,128)(2,1)} custom-call(bf16[4,640,128]{2,1,0:T(8,128)(2,1)} %bitcast.76, f32[640,128]{1,0:T(8,128)} %copy-done.6, f32[640,128]{1,0:T(8,128)} %get-tuple-element.199.sin_ref), custom_call_target="tpu_custom_call" | custom-call | flops 1 | bytes 1 | tf_op jit(solution)/shard_map/scatter_rows/pallas_call | solution.py:482
  470.9 59.7 %product_sum_7.1 = (f32[640,2048]{1,0:T(8,128)}, bf16[640,2048]{1,0:T(8,128)(2,1)}, f32[8,2048]{1,0:T(8,128)}, bf16[2048,1152]{1,0:T(8,128)(2,1)}) custom-call(bf16[640,512]{1,0:T(8,128)(2,1)} %get-tuple-element.99.refs_0_, bf16[640,128]{1,0:T(8,128)(2,1)} %scatter_rows.2.refs_1_, bf16[640,2048]{1,0:T(8,128)(2,1)} %get-tuple-element.86.refs_1_.refs_2_.out_zero, ...), custom_call_target="tpu_custom_call" | custom-call | flops 1 | bytes 1 | tf_op jit(solution)/shard_map/product_sum_7/pallas_call | solution.py:370
  532.6 10.1 %multiply_convert_fusion = (bf16[640,1408]{1,0:T(8,128)(2,1)}, bf16[640,1408]{1,0:T(8,128)(2,1)}) fusion(f32[640,2816]{1,0:T(8,128)} %copy-done.15, bf16[640,2048]{1,0:T(8,128)(2,1)S(1)} %copy-done.13, bf16[2048,4224]{1,0:T(8,128)(2,1)} %all-gather.7.cloned.1.call-done.refs_3_.refs_7_), kind=kOutput, calls=%fused_computation.15 | convolution fusion | flops 3702702080 | bytes 19202048 | tf_op jit(solution)/shard_map/dot_general | solution.py:24
  542.8 65.8 %product_sum_9.1 = (f32[640,2048]{1,0:T(8,128)}, bf16[640,2048]{1,0:T(8,128)(2,1)}, f32[8,2048]{1,0:T(8,128)}, bf16[2048,4224]{1,0:T(8,128)(2,1)}) custom-call(bf16[640,1408]{1,0:T(8,128)(2,1)} %get-tuple-element.203.refs_0_, bf16[640,1408]{1,0:T(8,128)(2,1)} %get-tuple-element.202.refs_1_, bf16[640,1408]{1,0:T(8,128)(2,1)} %multiply_convert_fusion.5.refs_0_.refs_2_, ...), custom_call_target="tpu_custom_call" | custom-call | flops 1 | bytes 1 | tf_op jit(solution)/shard_map/product_sum_9/pallas_call | solution.py:370
  610.4 4.3 fusion.15.do_ref
  614.7 24.4 %attend_back.3 = (bf16[640,512]{1,0:T(8,128)(2,1)}, bf16[2560,128]{1,0:T(8,128)(2,1)}) custom-call(s32[1]{0:T(128)} %bitcast.start_ref, f32[512,640]{1,0:T(8,128)} %copy-done.7, bf16[512,640]{1,0:T(8,128)(2,1)} %fusion.15.do_ref, bf16[512,640]{1,0:T(8,128)(2,1)} %get-tuple-element.106.o_ref, f32[4,5,1,256]{3,2,1,0:T(1,128)} %get-tuple-element.107.lse_ref, ...), custom_call_target="tpu_custom_call" | custom-call | flops 1 | bytes 1 | tf_op jit(solution)/shard_map/attend_back/pallas_call | solution.py:1022
  639.1 14.4 %scatter_rows.3.refs_1_ = bf16[640,128]{1,0:T(8,128)(2,1)} custom-call(bf16[4,640,128]{2,1,0:T(8,128)(2,1)} %bitcast.75, f32[640,128]{1,0:T(8,128)} %copy-done.6, f32[640,128]{1,0:T(8,128)} %get-tuple-element.199.sin_ref), custom_call_target="tpu_custom_call" | custom-call | flops 1 | bytes 1 | tf_op jit(solution)/shard_map/scatter_rows/pallas_call | solution.py:482
  653.6 65.6 %product_sum_11.1 = (f32[640,2048]{1,0:T(8,128)}, bf16[640,2048]{1,0:T(8,128)(2,1)}, f32[8,2048]{1,0:T(8,128)}, bf16[2048,1152]{1,0:T(8,128)(2,1)}) custom-call(bf16[640,512]{1,0:T(8,128)(2,1)} %get-tuple-element.110.refs_0_, bf16[640,128]{1,0:T(8,128)(2,1)} %scatter_rows.3.refs_1_, bf16[640,2048]{1,0:T(8,128)(2,1)} %get-tuple-element.201.refs_1_.refs_2_, ...), custom_call_target="tpu_custom_call" | custom-call | flops 1 | bytes 1 | tf_op jit(solution)/shard_map/product_sum_11/pallas_call | solution.py:370
  719.2 60.3 %product_sum_6.1.out_one = bf16[640,2048]{1,0:T(8,128)(2,1)} custom-call(bf16[640,1408]{1,0:T(8,128)(2,1)} %get-tuple-element.114.refs_2_.refs_0_, f32[640,2048]{1,0:T(8,128)} %get-tuple-element.95.refs_3_.refs_1_, bf16[2048,4224]{1,0:T(8,128)(2,1)} %all-gather.11.cloned.1.call-done.refs_7_.refs_2_), custom_call_target="tpu_custom_call" | custom-call | flops 1 | bytes 1 | tf_op jit(solution)/shard_map/product_sum_6/pallas_call | solution.py:370
  780.3 28.0 %finish.1 = (bf16[256,1152]{1,0:T(8,128)(2,1)}, f32[8,128]{1,0:T(8,128)}, bf16[640,2048]{1,0:T(8,128)(2,1)}, bf16[640,2048]{1,0:T(8,128)(2,1)}, bf16[256,4224]{1,0:T(8,128)(2,1)}, /*index=5*/bf16[256,1152]{1,0:T(8,128)(2,1)}) custom-call(bf16[8,256,1152]{2,1,0:T(8,128)(2,1)} %bitcast.71, f32[2,4,8,128]{3,2,1,0:T(8,128)} %reshape.82.gain_ref, ...), custom_call_target="tpu_custom_call" | custom-call | flops 1 | bytes 1 | tf_op jit(solution)/shard_map/finish/pallas_call | solution.py:616
  808.3 10.3 %write_results.1 = (bf16[2,640,2048]{2,1,0:T(8,128)(2,1)}, f32[2,640,2048]{2,1,0:T(8,128)}, f32[512,512]{1,0:T(8,128)}, f32[512,64]{1,0:T(8,128)}, f32[512,64]{1,0:T(8,128)}, /*index=5*/f32[512,512]{1,0:T(8,128)}) custom-call(bf16[640,2048]{1,0:T(8,128)(2,1)} %get-tuple-element.86.refs_1_.refs_2_.out_zero, bf16[640,2048]{1,0:T(8,128)(2,1)} %product_sum_6.1.out_one, ...), custom_call_target="tpu_custom_call" | custom-call | flops 1 | bytes 1 | tf_op jit(solution)/shard_map/write_results/pallas_call | solution.py:790
  818.6 3.7 collective-permute-start.2
  826.3 6.2 write_mlp.1
  (133 shorter events, 52.5 us)
Async XLA Ops:
  7.2 26.8 %copy-start = (s32[2,13]{1,0:T(2,128)S(1)}, s32[2,13]{1,0:T(2,128)}, u32[]{:S(2)}) copy-start(s32[2,13]{1,0:T(2,128)} %param.18) | copy-start | bytes 316
  7.2 55.9 %all-gather.5.cloned.1.call-start = ((), (), s32[]{:S(2)}) async-start(), calls=%async_computation.3 | async-start | bytes 5898240 | tf_op jit(solution)/shard_map/all_gather | solution.py:1125
  15.8 2.1 collective-permute-start
  18.3 6.3 copy-start.16
  19.3 169.1 %all-gather.7.cloned.1.call-start = ((), (), s32[]{:S(2)}) async-start(), calls=%async_computation.4 | async-start | bytes 19464192 | tf_op jit(solution)/shard_map/all_gather | solution.py:1125
  25.1 4.3 collective-permute-start.1
  31.9 1.7 copy-start.23
  31.9 1.8 copy-start.24
  31.9 220.4 %all-gather.9.cloned.1.call-start = ((), (), s32[]{:S(2)}) async-start(), calls=%async_computation.5 | async-start | bytes 5898240 | tf_op jit(solution)/shard_map/all_gather | solution.py:1125
  32.7 309.7 %all-gather.11.cloned.1.call-start = ((), (), s32[]{:S(2)}) async-start(), calls=%async_computation.6 | async-start | bytes 19464192 | tf_op jit(solution)/shard_map/all_gather | solution.py:1125
  32.7 8.7 %slice-start = ((s8[5242880]{0:T(1024)(128)(4,1)}), s8[1048576]{0:T(1024)(128)(4,1)S(1)}, s32[]{:S(2)}) async-start(s8[5242880]{0:T(1024)(128)(4,1)} %bitcast.73), calls=%async_computation.10 | async-start | bytes 2097152
  33.2 576.3 %reduce-scatter.4.cloned.1.call-start = ((), (), s32[]{:S(2)}) async-start(), calls=%async_computation.7 | async-start | bytes 19464192 | tf_op jit(solution)/shard_map/reduce_scatter | solution.py:1088
  34.0 7.4 slice-start.1
  40.5 211.9 %copy-start.6 = (f32[640,128]{1,0:T(8,128)}, f32[640,128]{1,0:T(8,128)S(1)}, u32[]{:S(2)}) copy-start(f32[640,128]{1,0:T(8,128)S(1)} %maximum_maximum_fusion.cos_ref) | copy-start | bytes 983044
  63.1 4.1 copy-start.2
  67.2 13.2 %copy-start.4 = (bf16[640,2048]{1,0:T(8,128)(2,1)}, bf16[640,2048]{1,0:T(8,128)(2,1)S(1)}, u32[]{:S(2)}) copy-start(bf16[640,2048]{1,0:T(8,128)(2,1)S(1)} %fusion.10.normed_ref.refs_5_) | copy-start | bytes 7864324
  80.5 1.1 copy-start.7
  200.5 3.5 copy-start.15
  252.4 2.6 copy-start.3
  254.9 1.7 copy-start.5
  272.5 1.1 copy-start.8
  342.4 12.1 %copy-start.14 = (bf16[640,2048]{1,0:T(8,128)(2,1)S(1)}, bf16[640,2048]{1,0:T(8,128)(2,1)}, u32[]{:S(2)}) copy-start(bf16[640,2048]{1,0:T(8,128)(2,1)} %dynamic-slice_bitcast_fusion.refs_4_) | copy-start | bytes 7864324
  426.1 1.7 copy-start.18
  426.1 227.5 %reduce-scatter.6.cloned.1.call-start = ((), (), s32[]{:S(2)}) async-start(), calls=%async_computation.8 | async-start | bytes 5308416 | tf_op jit(solution)/shard_map/reduce_scatter | solution.py:1088
  530.7 2.0 copy-start.13
  530.7 287.9 %reduce-scatter.8.cloned.1.call-start = ((), (), s32[]{:S(2)}) async-start(), calls=%async_computation.9 | async-start | bytes 19464192 | tf_op jit(solution)/shard_map/reduce_scatter | solution.py:1088
  608.6 0.9 copy-start.21
  608.6 1.8 copy-start.17
  719.2 60.3 %copy-start.22 = (f32[8,2048]{1,0:T(8,128)S(1)}, f32[8,2048]{1,0:T(8,128)}, u32[]{:S(2)}) copy-start(f32[8,2048]{1,0:T(8,128)} %get-tuple-element.116) | copy-start | bytes 196612
  808.3 17.4 %copy-start.25 = (f32[8,128]{1,0:T(8,128)S(1)}, f32[8,128]{1,0:T(8,128)}, u32[]{:S(2)}) copy-start(f32[8,128]{1,0:T(8,128)} %get-tuple-element.133) | copy-start | bytes 12292
  818.6 7.7 collective-permute-start.2
  826.3 6.2 copy-start.1
  (6 other events, 5.0 us)
Sparse Core Ops, SparseCore 0:
  19.4 43.6 all-gather.4
  65.6 93.5 all-gather.6
  161.1 41.2 all-gather.8
  204.1 99.0 all-gather.10
  426.2 116.6 reduce-scatter.3
  546.6 53.9 reduce-scatter.5
  608.7 118.4 reduce-scatter.7

commit v10 on v9

--- a/solution.py
+++ b/solution.py
@@ -295,11 +295,6 @@
             done(i)
 
         every_piece(arrive)
-        if stagger:
-
-            @pl.when(sec == 0)
-            def _():
-                pl.semaphore_signal(turn, inc=1, device_id=mate, device_id_type=MESH)
 
     chunks = 5 if n_rows % (5 * 32) == 0 else 1
     chunk = n_rows // chunks
@@ -341,6 +336,12 @@
         flush(blocks - 1, (blocks - 1) % 2).wait()
     for copy in stores:
         copy.wait()
+
+    if stagger:
+
+        @pl.when(outer & (sec == 0))
+        def _():
+            pl.semaphore_signal(turn, inc=1, device_id=mate, device_id_type=MESH)
 
 
 def product_sum(arrays, job, weights, sides=(), stagger=False, key=1):

time: 845 us -> 840 us (level)
  no operation moved by 1% of the time
where the time goes in v10:
time: 840 us; the launch traced here: 836 us
  Pallas kernels  678 us (81%)
  matrix products  56.1 us (7%)
  local copies, waits for them, and re-layouts  32.3 us (4%)
  other arithmetic  25 us (3%)
  waiting for transfers between devices  24.4 us (3%)
  between operations  15.3 us (2%)
    pallas_call x8, Pallas kernels, product_sum(): pl.pallas_call(functools.partial(product_sum_kernel, (len(first), len(arr...  491 us
    pallas_call x2, Pallas kernels, attend_back(): pl.pallas_call(functools.partial(attend_back_kernel, rows, step), out_sha...  49.7 us
    pallas_call x2, Pallas kernels, attend(): pl.pallas_call(functools.partial(attend_kernel, rows, step), out_shape=(j...  35.2 us
    pallas_call x1, Pallas kernels, finish(): pl.pallas_call(finish_kernel, out_shape=(jax.ShapeDtypeStruct((rows, widt...  29.2 us
    dot_general x4, matrix products, dot_f32(): lax.dot_general(a, b, (((ca,), (cb,)), ((), ())), preferred_element_type=...  28.7 us
    pallas_call x2, Pallas kernels, gather_rows(): pl.pallas_call(functools.partial(gather_kernel, count), out_shape=(jax.Sh...  28.6 us
    pallas_call x2, Pallas kernels, scatter_rows(): pl.pallas_call(functools.partial(scatter_kernel, count), out_shape=jax.Sh...  27.6 us
    unnamed x62, local copies, waits for them, and re-layouts  24.3 us
  transfers between devices with their start and end apart: 10, of which 3 were waited for; matrix products, arithmetic and copies ran while one was open for 8% of the time, Pallas kernels for 73%

profile of v10, /device:TPU:1, one launch (start us, length us, event | category | flops | bytes accessed | tf_op | source)
XLA Modules:
  0.0 835.7 jit_solution(9293211280288404439)
XLA Ops:
  21.5 3.0 convert_bitcast_fusion.1
  25.3 4.1 collective-permute-done.1
  34.0 3.9 fusion.8
  43.1 3.1 select_convert_fusion.bias_ref
  46.2 17.0 %all-gather.5.cloned.1.call-done.w_hbm.refs_3_.refs_8_ = bf16[2048,1155]{1,0:T(8,128)(2,1)} async-done(((bf16[256,1155]{1,0:T(8,128)(2,1)}), bf16[2048,1155]{1,0:T(8,128)(2,1)}) %all-gather.5.cloned.1.call-update) | async-done | bytes 4730896 | tf_op jit(solution)/shard_map/all_gather | solution.py:1126
  67.3 13.2 %gather_rows.2 = (bf16[4,640,128]{2,1,0:T(8,128)(2,1)S(1)}, bf16[128,2560]{1,0:T(8,128)(2,1)S(1)}, f32[512,640]{1,0:T(8,128)S(1)}) custom-call(bf16[640,2048]{1,0:T(8,128)(2,1)S(1)} %fusion.10.normed_ref.refs_5_, bf16[2048,1155]{1,0:T(8,128)(2,1)S(1)} %copy-done.2, f32[640,128]{1,0:T(8,128)S(1)} %maximum_maximum_fusion.cos_ref, ...), custom_call_target="tpu_custom_call" | custom-call | flops 1 | bytes 1 | tf_op jit(solution)/shard_map/gather_rows/pallas_call | solution.py:456
  83.2 17.6 %attend.2 = (bf16[512,640]{1,0:T(8,128)(2,1)}, bf16[640,512]{1,0:T(8,128)(2,1)}, f32[4,5,1,256]{3,2,1,0:T(1,128)}) custom-call(s32[1]{0:T(128)} %bitcast.start_ref, f32[512,640]{1,0:T(8,128)} %copy-done.7, bf16[2560,128]{1,0:T(8,128)(2,1)} %bitcast.66, bf16[128,2560]{1,0:T(8,128)(2,1)} %copy-done.10, bf16[2560,640]{1,0:T(8,128)(2,1)} %select_convert_fusion.bias_ref, ...), custom_call_target="tpu_custom_call" | custom-call | flops 1 | bytes 1 | tf_op jit(solution)/shard_map/attend/pallas_call | solution.py:987
  101.8 90.7 %product_sum_1.1 = (f32[640,2048]{1,0:T(8,128)}, bf16[640,2048]{1,0:T(8,128)(2,1)}) custom-call(bf16[640,512]{1,0:T(8,128)(2,1)} %get-tuple-element.81.refs_0_.refs_7_, bf16[640,2048]{1,0:T(8,128)(2,1)} %get-tuple-element.201.refs_1_.refs_2_, f32[3,2048]{1,0:T(4,128)} %copy.101.refs_2_.refs_6_.refs_4_, ...), custom_call_target="tpu_custom_call" | custom-call | flops 1 | bytes 1 | tf_op jit(solution)/shard_map/product_sum_1/pallas_call | solution.py:371
  192.5 12.0 %fusion.2 = f32[640,2816]{1,0:T(8,128)S(1)} fusion(bf16[640,2048]{1,0:T(8,128)(2,1)} %get-tuple-element.82.refs_5_, bf16[2048,4224]{1,0:T(8,128)(2,1)} %all-gather.7.cloned.1.call-done.refs_3_.refs_7_), kind=kOutput, calls=%fused_computation.2 | convolution fusion | flops 7381975040 | bytes 21364736 | tf_op jit(solution)/shard_map/dot_general | solution.py:1074
  204.5 2.8 multiply_convert_fusion.5.refs_0_.refs_2_
  208.1 45.9 %product_sum_5.1 = (bf16[640,2048]{1,0:T(8,128)(2,1)}, bf16[640,2048]{1,0:T(8,128)(2,1)}) custom-call(bf16[640,1408]{1,0:T(8,128)(2,1)} %multiply_convert_fusion.5.refs_0_.refs_2_, f32[640,2048]{1,0:T(8,128)} %get-tuple-element.83.refs_1_.refs_3_, f32[3,2048]{1,0:T(4,128)} %copy.101.refs_2_.refs_6_.refs_4_, ...), custom_call_target="tpu_custom_call" | custom-call | flops 1 | bytes 1 | tf_op jit(solution)/shard_map/product_sum_5/pallas_call | solution.py:371
  258.3 15.3 %gather_rows.3 = (bf16[4,640,128]{2,1,0:T(8,128)(2,1)S(1)}, bf16[128,2560]{1,0:T(8,128)(2,1)S(1)}, f32[512,640]{1,0:T(8,128)S(1)}) custom-call(bf16[640,2048]{1,0:T(8,128)(2,1)S(1)} %copy-done.5, bf16[2048,1154]{1,0:T(8,128)(2,1)S(1)} %copy-done.3, f32[640,128]{1,0:T(8,128)S(1)} %maximum_maximum_fusion.cos_ref, f32[640,128]{1,0:T(8,128)S(1)} %get-tuple-element.198.sin_ref), custom_call_target="tpu_custom_call" | custom-call | flops 1 | bytes 1 | tf_op jit(solution)/shard_map/gather_rows/pallas_call | solution.py:456
  276.4 17.6 %attend.3 = (bf16[512,640]{1,0:T(8,128)(2,1)}, bf16[640,512]{1,0:T(8,128)(2,1)}, f32[4,5,1,256]{3,2,1,0:T(1,128)}) custom-call(s32[1]{0:T(128)} %bitcast.start_ref, f32[512,640]{1,0:T(8,128)} %copy-done.8, bf16[2560,128]{1,0:T(8,128)(2,1)} %bitcast.68, bf16[128,2560]{1,0:T(8,128)(2,1)} %copy-done.12, bf16[2560,640]{1,0:T(8,128)(2,1)} %select_convert_fusion.bias_ref, ...), custom_call_target="tpu_custom_call" | custom-call | flops 1 | bytes 1 | tf_op jit(solution)/shard_map/attend/pallas_call | solution.py:987
  296.0 44.2 %product_sum_2.1 = (f32[640,2048]{1,0:T(8,128)}, bf16[640,2048]{1,0:T(8,128)(2,1)}) custom-call(bf16[640,512]{1,0:T(8,128)(2,1)} %get-tuple-element.92.refs_0_.refs_7_, bf16[640,2048]{1,0:T(8,128)(2,1)} %get-tuple-element.86.refs_1_.refs_2_.out_zero, f32[2,2048]{1,0:T(2,128)} %copy.104.refs_2_.refs_6_.refs_4_, ...), custom_call_target="tpu_custom_call" | custom-call | flops 1 | bytes 1 | tf_op jit(solution)/shard_map/product_sum_2/pallas_call | solution.py:371
  340.3 12.1 %fusion = f32[640,2816]{1,0:T(8,128)S(1)} fusion(bf16[640,2048]{1,0:T(8,128)(2,1)} %get-tuple-element.93.refs_5_, bf16[2048,4224]{1,0:T(8,128)(2,1)} %all-gather.11.cloned.1.call-done.refs_7_.refs_2_), kind=kOutput, calls=%fused_computation | convolution fusion | flops 7381975040 | bytes 21364736 | tf_op jit(solution)/shard_map/dot_general | solution.py:1074
  352.4 9.8 %multiply_convert_fusion.2 = (bf16[640,1408]{1,0:T(8,128)(2,1)}, bf16[640,1408]{1,0:T(8,128)(2,1)}, bf16[640,1408]{1,0:T(8,128)(2,1)}) fusion(f32[640,2816]{1,0:T(8,128)S(1)} %fusion, bf16[640,2048]{1,0:T(8,128)(2,1)S(1)} %copy-done.14, bf16[2048,4224]{1,0:T(8,128)(2,1)} %all-gather.11.cloned.1.call-done.refs_7_.refs_2_), kind=kOutput, calls=%fused_computation.17 | convolution fusion | flops 3705405440 | bytes 21004288 | tf_op jit(solution)/shard_map/dot_general | solution.py:24
  362.2 60.6 %product_sum_8.1 = (f32[640,2048]{1,0:T(8,128)}, bf16[640,2048]{1,0:T(8,128)(2,1)}, f32[8,2048]{1,0:T(8,128)}, bf16[2048,4224]{1,0:T(8,128)(2,1)}) custom-call(bf16[640,1408]{1,0:T(8,128)(2,1)} %get-tuple-element.205.refs_0_, bf16[640,1408]{1,0:T(8,128)(2,1)} %get-tuple-element.204.refs_1_, bf16[640,1408]{1,0:T(8,128)(2,1)} %get-tuple-element.114.refs_2_.refs_0_, ...), custom_call_target="tpu_custom_call" | custom-call | flops 1 | bytes 1 | tf_op jit(solution)/shard_map/product_sum_8/pallas_call | solution.py:371
  424.6 4.3 fusion.18.do_ref
  428.9 24.9 %attend_back.2 = (bf16[640,512]{1,0:T(8,128)(2,1)}, bf16[2560,128]{1,0:T(8,128)(2,1)}) custom-call(s32[1]{0:T(128)} %bitcast.start_ref, f32[512,640]{1,0:T(8,128)} %copy-done.8, bf16[512,640]{1,0:T(8,128)(2,1)} %fusion.18.do_ref, bf16[512,640]{1,0:T(8,128)(2,1)} %get-tuple-element.97.o_ref, f32[4,5,1,256]{3,2,1,0:T(1,128)} %get-tuple-element.98.lse_ref, ...), custom_call_target="tpu_custom_call" | custom-call | flops 1 | bytes 1 | tf_op jit(solution)/shard_map/attend_back/pallas_call | solution.py:1023
  453.8 13.6 %scatter_rows.2.refs_1_ = bf16[640,128]{1,0:T(8,128)(2,1)} custom-call(bf16[4,640,128]{2,1,0:T(8,128)(2,1)} %bitcast.76, f32[640,128]{1,0:T(8,128)} %copy-done.6, f32[640,128]{1,0:T(8,128)} %get-tuple-element.199.sin_ref), custom_call_target="tpu_custom_call" | custom-call | flops 1 | bytes 1 | tf_op jit(solution)/shard_map/scatter_rows/pallas_call | solution.py:483
  467.4 59.6 %product_sum_7.1 = (f32[640,2048]{1,0:T(8,128)}, bf16[640,2048]{1,0:T(8,128)(2,1)}, f32[8,2048]{1,0:T(8,128)}, bf16[2048,1152]{1,0:T(8,128)(2,1)}) custom-call(bf16[640,512]{1,0:T(8,128)(2,1)} %get-tuple-element.99.refs_0_, bf16[640,128]{1,0:T(8,128)(2,1)} %scatter_rows.2.refs_1_, bf16[640,2048]{1,0:T(8,128)(2,1)} %get-tuple-element.86.refs_1_.refs_2_.out_zero, ...), custom_call_target="tpu_custom_call" | custom-call | flops 1 | bytes 1 | tf_op jit(solution)/shard_map/product_sum_7/pallas_call | solution.py:371
  528.7 10.3 %multiply_convert_fusion = (bf16[640,1408]{1,0:T(8,128)(2,1)}, bf16[640,1408]{1,0:T(8,128)(2,1)}) fusion(f32[640,2816]{1,0:T(8,128)} %copy-done.15, bf16[640,2048]{1,0:T(8,128)(2,1)S(1)} %copy-done.13, bf16[2048,4224]{1,0:T(8,128)(2,1)} %all-gather.7.cloned.1.call-done.refs_3_.refs_7_), kind=kOutput, calls=%fused_computation.15 | convolution fusion | flops 3702702080 | bytes 19202048 | tf_op jit(solution)/shard_map/dot_general | solution.py:24
  539.0 65.8 %product_sum_9.1 = (f32[640,2048]{1,0:T(8,128)}, bf16[640,2048]{1,0:T(8,128)(2,1)}, f32[8,2048]{1,0:T(8,128)}, bf16[2048,4224]{1,0:T(8,128)(2,1)}) custom-call(bf16[640,1408]{1,0:T(8,128)(2,1)} %get-tuple-element.203.refs_0_, bf16[640,1408]{1,0:T(8,128)(2,1)} %get-tuple-element.202.refs_1_, bf16[640,1408]{1,0:T(8,128)(2,1)} %multiply_convert_fusion.5.refs_0_.refs_2_, ...), custom_call_target="tpu_custom_call" | custom-call | flops 1 | bytes 1 | tf_op jit(solution)/shard_map/product_sum_9/pallas_call | solution.py:371
  606.7 4.3 fusion.15.do_ref
  611.0 24.9 %attend_back.3 = (bf16[640,512]{1,0:T(8,128)(2,1)}, bf16[2560,128]{1,0:T(8,128)(2,1)}) custom-call(s32[1]{0:T(128)} %bitcast.start_ref, f32[512,640]{1,0:T(8,128)} %copy-done.7, bf16[512,640]{1,0:T(8,128)(2,1)} %fusion.15.do_ref, bf16[512,640]{1,0:T(8,128)(2,1)} %get-tuple-element.106.o_ref, f32[4,5,1,256]{3,2,1,0:T(1,128)} %get-tuple-element.107.lse_ref, ...), custom_call_target="tpu_custom_call" | custom-call | flops 1 | bytes 1 | tf_op jit(solution)/shard_map/attend_back/pallas_call | solution.py:1023
  635.8 14.0 %scatter_rows.3.refs_1_ = bf16[640,128]{1,0:T(8,128)(2,1)} custom-call(bf16[4,640,128]{2,1,0:T(8,128)(2,1)} %bitcast.75, f32[640,128]{1,0:T(8,128)} %copy-done.6, f32[640,128]{1,0:T(8,128)} %get-tuple-element.199.sin_ref), custom_call_target="tpu_custom_call" | custom-call | flops 1 | bytes 1 | tf_op jit(solution)/shard_map/scatter_rows/pallas_call | solution.py:483
  649.9 64.3 %product_sum_11.1 = (f32[640,2048]{1,0:T(8,128)}, bf16[640,2048]{1,0:T(8,128)(2,1)}, f32[8,2048]{1,0:T(8,128)}, bf16[2048,1152]{1,0:T(8,128)(2,1)}) custom-call(bf16[640,512]{1,0:T(8,128)(2,1)} %get-tuple-element.110.refs_0_, bf16[640,128]{1,0:T(8,128)(2,1)} %scatter_rows.3.refs_1_, bf16[640,2048]{1,0:T(8,128)(2,1)} %get-tuple-element.201.refs_1_.refs_2_, ...), custom_call_target="tpu_custom_call" | custom-call | flops 1 | bytes 1 | tf_op jit(solution)/shard_map/product_sum_11/pallas_call | solution.py:371
  714.2 59.9 %product_sum_6.1.out_one = bf16[640,2048]{1,0:T(8,128)(2,1)} custom-call(bf16[640,1408]{1,0:T(8,128)(2,1)} %get-tuple-element.114.refs_2_.refs_0_, f32[640,2048]{1,0:T(8,128)} %get-tuple-element.95.refs_3_.refs_1_, bf16[2048,4224]{1,0:T(8,128)(2,1)} %all-gather.11.cloned.1.call-done.refs_7_.refs_2_), custom_call_target="tpu_custom_call" | custom-call | flops 1 | bytes 1 | tf_op jit(solution)/shard_map/product_sum_6/pallas_call | solution.py:371
  774.9 29.2 %finish.1 = (bf16[256,1152]{1,0:T(8,128)(2,1)}, f32[8,128]{1,0:T(8,128)}, bf16[640,2048]{1,0:T(8,128)(2,1)}, bf16[640,2048]{1,0:T(8,128)(2,1)}, bf16[256,4224]{1,0:T(8,128)(2,1)}, /*index=5*/bf16[256,1152]{1,0:T(8,128)(2,1)}) custom-call(bf16[8,256,1152]{2,1,0:T(8,128)(2,1)} %bitcast.71, f32[2,4,8,128]{3,2,1,0:T(8,128)} %reshape.82.gain_ref, ...), custom_call_target="tpu_custom_call" | custom-call | flops 1 | bytes 1 | tf_op jit(solution)/shard_map/finish/pallas_call | solution.py:617
  804.1 10.3 %write_results.1 = (bf16[2,640,2048]{2,1,0:T(8,128)(2,1)}, f32[2,640,2048]{2,1,0:T(8,128)}, f32[512,512]{1,0:T(8,128)}, f32[512,64]{1,0:T(8,128)}, f32[512,64]{1,0:T(8,128)}, /*index=5*/f32[512,512]{1,0:T(8,128)}) custom-call(bf16[640,2048]{1,0:T(8,128)(2,1)} %get-tuple-element.86.refs_1_.refs_2_.out_zero, bf16[640,2048]{1,0:T(8,128)(2,1)} %product_sum_6.1.out_one, ...), custom_call_target="tpu_custom_call" | custom-call | flops 1 | bytes 1 | tf_op jit(solution)/shard_map/write_results/pallas_call | solution.py:791
  814.4 3.7 collective-permute-start.2
  822.1 6.2 write_mlp.1
  (133 shorter events, 52.3 us)
Async XLA Ops:
  7.2 26.8 %copy-start = (s32[2,13]{1,0:T(2,128)S(1)}, s32[2,13]{1,0:T(2,128)}, u32[]{:S(2)}) copy-start(s32[2,13]{1,0:T(2,128)} %param.18) | copy-start | bytes 316
  7.2 55.9 %all-gather.5.cloned.1.call-start = ((), (), s32[]{:S(2)}) async-start(), calls=%async_computation.3 | async-start | bytes 5898240 | tf_op jit(solution)/shard_map/all_gather | solution.py:1126
  15.8 2.1 collective-permute-start
  18.3 6.3 copy-start.16
  19.3 173.2 %all-gather.7.cloned.1.call-start = ((), (), s32[]{:S(2)}) async-start(), calls=%async_computation.4 | async-start | bytes 19464192 | tf_op jit(solution)/shard_map/all_gather | solution.py:1126
  25.1 4.3 collective-permute-start.1
  31.9 1.7 copy-start.23
  31.9 1.8 copy-start.24
  31.9 222.0 %all-gather.9.cloned.1.call-start = ((), (), s32[]{:S(2)}) async-start(), calls=%async_computation.5 | async-start | bytes 5898240 | tf_op jit(solution)/shard_map/all_gather | solution.py:1126
  32.7 307.6 %all-gather.11.cloned.1.call-start = ((), (), s32[]{:S(2)}) async-start(), calls=%async_computation.6 | async-start | bytes 19464192 | tf_op jit(solution)/shard_map/all_gather | solution.py:1126
  32.7 8.7 %slice-start = ((s8[5242880]{0:T(1024)(128)(4,1)}), s8[1048576]{0:T(1024)(128)(4,1)S(1)}, s32[]{:S(2)}) async-start(s8[5242880]{0:T(1024)(128)(4,1)} %bitcast.73), calls=%async_computation.10 | async-start | bytes 2097152
  33.2 572.5 %reduce-scatter.4.cloned.1.call-start = ((), (), s32[]{:S(2)}) async-start(), calls=%async_computation.7 | async-start | bytes 19464192 | tf_op jit(solution)/shard_map/reduce_scatter | solution.py:1089
  34.0 7.4 slice-start.1
  40.5 213.5 %copy-start.6 = (f32[640,128]{1,0:T(8,128)}, f32[640,128]{1,0:T(8,128)S(1)}, u32[]{:S(2)}) copy-start(f32[640,128]{1,0:T(8,128)S(1)} %maximum_maximum_fusion.cos_ref) | copy-start | bytes 983044
  63.1 4.1 copy-start.2
  67.2 13.2 %copy-start.4 = (bf16[640,2048]{1,0:T(8,128)(2,1)}, bf16[640,2048]{1,0:T(8,128)(2,1)S(1)}, u32[]{:S(2)}) copy-start(bf16[640,2048]{1,0:T(8,128)(2,1)S(1)} %fusion.10.normed_ref.refs_5_) | copy-start | bytes 7864324
  80.5 1.1 copy-start.7
  204.5 3.5 copy-start.15
  254.0 2.5 copy-start.3
  256.5 1.8 copy-start.5
  273.7 1.1 copy-start.8
  340.3 12.1 %copy-start.14 = (bf16[640,2048]{1,0:T(8,128)(2,1)S(1)}, bf16[640,2048]{1,0:T(8,128)(2,1)}, u32[]{:S(2)}) copy-start(bf16[640,2048]{1,0:T(8,128)(2,1)} %dynamic-slice_bitcast_fusion.refs_4_) | copy-start | bytes 7864324
  422.8 1.7 copy-start.18
  422.9 227.0 %reduce-scatter.6.cloned.1.call-start = ((), (), s32[]{:S(2)}) async-start(), calls=%async_computation.8 | async-start | bytes 5308416 | tf_op jit(solution)/shard_map/reduce_scatter | solution.py:1089
  527.0 1.7 copy-start.13
  527.0 287.4 %reduce-scatter.8.cloned.1.call-start = ((), (), s32[]{:S(2)}) async-start(), calls=%async_computation.9 | async-start | bytes 19464192 | tf_op jit(solution)/shard_map/reduce_scatter | solution.py:1089
  604.8 0.9 copy-start.21
  604.8 1.8 copy-start.17
  714.2 59.9 %copy-start.22 = (f32[8,2048]{1,0:T(8,128)S(1)}, f32[8,2048]{1,0:T(8,128)}, u32[]{:S(2)}) copy-start(f32[8,2048]{1,0:T(8,128)} %get-tuple-element.116) | copy-start | bytes 196612
  804.1 17.4 %copy-start.25 = (f32[8,128]{1,0:T(8,128)S(1)}, f32[8,128]{1,0:T(8,128)}, u32[]{:S(2)}) copy-start(f32[8,128]{1,0:T(8,128)} %get-tuple-element.133) | copy-start | bytes 12292
  814.4 7.7 collective-permute-start.2
  822.1 6.2 copy-start.1
  (6 other events, 5.0 us)
Sparse Core Ops, SparseCore 0:
  19.4 43.6 all-gather.4
  65.6 93.5 all-gather.6
  161.1 41.1 all-gather.8
  204.0 99.0 all-gather.10
  423.0 117.8 reduce-scatter.3
  544.6 53.8 reduce-scatter.5
  605.0 118.3 reduce-scatter.7

commit v11 on v10

--- a/solution.py
+++ b/solution.py
@@ -106,7 +106,7 @@
     blocks = pieces // per_block
     n_rows = p_buf.shape[1]
     early = len(xs)
-    lag = 2
+    lag = 1
     assert xs[0] == 0
 
     t = lax.axis_index("tensor")

time: 840 us -> 841 us (level)
  no operation moved by 1% of the time
where the time goes in v11:
time: 841 us; the launch traced here: 835 us
  Pallas kernels  678 us (81%)
  matrix products  56.1 us (7%)
  local copies, waits for them, and re-layouts  32.3 us (4%)
  other arithmetic  25 us (3%)
  waiting for transfers between devices  24.4 us (3%)
  between operations  15.3 us (2%)
    pallas_call x8, Pallas kernels, product_sum(): pl.pallas_call(functools.partial(product_sum_kernel, (len(first), len(arr...  491 us
    pallas_call x2, Pallas kernels, attend_back(): pl.pallas_call(functools.partial(attend_back_kernel, rows, step), out_sha...  49.7 us
    pallas_call x2, Pallas kernels, attend(): pl.pallas_call(functools.partial(attend_kernel, rows, step), out_shape=(j...  35.2 us
    pallas_call x1, Pallas kernels, finish(): pl.pallas_call(finish_kernel, out_shape=(jax.ShapeDtypeStruct((rows, widt...  29.3 us
    dot_general x4, matrix products, dot_f32(): lax.dot_general(a, b, (((ca,), (cb,)), ((), ())), preferred_element_type=...  28.7 us
    pallas_call x2, Pallas kernels, gather_rows(): pl.pallas_call(functools.partial(gather_kernel, count), out_shape=(jax.Sh...  28.6 us
    pallas_call x2, Pallas kernels, scatter_rows(): pl.pallas_call(functools.partial(scatter_kernel, count), out_shape=jax.Sh...  27.1 us
    unnamed x62, local copies, waits for them, and re-layouts  24.3 us
  transfers between devices with their start and end apart: 10, of which 3 were waited for; matrix products, arithmetic and copies ran while one was open for 8% of the time, Pallas kernels for 73%

profile of v11, /device:TPU:1, one launch (start us, length us, event | category | flops | bytes accessed | tf_op | source)
XLA Modules:
  0.0 835.5 jit_solution(12460100300836555965)
XLA Ops:
  21.5 3.0 convert_bitcast_fusion.1
  25.3 4.1 collective-permute-done.1
  34.0 3.9 fusion.8
  43.1 3.1 select_convert_fusion.bias_ref
  46.2 17.0 %all-gather.5.cloned.1.call-done.w_hbm.refs_3_.refs_8_ = bf16[2048,1155]{1,0:T(8,128)(2,1)} async-done(((bf16[256,1155]{1,0:T(8,128)(2,1)}), bf16[2048,1155]{1,0:T(8,128)(2,1)}) %all-gather.5.cloned.1.call-update) | async-done | bytes 4730896 | tf_op jit(solution)/shard_map/all_gather | solution.py:1126
  67.3 13.2 %gather_rows.2 = (bf16[4,640,128]{2,1,0:T(8,128)(2,1)S(1)}, bf16[128,2560]{1,0:T(8,128)(2,1)S(1)}, f32[512,640]{1,0:T(8,128)S(1)}) custom-call(bf16[640,2048]{1,0:T(8,128)(2,1)S(1)} %fusion.10.normed_ref.refs_5_, bf16[2048,1155]{1,0:T(8,128)(2,1)S(1)} %copy-done.2, f32[640,128]{1,0:T(8,128)S(1)} %maximum_maximum_fusion.cos_ref, ...), custom_call_target="tpu_custom_call" | custom-call | flops 1 | bytes 1 | tf_op jit(solution)/shard_map/gather_rows/pallas_call | solution.py:456
  83.2 17.6 %attend.2 = (bf16[512,640]{1,0:T(8,128)(2,1)}, bf16[640,512]{1,0:T(8,128)(2,1)}, f32[4,5,1,256]{3,2,1,0:T(1,128)}) custom-call(s32[1]{0:T(128)} %bitcast.start_ref, f32[512,640]{1,0:T(8,128)} %copy-done.7, bf16[2560,128]{1,0:T(8,128)(2,1)} %bitcast.66, bf16[128,2560]{1,0:T(8,128)(2,1)} %copy-done.10, bf16[2560,640]{1,0:T(8,128)(2,1)} %select_convert_fusion.bias_ref, ...), custom_call_target="tpu_custom_call" | custom-call | flops 1 | bytes 1 | tf_op jit(solution)/shard_map/attend/pallas_call | solution.py:987
  101.8 90.7 %product_sum_1.1 = (f32[640,2048]{1,0:T(8,128)}, bf16[640,2048]{1,0:T(8,128)(2,1)}) custom-call(bf16[640,512]{1,0:T(8,128)(2,1)} %get-tuple-element.81.refs_0_.refs_7_, bf16[640,2048]{1,0:T(8,128)(2,1)} %get-tuple-element.201.refs_1_.refs_2_, f32[3,2048]{1,0:T(4,128)} %copy.101.refs_2_.refs_6_.refs_4_, ...), custom_call_target="tpu_custom_call" | custom-call | flops 1 | bytes 1 | tf_op jit(solution)/shard_map/product_sum_1/pallas_call | solution.py:371
  192.5 12.0 %fusion.2 = f32[640,2816]{1,0:T(8,128)S(1)} fusion(bf16[640,2048]{1,0:T(8,128)(2,1)} %get-tuple-element.82.refs_5_, bf16[2048,4224]{1,0:T(8,128)(2,1)} %all-gather.7.cloned.1.call-done.refs_3_.refs_7_), kind=kOutput, calls=%fused_computation.2 | convolution fusion | flops 7381975040 | bytes 21364736 | tf_op jit(solution)/shard_map/dot_general | solution.py:1074
  204.5 2.8 multiply_convert_fusion.5.refs_0_.refs_2_
  208.1 45.9 %product_sum_5.1 = (bf16[640,2048]{1,0:T(8,128)(2,1)}, bf16[640,2048]{1,0:T(8,128)(2,1)}) custom-call(bf16[640,1408]{1,0:T(8,128)(2,1)} %multiply_convert_fusion.5.refs_0_.refs_2_, f32[640,2048]{1,0:T(8,128)} %get-tuple-element.83.refs_1_.refs_3_, f32[3,2048]{1,0:T(4,128)} %copy.101.refs_2_.refs_6_.refs_4_, ...), custom_call_target="tpu_custom_call" | custom-call | flops 1 | bytes 1 | tf_op jit(solution)/shard_map/product_sum_5/pallas_call | solution.py:371
  258.3 15.3 %gather_rows.3 = (bf16[4,640,128]{2,1,0:T(8,128)(2,1)S(1)}, bf16[128,2560]{1,0:T(8,128)(2,1)S(1)}, f32[512,640]{1,0:T(8,128)S(1)}) custom-call(bf16[640,2048]{1,0:T(8,128)(2,1)S(1)} %copy-done.5, bf16[2048,1154]{1,0:T(8,128)(2,1)S(1)} %copy-done.3, f32[640,128]{1,0:T(8,128)S(1)} %maximum_maximum_fusion.cos_ref, f32[640,128]{1,0:T(8,128)S(1)} %get-tuple-element.198.sin_ref), custom_call_target="tpu_custom_call" | custom-call | flops 1 | bytes 1 | tf_op jit(solution)/shard_map/gather_rows/pallas_call | solution.py:456
  276.4 17.6 %attend.3 = (bf16[512,640]{1,0:T(8,128)(2,1)}, bf16[640,512]{1,0:T(8,128)(2,1)}, f32[4,5,1,256]{3,2,1,0:T(1,128)}) custom-call(s32[1]{0:T(128)} %bitcast.start_ref, f32[512,640]{1,0:T(8,128)} %copy-done.8, bf16[2560,128]{1,0:T(8,128)(2,1)} %bitcast.68, bf16[128,2560]{1,0:T(8,128)(2,1)} %copy-done.12, bf16[2560,640]{1,0:T(8,128)(2,1)} %select_convert_fusion.bias_ref, ...), custom_call_target="tpu_custom_call" | custom-call | flops 1 | bytes 1 | tf_op jit(solution)/shard_map/attend/pallas_call | solution.py:987
  296.0 44.2 %product_sum_2.1 = (f32[640,2048]{1,0:T(8,128)}, bf16[640,2048]{1,0:T(8,128)(2,1)}) custom-call(bf16[640,512]{1,0:T(8,128)(2,1)} %get-tuple-element.92.refs_0_.refs_7_, bf16[640,2048]{1,0:T(8,128)(2,1)} %get-tuple-element.86.refs_1_.refs_2_.out_zero, f32[2,2048]{1,0:T(2,128)} %copy.104.refs_2_.refs_6_.refs_4_, ...), custom_call_target="tpu_custom_call" | custom-call | flops 1 | bytes 1 | tf_op jit(solution)/shard_map/product_sum_2/pallas_call | solution.py:371
  340.3 12.1 %fusion = f32[640,2816]{1,0:T(8,128)S(1)} fusion(bf16[640,2048]{1,0:T(8,128)(2,1)} %get-tuple-element.93.refs_5_, bf16[2048,4224]{1,0:T(8,128)(2,1)} %all-gather.11.cloned.1.call-done.refs_7_.refs_2_), kind=kOutput, calls=%fused_computation | convolution fusion | flops 7381975040 | bytes 21364736 | tf_op jit(solution)/shard_map/dot_general | solution.py:1074
  352.4 9.8 %multiply_convert_fusion.2 = (bf16[640,1408]{1,0:T(8,128)(2,1)}, bf16[640,1408]{1,0:T(8,128)(2,1)}, bf16[640,1408]{1,0:T(8,128)(2,1)}) fusion(f32[640,2816]{1,0:T(8,128)S(1)} %fusion, bf16[640,2048]{1,0:T(8,128)(2,1)S(1)} %copy-done.14, bf16[2048,4224]{1,0:T(8,128)(2,1)} %all-gather.11.cloned.1.call-done.refs_7_.refs_2_), kind=kOutput, calls=%fused_computation.17 | convolution fusion | flops 3705405440 | bytes 21004288 | tf_op jit(solution)/shard_map/dot_general | solution.py:24
  362.2 61.0 %product_sum_8.1 = (f32[640,2048]{1,0:T(8,128)}, bf16[640,2048]{1,0:T(8,128)(2,1)}, f32[8,2048]{1,0:T(8,128)}, bf16[2048,4224]{1,0:T(8,128)(2,1)}) custom-call(bf16[640,1408]{1,0:T(8,128)(2,1)} %get-tuple-element.205.refs_0_, bf16[640,1408]{1,0:T(8,128)(2,1)} %get-tuple-element.204.refs_1_, bf16[640,1408]{1,0:T(8,128)(2,1)} %get-tuple-element.114.refs_2_.refs_0_, ...), custom_call_target="tpu_custom_call" | custom-call | flops 1 | bytes 1 | tf_op jit(solution)/shard_map/product_sum_8/pallas_call | solution.py:371
  424.9 4.3 fusion.18.do_ref
  429.3 24.9 %attend_back.2 = (bf16[640,512]{1,0:T(8,128)(2,1)}, bf16[2560,128]{1,0:T(8,128)(2,1)}) custom-call(s32[1]{0:T(128)} %bitcast.start_ref, f32[512,640]{1,0:T(8,128)} %copy-done.8, bf16[512,640]{1,0:T(8,128)(2,1)} %fusion.18.do_ref, bf16[512,640]{1,0:T(8,128)(2,1)} %get-tuple-element.97.o_ref, f32[4,5,1,256]{3,2,1,0:T(1,128)} %get-tuple-element.98.lse_ref, ...), custom_call_target="tpu_custom_call" | custom-call | flops 1 | bytes 1 | tf_op jit(solution)/shard_map/attend_back/pallas_call | solution.py:1023
  454.1 13.6 %scatter_rows.2.refs_1_ = bf16[640,128]{1,0:T(8,128)(2,1)} custom-call(bf16[4,640,128]{2,1,0:T(8,128)(2,1)} %bitcast.76, f32[640,128]{1,0:T(8,128)} %copy-done.6, f32[640,128]{1,0:T(8,128)} %get-tuple-element.199.sin_ref), custom_call_target="tpu_custom_call" | custom-call | flops 1 | bytes 1 | tf_op jit(solution)/shard_map/scatter_rows/pallas_call | solution.py:483
  467.8 59.6 %product_sum_7.1 = (f32[640,2048]{1,0:T(8,128)}, bf16[640,2048]{1,0:T(8,128)(2,1)}, f32[8,2048]{1,0:T(8,128)}, bf16[2048,1152]{1,0:T(8,128)(2,1)}) custom-call(bf16[640,512]{1,0:T(8,128)(2,1)} %get-tuple-element.99.refs_0_, bf16[640,128]{1,0:T(8,128)(2,1)} %scatter_rows.2.refs_1_, bf16[640,2048]{1,0:T(8,128)(2,1)} %get-tuple-element.86.refs_1_.refs_2_.out_zero, ...), custom_call_target="tpu_custom_call" | custom-call | flops 1 | bytes 1 | tf_op jit(solution)/shard_map/product_sum_7/pallas_call | solution.py:371
  529.1 10.3 %multiply_convert_fusion = (bf16[640,1408]{1,0:T(8,128)(2,1)}, bf16[640,1408]{1,0:T(8,128)(2,1)}) fusion(f32[640,2816]{1,0:T(8,128)} %copy-done.15, bf16[640,2048]{1,0:T(8,128)(2,1)S(1)} %copy-done.13, bf16[2048,4224]{1,0:T(8,128)(2,1)} %all-gather.7.cloned.1.call-done.refs_3_.refs_7_), kind=kOutput, calls=%fused_computation.15 | convolution fusion | flops 3702702080 | bytes 19202048 | tf_op jit(solution)/shard_map/dot_general | solution.py:24
  539.4 65.7 %product_sum_9.1 = (f32[640,2048]{1,0:T(8,128)}, bf16[640,2048]{1,0:T(8,128)(2,1)}, f32[8,2048]{1,0:T(8,128)}, bf16[2048,4224]{1,0:T(8,128)(2,1)}) custom-call(bf16[640,1408]{1,0:T(8,128)(2,1)} %get-tuple-element.203.refs_0_, bf16[640,1408]{1,0:T(8,128)(2,1)} %get-tuple-element.202.refs_1_, bf16[640,1408]{1,0:T(8,128)(2,1)} %multiply_convert_fusion.5.refs_0_.refs_2_, ...), custom_call_target="tpu_custom_call" | custom-call | flops 1 | bytes 1 | tf_op jit(solution)/shard_map/product_sum_9/pallas_call | solution.py:371
  607.0 4.3 fusion.15.do_ref
  611.3 24.9 %attend_back.3 = (bf16[640,512]{1,0:T(8,128)(2,1)}, bf16[2560,128]{1,0:T(8,128)(2,1)}) custom-call(s32[1]{0:T(128)} %bitcast.start_ref, f32[512,640]{1,0:T(8,128)} %copy-done.7, bf16[512,640]{1,0:T(8,128)(2,1)} %fusion.15.do_ref, bf16[512,640]{1,0:T(8,128)(2,1)} %get-tuple-element.106.o_ref, f32[4,5,1,256]{3,2,1,0:T(1,128)} %get-tuple-element.107.lse_ref, ...), custom_call_target="tpu_custom_call" | custom-call | flops 1 | bytes 1 | tf_op jit(solution)/shard_map/attend_back/pallas_call | solution.py:1023
  636.2 13.4 %scatter_rows.3.refs_1_ = bf16[640,128]{1,0:T(8,128)(2,1)} custom-call(bf16[4,640,128]{2,1,0:T(8,128)(2,1)} %bitcast.75, f32[640,128]{1,0:T(8,128)} %copy-done.6, f32[640,128]{1,0:T(8,128)} %get-tuple-element.199.sin_ref), custom_call_target="tpu_custom_call" | custom-call | flops 1 | bytes 1 | tf_op jit(solution)/shard_map/scatter_rows/pallas_call | solution.py:483
  649.6 64.3 %product_sum_11.1 = (f32[640,2048]{1,0:T(8,128)}, bf16[640,2048]{1,0:T(8,128)(2,1)}, f32[8,2048]{1,0:T(8,128)}, bf16[2048,1152]{1,0:T(8,128)(2,1)}) custom-call(bf16[640,512]{1,0:T(8,128)(2,1)} %get-tuple-element.110.refs_0_, bf16[640,128]{1,0:T(8,128)(2,1)} %scatter_rows.3.refs_1_, bf16[640,2048]{1,0:T(8,128)(2,1)} %get-tuple-element.201.refs_1_.refs_2_, ...), custom_call_target="tpu_custom_call" | custom-call | flops 1 | bytes 1 | tf_op jit(solution)/shard_map/product_sum_11/pallas_call | solution.py:371
  714.0 59.8 %product_sum_6.1.out_one = bf16[640,2048]{1,0:T(8,128)(2,1)} custom-call(bf16[640,1408]{1,0:T(8,128)(2,1)} %get-tuple-element.114.refs_2_.refs_0_, f32[640,2048]{1,0:T(8,128)} %get-tuple-element.95.refs_3_.refs_1_, bf16[2048,4224]{1,0:T(8,128)(2,1)} %all-gather.11.cloned.1.call-done.refs_7_.refs_2_), custom_call_target="tpu_custom_call" | custom-call | flops 1 | bytes 1 | tf_op jit(solution)/shard_map/product_sum_6/pallas_call | solution.py:371
  774.6 29.3 %finish.1 = (bf16[256,1152]{1,0:T(8,128)(2,1)}, f32[8,128]{1,0:T(8,128)}, bf16[640,2048]{1,0:T(8,128)(2,1)}, bf16[640,2048]{1,0:T(8,128)(2,1)}, bf16[256,4224]{1,0:T(8,128)(2,1)}, /*index=5*/bf16[256,1152]{1,0:T(8,128)(2,1)}) custom-call(bf16[8,256,1152]{2,1,0:T(8,128)(2,1)} %bitcast.71, f32[2,4,8,128]{3,2,1,0:T(8,128)} %reshape.82.gain_ref, ...), custom_call_target="tpu_custom_call" | custom-call | flops 1 | bytes 1 | tf_op jit(solution)/shard_map/finish/pallas_call | solution.py:617
  803.9 10.3 %write_results.1 = (bf16[2,640,2048]{2,1,0:T(8,128)(2,1)}, f32[2,640,2048]{2,1,0:T(8,128)}, f32[512,512]{1,0:T(8,128)}, f32[512,64]{1,0:T(8,128)}, f32[512,64]{1,0:T(8,128)}, /*index=5*/f32[512,512]{1,0:T(8,128)}) custom-call(bf16[640,2048]{1,0:T(8,128)(2,1)} %get-tuple-element.86.refs_1_.refs_2_.out_zero, bf16[640,2048]{1,0:T(8,128)(2,1)} %product_sum_6.1.out_one, ...), custom_call_target="tpu_custom_call" | custom-call | flops 1 | bytes 1 | tf_op jit(solution)/shard_map/write_results/pallas_call | solution.py:791
  814.2 3.7 collective-permute-start.2
  821.9 6.2 write_mlp.1
  (133 shorter events, 52.3 us)
Async XLA Ops:
  7.2 26.8 %copy-start = (s32[2,13]{1,0:T(2,128)S(1)}, s32[2,13]{1,0:T(2,128)}, u32[]{:S(2)}) copy-start(s32[2,13]{1,0:T(2,128)} %param.18) | copy-start | bytes 316
  7.2 55.9 %all-gather.5.cloned.1.call-start = ((), (), s32[]{:S(2)}) async-start(), calls=%async_computation.3 | async-start | bytes 5898240 | tf_op jit(solution)/shard_map/all_gather | solution.py:1126
  15.8 2.1 collective-permute-start
  18.3 6.3 copy-start.16
  19.3 173.2 %all-gather.7.cloned.1.call-start = ((), (), s32[]{:S(2)}) async-start(), calls=%async_computation.4 | async-start | bytes 19464192 | tf_op jit(solution)/shard_map/all_gather | solution.py:1126
  25.1 4.3 collective-permute-start.1
  31.9 1.7 copy-start.23
  31.9 1.8 copy-start.24
  31.9 222.0 %all-gather.9.cloned.1.call-start = ((), (), s32[]{:S(2)}) async-start(), calls=%async_computation.5 | async-start | bytes 5898240 | tf_op jit(solution)/shard_map/all_gather | solution.py:1126
  32.7 307.6 %all-gather.11.cloned.1.call-start = ((), (), s32[]{:S(2)}) async-start(), calls=%async_computation.6 | async-start | bytes 19464192 | tf_op jit(solution)/shard_map/all_gather | solution.py:1126
  32.7 8.7 %slice-start = ((s8[5242880]{0:T(1024)(128)(4,1)}), s8[1048576]{0:T(1024)(128)(4,1)S(1)}, s32[]{:S(2)}) async-start(s8[5242880]{0:T(1024)(128)(4,1)} %bitcast.73), calls=%async_computation.10 | async-start | bytes 2097152
  33.2 572.8 %reduce-scatter.4.cloned.1.call-start = ((), (), s32[]{:S(2)}) async-start(), calls=%async_computation.7 | async-start | bytes 19464192 | tf_op jit(solution)/shard_map/reduce_scatter | solution.py:1089
  34.0 7.4 slice-start.1
  40.5 213.5 %copy-start.6 = (f32[640,128]{1,0:T(8,128)}, f32[640,128]{1,0:T(8,128)S(1)}, u32[]{:S(2)}) copy-start(f32[640,128]{1,0:T(8,128)S(1)} %maximum_maximum_fusion.cos_ref) | copy-start | bytes 983044
  63.1 4.1 copy-start.2
  67.2 13.2 %copy-start.4 = (bf16[640,2048]{1,0:T(8,128)(2,1)}, bf16[640,2048]{1,0:T(8,128)(2,1)S(1)}, u32[]{:S(2)}) copy-start(bf16[640,2048]{1,0:T(8,128)(2,1)S(1)} %fusion.10.normed_ref.refs_5_) | copy-start | bytes 7864324
  80.5 1.1 copy-start.7
  204.5 3.5 copy-start.15
  254.0 2.5 copy-start.3
  256.5 1.8 copy-start.5
  273.7 1.1 copy-start.8
  340.3 12.1 %copy-start.14 = (bf16[640,2048]{1,0:T(8,128)(2,1)S(1)}, bf16[640,2048]{1,0:T(8,128)(2,1)}, u32[]{:S(2)}) copy-start(bf16[640,2048]{1,0:T(8,128)(2,1)} %dynamic-slice_bitcast_fusion.refs_4_) | copy-start | bytes 7864324
  423.2 1.7 copy-start.18
  423.2 226.4 %reduce-scatter.6.cloned.1.call-start = ((), (), s32[]{:S(2)}) async-start(), calls=%async_computation.8 | async-start | bytes 5308416 | tf_op jit(solution)/shard_map/reduce_scatter | solution.py:1089
  527.3 1.7 copy-start.13
  527.4 286.8 %reduce-scatter.8.cloned.1.call-start = ((), (), s32[]{:S(2)}) async-start(), calls=%async_computation.9 | async-start | bytes 19464192 | tf_op jit(solution)/shard_map/reduce_scatter | solution.py:1089
  605.2 0.9 copy-start.21
  605.2 1.8 copy-start.17
  714.0 59.8 %copy-start.22 = (f32[8,2048]{1,0:T(8,128)S(1)}, f32[8,2048]{1,0:T(8,128)}, u32[]{:S(2)}) copy-start(f32[8,2048]{1,0:T(8,128)} %get-tuple-element.116) | copy-start | bytes 196612
  803.9 17.4 %copy-start.25 = (f32[8,128]{1,0:T(8,128)S(1)}, f32[8,128]{1,0:T(8,128)}, u32[]{:S(2)}) copy-start(f32[8,128]{1,0:T(8,128)} %get-tuple-element.133) | copy-start | bytes 12292
  814.2 7.7 collective-permute-start.2
  821.9 6.2 copy-start.1
  (6 other events, 5.0 us)
Sparse Core Ops, SparseCore 0:
  19.4 43.6 all-gather.4
  65.6 93.5 all-gather.6
  161.1 41.1 all-gather.8
  204.0 99.0 all-gather.10
  423.3 117.8 reduce-scatter.3
  545.0 53.9 reduce-scatter.5
  605.3 117.8 reduce-scatter.7
